TPU v7x, 32 devices: a whole 2x2x4 slice. The times are simulated.
32 devices in a mesh: dp: 16 (over z, x, core), tensor: 2 (over y).
Axes of the slice: x: 2, y: 2, z: 4, core: 2. Of those that a mesh axis runs over, the one named last changes fastest.
Arguments:
- block_input: float32 [1024, 16, 1024], P('tensor', 'dp'), may hold values from -6 to 6, as said below
- segment_ids: int32 [16, 1024], P('dp'), may hold values from 0 to 2, never falling along the last dimension, each value on 1 to 512 neighbouring positions
- random_blocks: int32 [16, 16, 16, 3], P('dp', 'tensor'), may hold values from 0 to 15
- w_qkv: float32 [2, 3, 1024, 1024], P(None, None, None, 'tensor'), may hold values from -0.125 to 0.125, as said below
- b_qv: float32 [2, 2, 1024], P(None, None, 'tensor'), may hold values from -3 to 3
- w_out: float32 [2, 1024, 1024], P(None, 'tensor'), may hold values from -3 to 3
- b_out: float32 [2, 1024], replicated, may hold values from -3 to 3
- w_in: float32 [2, 1024, 4096], P(None, None, 'tensor'), may hold values from -0.1875 to 0.1875
- b_in: float32 [2, 4096], P(None, 'tensor'), may hold values from -3 to 3
- w_down: float32 [2, 4096, 1024], P(None, 'tensor'), may hold values from -0.09375 to 0.09375
- b_down: float32 [2, 1024], replicated, may hold values from -3 to 3
- ln_gain: float32 [2, 2, 1024], replicated, may hold values from 0.5 to 1.5
- ln_bias: float32 [2, 2, 1024], replicated, may hold values from -2 to 2
- cotangent: float32 [1024, 16, 1024], P('tensor', 'dp'), may hold values from -6 to 6
Outputs:
- block_output: float32 [1024, 16, 1024], P('tensor', 'dp')
- input_grad: float32 [1024, 16, 1024], P('tensor', 'dp')
- grad_w_qkv: float32 [2, 3, 1024, 1024], P(None, None, None, 'tensor')
- grad_b_qv: float32 [2, 2, 1024], P(None, None, 'tensor')
- grad_w_out: float32 [2, 1024, 1024], P(None, 'tensor')
- grad_b_out: float32 [2, 1024], replicated
- grad_w_in: float32 [2, 1024, 4096], P(None, None, 'tensor')
- grad_b_in: float32 [2, 4096], P(None, 'tensor')
- grad_w_down: float32 [2, 4096, 1024], P(None, 'tensor')
- grad_b_down: float32 [2, 1024], replicated
- grad_ln_gain: float32 [2, 2, 1024], replicated
- grad_ln_bias: float32 [2, 2, 1024], replicated
Inputs may be any that keep to these rules, and one draw needn't show every extreme that they name: `segment_ids`: along each sequence the numbers never fall; each of 0 to 2 appears, on at most 512 positions. `block_input`: independent entries of mean 0 and deviation about 1. `w_qkv`: independent entries of mean 0 and deviation about 1 / sqrt(1024).
All inputs are finite; a program needn't handle non-finite values.
Results may differ from a plain program's by a relative error of at most 0.02.
Values may be sent and summed in bfloat16 or wider, within the bound.
A program may use at most 448 MiB of HBM per device.

v0:
```python
import jax
import jax.numpy as jnp
from jax import lax
from jax.sharding import PartitionSpec as P

HEAD_DIM = 64


def as_sent(array):

    def short(part):
        return part.astype(jnp.bfloat16) if part.dtype == jnp.float32 else part

    return jax.tree.map(short, array)


def norm_rows(values, gain_row, shift_row):
    row_mean = jnp.mean(values, axis=-1, keepdims=True)
    centred = values - row_mean
    variance = jnp.mean(centred * centred, axis=-1, keepdims=True)
    return centred * lax.rsqrt(variance + 1e-06) * gain_row + shift_row


def gelu_exact(values):
    return jax.nn.gelu(values, approximate=False)


def block_mask(chosen_blocks, segment_rows):
    nblocks = chosen_blocks.shape[2]
    block_index = jnp.arange(nblocks)
    near_blocks = jnp.abs(block_index[:, None] - block_index[None, :]) <= 1
    edge_blocks = (
        (block_index[None, :] == 0)
        | (block_index[None, :] == nblocks - 1)
        | (block_index[:, None] == 0)
        | (block_index[:, None] == nblocks - 1)
    )
    picked_blocks = jnp.any(chosen_blocks[..., None] == block_index, axis=3)
    allowed = near_blocks | edge_blocks | picked_blocks
    block_rows = segment_rows.shape[1] // nblocks
    allowed = jnp.repeat(jnp.repeat(allowed, block_rows, axis=2), block_rows, axis=3)
    same_doc = segment_rows[:, :, None] == segment_rows[:, None, :]
    return allowed & same_doc[:, None]


def masked_scores(queries, key_rows, allowed, score_scale):
    scores = (
        jnp.einsum("qshd,kshd->shqk", queries, key_rows, preferred_element_type=jnp.float32)
        * score_scale
    )
    return jnp.where(allowed, scores, -1e30)


def shards(
    block_input,
    segment_ids,
    random_blocks,
    w_qkv,
    b_qv,
    w_out,
    b_out,
    w_in,
    b_in,
    w_down,
    b_down,
    ln_gain,
    ln_bias,
    cotangent,
):
    score_scale = HEAD_DIM ** (-0.5)
    shard_rows, seq_count, model_width = block_input.shape
    layers = w_qkv.shape[0]
    local_width = w_qkv.shape[3]
    local_heads = local_width // HEAD_DIM
    allowed = block_mask(random_blocks, segment_ids)
    saved_acts = []
    stream = block_input
    for layer_index in range(layers):
        w_proj = w_qkv[layer_index].astype(jnp.bfloat16)
        w_mix = w_out[layer_index].astype(jnp.bfloat16)
        rows_low = stream.astype(jnp.bfloat16)
        full_rows = lax.all_gather(rows_low, "tensor", axis=0, tiled=True)
        length = full_rows.shape[0]
        projected = jnp.einsum(
            "lsd,tdc->tlsc", full_rows, w_proj, preferred_element_type=jnp.float32
        )
        qkv_bias = jnp.stack(
            [b_qv[layer_index, 0], jnp.zeros_like(b_qv[layer_index, 0]), b_qv[layer_index, 1]]
        )
        qkv_low = (projected + qkv_bias[:, None, None, :]).astype(jnp.bfloat16)
        head_view = qkv_low.reshape(3, length, seq_count, local_heads, HEAD_DIM)
        scores = masked_scores(head_view[0], head_view[1], allowed, score_scale)
        row_top = jnp.max(scores, axis=-1, keepdims=True)
        log_total = row_top + jnp.log(jnp.sum(jnp.exp(scores - row_top), axis=-1, keepdims=True))
        probs_low = jnp.exp(scores - log_total).astype(jnp.bfloat16)
        context = jnp.einsum(
            "shqk,kshd->qshd", probs_low, head_view[2], preferred_element_type=jnp.float32
        )
        context = context.reshape(length, seq_count, local_width).astype(jnp.bfloat16)
        mixed = lax.psum_scatter(
            jnp.einsum("lsc,cd->lsd", context, w_mix, preferred_element_type=jnp.float32).astype(
                jnp.bfloat16
            ),
            "tensor",
            scatter_dimension=0,
            tiled=True,
        ).astype(jnp.float32)
        first_sum = stream + mixed + b_out[layer_index]
        hidden_rows = norm_rows(first_sum, ln_gain[layer_index, 0], ln_bias[layer_index, 0])
        hidden_low = hidden_rows.astype(jnp.bfloat16)
        up_weight = w_in[layer_index].astype(jnp.bfloat16)
        backward_weight = w_down[layer_index].astype(jnp.bfloat16)
        hidden_full = lax.all_gather(hidden_low, "tensor", axis=0, tiled=True)
        preactivation = (
            jnp.einsum("twn,nj->twj", hidden_full, up_weight, preferred_element_type=jnp.float32)
            + b_in[layer_index]
        )
        activation_reduced = gelu_exact(preactivation).astype(jnp.bfloat16)
        grown = lax.psum_scatter(
            jnp.einsum(
                "unj,jp->unp",
                activation_reduced,
                backward_weight,
                preferred_element_type=jnp.float32,
            ).astype(jnp.bfloat16),
            "tensor",
            scatter_dimension=0,
            tiled=True,
        ).astype(jnp.float32)
        second_sum = hidden_rows + grown + b_down[layer_index]
        stream = norm_rows(second_sum, ln_gain[layer_index, 1], ln_bias[layer_index, 1])
        keep_rows, keep_hidden = (full_rows, hidden_full)
        saved_acts.append(
            (
                keep_rows,
                head_view,
                log_total,
                context,
                first_sum,
                keep_hidden,
                preactivation,
                activation_reduced,
                second_sum,
                up_weight,
                backward_weight,
            )
        )
    upstream = cotangent
    grads_by_layer = [None] * layers
    for layer_index in reversed(range(layers)):
        (
            keep_rows,
            head_view,
            log_total,
            context,
            first_sum,
            keep_hidden,
            preactivation,
            activation_reduced,
            second_sum,
            up_weight,
            backward_weight,
        ) = saved_acts[layer_index]
        full_rows, hidden_full = (keep_rows, keep_hidden)
        length = full_rows.shape[0]
        w_proj = w_qkv[layer_index].astype(jnp.bfloat16)
        w_mix = w_out[layer_index].astype(jnp.bfloat16)
        _, pull_second = jax.vjp(
            norm_rows, second_sum, ln_gain[layer_index, 1], ln_bias[layer_index, 1]
        )
        d_second, d_gain_two, d_shift_two = pull_second(upstream)
        _, pull_gelu = jax.vjp(gelu_exact, preactivation)
        widened_full = lax.all_gather(d_second.astype(jnp.bfloat16), "tensor", axis=0, tiled=True)
        down_gradient = jnp.einsum(
            "uxc,uxw->cw", activation_reduced, widened_full, preferred_element_type=jnp.float32
        )
        activation_gradient = jnp.einsum(
            "mra,xa->mrx", widened_full, backward_weight, preferred_element_type=jnp.float32
        )
        preactivation_gradient_reduced = pull_gelu(activation_gradient)[0].astype(jnp.bfloat16)
        up_gradient = jnp.einsum(
            "kmx,kmt->xt",
            hidden_full,
            preactivation_gradient_reduced,
            preferred_element_type=jnp.float32,
        )
        g_up_bias = jnp.sum(preactivation_gradient_reduced.astype(jnp.float32), axis=(0, 1))
        d_hidden = d_second + lax.psum_scatter(
            jnp.einsum(
                "hmp,tp->hmt",
                preactivation_gradient_reduced,
                up_weight,
                preferred_element_type=jnp.float32,
            ).astype(jnp.bfloat16),
            "tensor",
            scatter_dimension=0,
            tiled=True,
        ).astype(jnp.float32)
        _, pull_first = jax.vjp(
            norm_rows, first_sum, ln_gain[layer_index, 0], ln_bias[layer_index, 0]
        )
        d_first, d_gain_one, d_shift_one = pull_first(d_hidden)
        full_mixed = lax.all_gather(d_first.astype(jnp.bfloat16), "tensor", axis=0, tiled=True)
        g_out = jnp.einsum("lsc,lsd->cd", context, full_mixed, preferred_element_type=jnp.float32)
        d_context = jnp.einsum(
            "lsd,cd->lsc", full_mixed, w_mix, preferred_element_type=jnp.float32
        ).astype(jnp.bfloat16)
        d_context = d_context.reshape(length, seq_count, local_heads, HEAD_DIM)
        queries, key_rows, value_rows = (head_view[0], head_view[1], head_view[2])
        scores = masked_scores(queries, key_rows, allowed, score_scale)
        attn_probs = jnp.exp(scores - log_total)
        probs_low = attn_probs.astype(jnp.bfloat16)
        d_probs = jnp.einsum(
            "qshd,kshd->shqk", d_context, value_rows, preferred_element_type=jnp.float32
        )
        d_scores = attn_probs * (d_probs - jnp.sum(d_probs * attn_probs, axis=-1, keepdims=True))
        d_scores = d_scores.astype(jnp.bfloat16)
        d_query = (
            jnp.einsum("shqk,kshd->qshd", d_scores, key_rows, preferred_element_type=jnp.float32)
            * score_scale
        )
        d_key = (
            jnp.einsum("shqk,qshd->kshd", d_scores, queries, preferred_element_type=jnp.float32)
            * score_scale
        )
        d_value = jnp.einsum(
            "shqk,qshd->kshd", probs_low, d_context, preferred_element_type=jnp.float32
        )
        d_qkv = (
            jnp.stack([d_query, d_key, d_value])
            .reshape(3, length, seq_count, local_width)
            .astype(jnp.bfloat16)
        )
        g_proj = jnp.einsum("lsd,tlsc->tdc", full_rows, d_qkv, preferred_element_type=jnp.float32)
        qkv_sums = jnp.sum(d_qkv.astype(jnp.float32), axis=(1, 2))
        g_bias = jnp.stack([qkv_sums[0], qkv_sums[2]])
        upstream = d_first + lax.psum_scatter(
            jnp.einsum("tlsc,tdc->lsd", d_qkv, w_proj, preferred_element_type=jnp.float32).astype(
                jnp.bfloat16
            ),
            "tensor",
            scatter_dimension=0,
            tiled=True,
        ).astype(jnp.float32)
        weight_grads = (g_proj, g_bias, g_out, up_gradient, g_up_bias, down_gradient)
        small_grads = (
            jnp.sum(d_first, axis=(0, 1)),
            jnp.sum(d_second, axis=(0, 1)),
            jnp.stack([d_gain_one, d_gain_two]),
            jnp.stack([d_shift_one, d_shift_two]),
        )
        grads_by_layer[layer_index] = (weight_grads, small_grads)
    weight_stack = tuple(
        (
            jnp.stack([grads_by_layer[layer_index][0][member] for layer_index in range(layers)])
            for member in range(6)
        )
    )
    small_stack = tuple(
        (
            jnp.stack([grads_by_layer[layer_index][1][member] for layer_index in range(layers)])
            for member in range(4)
        )
    )
    weight_stack = jax.tree.map(
        lambda part: part.astype(jnp.float32), lax.psum(as_sent(weight_stack), "dp")
    )
    small_stack = lax.psum(small_stack, ("dp", "tensor"))
    return (
        stream,
        upstream,
        weight_stack[0],
        weight_stack[1],
        weight_stack[2],
        small_stack[0],
        weight_stack[3],
        weight_stack[4],
        weight_stack[5],
        small_stack[1],
        small_stack[2],
        small_stack[3],
    )


def solution(mesh):
    return jax.shard_map(
        shards,
        mesh=mesh,
        in_specs=(
            P("tensor", "dp", None),
            P("dp", None),
            P("dp", "tensor", None, None),
            P(None, None, None, "tensor"),
            P(None, None, "tensor"),
            P(None, "tensor", None),
            P(),
            P(None, None, "tensor"),
            P(None, "tensor"),
            P(None, "tensor", None),
            P(),
            P(),
            P(),
            P("tensor", "dp", None),
        ),
        out_specs=(
            P("tensor", "dp", None),
            P("tensor", "dp", None),
            P(None, None, None, "tensor"),
            P(None, None, "tensor"),
            P(None, "tensor", None),
            P(),
            P(None, None, "tensor"),
            P(None, "tensor"),
            P(None, "tensor", None),
            P(),
            P(),
            P(),
        ),
        check_vma=False,
    )
```

profile of v0, /device:TPU:0, one launch (start us, length us, event | category | flops | bytes accessed | tf_op | source)
XLA Modules:
  0.0 1497.5 jit_solution(14239218045943744761)
XLA Ops:
  11.3 3.8 convert.106
  15.2 7.5 fusion.137
  26.7 19.4 %all-gather.9.cloned.1.call-done = bf16[1024,1,1024]{2,0,1:T(8,128)(2,1)} async-done(((bf16[512,1,1024]{2,0,1:T(8,128)(2,1)}), bf16[1024,1,1024]{2,0,1:T(8,128)(2,1)}) %all-gather.9.cloned.1.call-update) | async-done | bytes 2097168 | tf_op jit(solution)/shard_map/all_gather | solution.py:82
  46.1 6.0 fusion.32
  52.5 14.8 fusion.147
  67.3 13.1 exponential_reduce_fusion.1
  80.4 13.9 fusion.83
  99.3 30.7 %reduce-scatter.9.cloned.1.call-done = bf16[512,1,1024]{2,0,1:T(8,128)(2,1)} async-done(((bf16[1024,1,1024]{2,0,1:T(8,128)(2,1)}), bf16[512,1,1024]{2,0,1:T(8,128)(2,1)}) %reduce-scatter.9.cloned.1.call-update) | async-done | bytes 1048592 | tf_op jit(solution)/shard_map/reduce_scatter | solution.py:100
  134.6 9.6 convert.107
  144.2 9.1 convert.108
  153.3 14.5 all-gather.11.cloned.1.call-done
  167.8 26.0 %multiply_convert_fusion.3 = (bf16[1024,2048]{1,0:T(8,128)(2,1)S(1)}, f32[1024,2048]{1,0:T(8,128)}, f32[1024,2048]{1,0:T(8,128)}) fusion(f32[2048]{0:T(1024)S(1)} %bitcast.412, bf16[2,1024,2048]{2,1,0:T(8,128)(2,1)} %convert.107, bf16[1024,1,1024]{2,0,1:T(8,128)(2,1)} %all-gather.11.cloned.1.call-done), kind=kOutput, calls=%fused_computation.34 | convolution fusion | flops 4433379328 | bytes 27271168 | tf_op jit(solution)/shard_map/twn,nj->twj/dot_general | solution.py:115
  195.8 5.6 convert_bitcast_fusion.10
  201.5 31.9 %reduce-scatter.11.cloned.1.call-done = bf16[512,1,1024]{2,0,1:T(8,128)(2,1)} async-done(((bf16[1024,1,1024]{2,0,1:T(8,128)(2,1)}), bf16[512,1,1024]{2,0,1:T(8,128)(2,1)}) %reduce-scatter.11.cloned.1.call-update) | async-done | bytes 1048592 | tf_op jit(solution)/shard_map/reduce_scatter | solution.py:119
  238.0 4.9 copy.96
  242.8 28.4 %all-gather.13.cloned.1.call-done = bf16[1024,1,1024]{2,0,1:T(8,128)(2,1)} async-done(((bf16[512,1,1024]{2,0,1:T(8,128)(2,1)}), bf16[1024,1,1024]{2,0,1:T(8,128)(2,1)}) %all-gather.13.cloned.1.call-update) | async-done | bytes 2097168 | tf_op jit(solution)/shard_map/all_gather | solution.py:82
  271.2 6.0 fusion.33
  278.5 14.8 fusion.148
  293.3 13.1 exponential_reduce_fusion
  306.4 13.5 fusion.89
  323.9 31.7 %reduce-scatter.13.cloned.1.call-done = bf16[512,1,1024]{2,0,1:T(8,128)(2,1)} async-done(((bf16[1024,1,1024]{2,0,1:T(8,128)(2,1)}), bf16[512,1,1024]{2,0,1:T(8,128)(2,1)}) %reduce-scatter.13.cloned.1.call-update) | async-done | bytes 1048592 | tf_op jit(solution)/shard_map/reduce_scatter | solution.py:100
  360.4 33.2 %all-gather.15.cloned.1.call-done = bf16[1024,1,1024]{2,0,1:T(8,128)(2,1)} async-done(((bf16[512,1,1024]{2,0,1:T(8,128)(2,1)}), bf16[1024,1,1024]{2,0,1:T(8,128)(2,1)}) %all-gather.15.cloned.1.call-update) | async-done | bytes 2097168 | tf_op jit(solution)/shard_map/all_gather | solution.py:113
  393.6 25.9 %multiply_convert_fusion.2 = (bf16[1024,2048]{1,0:T(8,128)(2,1)S(1)}, f32[1024,2048]{1,0:T(8,128)}, f32[1024,2048]{1,0:T(8,128)}) fusion(f32[2048]{0:T(1024)S(1)} %bitcast.414, bf16[2,1024,2048]{2,1,0:T(8,128)(2,1)} %convert.107, bf16[1024,1,1024]{2,0,1:T(8,128)(2,1)} %all-gather.15.cloned.1.call-done), kind=kOutput, calls=%fused_computation.21 | convolution fusion | flops 4433379328 | bytes 27271168 | tf_op jit(solution)/shard_map/twn,nj->twj/dot_general | solution.py:115
  421.5 8.1 convert_bitcast_fusion.8
  429.7 31.9 %reduce-scatter.15.cloned.1.call-done = bf16[512,1,1024]{2,0,1:T(8,128)(2,1)} async-done(((bf16[1024,1,1024]{2,0,1:T(8,128)(2,1)}), bf16[512,1,1024]{2,0,1:T(8,128)(2,1)}) %reduce-scatter.15.cloned.1.call-update) | async-done | bytes 1048592 | tf_op jit(solution)/shard_map/reduce_scatter | solution.py:119
  470.7 32.8 %all-gather.17.cloned.1.call-done = bf16[1024,1,1024]{2,0,1:T(8,128)(2,1)} async-done(((bf16[512,1,1024]{2,0,1:T(8,128)(2,1)}), bf16[1024,1,1024]{2,0,1:T(8,128)(2,1)}) %all-gather.17.cloned.1.call-update) | async-done | bytes 2097168 | tf_op jit(solution)/shard_map/all_gather | solution.py:173
  503.5 13.8 fusion.149
  519.4 7.9 convert_bitcast_fusion.7
  527.4 32.0 %reduce-scatter.17.cloned.1.call-done = bf16[512,1,1024]{2,0,1:T(8,128)(2,1)} async-done(((bf16[1024,1,1024]{2,0,1:T(8,128)(2,1)}), bf16[512,1,1024]{2,0,1:T(8,128)(2,1)}) %reduce-scatter.17.cloned.1.call-update) | async-done | bytes 1048592 | tf_op jit(solution)/shard_map/reduce_scatter | solution.py:188
  566.6 33.2 %all-gather.19.cloned.1.call-done = bf16[1024,1,1024]{2,0,1:T(8,128)(2,1)} async-done(((bf16[512,1,1024]{2,0,1:T(8,128)(2,1)}), bf16[1024,1,1024]{2,0,1:T(8,128)(2,1)}) %all-gather.19.cloned.1.call-update) | async-done | bytes 2097168 | tf_op jit(solution)/shard_map/all_gather | solution.py:203
  602.9 13.6 fusion.92
  616.5 22.4 %multiply_reduce_fusion.1 = (f32[8,1024]{1,0:T(8,128)S(1)}, f32[8,1024,1024]{1,2,0:T(8,128)}) fusion(f32[8,1024,1024]{1,2,0:T(8,128)} %get-tuple-element.119, f32[8,1024]{1,0:T(8,128)S(1)} %log_add_fusion, bf16[1024,8,64]{0,2,1:T(8,128)(2,1)S(1)} %bitcast.368, bf16[1024,8,64]{0,2,1:T(8,128)(2,1)S(1)} %bitcast.344), kind=kOutput, calls=%fused_computation.3 | convolution fusion | flops 1098899456 | bytes 69271552 | tf_op jit(solution)/shard_map/qshd,kshd->shqk/dot_general | solution.py:213
  638.9 28.0 %multiply_convert_fusion.1 = bf16[8,1024,1024]{1,2,0:T(8,128)(2,1)} fusion(f32[8,1024,1024]{1,2,0:T(8,128)} %get-tuple-element.122, f32[8,1024,1024]{1,2,0:T(8,128)} %get-tuple-element.119, f32[8,1024]{1,0:T(8,128)S(1)} %get-tuple-element.121, f32[8,1024]{1,0:T(8,128)S(1)} %log_add_fusion), kind=kLoop, calls=%fused_computation.2 | loop fusion | flops 33554432 | bytes 83951616 | tf_op jit(solution)/shard_map/convert_element_type | solution.py:217
  667.0 11.0 multiply_convert_fusion.6
  677.9 9.5 multiply_convert_fusion.7
  691.9 7.7 fusion.42
  699.7 31.9 %reduce-scatter.19.cloned.1.call-done = bf16[512,1,1024]{2,0,1:T(8,128)(2,1)} async-done(((bf16[1024,1,1024]{2,0,1:T(8,128)(2,1)}), bf16[512,1,1024]{2,0,1:T(8,128)(2,1)}) %reduce-scatter.19.cloned.1.call-update) | async-done | bytes 1048592 | tf_op jit(solution)/shard_map/reduce_scatter | solution.py:237
  738.9 33.2 %all-gather.21.cloned.1.call-done = bf16[1024,1,1024]{2,0,1:T(8,128)(2,1)} async-done(((bf16[512,1,1024]{2,0,1:T(8,128)(2,1)}), bf16[1024,1,1024]{2,0,1:T(8,128)(2,1)}) %all-gather.21.cloned.1.call-update) | async-done | bytes 2097168 | tf_op jit(solution)/shard_map/all_gather | solution.py:173
  772.1 13.8 fusion.150
  788.0 8.1 convert_bitcast_fusion.6
  796.1 31.9 %reduce-scatter.21.cloned.1.call-done = bf16[512,1,1024]{2,0,1:T(8,128)(2,1)} async-done(((bf16[1024,1,1024]{2,0,1:T(8,128)(2,1)}), bf16[512,1,1024]{2,0,1:T(8,128)(2,1)}) %reduce-scatter.21.cloned.1.call-update) | async-done | bytes 1048592 | tf_op jit(solution)/shard_map/reduce_scatter | solution.py:188
  834.8 9.6 convert_bitcast_fusion
  844.4 6.4 convert_bitcast_fusion.2
  853.8 5.0 convert_bitcast_fusion.4
  858.7 9.3 all-gather.23.cloned.1.call-done
  870.9 13.5 fusion.86
  884.4 22.4 %multiply_reduce_fusion = (f32[8,1024]{1,0:T(8,128)S(1)}, f32[8,1024,1024]{1,2,0:T(8,128)}) fusion(f32[8,1024,1024]{1,2,0:T(8,128)} %get-tuple-element.116, f32[8,1024]{1,0:T(8,128)S(1)} %copy-done.43, bf16[1024,8,64]{0,2,1:T(8,128)(2,1)S(1)} %bitcast.366, bf16[1024,8,64]{0,2,1:T(8,128)(2,1)S(1)} %bitcast.342), kind=kOutput, calls=%fused_computation.1 | convolution fusion | flops 1098899456 | bytes 69271552 | tf_op jit(solution)/shard_map/qshd,kshd->shqk/dot_general | solution.py:213
  906.8 28.4 %multiply_convert_fusion = bf16[8,1024,1024]{1,2,0:T(8,128)(2,1)} fusion(f32[8,1024,1024]{1,2,0:T(8,128)} %get-tuple-element.124, f32[8,1024,1024]{1,2,0:T(8,128)} %get-tuple-element.116, f32[8,1024]{1,0:T(8,128)S(1)} %get-tuple-element.123, f32[8,1024]{1,0:T(8,128)S(1)} %copy-done.43), kind=kLoop, calls=%fused_computation | loop fusion | flops 33554432 | bytes 83951616 | tf_op jit(solution)/shard_map/convert_element_type | solution.py:217
  935.3 11.0 multiply_convert_fusion.4
  946.3 9.5 multiply_convert_fusion.5
  959.0 7.3 fusion.43
  966.4 9.5 convert_bitcast_fusion.1
  975.9 6.5 pad_maximum_fusion.1
  982.4 8.6 convert_bitcast_fusion.3
  991.1 6.5 pad_maximum_fusion
  1002.2 3.7 convert_bitcast_fusion.5
  1012.1 5.2 copy.80
  1018.1 42.6 %all-reduce = (f32[2,1024]{1,0:T(2,128)}, f32[2,1024]{1,0:T(2,128)}, f32[2,2,1024]{2,1,0:T(2,128)}, f32[2,2,1024]{2,1,0:T(2,128)}) all-reduce(f32[2,1024]{1,0:T(2,128)S(1)} %pad_maximum_fusion.14, f32[2,1024]{1,0:T(2,128)S(1)} %pad_maximum_fusion.16, ...), channel_id=1, replica_groups=mesh['dp'=16,'tensor'=2] {'dp','tensor'}, use_global_device_ids=true, to_apply=%region_38.39 | all-reduce | flops 12288 | bytes 98304 | tf_op jit(solution)/shard_map/psum | solution.py:268
  1063.1 63.6 %all-reduce.1 = (bf16[2,2,512]{2,1,0:T(2,128)(2,1)S(1)}, bf16[2,2048]{1,0:T(2,128)(2,1)S(1)}) all-reduce(bf16[2,2,512]{2,1,0:T(2,128)(2,1)S(1)} %pad_maximum_fusion.17, bf16[2,2048]{1,0:T(2,128)(2,1)S(1)} %pad_maximum_fusion.15), channel_id=1, replica_groups=mesh['dp'=16,'tensor'=2] {'dp'}, use_global_device_ids=true, to_apply=%region_34.35 | all-reduce | flops 6144 | bytes 24576 | tf_op jit(solution)/shard_map/psum | solution.py:266
  1133.0 320.9 %all-reduce.5.cloned.1.call-done = (bf16[2,3,1024,512]{2,3,1,0:T(8,128)(2,1)}, bf16[2,512,1024]{2,1,0:T(8,128)(2,1)}, bf16[2,1024,2048]{2,1,0:T(8,128)(2,1)}, bf16[2,2048,1024]{2,1,0:T(8,128)(2,1)}) async-done(((bf16[2,3,1024,512]{2,3,1,0:T(8,128)(2,1)}, bf16[2,512,1024]{2,1,0:T(8,128)(2,1)}, bf16[2,1024,2048]{2,1,0:T(8,128)(2,1)}, bf16[2,2048,1024]{2,1,0:T(8,128)(2,1)}), ...) | async-done | bytes 25165840 | tf_op jit(solution)/shard_map/psum | solution.py:266
  1453.9 4.1 convert_element_type.378
  1458.0 9.4 copy.82
  1467.4 11.7 convert_element_type.379
  1479.1 11.7 convert_element_type.383
  (351 shorter events, 107.3 us)
Async XLA Ops:
  7.2 38.9 %all-gather.9.cloned.1.call-start = ((), (), s32[]{:S(2)}) async-start(), calls=%async_computation.8 | async-start | bytes 3145728 | tf_op jit(solution)/shard_map/all_gather | solution.py:82
  10.1 119.9 %reduce-scatter.9.cloned.1.call-start = ((), (), s32[]{:S(2)}) async-start(), calls=%async_computation.9 | async-start | bytes 3145728 | tf_op jit(solution)/shard_map/reduce_scatter | solution.py:100
  26.7 25.8 %copy-start.33 = (pred[1024,1024]{0,1:T(8,128)(4,1)}, pred[1024,1024]{0,1:T(8,128)(4,1)S(1)}, u32[]{:S(2)}) copy-start(pred[1024,1024]{0,1:T(8,128)(4,1)S(1)} %broadcast_compare_fusion) | copy-start | bytes 3145732
  52.5 14.9 copy-start.27
  52.5 14.8 copy-start.28
  52.5 27.9 %copy-start.16 = (bf16[1,1024,1,512]{1,3,0,2:T(8,128)(2,1)}, bf16[1,1024,1,512]{1,3,0,2:T(8,128)(2,1)S(1)}, u32[]{:S(2)}) copy-start(bf16[1,1024,1,512]{1,3,0,2:T(8,128)(2,1)S(1)} %get-tuple-element.87) | copy-start | bytes 3145732
  80.4 14.0 copy-start.42
  80.4 14.9 copy-start.49
  95.4 34.7 %copy-start.36 = (f32[512,1,1024]{2,1,0:T(1,128)S(1)}, f32[512,1,1024]{2,1,0:T(1,128)}, u32[]{:S(2)}) copy-start(f32[512,1,1024]{2,1,0:T(1,128)} %param.14) | copy-start | bytes 6291460
  98.0 69.8 %all-gather.11.cloned.1.call-start = ((), (), s32[]{:S(2)}) async-start(), calls=%async_computation.10 | async-start | bytes 3145728 | tf_op jit(solution)/shard_map/all_gather | solution.py:113
  98.7 134.7 %copy-start.61 = (f32[1,1,1024]{2,1,0:T(1,128)}, f32[1,1,1024]{2,1,0:T(1,128)S(1)}, u32[]{:S(2)}) copy-start(f32[1,1,1024]{2,1,0:T(1,128)S(1)} %get-tuple-element.93) | copy-start | bytes 12292
  98.7 256.9 %copy-start.63 = (f32[1,1,1024]{2,1,0:T(1,128)}, f32[1,1,1024]{2,1,0:T(1,128)S(1)}, u32[]{:S(2)}) copy-start(f32[1,1,1024]{2,1,0:T(1,128)S(1)} %get-tuple-element.92) | copy-start | bytes 12292
  131.8 101.7 %copy-start.65 = (f32[512]{0:T(512)}, f32[512]{0:T(512)S(1)}, u32[]{:S(2)}) copy-start(f32[512]{0:T(512)S(1)} %broadcast_multiply_fusion.3) | copy-start | bytes 6148
  132.1 12.1 copy-start.74
  132.1 101.3 %copy-start.69 = (f32[512]{0:T(512)}, f32[512]{0:T(512)S(1)}, u32[]{:S(2)}) copy-start(f32[512]{0:T(512)S(1)} %fusion.115) | copy-start | bytes 6148
  134.5 98.9 %reduce-scatter.11.cloned.1.call-start = ((), (), s32[]{:S(2)}) async-start(), calls=%async_computation.11 | async-start | bytes 3145728 | tf_op jit(solution)/shard_map/reduce_scatter | solution.py:119
  153.3 40.5 %copy-start.94 = (f32[1,2048]{1,0:T(1,128)}, f32[1,2048]{1,0:T(1,128)S(1)}, u32[]{:S(2)}) copy-start(f32[1,2048]{1,0:T(1,128)S(1)} %get-tuple-element.100) | copy-start | bytes 24580
  167.8 28.0 %copy-start.35 = (bf16[2,2048,1024]{2,1,0:T(8,128)(2,1)S(1)}, bf16[2,2048,1024]{2,1,0:T(8,128)(2,1)}, u32[]{:S(2)}) copy-start(bf16[2,2048,1024]{2,1,0:T(8,128)(2,1)} %convert.108) | copy-start | bytes 25165828
  201.4 69.8 %all-gather.13.cloned.1.call-start = ((), (), s32[]{:S(2)}) async-start(), calls=%async_computation.12 | async-start | bytes 3145728 | tf_op jit(solution)/shard_map/all_gather | solution.py:82
  236.1 119.5 %copy-start = (f32[512,1,1024]{2,0,1:T(8,128)}, f32[512,1,1024]{2,0,1:T(8,128)S(1)}, u32[]{:S(2)}) copy-start(f32[512,1,1024]{2,0,1:T(8,128)S(1)} %get-tuple-element.75) | copy-start | bytes 6291460
  236.2 119.5 %copy-start.67 = (f32[512]{0:T(512)}, f32[512]{0:T(512)S(1)}, u32[]{:S(2)}) copy-start(f32[512]{0:T(512)S(1)} %broadcast_multiply_fusion.2) | copy-start | bytes 6148
  236.5 119.1 %copy-start.71 = (f32[512]{0:T(512)}, f32[512]{0:T(512)S(1)}, u32[]{:S(2)}) copy-start(f32[512]{0:T(512)S(1)} %fusion.116) | copy-start | bytes 6148
  237.9 117.7 %reduce-scatter.13.cloned.1.call-start = ((), (), s32[]{:S(2)}) async-start(), calls=%async_computation.13 | async-start | bytes 3145728 | tf_op jit(solution)/shard_map/reduce_scatter | solution.py:100
  277.6 15.7 %copy-start.30 = (bf16[1,1024,1,512]{1,3,0,2:T(8,128)(2,1)}, bf16[1,1024,1,512]{1,3,0,2:T(8,128)(2,1)S(1)}, u32[]{:S(2)}) copy-start(bf16[1,1024,1,512]{1,3,0,2:T(8,128)(2,1)S(1)} %get-tuple-element.82) | copy-start | bytes 3145732
  277.6 15.7 %copy-start.31 = (bf16[1,1024,1,512]{1,3,0,2:T(8,128)(2,1)}, bf16[1,1024,1,512]{1,3,0,2:T(8,128)(2,1)S(1)}, u32[]{:S(2)}) copy-start(bf16[1,1024,1,512]{1,3,0,2:T(8,128)(2,1)S(1)} %get-tuple-element.83) | copy-start | bytes 3145732
  306.4 14.6 copy-start.50
  323.6 70.0 %all-gather.15.cloned.1.call-start = ((), (), s32[]{:S(2)}) async-start(), calls=%async_computation.14 | async-start | bytes 3145728 | tf_op jit(solution)/shard_map/all_gather | solution.py:113
  360.4 101.3 %reduce-scatter.15.cloned.1.call-start = ((), (), s32[]{:S(2)}) async-start(), calls=%async_computation.15 | async-start | bytes 3145728 | tf_op jit(solution)/shard_map/reduce_scatter | solution.py:119
  421.5 40.1 %copy-start.3 = (f32[512,1,1024]{2,0,1:T(8,128)S(1)}, f32[512,1,1024]{2,0,1:T(8,128)}, u32[]{:S(2)}) copy-start(f32[512,1,1024]{2,0,1:T(8,128)} %copy-done.2) | copy-start | bytes 6291460
  429.6 34.5 %copy-start.73 = (f32[1,1,1024]{2,1,0:T(1,128)S(1)}, f32[1,1,1024]{2,1,0:T(1,128)}, u32[]{:S(2)}) copy-start(f32[1,1,1024]{2,1,0:T(1,128)} %get-tuple-element.91) | copy-start | bytes 12292
  429.6 73.9 %all-gather.17.cloned.1.call-start = ((), (), s32[]{:S(2)}) async-start(), calls=%async_computation.16 | async-start | bytes 3145728 | tf_op jit(solution)/shard_map/all_gather | solution.py:173
  470.2 89.1 %reduce-scatter.17.cloned.1.call-start = ((), (), s32[]{:S(2)}) async-start(), calls=%async_computation.17 | async-start | bytes 3145728 | tf_op jit(solution)/shard_map/reduce_scatter | solution.py:188
  527.3 72.5 %all-gather.19.cloned.1.call-start = ((), (), s32[]{:S(2)}) async-start(), calls=%async_computation.18 | async-start | bytes 3145728 | tf_op jit(solution)/shard_map/all_gather | solution.py:203
  566.5 165.1 %reduce-scatter.19.cloned.1.call-start = ((), (), s32[]{:S(2)}) async-start(), calls=%async_computation.19 | async-start | bytes 3145728 | tf_op jit(solution)/shard_map/reduce_scatter | solution.py:237
  616.5 71.0 %copy-start.18 = (bf16[8,64,1024]{2,1,0:T(8,128)(2,1)}, bf16[8,64,1024]{2,1,0:T(8,128)(2,1)S(1)}, u32[]{:S(2)}) copy-start(bf16[8,64,1024]{2,1,0:T(8,128)(2,1)S(1)} %fusion.92) | copy-start | bytes 3145732
  638.9 28.1 %copy-start.32 = (bf16[1,1024,1,512]{1,3,0,2:T(8,128)(2,1)S(1)}, bf16[1,1024,1,512]{1,3,0,2:T(8,128)(2,1)}, u32[]{:S(2)}) copy-start(bf16[1,1024,1,512]{1,3,0,2:T(8,128)(2,1)} %copy-done.31) | copy-start | bytes 3145732
  677.9 10.9 copy-start.20
  687.4 12.2 copy-start.22
  691.9 39.8 %copy-start.1 = (f32[512,1,1024]{2,0,1:T(8,128)S(1)}, f32[512,1,1024]{2,0,1:T(8,128)}, u32[]{:S(2)}) copy-start(f32[512,1,1024]{2,0,1:T(8,128)} %copy-done) | copy-start | bytes 6291460
  691.9 39.8 %copy-start.64 = (f32[1,1,1024]{2,1,0:T(1,128)S(1)}, f32[1,1,1024]{2,1,0:T(1,128)}, u32[]{:S(2)}) copy-start(f32[1,1,1024]{2,1,0:T(1,128)} %copy-done.63) | copy-start | bytes 12292
  691.9 39.8 %copy-start.68 = (f32[512]{0:T(512)S(1)}, f32[512]{0:T(512)}, u32[]{:S(2)}) copy-start(f32[512]{0:T(512)} %copy-done.67) | copy-start | bytes 6148
  691.9 39.8 %copy-start.72 = (f32[512]{0:T(512)S(1)}, f32[512]{0:T(512)}, u32[]{:S(2)}) copy-start(f32[512]{0:T(512)} %copy-done.71) | copy-start | bytes 6148
  699.6 35.8 %copy-start.77 = (f32[512]{0:T(512)S(1)}, f32[512]{0:T(512)}, u32[]{:S(2)}) copy-start(f32[512]{0:T(512)} %copy-done.76) | copy-start | bytes 6148
  699.6 72.5 %all-gather.21.cloned.1.call-start = ((), (), s32[]{:S(2)}) async-start(), calls=%async_computation.20 | async-start | bytes 3145728 | tf_op jit(solution)/shard_map/all_gather | solution.py:173
  735.4 36.7 %copy-start.95 = (f32[1,2048]{1,0:T(1,128)S(1)}, f32[1,2048]{1,0:T(1,128)}, u32[]{:S(2)}) copy-start(f32[1,2048]{1,0:T(1,128)} %copy-done.94) | copy-start | bytes 24580
  738.8 89.2 %reduce-scatter.21.cloned.1.call-start = ((), (), s32[]{:S(2)}) async-start(), calls=%async_computation.21 | async-start | bytes 3145728 | tf_op jit(solution)/shard_map/reduce_scatter | solution.py:188
  788.0 40.1 %copy-start.5 = (f32[512,1,1024]{2,0,1:T(8,128)S(1)}, f32[512,1,1024]{2,0,1:T(8,128)}, u32[]{:S(2)}) copy-start(f32[512,1,1024]{2,0,1:T(8,128)} %copy-done.4) | copy-start | bytes 6291460
  788.0 40.1 %copy-start.62 = (f32[1,1,1024]{2,1,0:T(1,128)S(1)}, f32[1,1,1024]{2,1,0:T(1,128)}, u32[]{:S(2)}) copy-start(f32[1,1,1024]{2,1,0:T(1,128)} %copy-done.61) | copy-start | bytes 12292
  788.0 40.1 %copy-start.66 = (f32[512]{0:T(512)S(1)}, f32[512]{0:T(512)}, u32[]{:S(2)}) copy-start(f32[512]{0:T(512)} %copy-done.65) | copy-start | bytes 6148
  788.0 40.1 %copy-start.70 = (f32[512]{0:T(512)S(1)}, f32[512]{0:T(512)}, u32[]{:S(2)}) copy-start(f32[512]{0:T(512)} %copy-done.69) | copy-start | bytes 6148
  796.1 35.2 %copy-start.75 = (f32[512]{0:T(512)S(1)}, f32[512]{0:T(512)}, u32[]{:S(2)}) copy-start(f32[512]{0:T(512)} %copy-done.74) | copy-start | bytes 6148
  796.1 71.9 %all-gather.23.cloned.1.call-start = ((), (), s32[]{:S(2)}) async-start(), calls=%async_computation.22 | async-start | bytes 3145728 | tf_op jit(solution)/shard_map/all_gather | solution.py:203
  834.8 9.7 copy-start.101
  834.8 293.2 %reduce-scatter.23.cloned.1.call-start = ((), (), s32[]{:S(2)}) async-start(), calls=%async_computation.23 | async-start | bytes 3145728 | tf_op jit(solution)/shard_map/reduce_scatter | solution.py:237
  834.8 9.6 copy-start.104
  853.8 14.3 copy-start.51
  858.7 12.2 copy-start.43
  870.9 13.5 copy-start.17
  884.4 71.4 %copy-start.24 = (bf16[8,64,1024]{2,1,0:T(8,128)(2,1)}, bf16[8,64,1024]{2,1,0:T(8,128)(2,1)S(1)}, u32[]{:S(2)}) copy-start(bf16[8,64,1024]{2,1,0:T(8,128)(2,1)S(1)} %fusion.86) | copy-start | bytes 3145732
  906.8 28.4 %copy-start.29 = (bf16[1,1024,1,512]{1,3,0,2:T(8,128)(2,1)S(1)}, bf16[1,1024,1,512]{1,3,0,2:T(8,128)(2,1)}, u32[]{:S(2)}) copy-start(bf16[1,1024,1,512]{1,3,0,2:T(8,128)(2,1)} %copy-done.28) | copy-start | bytes 3145732
  946.2 10.8 copy-start.25
  955.7 10.5 copy-start.26
  966.3 487.6 %all-reduce.5.cloned.1.call-start = ((), (), s32[]{:S(2)}) async-start(), calls=%async_computation.24 | async-start | bytes 50331648 | tf_op jit(solution)/shard_map/psum | solution.py:266
  1017.3 110.7 %copy-start.13 = (f32[512,1,1024]{2,0,1:T(8,128)S(1)}, f32[512,1,1024]{2,0,1:T(8,128)}, u32[]{:S(2)}) copy-start(f32[512,1,1024]{2,0,1:T(8,128)} %copy-done.12) | copy-start | bytes 6291460
  (61 other events, 247.5 us)
Sparse Core Ops, SparseCore 0:
  10.3 35.8 all-gather.8
  98.1 31.8 reduce-scatter.8
  134.7 33.0 all-gather.10
  201.6 31.8 reduce-scatter.10
  238.1 33.1 all-gather.12
  323.7 31.8 reduce-scatter.12
  360.5 33.0 all-gather.14
  429.7 31.8 reduce-scatter.14
  470.4 33.1 all-gather.16
  527.4 31.8 reduce-scatter.16
  566.6 33.0 all-gather.18
  699.8 31.8 reduce-scatter.18
  739.0 33.1 all-gather.20
  796.2 31.8 reduce-scatter.20
  834.9 33.1 all-gather.22
  966.4 31.8 reduce-scatter.22
  1009.3 444.5 all-reduce.4
where the time goes:
time: 1500 us
  waiting for transfers between devices  747 us (50%)
  matrix products  365 us (24%)
  other arithmetic  194 us (13%)
  blocking collectives  106 us (7%)
  local copies, waits for them, and re-layouts  67.8 us (5%)
  between operations  15.5 us (1%)
    psum x1, waiting for transfers between devices, shards(): lax.psum(as_sent(weight_stack), 'dp')  321 us
    all_gather x2, waiting for transfers between devices, shards(): lax.all_gather(d_second.astype(jnp.bfloat16), 'tensor', axis=0, tiled=True)  66 us
    reduce_scatter x2, waiting for transfers between devices, shards(): lax.psum_scatter(jnp.einsum('hmp,tp->hmt', preactivation_gradient_reduced...  63.9 us
    reduce_scatter x2, waiting for transfers between devices, shards(): lax.psum_scatter(jnp.einsum('unj,jp->unp', activation_reduced, backward_w...  63.8 us
    psum x1, blocking collectives, shards(): lax.psum(as_sent(weight_stack), 'dp')  63.6 us
    reduce_scatter x2, waiting for transfers between devices, shards(): lax.psum_scatter(jnp.einsum('lsc,cd->lsd', context, w_mix, preferred_elem...  62.4 us
    convert_element_type x2, other arithmetic, shards(): d_scores = d_scores.astype(jnp.bfloat16)  56.5 us
    dot_general x2, matrix products, shards(): jnp.einsum('twn,nj->twj', hidden_full, up_weight, preferred_element_type=...  51.9 us
  transfers between devices with their start and end apart: 17, of which 16 were waited for; matrix products, arithmetic and copies ran while one was open for 8% of the time, Pallas kernels for 0%

commit v1 on v0

--- a/solution.py
+++ b/solution.py
@@ -1,9 +1,959 @@
+import functools
+
 import jax
 import jax.numpy as jnp
 from jax import lax
+from jax.experimental import pallas as pl
+from jax.experimental.pallas import tpu as pltpu
 from jax.sharding import PartitionSpec as P
 
 HEAD_DIM = 64
+BIG = -1e30
+BF16 = jnp.bfloat16
+F32 = jnp.float32
+MESH = pl.DeviceIdType.MESH
+VMEM_LIMIT = 56 << 20
+
+FLIP_Y, FLIP_C, FLIP_X, FLIP_Z0, FLIP_Z1 = 1, 2, 4, 8, 16
+DEVICES = 32
+
+GROUPS = 12
+OUT_GROUP = 3
+FF_GROUPS = 4
+
+
+def in_group(s):
+    return 4 + 2 * s
+
+
+def down_group(s):
+    return 5 + 2 * s
+
+
+def flip(values, bit):
+    pairs = [(i, i ^ bit) for i in range(DEVICES)]
+    return jax.tree.map(lambda v: lax.ppermute(v, ("dp", "tensor"), pairs), values)
+
+
+def swap_core_and_y(values):
+    pairs = [(i, i ^ 3 if (i & 1) != ((i >> 1) & 1) else i) for i in range(DEVICES)]
+    return jax.tree.map(lambda v: lax.ppermute(v, ("dp", "tensor"), pairs), values)
+
+
+def nt(a, b):
+    return lax.dot_general(a, b, (((1,), (1,)), ((), ())), preferred_element_type=F32)
+
+
+def nn(a, b):
+    return lax.dot_general(a, b, (((1,), (0,)), ((), ())), preferred_element_type=F32)
+
+
+def tn(a, b):
+    return lax.dot_general(a, b, (((0,), (0,)), ((), ())), preferred_element_type=F32)
+
+
+def block_of(ref):
+    width = ref.shape[-1]
+    return ref[...].reshape(-1, width)
+
+
+def convert_kernel(transposed, code_ref, w_ref, *refs):
+    o_ref, t_ref = refs[-2:]
+    code = code_ref[0]
+    half = w_ref[...].reshape(w_ref.shape[-2:])
+    t_ref[...] = half.T if transposed else half
+    for j in range(16):
+        start = pl.multiple_of((j ^ code) * 32, 32)
+        o_ref[j // 8, 0, 0, (j % 8) * 32 : (j % 8 + 1) * 32, :] = t_ref[pl.ds(start, 32), :].astype(BF16)
+
+
+def convert(w, block, index, transposed, count, group, into, total, code):
+    width = 1024
+    more = [] if into is None else [into]
+    return pl.pallas_call(
+        functools.partial(convert_kernel, transposed),
+        out_shape=jax.ShapeDtypeStruct((2, total, 2, 256, width), BF16),
+        grid_spec=pltpu.PrefetchScalarGridSpec(
+            num_scalar_prefetch=1,
+            grid=(count,),
+            in_specs=[pl.BlockSpec(block, lambda i, code: index(i))]
+            + [pl.BlockSpec(memory_space=pl.ANY) for _ in more],
+            out_specs=pl.BlockSpec((2, 1, 1, 256, width), lambda i, code: (0, group(i), 0, 0, 0)),
+            scratch_shapes=[pltpu.VMEM((512, width), F32)],
+        ),
+        input_output_aliases={2: 0} if more else {},
+        compiler_params=pltpu.CompilerParams(vmem_limit_bytes=VMEM_LIMIT),
+        cost_estimate=pl.CostEstimate(flops=0, bytes_accessed=count * 512 * width * 6, transcendentals=0),
+        name="convert",
+    )(code, w, *more)
+
+
+def place_kernel(transposed, code_ref, g_ref, *refs):
+    o_ref, t_ref = refs[-2:]
+    code = code_ref[0]
+    for j in range(16):
+        start = pl.multiple_of((j ^ code) * 32, 32)
+        t_ref[j * 32 : (j + 1) * 32, :] = g_ref[0, pl.ds(start, 32), :].astype(F32)
+    placed = t_ref[...].T if transposed else t_ref[...]
+    o_ref[...] = placed.reshape(o_ref.shape)
+
+
+def place(grads, shape, block, index, transposed, count, group, into, code):
+    width = grads.shape[-1]
+    more = [] if into is None else [into]
+    return pl.pallas_call(
+        functools.partial(place_kernel, transposed),
+        out_shape=jax.ShapeDtypeStruct(shape, F32),
+        grid_spec=pltpu.PrefetchScalarGridSpec(
+            num_scalar_prefetch=1,
+            grid=(count,),
+            in_specs=[pl.BlockSpec((1, 512, width), lambda i, code: (group(i), 0, 0))]
+            + [pl.BlockSpec(memory_space=pl.ANY) for _ in more],
+            out_specs=pl.BlockSpec(block, lambda i, code: index(i)),
+            scratch_shapes=[pltpu.VMEM((512, width), F32)],
+        ),
+        input_output_aliases={2: 0} if more else {},
+        compiler_params=pltpu.CompilerParams(vmem_limit_bytes=VMEM_LIMIT),
+        cost_estimate=pl.CostEstimate(flops=0, bytes_accessed=count * 512 * width * 6, transcendentals=0),
+        name="place",
+    )(code, grads, *more)
+
+
+def partner(bit):
+    dp, y = lax.axis_index("dp"), lax.axis_index("tensor")
+    if bit == FLIP_Y:
+        return (dp, 1 - y)
+    step = bit // 2
+    up = (dp // step) % 2
+    return (dp + step * (1 - 2 * up), y)
+
+
+def greet(bits):
+    barrier = pltpu.get_barrier_semaphore()
+    for bit in bits:
+        pl.semaphore_signal(barrier, inc=1, device_id=partner(bit), device_id_type=MESH)
+    pl.semaphore_wait(barrier, len(bits))
+
+
+class Link:
+    def __init__(self, send_sem, recv_sem):
+        self.send_sem, self.recv_sem, self.used, self.open = send_sem, recv_sem, 0, []
+
+    def start(self, source, target, bit):
+        copy = pltpu.make_async_remote_copy(
+            src_ref=source,
+            dst_ref=target,
+            send_sem=self.send_sem.at[self.used],
+            recv_sem=self.recv_sem.at[self.used],
+            device_id=partner(bit),
+            device_id_type=MESH,
+        )
+        copy.start()
+        self.used += 1
+        self.open.append(copy)
+        return copy
+
+    def finish(self):
+        for copy in self.open:
+            copy.wait_send()
+
+
+def timetable(chains, window):
+    events, clock = [], 0.0
+    queue = {}
+    ready = [(i, 0) for i in range(len(chains))]
+    flying = []
+    free = {}
+    while ready or flying:
+        moved = True
+        while moved:
+            moved = False
+            for item in sorted(ready, key=lambda it: (it[0], it[1])):
+                link, time = chains[item[0]][item[1]]
+                if sum(1 for f in flying if f[2] == link) < window:
+                    begin = max(clock, free.get(link, 0.0))
+                    free[link] = begin + time
+                    flying.append((begin + time + 2.0, item, link))
+                    events.append(("start",) + item)
+                    ready.remove(item)
+                    moved = True
+                    break
+        flying.sort()
+        clock, item, _ = flying.pop(0)
+        events.append(("land",) + item)
+        if item[1] + 1 < len(chains[item[0]]):
+            ready.append((item[0], item[1] + 1))
+    return events
+
+
+def spread_kernel(chunks, w_in_ref, w_ref, send_sem, recv_sem):
+    del w_in_ref
+    greet((FLIP_Y, FLIP_X, FLIP_Z0, FLIP_C))
+    chains, copies = [], []
+    for k in chunks:
+        if k % GROUPS < 4:
+            steps = [
+                (FLIP_Y, 5.7, w_ref.at[0, k, 0, pl.ds(0, 128)], w_ref.at[0, k, 1, pl.ds(0, 128)]),
+                (FLIP_X, 5.7, w_ref.at[0, k, 1, pl.ds(0, 128)], w_ref.at[0, k, 1, pl.ds(128, 128)]),
+            ]
+        else:
+            steps = [
+                (FLIP_Y, 2.9, w_ref.at[0, k, 0, pl.ds(0, 64)], w_ref.at[0, k, 1, pl.ds(0, 64)]),
+                (FLIP_Z0, 2.9, w_ref.at[0, k, 1, pl.ds(0, 64)], w_ref.at[0, k, 1, pl.ds(64, 64)]),
+                (FLIP_X, 5.7, w_ref.at[0, k, 1, pl.ds(0, 128)], w_ref.at[0, k, 1, pl.ds(128, 128)]),
+            ]
+            if (k // 2) % 2 == 0:
+                steps = [
+                    (FLIP_Y, 2.9, w_ref.at[0, k, 0, pl.ds(0, 64)], w_ref.at[0, k, 1, pl.ds(0, 64)]),
+                    (FLIP_X, 2.9, w_ref.at[0, k, 1, pl.ds(0, 64)], w_ref.at[0, k, 1, pl.ds(128, 64)]),
+                    (FLIP_Z0, 2.9, w_ref.at[0, k, 1, pl.ds(0, 64)], w_ref.at[0, k, 1, pl.ds(64, 64)]),
+                    (FLIP_Z0, 2.9, w_ref.at[0, k, 1, pl.ds(128, 64)], w_ref.at[0, k, 1, pl.ds(192, 64)]),
+                ]
+        steps.append((FLIP_C, 0.9, w_ref.at[0, k, 1], w_ref.at[1, k, 1]))
+        chains.append(steps)
+        copies.append([None] * len(steps))
+    link = Link(send_sem, recv_sem)
+    for event, i, step in timetable([[(s[0], s[1]) for s in chain] for chain in chains], 2):
+        bit, _, source, target = chains[i][step]
+        if event == "start":
+            copies[i][step] = link.start(source, target, bit)
+        else:
+            copies[i][step].wait_recv()
+    link.finish()
+
+
+def spread_weights(weights, chunks):
+    count = sum(3 if k % GROUPS < 4 else (5 if (k // 2) % 2 == 0 else 4) for k in chunks)
+    return pl.pallas_call(
+        functools.partial(spread_kernel, chunks),
+        out_shape=jax.ShapeDtypeStruct(weights.shape, weights.dtype),
+        in_specs=[pl.BlockSpec(memory_space=pl.ANY)],
+        out_specs=pl.BlockSpec(memory_space=pl.ANY),
+        scratch_shapes=[pltpu.SemaphoreType.DMA((count,)), pltpu.SemaphoreType.DMA((count,))],
+        input_output_aliases={0: 0},
+        compiler_params=pltpu.CompilerParams(collective_id=0, has_side_effects=True),
+        cost_estimate=pl.CostEstimate(flops=0, bytes_accessed=50 << 20, transcendentals=0),
+        name="spread_weights",
+    )(weights)
+
+
+def add_rows(into, other, rows):
+    def step(i, _):
+        at = pl.ds(pl.multiple_of(i * 32, 32), 32)
+        into[at, :] = (into[at, :].astype(F32) + other[at, :].astype(F32)).astype(BF16)
+        return 0
+
+    lax.fori_loop(0, rows // 32, step, 0)
+
+
+def reduce_kernel(chunks, g_ref, o_ref, y_buf, x_buf, z0_buf, z1_buf, all_buf, keep_buf, send_sem, recv_sem, keep_sem, out_sem):
+    greet((FLIP_Y, FLIP_X, FLIP_Z0, FLIP_Z1, FLIP_C))
+    chains, copies = [], []
+    for i, k in enumerate(chunks):
+        ys, al = y_buf.at[i], all_buf.at[i]
+        chains.append(
+            [
+                (FLIP_Y, 11.4, g_ref.at[k, pl.ds(256, 256)], ys),
+                (FLIP_X, 5.7, ys.at[pl.ds(128, 128)], x_buf.at[i]),
+                (FLIP_Z0, 2.9, ys.at[pl.ds(64, 64)], z0_buf.at[i]),
+                (FLIP_Z1, 2.9, ys.at[pl.ds(32, 32)], z1_buf.at[i]),
+                (FLIP_Z1, 2.9, al.at[pl.ds(0, 32)], al.at[pl.ds(32, 32)]),
+                (FLIP_Z0, 2.9, al.at[pl.ds(0, 64)], al.at[pl.ds(64, 64)]),
+                (FLIP_X, 5.7, al.at[pl.ds(0, 128)], al.at[pl.ds(128, 128)]),
+                (FLIP_C, 0.9, al, o_ref.at[k, pl.ds(256, 256)]),
+            ]
+        )
+        copies.append([None] * 8)
+    link = Link(send_sem, recv_sem)
+    keeps, outs = {}, {}
+
+    def fetch(i):
+        if i < len(chunks):
+            keeps[i] = pltpu.make_async_copy(
+                g_ref.at[chunks[i], pl.ds(0, 256)], keep_buf.at[i % 2], keep_sem.at[i % 2]
+            )
+            keeps[i].start()
+
+    fetch(0)
+    fetch(1)
+    for event, i, step in timetable([[(s[0], s[1]) for s in chain] for chain in chains], 2):
+        bit, _, source, target = chains[i][step]
+        if event == "start":
+            if step == 7:
+                outs[i] = pltpu.make_async_copy(source, o_ref.at[chunks[i], pl.ds(0, 256)], out_sem.at[i])
+                outs[i].start()
+            copies[i][step] = link.start(source, target, bit)
+            continue
+        copies[i][step].wait_recv()
+        if step == 0:
+            keeps[i].wait()
+            add_rows(y_buf.at[i], keep_buf.at[i % 2], 256)
+            fetch(i + 2)
+        elif step == 1:
+            add_rows(y_buf.at[i], x_buf.at[i], 128)
+        elif step == 2:
+            add_rows(y_buf.at[i], z0_buf.at[i], 64)
+        elif step == 3:
+            add_rows(y_buf.at[i], z1_buf.at[i], 32)
+            all_buf[i, 0:32, :] = y_buf[i, 0:32, :]
+    link.finish()
+    for copy in outs.values():
+        copy.wait()
+
+
+def reduce_gradients(grads, chunks):
+    n = len(chunks)
+    width = grads.shape[-1]
+    return pl.pallas_call(
+        functools.partial(reduce_kernel, chunks),
+        out_shape=jax.ShapeDtypeStruct(grads.shape, grads.dtype),
+        in_specs=[pl.BlockSpec(memory_space=pl.ANY)],
+        out_specs=pl.BlockSpec(memory_space=pl.ANY),
+        scratch_shapes=[
+            pltpu.VMEM((n, 256, width), BF16),
+            pltpu.VMEM((n, 128, width), BF16),
+            pltpu.VMEM((n, 64, width), BF16),
+            pltpu.VMEM((n, 32, width), BF16),
+            pltpu.VMEM((n, 256, width), BF16),
+            pltpu.VMEM((2, 256, width), BF16),
+            pltpu.SemaphoreType.DMA((8 * n,)),
+            pltpu.SemaphoreType.DMA((8 * n,)),
+            pltpu.SemaphoreType.DMA((2,)),
+            pltpu.SemaphoreType.DMA((n,)),
+        ],
+        compiler_params=pltpu.CompilerParams(
+            collective_id=1, has_side_effects=True, vmem_limit_bytes=VMEM_LIMIT
+        ),
+        cost_estimate=pl.CostEstimate(flops=0, bytes_accessed=100 << 20, transcendentals=0),
+        name="reduce_gradients",
+    )(grads)
+
+
+def qkv_kernel(x_ref, w_ref, bias_ref, o_ref):
+    o_ref[0] = (nt(x_ref[...], block_of(w_ref)) + bias_ref[0, 0]).astype(BF16)
+
+
+def project_qkv(x_low, weights, bias, first):
+    rows, width = x_low.shape
+    return pl.pallas_call(
+        qkv_kernel,
+        out_shape=jax.ShapeDtypeStruct((3, rows, width), BF16),
+        grid=(2, 3),
+        in_specs=[
+            pl.BlockSpec((rows, width), lambda a, t: (0, 0)),
+            pl.BlockSpec((1, 1, 2, 256, width), lambda a, t: (a, first + t, 0, 0, 0)),
+            pl.BlockSpec((1, 1, 1, 512), lambda a, t: (t, a, 0, 0)),
+        ],
+        out_specs=pl.BlockSpec((1, rows, 512), lambda a, t: (t, 0, a)),
+        compiler_params=pltpu.CompilerParams(vmem_limit_bytes=VMEM_LIMIT),
+        cost_estimate=pl.CostEstimate(flops=6 * rows * width * width, bytes_accessed=10 << 20, transcendentals=0),
+        name="project_qkv",
+    )(x_low, weights, bias)
+
+
+def norm(r, gain, shift):
+    centred = r - jnp.mean(r, axis=-1, keepdims=True)
+    rstd = lax.rsqrt(jnp.mean(centred * centred, axis=-1, keepdims=True) + 1e-06)
+    return centred * rstd * gain + shift
+
+
+def norm_back(dy, r, gain):
+    centred = r - jnp.mean(r, axis=-1, keepdims=True)
+    rstd = lax.rsqrt(jnp.mean(centred * centred, axis=-1, keepdims=True) + 1e-06)
+    unit = centred * rstd
+    dunit = dy * gain
+    dr = rstd * (
+        dunit
+        - jnp.mean(dunit, axis=-1, keepdims=True)
+        - unit * jnp.mean(dunit * unit, axis=-1, keepdims=True)
+    )
+    return dr, dy * unit
+
+
+def gelu_and_slope(u):
+    cdf = 0.5 * (1.0 + lax.erf(u * (0.5**0.5)))
+    pdf = jnp.exp(-0.5 * u * u) * 0.3989422804014327
+    return u * cdf, cdf + u * pdf
+
+
+TILE = 64
+
+
+def row_tiles(rows, body):
+    def step(i, _):
+        body(pl.ds(pl.multiple_of(i * TILE, TILE), TILE))
+        return 0
+
+    lax.fori_loop(0, rows // TILE, step, 0)
+
+
+def forward_kernel(
+    ctx_ref, x_ref, wo_ref, wi_ref, wd_ref, bi_ref, vec_ref,
+    r1_ref, hl_ref, g_ref, slope_ref, r2_ref, x2_ref, xl_ref, acc_ref,
+):
+    step = pl.program_id(0) * pl.num_programs(1) + pl.program_id(1)
+    rows = x_ref.shape[0]
+
+    @pl.when(step == 0)
+    def _():
+        acc_ref[...] = nn(ctx_ref[:, :512], block_of(wo_ref.at[0])) + nn(ctx_ref[:, 512:], block_of(wo_ref.at[1]))
+
+        def body(at):
+            r1 = x_ref[at, :] + acc_ref[at, :] + vec_ref[0:1, :]
+            r1_ref[at, :] = r1
+            h = norm(r1, vec_ref[1:2, :], vec_ref[2:3, :])
+            hl_ref[at, :] = h.astype(BF16)
+            acc_ref[at, :] = h + vec_ref[3:4, :]
+
+        row_tiles(rows, body)
+
+    u = nt(hl_ref[...], block_of(wi_ref)) + bi_ref[0, 0]
+    g, slope = gelu_and_slope(u)
+    g = g.astype(BF16)
+    g_ref[...] = g
+    slope_ref[...] = slope.astype(BF16)
+    acc_ref[...] += nn(g, block_of(wd_ref))
+
+    @pl.when(step == 2 * FF_GROUPS - 1)
+    def _():
+        def body(at):
+            r2 = acc_ref[at, :]
+            r2_ref[at, :] = r2
+            x2 = norm(r2, vec_ref[4:5, :], vec_ref[5:6, :])
+            x2_ref[at, :] = x2
+            xl_ref[at, :] = x2.astype(BF16)
+
+        row_tiles(rows, body)
+
+
+def weight_spec(group, width):
+    return pl.BlockSpec((1, 1, 2, 256, width), lambda a, s: (a, group(s), 0, 0, 0))
+
+
+def forward_tail(ctx, x, weights, bias_in, vectors, first):
+    rows, width = x.shape
+    whole = pl.BlockSpec((rows, width), lambda a, s: (0, 0))
+    hidden = pl.BlockSpec((rows, 512), lambda a, s: (0, a * FF_GROUPS + s))
+    sums = jax.ShapeDtypeStruct((rows, width), F32)
+    low = jax.ShapeDtypeStruct((rows, width), BF16)
+    wide = jax.ShapeDtypeStruct((rows, 4 * width), BF16)
+    return pl.pallas_call(
+        forward_kernel,
+        out_shape=(sums, low, wide, wide, sums, sums, low),
+        grid=(2, FF_GROUPS),
+        in_specs=[
+            whole,
+            whole,
+            pl.BlockSpec((2, 1, 2, 256, width), lambda a, s: (0, first + OUT_GROUP, 0, 0, 0)),
+            weight_spec(lambda s: first + in_group(s), width),
+            weight_spec(lambda s: first + down_group(s), width),
+            pl.BlockSpec((1, 1, 1, 512), lambda a, s: (a, s, 0, 0)),
+            pl.BlockSpec((8, width), lambda a, s: (0, 0)),
+        ],
+        out_specs=(whole, whole, hidden, hidden, whole, whole, whole),
+        scratch_shapes=[pltpu.VMEM((rows, width), F32)],
+        compiler_params=pltpu.CompilerParams(vmem_limit_bytes=VMEM_LIMIT),
+        cost_estimate=pl.CostEstimate(
+            flops=18 * rows * width * width, bytes_accessed=40 << 20, transcendentals=8 * rows * width
+        ),
+        name="forward_tail",
+    )(ctx, x, weights, weights, weights, bias_in, vectors)
+
+
+def backward_kernel(
+    dx_ref, r2_ref, r1_ref, slope_ref, wo_ref, wi_ref, wd_ref, vec_ref,
+    dm_ref, du_ref, dr1_ref, da_ref, dctx_ref, dbi_ref, small_ref, acc_ref,
+):
+    step = pl.program_id(0) * pl.num_programs(1) + pl.program_id(1)
+    rows = dx_ref.shape[0]
+
+    def column_sums(parts):
+        return [jnp.sum(p, axis=0, keepdims=True) for p in parts]
+
+    @pl.when(step == 0)
+    def _():
+        small_ref[...] = jnp.zeros_like(small_ref)
+
+        def body(at):
+            dy = dx_ref[at, :]
+            dr, gain_part = norm_back(dy, r2_ref[at, :], vec_ref[4:5, :])
+            acc_ref[at, :] = dr
+            dm_ref[at, :] = dr.astype(BF16)
+            for i, p in enumerate(column_sums((gain_part, dy, dr))):
+                small_ref[i : i + 1, :] += p
+
+        row_tiles(rows, body)
+
+    dg = nt(dm_ref[...], block_of(wd_ref))
+    du = (dg * slope_ref[...].astype(F32)).astype(BF16)
+    du_ref[...] = du
+    dbi_ref[0, 0] = jnp.sum(du.astype(F32), axis=0, keepdims=True)
+    acc_ref[...] += nn(du, block_of(wi_ref))
+
+    @pl.when(step == 2 * FF_GROUPS - 1)
+    def _():
+        def body(at):
+            dy = acc_ref[at, :]
+            dr, gain_part = norm_back(dy, r1_ref[at, :], vec_ref[1:2, :])
+            dr1_ref[at, :] = dr
+            da_ref[at, :] = dr.astype(BF16)
+            for i, p in enumerate(column_sums((gain_part, dy, dr))):
+                small_ref[3 + i : 4 + i, :] += p
+
+        row_tiles(rows, body)
+        for a in range(2):
+            dctx_ref[:, a * 512 : (a + 1) * 512] = nt(da_ref[...], block_of(wo_ref.at[a])).astype(BF16)
+
+
+def backward_head(dx, r2, r1, slope, weights, vectors, first):
+    rows, width = dx.shape
+    whole = pl.BlockSpec((rows, width), lambda a, s: (0, 0))
+    hidden = pl.BlockSpec((rows, 512), lambda a, s: (0, a * FF_GROUPS + s))
+    sums = jax.ShapeDtypeStruct((rows, width), F32)
+    low = jax.ShapeDtypeStruct((rows, width), BF16)
+    return pl.pallas_call(
+        backward_kernel,
+        out_shape=(
+            low,
+            jax.ShapeDtypeStruct((rows, 4 * width), BF16),
+            sums,
+            low,
+            low,
+            jax.ShapeDtypeStruct((2, FF_GROUPS, 1, 512), F32),
+            jax.ShapeDtypeStruct((8, width), F32),
+        ),
+        grid=(2, FF_GROUPS),
+        in_specs=[
+            whole,
+            whole,
+            whole,
+            hidden,
+            pl.BlockSpec((2, 1, 2, 256, width), lambda a, s: (0, first + OUT_GROUP, 0, 0, 0)),
+            weight_spec(lambda s: first + in_group(s), width),
+            weight_spec(lambda s: first + down_group(s), width),
+            pl.BlockSpec((8, width), lambda a, s: (0, 0)),
+        ],
+        out_specs=(
+            whole,
+            hidden,
+            whole,
+            whole,
+            whole,
+            pl.BlockSpec((1, 1, 1, 512), lambda a, s: (a, s, 0, 0)),
+            pl.BlockSpec((8, width), lambda a, s: (0, 0)),
+        ),
+        scratch_shapes=[pltpu.VMEM((rows, width), F32)],
+        compiler_params=pltpu.CompilerParams(vmem_limit_bytes=VMEM_LIMIT),
+        cost_estimate=pl.CostEstimate(flops=18 * rows * width * width, bytes_accessed=40 << 20, transcendentals=0),
+        name="backward_head",
+    )(dx, r2, r1, slope, weights, weights, weights, vectors)
+
+
+def input_kernel(d_ref, dr1_ref, w_ref, dx_ref, sums_ref):
+    @pl.when((pl.program_id(0) == 0) & (pl.program_id(1) == 0))
+    def _():
+        dx_ref[...] = dr1_ref[...]
+
+    d = d_ref[0]
+    sums_ref[0, 0] = jnp.sum(d.astype(F32), axis=0, keepdims=True)
+    dx_ref[...] += nn(d, block_of(w_ref))
+
+
+def input_gradient(d_qkv, dr1, weights, first):
+    rows, width = dr1.shape
+    whole = pl.BlockSpec((rows, width), lambda a, t: (0, 0))
+    return pl.pallas_call(
+        input_kernel,
+        out_shape=(jax.ShapeDtypeStruct((rows, width), F32), jax.ShapeDtypeStruct((3, 2, 1, 512), F32)),
+        grid=(2, 3),
+        in_specs=[
+            pl.BlockSpec((1, rows, 512), lambda a, t: (t, 0, a)),
+            whole,
+            weight_spec(lambda t: first + t, width),
+        ],
+        out_specs=(whole, pl.BlockSpec((1, 1, 1, 512), lambda a, t: (t, a, 0, 0))),
+        compiler_params=pltpu.CompilerParams(vmem_limit_bytes=VMEM_LIMIT),
+        cost_estimate=pl.CostEstimate(flops=6 * rows * width * width, bytes_accessed=12 << 20, transcendentals=0),
+        name="input_gradient",
+    )(d_qkv, dr1, weights)
+
+
+def unit_kernel(left_ref, left_sib_ref, right_ref, right_sib_ref, *refs):
+    o_ref = refs[-1]
+    left = left_ref[...].reshape(left_ref.shape[-2:])
+    left_sib = left_sib_ref[...].reshape(left_sib_ref.shape[-2:])
+    o_ref[0] = (tn(left, right_ref[...]) + tn(left_sib, right_sib_ref[...])).astype(BF16)
+
+
+def unit_gradient(left, left_sib, right, right_sib, into, total, count, group):
+    rows, width = right.shape
+    more = [] if into is None else [into]
+    side = (
+        pl.BlockSpec((1, rows, 512), lambda i: (i, 0, 0))
+        if left.ndim == 3
+        else pl.BlockSpec((rows, 512), lambda i: (0, i))
+    )
+    whole = pl.BlockSpec((rows, width), lambda i: (0, 0))
+    return pl.pallas_call(
+        unit_kernel,
+        out_shape=jax.ShapeDtypeStruct((total, 512, width), BF16),
+        grid=(count,),
+        in_specs=[side, side, whole, whole] + [pl.BlockSpec(memory_space=pl.ANY) for _ in more],
+        out_specs=pl.BlockSpec((1, 512, width), lambda i: (group(i), 0, 0)),
+        input_output_aliases={4: 0} if more else {},
+        compiler_params=pltpu.CompilerParams(vmem_limit_bytes=VMEM_LIMIT),
+        cost_estimate=pl.CostEstimate(
+            flops=4 * rows * width * 512 * count, bytes_accessed=(count * 2 + 2) << 20, transcendentals=0
+        ),
+        name="unit_gradient",
+    )(left, left_sib, right, right_sib, *more)
+
+
+def pair_lanes(values, e):
+    lane = lax.broadcasted_iota(jnp.int32, values.shape, 1)
+    return jnp.where(lane // HEAD_DIM == e, values, jnp.zeros_like(values))
+
+
+def attend_kernel(q_ref, ko_ref, vo_ref, ks_ref, vs_ref, hot_ref, mask_ref, ctx_ref, lse_ref):
+    scale = HEAD_DIM**-0.5
+    keys = jnp.concatenate([ko_ref[...], ks_ref[...]], axis=0)
+    values_t = jnp.concatenate([vo_ref[...], vs_ref[...]], axis=0).T
+    query = q_ref[...] * jnp.asarray(scale, BF16)
+    heads = []
+    for e in range(2):
+        right = jnp.concatenate([pair_lanes(query, e), hot_ref[...]], axis=1)
+        left = jnp.concatenate([keys, mask_ref[e]], axis=1)
+        s = nt(left, right)
+        top = jnp.max(s, axis=0, keepdims=True)
+        p = jnp.exp(s - top)
+        total = jnp.sum(p, axis=0, keepdims=True)
+        c = nn(values_t[e * HEAD_DIM : (e + 1) * HEAD_DIM, :], p.astype(BF16))
+        heads.append(c * (1.0 / total))
+        lse_ref[0, e : e + 1, :] = top + jnp.log(total)
+    ctx_ref[...] = jnp.concatenate(heads, axis=0).T.astype(BF16)
+
+
+def attend(q, k, v, k_sib, v_sib, hot, mask):
+    rows, width = q.shape
+    pairs = width // 128
+    own = pl.BlockSpec((rows, 128), lambda p: (0, p))
+    sib = pl.BlockSpec((rows, 128), lambda p: (0, p ^ (pairs // 2)))
+    return pl.pallas_call(
+        attend_kernel,
+        out_shape=(
+            jax.ShapeDtypeStruct((rows, width), BF16),
+            jax.ShapeDtypeStruct((pairs, 2, rows), F32),
+        ),
+        grid=(pairs,),
+        in_specs=[
+            own,
+            own,
+            own,
+            sib,
+            sib,
+            pl.BlockSpec((rows, 128), lambda p: (0, 0)),
+            pl.BlockSpec((2, 2 * rows, 128), lambda p: (p, 0, 0)),
+        ],
+        out_specs=(own, pl.BlockSpec((1, 2, rows), lambda p: (p, 0, 0))),
+        compiler_params=pltpu.CompilerParams(vmem_limit_bytes=VMEM_LIMIT),
+        cost_estimate=pl.CostEstimate(
+            flops=8 * rows * rows * 128 * pairs * 2, bytes_accessed=16 << 20, transcendentals=4 * rows * rows * pairs
+        ),
+        name="attend",
+    )(q, k, v, k_sib, v_sib, hot, mask)
+
+
+def attend_back_kernel(
+    q_ref, ko_ref, vo_ref, ks_ref, vs_ref, hot_ref, mask_ref, ctx_ref, lse_ref, dctx_ref,
+    dq_ref, dko_ref, dvo_ref, dks_ref, dvs_ref,
+):
+    scale = HEAD_DIM**-0.5
+    rows = q_ref.shape[0]
+    keys = jnp.concatenate([ko_ref[...], ks_ref[...]], axis=0)
+    keys_t = keys.T
+    values = jnp.concatenate([vo_ref[...], vs_ref[...]], axis=0)
+    query = q_ref[...] * jnp.asarray(scale, BF16)
+    dctx = dctx_ref[...]
+    delta_t = (dctx.astype(F32) * ctx_ref[...].astype(F32)).T
+    dq_heads, dk, dv = [], 0.0, 0.0
+    for e in range(2):
+        query_e = pair_lanes(query, e)
+        dctx_e = pair_lanes(dctx, e)
+        right = jnp.concatenate([query_e, hot_ref[...]], axis=1)
+        left = jnp.concatenate([keys, mask_ref[e]], axis=1)
+        p = jnp.exp(nt(left, right) - lse_ref[0, e : e + 1, :])
+        dp = nt(values, dctx_e)
+        delta = jnp.sum(delta_t[e * HEAD_DIM : (e + 1) * HEAD_DIM, :], axis=0, keepdims=True)
+        ds = (p * (dp - delta)).astype(BF16)
+        dk = dk + nn(ds, query_e)
+        dv = dv + nn(p.astype(BF16), dctx_e)
+        dq_heads.append(nn(keys_t[e * HEAD_DIM : (e + 1) * HEAD_DIM, :], ds) * scale)
+    dq_ref[...] = jnp.concatenate(dq_heads, axis=0).T.astype(BF16)
+    dko_ref[...] = dk[:rows]
+    dvo_ref[...] = dv[:rows]
+    dks_ref[...] = dk[rows:].astype(BF16)
+    dvs_ref[...] = dv[rows:].astype(BF16)
+
+
+def attend_back(q, k, v, k_sib, v_sib, hot, mask, ctx, lse, dctx):
+    rows, width = q.shape
+    pairs = width // 128
+    own = pl.BlockSpec((rows, 128), lambda p: (0, p))
+    sib = pl.BlockSpec((rows, 128), lambda p: (0, p ^ (pairs // 2)))
+    return pl.pallas_call(
+        attend_back_kernel,
+        out_shape=(
+            jax.ShapeDtypeStruct((rows, width), BF16),
+            jax.ShapeDtypeStruct((rows, width), F32),
+            jax.ShapeDtypeStruct((rows, width), F32),
+            jax.ShapeDtypeStruct((rows, width), BF16),
+            jax.ShapeDtypeStruct((rows, width), BF16),
+        ),
+        grid=(pairs,),
+        in_specs=[
+            own,
+            own,
+            own,
+            sib,
+            sib,
+            pl.BlockSpec((rows, 128), lambda p: (0, 0)),
+            pl.BlockSpec((2, 2 * rows, 128), lambda p: (p, 0, 0)),
+            own,
+            pl.BlockSpec((1, 2, rows), lambda p: (p, 0, 0)),
+            own,
+        ],
+        out_specs=(own, own, own, sib, sib),
+        compiler_params=pltpu.CompilerParams(vmem_limit_bytes=VMEM_LIMIT),
+        cost_estimate=pl.CostEstimate(
+            flops=20 * rows * rows * 128 * pairs * 2, bytes_accessed=24 << 20, transcendentals=4 * rows * rows * pairs
+        ),
+        name="attend_back",
+    )(q, k, v, k_sib, v_sib, hot, mask, ctx, lse, dctx)
+
+
+def flip_order(values, axis, bits):
+    for i, bit in enumerate(bits):
+        values = jnp.where(bit == 0, values, jnp.flip(values, axis + i))
+    return values
+
+
+def sum_everywhere(values):
+    for bit in (FLIP_C, FLIP_Y, FLIP_X, FLIP_Z0, FLIP_Z1):
+        values = values + flip(values, bit)
+    return values
+
+
+def sequence_shards(
+    block_input, segment_ids, random_blocks, w_qkv, b_qv, w_out, b_out, w_in, b_in, w_down, b_down,
+    ln_gain, ln_bias, cotangent,
+):
+    y = lax.axis_index("tensor")
+    dp = lax.axis_index("dp")
+    core, x_bit, z0, z1 = dp % 2, (dp // 2) % 2, (dp // 4) % 2, dp // 8
+    code = core * 8 + x_bit * 4 + z0 * 2 + z1
+    code_arg = code.reshape(1).astype(jnp.int32)
+    device_bits = (core, x_bit, z0, z1)
+
+    rows, _, width = block_input.shape
+    layers = w_qkv.shape[0]
+    blocks = random_blocks.shape[2]
+    own_blocks = blocks // 2
+    heads = random_blocks.shape[1] * 2
+
+    stream_low = swap_core_and_y(block_input[:, 0].astype(BF16))
+    upstream_low = swap_core_and_y(cotangent[:, 0].astype(BF16))
+
+    chosen = random_blocks[0]
+    packed = jnp.concatenate(
+        [chosen.reshape(-1), flip(chosen, FLIP_Y).reshape(-1), segment_ids[0]]
+    )
+    packed = jnp.where(core == y, packed, flip(packed, FLIP_C))
+    chosen = packed[: 2 * chosen.size].reshape(2, heads // 2, blocks, -1)
+    segments = packed[2 * random_blocks.size :]
+    chosen = flip_order(chosen.reshape(2, 2, 2, 2, blocks, -1), 1, device_bits[:3])
+    chosen = chosen.transpose(1, 0, 2, 3, 4, 5).reshape(heads, blocks, -1)
+    segments = segments.reshape(2, rows)
+    segments = jnp.where(core == 0, segments, segments[::-1]).reshape(-1)
+    query_block = core * own_blocks + jnp.arange(own_blocks)
+    key_block = jnp.arange(blocks) ^ (core * own_blocks)
+    allowed = (
+        (jnp.abs(query_block[:, None] - key_block[None, :]) <= 1)
+        | (key_block[None, :] == 0)
+        | (key_block[None, :] == blocks - 1)
+        | (query_block[:, None] == 0)
+        | (query_block[:, None] == blocks - 1)
+    )
+    chosen = lax.dynamic_slice_in_dim(chosen, core * own_blocks, own_blocks, axis=1)
+    allowed = allowed[None] | jnp.any(chosen[:, :, None, :] == key_block[None, None, :, None], axis=3)
+    block_rows = rows // own_blocks
+    block_part = jnp.where(allowed, 0.0, BIG).astype(BF16).transpose(0, 2, 1)
+    block_part = jnp.repeat(block_part, block_rows, axis=1)
+    documents = jnp.arange(128 - own_blocks)
+    document_part = jnp.where(
+        (segments[:, None] == documents[None, :]) | (documents[None, :] > 7), 0.0, BIG
+    ).astype(BF16)
+    mask = jnp.concatenate(
+        [block_part, jnp.broadcast_to(document_part[None], (heads,) + document_part.shape)], axis=2
+    )
+    hot = jnp.concatenate(
+        [
+            jnp.repeat(jnp.eye(own_blocks, dtype=BF16), block_rows, axis=0),
+            (segments[:rows, None] == documents[None, :]).astype(BF16),
+        ],
+        axis=1,
+    )
+
+    bias_pack = jnp.concatenate(
+        [
+            flip_order(b_qv.reshape(layers * 2, 2, 2, 2, 2, -1), 1, device_bits).reshape(-1),
+            flip_order(b_in.reshape(layers * FF_GROUPS, 2, 2, 2, 2, -1), 1, device_bits).reshape(-1),
+        ]
+    )
+    bias_far = flip(bias_pack, FLIP_Y)
+    n_qv = b_qv.size
+
+    def local_bias(near, far, count):
+        near, far = near.reshape(count, 2, 1, 256), far.reshape(count, 2, 1, 256)
+        return jnp.concatenate([near, far], axis=2).reshape(count, 2, 512)
+
+    bias_qv = local_bias(bias_pack[:n_qv], bias_far[:n_qv], layers * 2).reshape(layers, 2, 2, 1, 512)
+    bias_qkv = jnp.stack([bias_qv[:, 0], jnp.zeros_like(bias_qv[:, 0]), bias_qv[:, 1]], axis=1)
+    bias_in = local_bias(bias_pack[n_qv:], bias_far[n_qv:], layers * FF_GROUPS)
+    bias_in = bias_in.reshape(layers, FF_GROUPS, 2, 1, 512).swapaxes(1, 2)
+
+    total = layers * GROUPS
+    weights = None
+    for layer in range(layers):
+        first = layer * GROUPS
+        put = functools.partial(convert, total=total, code=code_arg)
+        weights = put(
+            w_qkv, (1, 1, width, 512), lambda i, l=layer: (l, i, 0, 0), True, 3, lambda i, f=first: f + i, weights
+        )
+        weights = put(
+            w_out, (1, 512, width), lambda i, l=layer: (l, 0, 0), False, 1, lambda i, f=first: f + OUT_GROUP, weights
+        )
+        weights = put(
+            w_in, (1, width, 512), lambda i, l=layer: (l, 0, i), True, FF_GROUPS,
+            lambda i, f=first: f + in_group(i), weights,
+        )
+        weights = put(
+            w_down, (1, 512, width), lambda i, l=layer: (l, i, 0), False, FF_GROUPS,
+            lambda i, f=first: f + down_group(i), weights,
+        )
+    weights = spread_weights(weights, tuple(range(total)))
+
+    vectors = [
+        jnp.stack(
+            [
+                b_out[l], ln_gain[l, 0], ln_bias[l, 0], b_down[l], ln_gain[l, 1], ln_bias[l, 1],
+                b_out[l], b_out[l],
+            ]
+        )
+        for l in range(layers)
+    ]
+    stream, stream_now = stream_low.astype(F32), stream_low
+    saved = []
+    half = width // 2
+    for layer in range(layers):
+        first = layer * GROUPS
+        xb = stream_now
+        qkv = project_qkv(xb, weights, bias_qkv[layer], first)
+        q, k, v = qkv[0], qkv[1], qkv[2]
+        k_sib, v_sib = flip((k, v), FLIP_C)
+        ctx, lse = attend(q, k, v, k_sib, v_sib, hot, mask)
+        r1, hidden, g, slope, r2, stream, stream_now = forward_tail(
+            ctx, stream, weights, bias_in[layer], vectors[layer], first
+        )
+        xb_sib, hidden_sib = flip((xb, hidden), FLIP_C)
+        ctx_sib = flip(ctx[:, half:], FLIP_C)
+        g_sib = flip(g[:, 4 * half :], FLIP_C)
+        saved.append((xb, xb_sib, q, k, v, k_sib, v_sib, ctx, ctx_sib, lse, r1, hidden, hidden_sib, g, g_sib, slope, r2))
+    block_output = swap_core_and_y(stream_now).astype(F32)[:, None]
+
+    upstream = upstream_low.astype(F32)
+    grads = None
+    small = [None] * layers
+    for layer in reversed(range(layers)):
+        first = layer * GROUPS
+        xb, xb_sib, q, k, v, k_sib, v_sib, ctx, ctx_sib, lse, r1, hidden, hidden_sib, g, g_sib, slope, r2 = saved[layer]
+        dm, du, dr1, da, dctx, d_b_in, rows_small = backward_head(
+            upstream, r2, r1, slope, weights, vectors[layer], first
+        )
+        dm_sib, da_sib = flip((dm, da), FLIP_C)
+        du_sib = flip(du[:, 4 * half :], FLIP_C)
+        unit = functools.partial(unit_gradient, total=total)
+        grads = unit(g, g_sib, dm, dm_sib, grads, count=FF_GROUPS, group=lambda i, f=first: f + down_group(i))
+        grads = unit(du, du_sib, hidden, hidden_sib, grads, count=FF_GROUPS, group=lambda i, f=first: f + in_group(i))
+        grads = unit(ctx, ctx_sib, da, da_sib, grads, count=1, group=lambda i, f=first: f + OUT_GROUP)
+        dq, dk, dv, dk_sib, dv_sib = attend_back(q, k, v, k_sib, v_sib, hot, mask, ctx, lse, dctx)
+        dk_far, dv_far = flip((dk_sib, dv_sib), FLIP_C)
+        d_qkv = jnp.stack(
+            [dq, (dk + dk_far.astype(F32)).astype(BF16), (dv + dv_far.astype(F32)).astype(BF16)]
+        )
+        d_qkv_sib = flip(d_qkv[:, :, half:], FLIP_C)
+        grads = unit(d_qkv, d_qkv_sib, xb, xb_sib, grads, count=3, group=lambda i, f=first: f + i)
+        upstream, qkv_sums = input_gradient(d_qkv, dr1, weights, first)
+        small[layer] = (
+            jnp.stack([qkv_sums[0], qkv_sums[2]]),
+            rows_small[5],
+            d_b_in,
+            rows_small[2],
+            jnp.stack([rows_small[3], rows_small[0]]),
+            jnp.stack([rows_small[4], rows_small[1]]),
+        )
+    input_grad = swap_core_and_y(upstream.astype(BF16)).astype(F32)[:, None]
+    grads = reduce_gradients(grads, tuple(range(total)))
+
+    placed = [None] * 4
+    for layer in range(layers):
+        first = layer * GROUPS
+        put = functools.partial(place, grads, code=code_arg)
+        placed[0] = put(
+            w_qkv.shape, (1, 1, width, 512), lambda i, l=layer: (l, i, 0, 0), True, 3, lambda i, f=first: f + i, placed[0]
+        )
+        placed[1] = put(
+            w_out.shape, (1, 512, width), lambda i, l=layer: (l, 0, 0), False, 1,
+            lambda i, f=first: f + OUT_GROUP, placed[1],
+        )
+        placed[2] = put(
+            w_in.shape, (1, width, 512), lambda i, l=layer: (l, 0, i), True, FF_GROUPS,
+            lambda i, f=first: f + in_group(i), placed[2],
+        )
+        placed[3] = put(
+            w_down.shape, (1, 512, width), lambda i, l=layer: (l, i, 0), False, FF_GROUPS,
+            lambda i, f=first: f + down_group(i), placed[3],
+        )
+    stacks = [jnp.stack([small[layer][member] for layer in range(layers)]) for member in range(6)]
+    stacks[2] = stacks[2].swapaxes(1, 2)
+
+    def global_order(values, lead):
+        values = values.reshape(lead, 2, 2, 2, 2, 2, 32).swapaxes(1, 2)
+        values = flip_order(values, 1, (y,) + device_bits)
+        return values.swapaxes(0, 1).reshape(2, -1)
+
+    stacks[0] = global_order(stacks[0], layers * 2)
+    stacks[2] = global_order(stacks[2], layers * FF_GROUPS)
+    summed = sum_everywhere(jnp.concatenate([s.reshape(-1) for s in stacks]))
+    parts, at = [], 0
+    for s in stacks:
+        parts.append(summed[at : at + s.size].reshape(s.shape))
+        at += s.size
+    g_b_qv = lax.dynamic_index_in_dim(parts[0], y, axis=0, keepdims=False).reshape(b_qv.shape)
+    g_b_in = lax.dynamic_index_in_dim(parts[2], y, axis=0, keepdims=False).reshape(b_in.shape)
+    return (
+        block_output,
+        input_grad,
+        placed[0],
+        g_b_qv,
+        placed[1],
+        parts[1],
+        placed[2],
+        g_b_in,
+        placed[3],
+        parts[3],
+        parts[4],
+        parts[5],
+    )
 
 
 def as_sent(array):
@@ -283,8 +1233,9 @@
 
 
 def solution(mesh):
+    by_sequence = mesh.shape["tensor"] == 2 and mesh.shape["dp"] == 16
     return jax.shard_map(
-        shards,
+        sequence_shards if by_sequence else shards,
         mesh=mesh,
         in_specs=(
             P("tensor", "dp", None),

time: 1500 us -> 977 us (0.65)
  Pallas kernels: 0 us -> 816 us
  waiting for transfers between devices: 747 us -> 4.98 us
  matrix products: 365 us -> 0 us
  other arithmetic: 194 us -> 30.7 us
  blocking collectives: 106 us -> 0 us
  starting transfers between devices: 1.33 us -> 48.6 us
    pallas_call x0 -> x38, Pallas kernels: none -> 816 us  [the longest x1 310 us: reduce_gradients(): pl.pallas_call(functools.partial(reduce_kernel, chunks), out_shape=jax.Sh...]
    dot_general x36 -> x0, matrix products: 365 us -> none  [the longest x2 51.9 us: shards(): jnp.einsum('twn,nj->twj', hidden_full, up_weight, preferred_element_type=...]
    psum x1 -> x0, waiting for transfers between devices: 321 us -> none  [shards(): lax.psum(as_sent(weight_stack), 'dp')]
    reduce_scatter x8 -> x0, waiting for transfers between devices: 222 us -> none  [the longest x2 63.9 us: shards(): lax.psum_scatter(jnp.einsum('hmp,tp->hmt', preactivation_gradient_reduced...]
    all_gather x8 -> x0, waiting for transfers between devices: 204 us -> none  [the longest x2 66 us: shards(): lax.all_gather(d_second.astype(jnp.bfloat16), 'tensor', axis=0, tiled=True)]
    psum x2 -> x0, blocking collectives: 106 us -> none  [the longest x1 63.6 us: shards(): lax.psum(as_sent(weight_stack), 'dp')]
    convert_element_type x13 -> x7, other arithmetic: 92.7 us -> 7.64 us  [the longest x1 2.81 us: sequence_shards(): upstream = upstream_low.astype(F32)]
    reduce_sum x22 -> x0, other arithmetic: 58.2 us -> none  [the longest x2 26.1 us: shards(): jnp.sum(jnp.exp(scores - row_top), axis=-1, keepdims=True)]
  transfers between devices with their start and end apart: 17 -> 36, of which waited for: 16 -> 5; matrix products, arithmetic and copies ran while one was open for 8% -> 8% of each run, Pallas kernels for 0% -> 38%
where the time goes in v1:
time: 977 us; the launch traced here: 961 us
  Pallas kernels  816 us (84%)
  local copies, waits for them, and re-layouts  58.7 us (6%)
  starting transfers between devices  48.6 us (5%)
  other arithmetic  30.7 us (3%)
    pallas_call x1, Pallas kernels, reduce_gradients(): pl.pallas_call(functools.partial(reduce_kernel, chunks), out_shape=jax.Sh...  310 us
    pallas_call x1, Pallas kernels, spread_weights(): pl.pallas_call(functools.partial(spread_kernel, chunks), out_shape=jax.Sh...  135 us
    pallas_call x8, Pallas kernels, unit_gradient(): pl.pallas_call(unit_kernel, out_shape=jax.ShapeDtypeStruct((total, 512, w...  56.4 us
    pallas_call x2, Pallas kernels, backward_head(): pl.pallas_call(backward_kernel, out_shape=(low, jax.ShapeDtypeStruct((row...  52.1 us
    pallas_call x2, Pallas kernels, forward_tail(): pl.pallas_call(forward_kernel, out_shape=(sums, low, wide, wide, sums, su...  51.7 us
    pallas_call x2, Pallas kernels, attend_back(): pl.pallas_call(attend_back_kernel, out_shape=(jax.ShapeDtypeStruct((rows,...  51.5 us
    pallas_call x8, Pallas kernels, convert(): pl.pallas_call(functools.partial(convert_kernel, transposed), out_shape=j...  44.8 us
    pallas_call x8, Pallas kernels, place(): pl.pallas_call(functools.partial(place_kernel, transposed), out_shape=jax...  40.8 us
  transfers between devices with their start and end apart: 36, of which 5 were waited for; matrix products, arithmetic and copies ran while one was open for 8% of the time, Pallas kernels for 38%

profile of v1, /device:TPU:0, one launch (start us, length us, event | category | flops | bytes accessed | tf_op | source)
XLA Modules:
  0.0 961.4 jit_solution(8215927342802044722)
XLA Ops:
  0.7 3.0 copy.89
  3.7 9.6 %collective-permute-start = (bf16[512,1024]{1,0:T(8,128)(2,1)}, bf16[512,1024]{1,0:T(8,128)(2,1)}, u32[]{:S(2)}, u32[]{:S(2)}) collective-permute-start(bf16[512,1024]{1,0:T(8,128)(2,1)} %bitcast.117), channel_id=1, source_target_pairs={{0,0},{1,2},{2,1},{3,3},{4,4},{5,6},{6,5},{7,7},{8,8},{9,10},{10,9... | collective-permute-start | bytes 3145736 | tf_op jit(solution)/shard_map/ppermute | solution.py:40
  15.0 2.0 collective-permute-start.4
  18.3 9.5 collective-permute-start.9
  33.7 6.3 convert.20.refs_0_
  40.0 2.8 convert.21.refs_0_
  42.8 7.1 convert.22.refs_0_
  49.9 6.1 convert.23.refs_0_
  56.0 6.4 convert.24.refs_0_
  62.4 2.8 convert.25.refs_0_
  65.2 7.1 convert.26.refs_0_
  72.4 6.1 convert.27.w_in_ref
  78.6 134.7 %spread_weights.1.w_ref.wo_ref.wi_ref.wd_ref = bf16[2,24,2,256,1024]{4,3,2,1,0:T(8,128)(2,1)} custom-call(bf16[2,24,2,256,1024]{4,3,2,1,0:T(8,128)(2,1)} %convert.27.w_in_ref), custom_call_target="tpu_custom_call", output_to_operand_aliasing={{}: (0, {})} | custom-call | bytes 52428800 | tf_op jit(solution)/shard_map/spread_weights/pallas_call | solution.py:227
  216.6 8.4 project_qkv.2
  225.0 3.2 slice_bitcast_fusion.3
  231.8 3.7 pad_maximum_fusion.mask_ref
  237.0 2.8 convert_element_type.70.x_ref
  240.7 19.0 %attend.2 = (bf16[512,1024]{1,0:T(8,128)(2,1)}, f32[8,2,512]{2,1,0:T(2,128)}) custom-call(bf16[512,1024]{1,0:T(8,128)(2,1)} %get-tuple-element.143.q_ref, bf16[512,1024]{1,0:T(8,128)(2,1)} %copy-done.20, bf16[512,1024]{1,0:T(8,128)(2,1)} %copy-done.19, bf16[512,1024]{1,0:T(8,128)(2,1)} %copy-done.63, bf16[512,1024]{1,0:T(8,128)(2,1)} %collective-permute-done.3.vs_ref, ...), custom_call_target="tpu_custom_call" | custom-call | flops 4294967296 | bytes 16777216 | tf_op jit(solution)/shard_map/attend/pallas_call | solution.py:641
  259.8 26.0 %forward_tail.2 = (f32[512,1024]{1,0:T(8,128)}, bf16[512,1024]{1,0:T(8,128)(2,1)}, bf16[512,4096]{1,0:T(8,128)(2,1)}, bf16[512,4096]{1,0:T(8,128)(2,1)}, f32[512...) custom-call(bf16[512,1024]{1,0:T(8,128)(2,1)} %get-tuple-element.57.ctx_ref.left_ref, ...), custom_call_target="tpu_custom_call" | custom-call | flops 9663676416 | bytes 41943040 | tf_op jit(solution)/shard_map/forward_tail/pallas_call | solution.py:440
  285.8 8.4 project_qkv.3
  294.3 3.2 slice_bitcast_fusion
  298.8 2.8 convert_element_type.73.dx_ref
  302.6 19.1 %attend.3 = (bf16[512,1024]{1,0:T(8,128)(2,1)}, f32[8,2,512]{2,1,0:T(2,128)}) custom-call(bf16[512,1024]{1,0:T(8,128)(2,1)} %get-tuple-element.140.q_ref, bf16[512,1024]{1,0:T(8,128)(2,1)} %copy-done.23, bf16[512,1024]{1,0:T(8,128)(2,1)} %copy-done.22, bf16[512,1024]{1,0:T(8,128)(2,1)} %copy-done.64, bf16[512,1024]{1,0:T(8,128)(2,1)} %collective-permute-done.7.vs_ref, ...), custom_call_target="tpu_custom_call" | custom-call | flops 4294967296 | bytes 16777216 | tf_op jit(solution)/shard_map/attend/pallas_call | solution.py:641
  321.7 25.6 %forward_tail.3 = (f32[512,1024]{1,0:T(8,128)}, bf16[512,1024]{1,0:T(8,128)(2,1)}, bf16[512,4096]{1,0:T(8,128)(2,1)}, bf16[512,4096]{1,0:T(8,128)(2,1)}, f32[512...) custom-call(bf16[512,1024]{1,0:T(8,128)(2,1)} %get-tuple-element.59.ctx_ref.left_ref, ...), custom_call_target="tpu_custom_call" | custom-call | flops 9663676416 | bytes 41943040 | tf_op jit(solution)/shard_map/forward_tail/pallas_call | solution.py:440
  347.4 26.1 %backward_head.2 = (bf16[512,1024]{1,0:T(8,128)(2,1)}, bf16[512,4096]{1,0:T(8,128)(2,1)}, f32[512,1024]{1,0:T(8,128)}, bf16[512,1024]{1,0:T(8,128)(2,1)}, bf16[5...) custom-call(f32[512,1024]{1,0:T(8,128)} %convert_element_type.73.dx_ref, ...), custom_call_target="tpu_custom_call" | custom-call | flops 9663676416 | bytes 41943040 | tf_op jit(solution)/shard_map/backward_head/pallas_call | solution.py:514
  373.5 25.9 %attend_back.2 = (bf16[512,1024]{1,0:T(8,128)(2,1)}, f32[512,1024]{1,0:T(8,128)}, f32[512,1024]{1,0:T(8,128)}, bf16[512,1024]{1,0:T(8,128)(2,1)}, bf16[512,1024]{1,0:T(8,128)(2,1)}) custom-call(bf16[512,1024]{1,0:T(8,128)(2,1)} %get-tuple-element.140.q_ref, bf16[512,1024]{1,0:T(8,128)(2,1)} %copy-done.23, bf16[512,1024]{1,0:T(8,128)(2,1)} %copy-done.22, ...), custom_call_target="tpu_custom_call" | custom-call | flops 10737418240 | bytes 25165824 | tf_op jit(solution)/shard_map/attend_back/pallas_call | solution.py:703
  401.2 9.6 collective-permute-start.8
  410.9 3.2 slice.289
  419.6 2.0 pad_maximum_fusion.1.d_ref.left_ref
  421.7 9.6 input_gradient.2
  431.2 26.0 %backward_head.3 = (bf16[512,1024]{1,0:T(8,128)(2,1)}, bf16[512,4096]{1,0:T(8,128)(2,1)}, f32[512,1024]{1,0:T(8,128)}, bf16[512,1024]{1,0:T(8,128)(2,1)}, bf16[5...) custom-call(f32[512,1024]{1,0:T(8,128)} %get-tuple-element.74.dx_ref, ...), custom_call_target="tpu_custom_call" | custom-call | flops 9663676416 | bytes 41943040 | tf_op jit(solution)/shard_map/backward_head/pallas_call | solution.py:514
  457.2 25.6 %attend_back.3 = (bf16[512,1024]{1,0:T(8,128)(2,1)}, f32[512,1024]{1,0:T(8,128)}, f32[512,1024]{1,0:T(8,128)}, bf16[512,1024]{1,0:T(8,128)(2,1)}, bf16[512,1024]{1,0:T(8,128)(2,1)}) custom-call(bf16[512,1024]{1,0:T(8,128)(2,1)} %get-tuple-element.143.q_ref, bf16[512,1024]{1,0:T(8,128)(2,1)} %copy-done.20, bf16[512,1024]{1,0:T(8,128)(2,1)} %copy-done.19, ...), custom_call_target="tpu_custom_call" | custom-call | flops 10737418240 | bytes 25165824 | tf_op jit(solution)/shard_map/attend_back/pallas_call | solution.py:703
  489.3 2.2 fusion.3
  491.7 1.7 fusion.2
  493.4 2.0 pad_maximum_fusion.2.d_ref.left_ref
  495.4 9.8 %input_gradient.3 = (f32[512,1024]{1,0:T(8,128)}, f32[3,2,1,512]{3,2,1,0:T(1,128)}) custom-call(bf16[3,512,1024]{2,1,0:T(8,128)(2,1)} %pad_maximum_fusion.2.d_ref.left_ref, f32[512,1024]{1,0:T(8,128)} %get-tuple-element.84.dr1_ref, bf16[2,24,2,256,1024]{4,3,2,1,0:T(8,128)(2,1)} %spread_weights.1.w_ref.wo_ref.wi_ref.wd_ref), custom_call_target="tpu_custom_call" | custom-call | flops 3221225472 | bytes 12582912 | tf_op jit(solution)/shard_map/input_gradient/pallas_call | solution.py:565
  507.6 2.0 collective-permute-done.31
  510.9 1.7 collective-permute-start.32
  512.7 3.2 slice.286
  516.0 1.8 collective-permute-start.33
  519.3 2.0 collective-permute-done.33
  522.8 1.9 slice.284
  528.1 3.5 copy.72
  532.1 2.6 collective-permute-start.35
  534.7 8.4 unit_gradient.8.refs_0_
  543.2 8.6 unit_gradient.9.refs_0_
  555.1 4.1 unit_gradient.10.refs_0_
  564.6 2.0 collective-permute-start.14
  566.6 7.3 unit_gradient.11.refs_0_
  573.9 1.9 collective-permute-start.16
  575.9 8.4 unit_gradient.12.refs_0_
  584.3 8.5 unit_gradient.13.refs_0_
  594.6 4.1 unit_gradient.14.refs_0_
  598.9 3.5 copy.73
  603.4 7.0 unit_gradient.15.g_ref
  610.4 309.7 %reduce_gradients.1.g_ref = bf16[24,512,1024]{2,1,0:T(8,128)(2,1)} custom-call(bf16[24,512,1024]{2,1,0:T(8,128)(2,1)} %unit_gradient.15.g_ref), custom_call_target="tpu_custom_call" | custom-call | bytes 104857600 | tf_op jit(solution)/shard_map/reduce_gradients/pallas_call | solution.py:307
  920.1 5.3 place.8.refs_0_
  925.5 2.7 place.10.refs_0_
  928.1 6.4 place.12.refs_0_
  934.6 5.9 place.14.refs_0_
  940.5 5.3 place.9
  945.9 2.7 place.11
  948.5 6.4 place.13
  955.0 5.9 place.15
  (332 shorter events, 56.4 us)
Async XLA Ops:
  0.6 12.7 %copy-start.37 = (f32[2,2048]{1,0:T(2,128)S(1)}, f32[2,2048]{1,0:T(2,128)}, u32[]{:S(2)}) copy-start(f32[2,2048]{1,0:T(2,128)} %param.22) | copy-start | bytes 49156
  0.7 13.3 %copy-start.56 = (f32[2,2,512]{2,1,0:T(2,128)S(1)}, f32[2,2,512]{2,1,0:T(2,128)}, u32[]{:S(2)}) copy-start(f32[2,2,512]{2,1,0:T(2,128)} %param.18) | copy-start | bytes 24580
  0.7 14.3 %copy-start.54 = (s32[1,8,16,3]{2,1,3,0:T(8,128)S(1)}, s32[1,8,16,3]{2,1,3,0:T(8,128)}, u32[]{:S(2)}) copy-start(s32[1,8,16,3]{2,1,3,0:T(8,128)} %param.16) | copy-start | bytes 4612
  0.7 16.3 %copy-start.6 = (f32[512,1,1024]{2,1,0:T(1,128)S(1)}, f32[512,1,1024]{2,1,0:T(1,128)}, u32[]{:S(2)}) copy-start(f32[512,1,1024]{2,1,0:T(1,128)} %param.27) | copy-start | bytes 6291460
  0.7 27.2 %copy-start.57 = (f32[2,1024]{1,0:T(2,128)S(1)}, f32[2,1024]{1,0:T(2,128)}, u32[]{:S(2)}) copy-start(f32[2,1024]{1,0:T(2,128)} %param.24) | copy-start | bytes 24580
  0.7 27.2 %copy-start.58 = (f32[2,1024]{1,0:T(2,128)S(1)}, f32[2,1024]{1,0:T(2,128)}, u32[]{:S(2)}) copy-start(f32[2,1024]{1,0:T(2,128)} %param.20) | copy-start | bytes 24580
  0.7 27.8 %copy-start.48 = (f32[2,2,1024]{2,1,0:T(2,128)S(1)}, f32[2,2,1024]{2,1,0:T(2,128)}, u32[]{:S(2)}) copy-start(f32[2,2,1024]{2,1,0:T(2,128)} %param.26) | copy-start | bytes 49156
  0.7 27.8 %copy-start.49 = (f32[2,2,1024]{2,1,0:T(2,128)S(1)}, f32[2,2,1024]{2,1,0:T(2,128)}, u32[]{:S(2)}) copy-start(f32[2,2,1024]{2,1,0:T(2,128)} %param.25) | copy-start | bytes 49156
  3.7 27.3 %copy-start.46 = (s32[1,1024]{1,0:T(1,128)S(1)}, s32[1,1024]{1,0:T(1,128)}, u32[]{:S(2)}) copy-start(s32[1,1024]{1,0:T(1,128)} %param.15) | copy-start | bytes 12292
  3.7 212.9 %collective-permute-start = (bf16[512,1024]{1,0:T(8,128)(2,1)}, bf16[512,1024]{1,0:T(8,128)(2,1)}, u32[]{:S(2)}, u32[]{:S(2)}) collective-permute-start(bf16[512,1024]{1,0:T(8,128)(2,1)} %bitcast.117), channel_id=1, source_target_pairs={{0,0},{1,2},{2,1},{3,3},{4,4},{5,6},{6,5},{7,7},{8,8},{9,10},{10,9... | collective-permute-start | bytes 3145736 | tf_op jit(solution)/shard_map/ppermute | solution.py:40
  15.0 200.2 %collective-permute-start.1 = (f32[6144]{0:T(1024)}, f32[6144]{0:T(1024)}, u32[]{:S(2)}, u32[]{:S(2)}) collective-permute-start(f32[6144]{0:T(1024)} %pad_maximum_fusion.5), channel_id=1, source_target_pairs={{0,1},{1,0},{2,3},{3,2},{4,5},{5,4},{6,7},{7,6},{8,9},{9,8},{10,11... | collective-permute-start | bytes 73736 | tf_op jit(solution)/shard_map/ppermute | solution.py:35
  15.0 15.7 %collective-permute-start.4 = (s32[8,16,3]{1,0,2:T(8,128)S(1)}, s32[8,16,3]{1,0,2:T(8,128)S(1)}, u32[]{:S(2)}, u32[]{:S(2)}) collective-permute-start(s32[8,16,3]{1,0,2:T(8,128)S(1)} %bitcast.139), channel_id=1, source_target_pairs={{0,1},{1,0},{2,3},{3,2},{4,5},{5,4},{6,7},{7,6},{8,9},{9,8},{10,11... | collective-permute-start | bytes 4616 | tf_op jit(solution)/shard_map/ppermute | solution.py:35
  18.3 280.5 %collective-permute-start.9 = (bf16[512,1024]{1,0:T(8,128)(2,1)}, bf16[512,1024]{1,0:T(8,128)(2,1)}, u32[]{:S(2)}, u32[]{:S(2)}) collective-permute-start(bf16[512,1024]{1,0:T(8,128)(2,1)} %bitcast.118), channel_id=1, source_target_pairs={{0,0},{1,2},{2,1},{3,3},{4,4},{5,6},{6,5},{7,7},{8,8},{9,10},{10,9... | collective-permute-start | bytes 3145736 | tf_op jit(solution)/shard_map/ppermute | solution.py:40
  27.8 12.2 %copy-start.60 = (s32[16]{0:T(128)}, s32[16]{0:T(128)S(1)}, u32[]{:S(2)}) copy-start(s32[16]{0:T(128)S(1)} %iota_xor_fusion) | copy-start | bytes 196
  31.6 182.4 %collective-permute-start.5 = (s32[1792]{0:T(1024)}, s32[1792]{0:T(1024)}, u32[]{:S(2)}, u32[]{:S(2)}) collective-permute-start(s32[1792]{0:T(1024)} %pad_add_fusion), channel_id=1, source_target_pairs={{0,2},{1,3},{2,0},{3,1},{4,6},{5,7},{6,4},{7,5},{8,10},{9,11},{10,... | collective-permute-start | bytes 21512 | tf_op jit(solution)/shard_map/ppermute | solution.py:35
  78.5 134.9 %copy-start.29 = (f32[1,1024]{1,0:T(1,128)S(1)}, f32[1,1024]{1,0:T(1,128)}, u32[]{:S(2)}) copy-start(f32[1,1024]{1,0:T(1,128)} %get-tuple-element.191) | copy-start | bytes 12292
  78.5 134.9 %copy-start.42 = (f32[1,1024]{1,0:T(1,128)S(1)}, f32[1,1024]{1,0:T(1,128)}, u32[]{:S(2)}) copy-start(f32[1,1024]{1,0:T(1,128)} %get-tuple-element.166) | copy-start | bytes 12292
  78.5 134.9 %copy-start.43 = (f32[1,1024]{1,0:T(1,128)S(1)}, f32[1,1024]{1,0:T(1,128)}, u32[]{:S(2)}) copy-start(f32[1,1024]{1,0:T(1,128)} %get-tuple-element.167) | copy-start | bytes 12292
  78.5 134.9 %copy-start.44 = (f32[1,1024]{1,0:T(1,128)S(1)}, f32[1,1024]{1,0:T(1,128)}, u32[]{:S(2)}) copy-start(f32[1,1024]{1,0:T(1,128)} %get-tuple-element.188) | copy-start | bytes 12292
  78.5 134.9 %copy-start.45 = (f32[1,1024]{1,0:T(1,128)S(1)}, f32[1,1024]{1,0:T(1,128)}, u32[]{:S(2)}) copy-start(f32[1,1024]{1,0:T(1,128)} %get-tuple-element.189) | copy-start | bytes 12292
  78.5 134.9 %copy-start.53 = (f32[1,1024]{1,0:T(1,128)S(1)}, f32[1,1024]{1,0:T(1,128)}, u32[]{:S(2)}) copy-start(f32[1,1024]{1,0:T(1,128)} %get-tuple-element.180) | copy-start | bytes 12292
  78.5 135.6 %copy-start.34 = (s32[384]{0:T(512)S(1)}, s32[384]{0:T(512)}, u32[]{:S(2)}) copy-start(s32[384]{0:T(512)} %copy-done.33) | copy-start | bytes 4612
  78.5 135.6 %copy-start.36 = (s32[384]{0:T(512)S(1)}, s32[384]{0:T(512)}, u32[]{:S(2)}) copy-start(s32[384]{0:T(512)} %copy-done.35) | copy-start | bytes 4612
  78.5 135.6 %copy-start.47 = (s32[1,1024]{1,0:T(1,128)S(1)}, s32[1,1024]{1,0:T(1,128)}, u32[]{:S(2)}) copy-start(s32[1,1024]{1,0:T(1,128)} %param.15) | copy-start | bytes 12292
  78.5 136.1 %copy-start.61 = (s32[16]{0:T(128)S(1)}, s32[16]{0:T(128)}, u32[]{:S(2)}) copy-start(s32[16]{0:T(128)} %copy-done.60) | copy-start | bytes 196
  78.5 136.3 %copy-start.59 = (pred[16,8]{0,1:T(8,128)(4,1)S(1)}, pred[16,8]{0,1:T(8,128)(4,1)}, u32[]{:S(2)}) copy-start(pred[16,8]{0,1:T(8,128)(4,1)} %fusion.12) | copy-start | bytes 388
  78.5 137.3 %copy-start.30 = (f32[4,2,1,256]{3,2,1,0:T(1,128)S(1)}, f32[4,2,1,256]{3,2,1,0:T(1,128)}, u32[]{:S(2)}) copy-start(f32[4,2,1,256]{3,2,1,0:T(1,128)} %reshape_reshape.21) | copy-start | bytes 24580
  228.3 11.5 %collective-permute-start.2 = (bf16[512,1024]{1,0:T(8,128)(2,1)S(1)}, bf16[512,1024]{1,0:T(8,128)(2,1)S(1)}, u32[]{:S(2)}, u32[]{:S(2)}) collective-permute-start(bf16[512,1024]{1,0:T(8,128)(2,1)S(1)} %get-tuple-element.142.ko_ref), channel_id=1, source_target_pairs={{0,2},{1,3},{2,0},{3,1},{4,6},{5,7},{6,4},{7,5},{8,10},{9,11},{10,... | collective-permute-start | bytes 3145736 | tf_op jit(solution)/shard_map/ppermute | solution.py:35
  229.2 10.5 %collective-permute-start.3 = (bf16[512,1024]{1,0:T(8,128)(2,1)S(1)}, bf16[512,1024]{1,0:T(8,128)(2,1)}, u32[]{:S(2)}, u32[]{:S(2)}) collective-permute-start(bf16[512,1024]{1,0:T(8,128)(2,1)S(1)} %get-tuple-element.141.vo_ref), channel_id=1, source_target_pairs={{0,2},{1,3},{2,0},{3,1},{4,6},{5,7},{6,4},{7,5},{8,10},{9,11},{10,... | collective-permute-start | bytes 3145736 | tf_op jit(solution)/shard_map/ppermute | solution.py:35
  297.5 4.1 collective-permute-start.6
  297.9 3.9 collective-permute-start.7
  373.4 26.5 %copy-start.12 = (bf16[512,1024]{1,0:T(8,128)(2,1)S(1)}, bf16[512,1024]{1,0:T(8,128)(2,1)}, u32[]{:S(2)}) copy-start(bf16[512,1024]{1,0:T(8,128)(2,1)} %get-tuple-element.88.right_ref) | copy-start | bytes 3145732
  373.5 26.9 %copy-start.4 = (bf16[512,1024]{1,0:T(8,128)(2,1)S(1)}, bf16[512,1024]{1,0:T(8,128)(2,1)}, u32[]{:S(2)}) copy-start(bf16[512,1024]{1,0:T(8,128)(2,1)} %get-tuple-element.59.ctx_ref.left_ref) | copy-start | bytes 3145732
  399.4 17.4 %collective-permute-start.11 = (bf16[512,1024]{1,0:T(8,128)(2,1)}, bf16[512,1024]{1,0:T(8,128)(2,1)}, u32[]{:S(2)}, u32[]{:S(2)}) collective-permute-start(bf16[512,1024]{1,0:T(8,128)(2,1)} %get-tuple-element.72), channel_id=1, source_target_pairs={{0,2},{1,3},{2,0},{3,1},{4,6},{5,7},{6,4},{7,5},{8,10},{9,11},{10,... | collective-permute-start | bytes 3145736 | tf_op jit(solution)/shard_map/ppermute | solution.py:35
  399.9 18.6 %collective-permute-start.10 = (bf16[512,1024]{1,0:T(8,128)(2,1)}, bf16[512,1024]{1,0:T(8,128)(2,1)S(1)}, u32[]{:S(2)}, u32[]{:S(2)}) collective-permute-start(bf16[512,1024]{1,0:T(8,128)(2,1)} %get-tuple-element.70), channel_id=1, source_target_pairs={{0,2},{1,3},{2,0},{3,1},{4,6},{5,7},{6,4},{7,5},{8,10},{9,11},{10,... | collective-permute-start | bytes 3145736 | tf_op jit(solution)/shard_map/ppermute | solution.py:35
  399.9 14.1 %copy-start.3 = (bf16[512,4096]{1,0:T(8,128)(2,1)S(1)}, bf16[512,4096]{1,0:T(8,128)(2,1)}, u32[]{:S(2)}) copy-start(bf16[512,4096]{1,0:T(8,128)(2,1)} %get-tuple-element.94.left_ref) | copy-start | bytes 12582916
  399.9 106.6 %collective-permute-start.20 = (bf16[512,1024]{1,0:T(8,128)(2,1)S(1)}, bf16[512,1024]{1,0:T(8,128)(2,1)}, u32[]{:S(2)}, u32[]{:S(2)}) collective-permute-start(bf16[512,1024]{1,0:T(8,128)(2,1)S(1)} %copy-done.12), channel_id=1, source_target_pairs={{0,2},{1,3},{2,0},{3,1},{4,6},{5,7},{6,4},{7,5},{8,10},{9,11},{10,... | collective-permute-start | bytes 3145736 | tf_op jit(solution)/shard_map/ppermute | solution.py:35
  401.2 106.0 %collective-permute-start.8 = (bf16[512,1024]{1,0:T(8,128)(2,1)}, bf16[512,1024]{1,0:T(8,128)(2,1)}, u32[]{:S(2)}, u32[]{:S(2)}) collective-permute-start(bf16[512,1024]{1,0:T(8,128)(2,1)} %get-tuple-element.61), channel_id=1, source_target_pairs={{0,0},{1,2},{2,1},{3,3},{4,4},{5,6},{6,5},{7,7},{8,8},{9,10},{10,9... | collective-permute-start | bytes 3145736 | tf_op jit(solution)/shard_map/ppermute | solution.py:40
  410.9 96.1 %collective-permute-start.25 = (bf16[512,512]{1,0:T(8,128)(2,1)}, bf16[512,512]{1,0:T(8,128)(2,1)}, u32[]{:S(2)}, u32[]{:S(2)}) collective-permute-start(bf16[512,512]{1,0:T(8,128)(2,1)} %slice.288), channel_id=1, source_target_pairs={{0,2},{1,3},{2,0},{3,1},{4,6},{5,7},{6,4},{7,5},{8,10},{9,11},{10,... | collective-permute-start | bytes 1572872 | tf_op jit(solution)/shard_map/ppermute | solution.py:35
  457.2 26.3 %copy-start.32 = (f32[8,1024]{1,0:T(8,128)S(1)}, f32[8,1024]{1,0:T(8,128)}, u32[]{:S(2)}) copy-start(f32[8,1024]{1,0:T(8,128)} %get-tuple-element.98) | copy-start | bytes 98308
  457.2 26.9 %copy-start.50 = (f32[2,4,1,512]{3,2,1,0:T(1,128)S(1)}, f32[2,4,1,512]{3,2,1,0:T(1,128)}, u32[]{:S(2)}) copy-start(f32[2,4,1,512]{3,2,1,0:T(1,128)} %get-tuple-element.101) | copy-start | bytes 49156
  457.2 26.9 %copy-start.51 = (f32[2,4,1,512]{3,2,1,0:T(1,128)S(1)}, f32[2,4,1,512]{3,2,1,0:T(1,128)}, u32[]{:S(2)}) copy-start(f32[2,4,1,512]{3,2,1,0:T(1,128)} %get-tuple-element.100) | copy-start | bytes 49156
  482.9 5.9 collective-permute-start.13
  483.4 8.1 collective-permute-start.12
  488.8 42.7 %collective-permute-start.27 = (bf16[512,2048]{1,0:T(8,128)(2,1)}, bf16[512,2048]{1,0:T(8,128)(2,1)}, u32[]{:S(2)}, u32[]{:S(2)}) collective-permute-start(bf16[512,2048]{1,0:T(8,128)(2,1)} %slice.289), channel_id=1, source_target_pairs={{0,2},{1,3},{2,0},{3,1},{4,6},{5,7},{6,4},{7,5},{8,10},{9,11},{10,... | collective-permute-start | bytes 6291464 | tf_op jit(solution)/shard_map/ppermute | solution.py:35
  491.5 40.6 %collective-permute-start.29 = (bf16[512,2048]{1,0:T(8,128)(2,1)}, bf16[512,2048]{1,0:T(8,128)(2,1)}, u32[]{:S(2)}, u32[]{:S(2)}) collective-permute-start(bf16[512,2048]{1,0:T(8,128)(2,1)} %slice.290), channel_id=1, source_target_pairs={{0,2},{1,3},{2,0},{3,1},{4,6},{5,7},{6,4},{7,5},{8,10},{9,11},{10,... | collective-permute-start | bytes 6291464 | tf_op jit(solution)/shard_map/ppermute | solution.py:35
  506.6 3.4 collective-permute-start.26
  507.0 9.0 collective-permute-start.28
  507.2 2.4 collective-permute-start.31
  509.6 11.7 %collective-permute-start.30 = (bf16[512,1024]{1,0:T(8,128)(2,1)}, bf16[512,1024]{1,0:T(8,128)(2,1)}, u32[]{:S(2)}, u32[]{:S(2)}) collective-permute-start(bf16[512,1024]{1,0:T(8,128)(2,1)} %get-tuple-element.95.right_ref), channel_id=1, source_target_pairs={{0,2},{1,3},{2,0},{3,1},{4,6},{5,7},{6,4},{7,5},{8,10},{9,11},{10,... | collective-permute-start | bytes 3145736 | tf_op jit(solution)/shard_map/ppermute | solution.py:35
  510.9 5.0 collective-permute-start.32
  516.0 48.6 %collective-permute-start.21 = (bf16[512,2048]{1,0:T(8,128)(2,1)}, bf16[512,2048]{1,0:T(8,128)(2,1)}, u32[]{:S(2)}, u32[]{:S(2)}) collective-permute-start(bf16[512,2048]{1,0:T(8,128)(2,1)} %slice.286), channel_id=1, source_target_pairs={{0,2},{1,3},{2,0},{3,1},{4,6},{5,7},{6,4},{7,5},{8,10},{9,11},{10,... | collective-permute-start | bytes 6291464 | tf_op jit(solution)/shard_map/ppermute | solution.py:35
  516.0 5.3 collective-permute-start.33
  521.3 54.5 %collective-permute-start.19 = (bf16[512,2048]{1,0:T(8,128)(2,1)}, bf16[512,2048]{1,0:T(8,128)(2,1)}, u32[]{:S(2)}, u32[]{:S(2)}) collective-permute-start(bf16[512,2048]{1,0:T(8,128)(2,1)} %slice.285), channel_id=1, source_target_pairs={{0,2},{1,3},{2,0},{3,1},{4,6},{5,7},{6,4},{7,5},{8,10},{9,11},{10,... | collective-permute-start | bytes 6291464 | tf_op jit(solution)/shard_map/ppermute | solution.py:35
  521.3 5.3 collective-permute-start.34
  526.6 38.0 %collective-permute-start.23 = (bf16[3,512,512]{2,1,0:T(8,128)(2,1)}, bf16[3,512,512]{2,1,0:T(8,128)(2,1)S(1)}, u32[]{:S(2)}, u32[]{:S(2)}) collective-permute-start(bf16[3,512,512]{2,1,0:T(8,128)(2,1)} %slice.336), channel_id=1, source_target_pairs={{0,2},{1,3},{2,0},{3,1},{4,6},{5,7},{6,4},{7,5},{8,10},{9,11},{10,... | collective-permute-start | bytes 4718600 | tf_op jit(solution)/shard_map/ppermute | solution.py:35
  531.6 27.7 %collective-permute-start.24 = (bf16[512,1024]{1,0:T(8,128)(2,1)S(1)}, bf16[512,1024]{1,0:T(8,128)(2,1)S(1)}, u32[]{:S(2)}, u32[]{:S(2)}) collective-permute-start(bf16[512,1024]{1,0:T(8,128)(2,1)S(1)} %copy-done.5), channel_id=1, source_target_pairs={{0,2},{1,3},{2,0},{3,1},{4,6},{5,7},{6,4},{7,5},{8,10},{9,11},{10,... | collective-permute-start | bytes 3145736 | tf_op jit(solution)/shard_map/ppermute | solution.py:35
  532.1 11.0 %collective-permute-start.35 = (f32[24576]{0:T(1024)S(1)}, f32[24576]{0:T(1024)S(1)}, u32[]{:S(2)}, u32[]{:S(2)}) collective-permute-start(f32[24576]{0:T(1024)S(1)} %add.90), channel_id=1, source_target_pairs={{0,16},{1,17},{2,18},{3,19},{4,20},{5,21},{6,22},{7,23},{8,24},{9,... | collective-permute-start | bytes 294920 | tf_op jit(solution)/shard_map/ppermute | solution.py:35
  543.1 30.8 %collective-permute-start.22 = (bf16[512,1024]{1,0:T(8,128)(2,1)}, bf16[512,1024]{1,0:T(8,128)(2,1)}, u32[]{:S(2)}, u32[]{:S(2)}) collective-permute-start(bf16[512,1024]{1,0:T(8,128)(2,1)} %get-tuple-element.90.right_ref), channel_id=1, source_target_pairs={{0,2},{1,3},{2,0},{3,1},{4,6},{5,7},{6,4},{7,5},{8,10},{9,11},{10,... | collective-permute-start | bytes 3145736 | tf_op jit(solution)/shard_map/ppermute | solution.py:35
  560.3 42.1 %collective-permute-start.15 = (bf16[3,512,512]{2,1,0:T(8,128)(2,1)}, bf16[3,512,512]{2,1,0:T(8,128)(2,1)}, u32[]{:S(2)}, u32[]{:S(2)}) collective-permute-start(bf16[3,512,512]{2,1,0:T(8,128)(2,1)} %slice.335), channel_id=1, source_target_pairs={{0,2},{1,3},{2,0},{3,1},{4,6},{5,7},{6,4},{7,5},{8,10},{9,11},{10,... | collective-permute-start | bytes 4718600 | tf_op jit(solution)/shard_map/ppermute | solution.py:35
  564.6 28.2 %collective-permute-start.18 = (bf16[512,1024]{1,0:T(8,128)(2,1)}, bf16[512,1024]{1,0:T(8,128)(2,1)S(1)}, u32[]{:S(2)}, u32[]{:S(2)}) collective-permute-start(bf16[512,1024]{1,0:T(8,128)(2,1)} %get-tuple-element.86.right_ref), channel_id=1, source_target_pairs={{0,2},{1,3},{2,0},{3,1},{4,6},{5,7},{6,4},{7,5},{8,10},{9,11},{10,... | collective-permute-start | bytes 3145736 | tf_op jit(solution)/shard_map/ppermute | solution.py:35
  564.6 34.1 %collective-permute-start.14 = (bf16[512,1024]{1,0:T(8,128)(2,1)}, bf16[512,1024]{1,0:T(8,128)(2,1)S(1)}, u32[]{:S(2)}, u32[]{:S(2)}) collective-permute-start(bf16[512,1024]{1,0:T(8,128)(2,1)} %convert_element_type.82), channel_id=1, source_target_pairs={{0,0},{1,2},{2,1},{3,3},{4,4},{5,6},{6,5},{7,7},{8,8},{9,10},{10,9... | collective-permute-start | bytes 3145736 | tf_op jit(solution)/shard_map/ppermute | solution.py:40
  573.9 28.5 %collective-permute-start.16 = (bf16[512,1024]{1,0:T(8,128)(2,1)}, bf16[512,1024]{1,0:T(8,128)(2,1)S(1)}, u32[]{:S(2)}, u32[]{:S(2)}) collective-permute-start(bf16[512,1024]{1,0:T(8,128)(2,1)} %collective-permute-done.x_ref.right_ref), channel_id=1, source_target_pairs={{0,2},{1,3},{2,0},{3,1},{4,6},{5,7},{6,4},{7,5},{8,10},{9,11},{10,... | collective-permute-start | bytes 3145736 | tf_op jit(solution)/shard_map/ppermute | solution.py:35
  575.8 17.0 %collective-permute-start.17 = (bf16[512,512]{1,0:T(8,128)(2,1)S(1)}, bf16[512,512]{1,0:T(8,128)(2,1)S(1)}, u32[]{:S(2)}, u32[]{:S(2)}) collective-permute-start(bf16[512,512]{1,0:T(8,128)(2,1)S(1)} %copy-done.26), channel_id=1, source_target_pairs={{0,2},{1,3},{2,0},{3,1},{4,6},{5,7},{6,4},{7,5},{8,10},{9,11},{10,... | collective-permute-start | bytes 1572872 | tf_op jit(solution)/shard_map/ppermute | solution.py:35
  (37 other events, 159.2 us)

commit v2 on v1

--- a/solution.py
+++ b/solution.py
@@ -246,87 +246,148 @@
     lax.fori_loop(0, rows // 32, step, 0)
 
 
-def reduce_kernel(chunks, g_ref, o_ref, y_buf, x_buf, z0_buf, z1_buf, all_buf, keep_buf, send_sem, recv_sem, keep_sem, out_sem):
-    greet((FLIP_Y, FLIP_X, FLIP_Z0, FLIP_Z1, FLIP_C))
-    chains, copies = [], []
-    for i, k in enumerate(chunks):
-        ys, al = y_buf.at[i], all_buf.at[i]
-        chains.append(
-            [
-                (FLIP_Y, 11.4, g_ref.at[k, pl.ds(256, 256)], ys),
-                (FLIP_X, 5.7, ys.at[pl.ds(128, 128)], x_buf.at[i]),
-                (FLIP_Z0, 2.9, ys.at[pl.ds(64, 64)], z0_buf.at[i]),
-                (FLIP_Z1, 2.9, ys.at[pl.ds(32, 32)], z1_buf.at[i]),
-                (FLIP_Z1, 2.9, al.at[pl.ds(0, 32)], al.at[pl.ds(32, 32)]),
-                (FLIP_Z0, 2.9, al.at[pl.ds(0, 64)], al.at[pl.ds(64, 64)]),
-                (FLIP_X, 5.7, al.at[pl.ds(0, 128)], al.at[pl.ds(128, 128)]),
-                (FLIP_C, 0.9, al, o_ref.at[k, pl.ds(256, 256)]),
-            ]
-        )
-        copies.append([None] * 8)
-    link = Link(send_sem, recv_sem)
-    keeps, outs = {}, {}
-
-    def fetch(i):
-        if i < len(chunks):
-            keeps[i] = pltpu.make_async_copy(
-                g_ref.at[chunks[i], pl.ds(0, 256)], keep_buf.at[i % 2], keep_sem.at[i % 2]
-            )
-            keeps[i].start()
-
-    fetch(0)
-    fetch(1)
-    for event, i, step in timetable([[(s[0], s[1]) for s in chain] for chain in chains], 2):
-        bit, _, source, target = chains[i][step]
-        if event == "start":
-            if step == 7:
-                outs[i] = pltpu.make_async_copy(source, o_ref.at[chunks[i], pl.ds(0, 256)], out_sem.at[i])
-                outs[i].start()
-            copies[i][step] = link.start(source, target, bit)
-            continue
-        copies[i][step].wait_recv()
-        if step == 0:
-            keeps[i].wait()
-            add_rows(y_buf.at[i], keep_buf.at[i % 2], 256)
-            fetch(i + 2)
-        elif step == 1:
-            add_rows(y_buf.at[i], x_buf.at[i], 128)
-        elif step == 2:
-            add_rows(y_buf.at[i], z0_buf.at[i], 64)
-        elif step == 3:
-            add_rows(y_buf.at[i], z1_buf.at[i], 32)
-            all_buf[i, 0:32, :] = y_buf[i, 0:32, :]
-    link.finish()
-    for copy in outs.values():
-        copy.wait()
-
-
-def reduce_gradients(grads, chunks):
-    n = len(chunks)
-    width = grads.shape[-1]
-    return pl.pallas_call(
-        functools.partial(reduce_kernel, chunks),
-        out_shape=jax.ShapeDtypeStruct(grads.shape, grads.dtype),
-        in_specs=[pl.BlockSpec(memory_space=pl.ANY)],
-        out_specs=pl.BlockSpec(memory_space=pl.ANY),
-        scratch_shapes=[
-            pltpu.VMEM((n, 256, width), BF16),
-            pltpu.VMEM((n, 128, width), BF16),
-            pltpu.VMEM((n, 64, width), BF16),
-            pltpu.VMEM((n, 32, width), BF16),
-            pltpu.VMEM((n, 256, width), BF16),
-            pltpu.VMEM((2, 256, width), BF16),
-            pltpu.SemaphoreType.DMA((8 * n,)),
-            pltpu.SemaphoreType.DMA((8 * n,)),
-            pltpu.SemaphoreType.DMA((2,)),
-            pltpu.SemaphoreType.DMA((n,)),
-        ],
-        compiler_params=pltpu.CompilerParams(
-            collective_id=1, has_side_effects=True, vmem_limit_bytes=VMEM_LIMIT
-        ),
-        cost_estimate=pl.CostEstimate(flops=0, bytes_accessed=100 << 20, transcendentals=0),
-        name="reduce_gradients",
-    )(grads)
+SLOTS = 8
+LAST_TICK = 10
+
+
+class Reduction:
+    def __init__(self, grads, sums, count, bufs, sems):
+        self.grads, self.sums, self.count = grads, sums, count
+        self.y_buf, self.x_buf, self.z0_buf, self.z1_buf, self.all_buf, self.keep_buf = bufs
+        self.send_sem, self.recv_sem, self.keep_sem, self.out_sem, self.in_free, self.out_free = sems
+
+    def copy(self, step, i):
+        slot = lax.rem(i, SLOTS)
+        ys, al = self.y_buf.at[slot], self.all_buf.at[slot]
+        bit, source, target = (
+            (FLIP_Y, self.grads.at[i, pl.ds(256, 256)], ys),
+            (FLIP_X, ys.at[pl.ds(128, 128)], self.x_buf.at[slot]),
+            (FLIP_Z0, ys.at[pl.ds(64, 64)], self.z0_buf.at[slot]),
+            (FLIP_Z1, ys.at[pl.ds(32, 32)], self.z1_buf.at[slot]),
+            (FLIP_Z1, al.at[pl.ds(0, 32)], al.at[pl.ds(32, 32)]),
+            (FLIP_Z0, al.at[pl.ds(0, 64)], al.at[pl.ds(64, 64)]),
+            (FLIP_X, al.at[pl.ds(0, 128)], al.at[pl.ds(128, 128)]),
+            (FLIP_C, al, self.sums.at[i, pl.ds(256, 256)]),
+        )[step]
+        return pltpu.make_async_remote_copy(
+            src_ref=source,
+            dst_ref=target,
+            send_sem=self.send_sem.at[step, slot],
+            recv_sem=self.recv_sem.at[step, slot],
+            device_id=partner(bit),
+            device_id_type=MESH,
+        )
+
+    def keep(self, i):
+        slot = lax.rem(i, 2)
+        return pltpu.make_async_copy(
+            self.grads.at[i, pl.ds(0, 256)], self.keep_buf.at[slot], self.keep_sem.at[slot]
+        )
+
+    def out(self, i):
+        slot = lax.rem(i, SLOTS)
+        return pltpu.make_async_copy(
+            self.all_buf.at[slot], self.sums.at[i, pl.ds(0, 256)], self.out_sem.at[slot]
+        )
+
+    def take(self, sem, i):
+        @pl.when(i >= SLOTS)
+        def _():
+            pl.semaphore_wait(sem, 1)
+
+    def give(self, sem, bit, i):
+        @pl.when(i + SLOTS < self.count)
+        def _():
+            pl.semaphore_signal(sem, inc=1, device_id=partner(bit), device_id_type=MESH)
+
+    def tick(self, t):
+        def at(offset, body):
+            i = t - offset
+            pl.when((i >= 0) & (i < self.count))(lambda: body(i, lax.rem(i, SLOTS)))
+
+        def set_out(i, slot):
+            self.take(self.in_free.at[0], i)
+            self.copy(0, i).start()
+            self.keep(i).start()
+
+        def finish(i, slot):
+            self.copy(7, i).wait()
+            self.out(i).wait()
+            for n, bit in enumerate((FLIP_X, FLIP_Z0, FLIP_Z1)):
+                self.give(self.out_free.at[n], bit, i)
+
+        def to_core(i, slot):
+            self.copy(6, i).wait()
+            self.copy(7, i).start()
+            self.out(i).start()
+
+        def back_x(i, slot):
+            self.copy(5, i).wait()
+            self.take(self.out_free.at[0], i)
+            self.copy(6, i).start()
+
+        def back_z0(i, slot):
+            self.copy(4, i).wait()
+            self.take(self.out_free.at[1], i)
+            self.copy(5, i).start()
+
+        def back_z1(i, slot):
+            self.copy(3, i).wait()
+            add_rows(self.y_buf.at[slot], self.z1_buf.at[slot], 32)
+            self.all_buf[slot, 0:32, :] = self.y_buf[slot, 0:32, :]
+            for n, bit in enumerate((FLIP_Y, FLIP_X, FLIP_Z0, FLIP_Z1)):
+                self.give(self.in_free.at[n], bit, i)
+            self.take(self.out_free.at[2], i)
+            self.copy(4, i).start()
+
+        def on_z1(i, slot):
+            self.copy(2, i).wait()
+            add_rows(self.y_buf.at[slot], self.z0_buf.at[slot], 64)
+            self.take(self.in_free.at[3], i)
+            self.copy(3, i).start()
+
+        def on_z0(i, slot):
+            self.copy(1, i).wait()
+            add_rows(self.y_buf.at[slot], self.x_buf.at[slot], 128)
+            self.take(self.in_free.at[2], i)
+            self.copy(2, i).start()
+
+        def on_x(i, slot):
+            self.copy(0, i).wait()
+            self.keep(i).wait()
+            add_rows(self.y_buf.at[slot], self.keep_buf.at[lax.rem(i, 2)], 256)
+            self.take(self.in_free.at[1], i)
+            self.copy(1, i).start()
+
+        at(0, set_out)
+        at(10, finish)
+        at(9, to_core)
+        at(7, back_x)
+        at(6, back_z0)
+        at(5, back_z1)
+        at(4, on_z1)
+        at(3, on_z0)
+        at(1, on_x)
+
+
+def stream(count, feeds, body):
+    for copy in feeds(0, 0):
+        copy.start()
+
+    def step(i, _):
+        slot = lax.rem(i, 2)
+
+        @pl.when(i + 1 < count)
+        def _():
+            for copy in feeds(i + 1, 1 - slot):
+                copy.start()
+
+        for copy in feeds(i, slot):
+            copy.wait()
+        body(i, slot)
+        return 0
+
+    lax.fori_loop(0, count, step, 0)
 
 
 def qkv_kernel(x_ref, w_ref, bias_ref, o_ref):
@@ -460,155 +521,6 @@
     )(ctx, x, weights, weights, weights, bias_in, vectors)
 
 
-def backward_kernel(
-    dx_ref, r2_ref, r1_ref, slope_ref, wo_ref, wi_ref, wd_ref, vec_ref,
-    dm_ref, du_ref, dr1_ref, da_ref, dctx_ref, dbi_ref, small_ref, acc_ref,
-):
-    step = pl.program_id(0) * pl.num_programs(1) + pl.program_id(1)
-    rows = dx_ref.shape[0]
-
-    def column_sums(parts):
-        return [jnp.sum(p, axis=0, keepdims=True) for p in parts]
-
-    @pl.when(step == 0)
-    def _():
-        small_ref[...] = jnp.zeros_like(small_ref)
-
-        def body(at):
-            dy = dx_ref[at, :]
-            dr, gain_part = norm_back(dy, r2_ref[at, :], vec_ref[4:5, :])
-            acc_ref[at, :] = dr
-            dm_ref[at, :] = dr.astype(BF16)
-            for i, p in enumerate(column_sums((gain_part, dy, dr))):
-                small_ref[i : i + 1, :] += p
-
-        row_tiles(rows, body)
-
-    dg = nt(dm_ref[...], block_of(wd_ref))
-    du = (dg * slope_ref[...].astype(F32)).astype(BF16)
-    du_ref[...] = du
-    dbi_ref[0, 0] = jnp.sum(du.astype(F32), axis=0, keepdims=True)
-    acc_ref[...] += nn(du, block_of(wi_ref))
-
-    @pl.when(step == 2 * FF_GROUPS - 1)
-    def _():
-        def body(at):
-            dy = acc_ref[at, :]
-            dr, gain_part = norm_back(dy, r1_ref[at, :], vec_ref[1:2, :])
-            dr1_ref[at, :] = dr
-            da_ref[at, :] = dr.astype(BF16)
-            for i, p in enumerate(column_sums((gain_part, dy, dr))):
-                small_ref[3 + i : 4 + i, :] += p
-
-        row_tiles(rows, body)
-        for a in range(2):
-            dctx_ref[:, a * 512 : (a + 1) * 512] = nt(da_ref[...], block_of(wo_ref.at[a])).astype(BF16)
-
-
-def backward_head(dx, r2, r1, slope, weights, vectors, first):
-    rows, width = dx.shape
-    whole = pl.BlockSpec((rows, width), lambda a, s: (0, 0))
-    hidden = pl.BlockSpec((rows, 512), lambda a, s: (0, a * FF_GROUPS + s))
-    sums = jax.ShapeDtypeStruct((rows, width), F32)
-    low = jax.ShapeDtypeStruct((rows, width), BF16)
-    return pl.pallas_call(
-        backward_kernel,
-        out_shape=(
-            low,
-            jax.ShapeDtypeStruct((rows, 4 * width), BF16),
-            sums,
-            low,
-            low,
-            jax.ShapeDtypeStruct((2, FF_GROUPS, 1, 512), F32),
-            jax.ShapeDtypeStruct((8, width), F32),
-        ),
-        grid=(2, FF_GROUPS),
-        in_specs=[
-            whole,
-            whole,
-            whole,
-            hidden,
-            pl.BlockSpec((2, 1, 2, 256, width), lambda a, s: (0, first + OUT_GROUP, 0, 0, 0)),
-            weight_spec(lambda s: first + in_group(s), width),
-            weight_spec(lambda s: first + down_group(s), width),
-            pl.BlockSpec((8, width), lambda a, s: (0, 0)),
-        ],
-        out_specs=(
-            whole,
-            hidden,
-            whole,
-            whole,
-            whole,
-            pl.BlockSpec((1, 1, 1, 512), lambda a, s: (a, s, 0, 0)),
-            pl.BlockSpec((8, width), lambda a, s: (0, 0)),
-        ),
-        scratch_shapes=[pltpu.VMEM((rows, width), F32)],
-        compiler_params=pltpu.CompilerParams(vmem_limit_bytes=VMEM_LIMIT),
-        cost_estimate=pl.CostEstimate(flops=18 * rows * width * width, bytes_accessed=40 << 20, transcendentals=0),
-        name="backward_head",
-    )(dx, r2, r1, slope, weights, weights, weights, vectors)
-
-
-def input_kernel(d_ref, dr1_ref, w_ref, dx_ref, sums_ref):
-    @pl.when((pl.program_id(0) == 0) & (pl.program_id(1) == 0))
-    def _():
-        dx_ref[...] = dr1_ref[...]
-
-    d = d_ref[0]
-    sums_ref[0, 0] = jnp.sum(d.astype(F32), axis=0, keepdims=True)
-    dx_ref[...] += nn(d, block_of(w_ref))
-
-
-def input_gradient(d_qkv, dr1, weights, first):
-    rows, width = dr1.shape
-    whole = pl.BlockSpec((rows, width), lambda a, t: (0, 0))
-    return pl.pallas_call(
-        input_kernel,
-        out_shape=(jax.ShapeDtypeStruct((rows, width), F32), jax.ShapeDtypeStruct((3, 2, 1, 512), F32)),
-        grid=(2, 3),
-        in_specs=[
-            pl.BlockSpec((1, rows, 512), lambda a, t: (t, 0, a)),
-            whole,
-            weight_spec(lambda t: first + t, width),
-        ],
-        out_specs=(whole, pl.BlockSpec((1, 1, 1, 512), lambda a, t: (t, a, 0, 0))),
-        compiler_params=pltpu.CompilerParams(vmem_limit_bytes=VMEM_LIMIT),
-        cost_estimate=pl.CostEstimate(flops=6 * rows * width * width, bytes_accessed=12 << 20, transcendentals=0),
-        name="input_gradient",
-    )(d_qkv, dr1, weights)
-
-
-def unit_kernel(left_ref, left_sib_ref, right_ref, right_sib_ref, *refs):
-    o_ref = refs[-1]
-    left = left_ref[...].reshape(left_ref.shape[-2:])
-    left_sib = left_sib_ref[...].reshape(left_sib_ref.shape[-2:])
-    o_ref[0] = (tn(left, right_ref[...]) + tn(left_sib, right_sib_ref[...])).astype(BF16)
-
-
-def unit_gradient(left, left_sib, right, right_sib, into, total, count, group):
-    rows, width = right.shape
-    more = [] if into is None else [into]
-    side = (
-        pl.BlockSpec((1, rows, 512), lambda i: (i, 0, 0))
-        if left.ndim == 3
-        else pl.BlockSpec((rows, 512), lambda i: (0, i))
-    )
-    whole = pl.BlockSpec((rows, width), lambda i: (0, 0))
-    return pl.pallas_call(
-        unit_kernel,
-        out_shape=jax.ShapeDtypeStruct((total, 512, width), BF16),
-        grid=(count,),
-        in_specs=[side, side, whole, whole] + [pl.BlockSpec(memory_space=pl.ANY) for _ in more],
-        out_specs=pl.BlockSpec((1, 512, width), lambda i: (group(i), 0, 0)),
-        input_output_aliases={4: 0} if more else {},
-        compiler_params=pltpu.CompilerParams(vmem_limit_bytes=VMEM_LIMIT),
-        cost_estimate=pl.CostEstimate(
-            flops=4 * rows * width * 512 * count, bytes_accessed=(count * 2 + 2) << 20, transcendentals=0
-        ),
-        name="unit_gradient",
-    )(left, left_sib, right, right_sib, *more)
-
-
 def pair_lanes(values, e):
     lane = lax.broadcasted_iota(jnp.int32, values.shape, 1)
     return jnp.where(lane // HEAD_DIM == e, values, jnp.zeros_like(values))
@@ -663,72 +575,376 @@
     )(q, k, v, k_sib, v_sib, hot, mask)
 
 
-def attend_back_kernel(
-    q_ref, ko_ref, vo_ref, ks_ref, vs_ref, hot_ref, mask_ref, ctx_ref, lse_ref, dctx_ref,
-    dq_ref, dko_ref, dvo_ref, dks_ref, dvs_ref,
-):
+def attend_back_pair(query, keys, values, hot, mask, ctx, lse, dctx):
     scale = HEAD_DIM**-0.5
-    rows = q_ref.shape[0]
-    keys = jnp.concatenate([ko_ref[...], ks_ref[...]], axis=0)
+    rows = query.shape[0]
+    query = query * jnp.asarray(scale, BF16)
     keys_t = keys.T
-    values = jnp.concatenate([vo_ref[...], vs_ref[...]], axis=0)
-    query = q_ref[...] * jnp.asarray(scale, BF16)
-    dctx = dctx_ref[...]
-    delta_t = (dctx.astype(F32) * ctx_ref[...].astype(F32)).T
-    dq_heads, dk, dv = [], 0.0, 0.0
-    for e in range(2):
-        query_e = pair_lanes(query, e)
-        dctx_e = pair_lanes(dctx, e)
-        right = jnp.concatenate([query_e, hot_ref[...]], axis=1)
-        left = jnp.concatenate([keys, mask_ref[e]], axis=1)
-        p = jnp.exp(nt(left, right) - lse_ref[0, e : e + 1, :])
-        dp = nt(values, dctx_e)
-        delta = jnp.sum(delta_t[e * HEAD_DIM : (e + 1) * HEAD_DIM, :], axis=0, keepdims=True)
-        ds = (p * (dp - delta)).astype(BF16)
-        dk = dk + nn(ds, query_e)
-        dv = dv + nn(p.astype(BF16), dctx_e)
-        dq_heads.append(nn(keys_t[e * HEAD_DIM : (e + 1) * HEAD_DIM, :], ds) * scale)
-    dq_ref[...] = jnp.concatenate(dq_heads, axis=0).T.astype(BF16)
-    dko_ref[...] = dk[:rows]
-    dvo_ref[...] = dv[:rows]
-    dks_ref[...] = dk[rows:].astype(BF16)
-    dvs_ref[...] = dv[rows:].astype(BF16)
-
-
-def attend_back(q, k, v, k_sib, v_sib, hot, mask, ctx, lse, dctx):
-    rows, width = q.shape
-    pairs = width // 128
-    own = pl.BlockSpec((rows, 128), lambda p: (0, p))
-    sib = pl.BlockSpec((rows, 128), lambda p: (0, p ^ (pairs // 2)))
+    delta_t = (dctx.astype(F32) * ctx.astype(F32)).T
+    tile = rows // 2
+    dk, dv, dq = 0.0, 0.0, []
+    for part in range(2):
+        at = slice(part * tile, (part + 1) * tile)
+        heads = []
+        for e in range(2):
+            lanes = slice(e * HEAD_DIM, (e + 1) * HEAD_DIM)
+            query_e = pair_lanes(query[at], e)
+            dctx_e = pair_lanes(dctx[at], e)
+            right = jnp.concatenate([query_e, hot[at]], axis=1)
+            left = jnp.concatenate([keys, mask[e]], axis=1)
+            p = jnp.exp(nt(left, right) - lse[e : e + 1, at])
+            dp = nt(values, dctx_e)
+            delta = jnp.sum(delta_t[lanes, at], axis=0, keepdims=True)
+            ds = (p * (dp - delta)).astype(BF16)
+            dk = dk + nn(ds, query_e)
+            dv = dv + nn(p.astype(BF16), dctx_e)
+            heads.append(nn(keys_t[lanes, :], ds) * scale)
+        dq.append(jnp.concatenate(heads, axis=0).T)
+    return jnp.concatenate(dq, axis=0), dk, dv
+
+
+PER_LAYER = 14
+
+
+def backward_kernel(layers, *refs):
+    refs = list(refs)
+    up_ref, w_ref, hot_ref, mask_ref, vec_ref = refs[:5]
+    saved = [refs[5 + PER_LAYER * l : 5 + PER_LAYER * (l + 1)] for l in range(layers)]
+    at_ref = 5 + PER_LAYER * layers
+    grads, sums, dx_out, dbi_ref, qkv_sums_ref, small_ref = refs[at_ref : at_ref + 6]
+    (
+        acc, dr1, dm, dm_sib, da, da_sib, du, du_sib, dctx, dqkv, d_sib, kv_out, kv_far,
+        wa_buf, wb_buf, r_buf, slope_buf, left_buf, left_sib_buf, right_buf, right_sib_buf,
+        pair_buf, lse_buf, mask_buf, hot_buf, unit_buf,
+        y_buf, x_buf, z0_buf, z1_buf, all_buf, keep_buf,
+        feed_sem, load_sem, store_sem, core_send, core_recv, du_send, du_recv,
+        send_sem, recv_sem, keep_sem, out_sem, in_free, out_free,
+    ) = refs[at_ref + 6 :]
+    rows, width = acc.shape
+    total = layers * GROUPS
+    reduction = Reduction(
+        grads, sums, total,
+        (y_buf, x_buf, z0_buf, z1_buf, all_buf, keep_buf),
+        (send_sem, recv_sem, keep_sem, out_sem, in_free, out_free),
+    )
+    greet((FLIP_Y, FLIP_X, FLIP_Z0, FLIP_Z1, FLIP_C))
+
+    def feed(n, slot, source, target):
+        return pltpu.make_async_copy(source, target, feed_sem.at[n, slot])
+
+    def load(n, source, target):
+        return pltpu.make_async_copy(source, target, load_sem.at[n])
+
+    def exchange(n, source, target):
+        return pltpu.make_async_remote_copy(
+            src_ref=source, dst_ref=target, send_sem=core_send.at[n], recv_sem=core_recv.at[n],
+            device_id=partner(FLIP_C), device_id_type=MESH,
+        )
+
+    def give_du(j, n):
+        return pltpu.make_async_remote_copy(
+            src_ref=du.at[j], dst_ref=du_sib.at[n], send_sem=du_send.at[n], recv_sem=du_recv.at[n],
+            device_id=partner(FLIP_C), device_id_type=MESH,
+        )
+
+    def weight(a, group):
+        return w_ref.at[a, group]
+
+    def columns(ref, i, size):
+        return ref.at[:, pl.ds(pl.multiple_of(i * size, size), size)]
+
+    def unit(left, left_sib, right, right_sib, index):
+        unit_buf[...] = (tn(left, right) + tn(left_sib, right_sib)).astype(BF16)
+        store = pltpu.make_async_copy(unit_buf, grads.at[index], store_sem.at[0])
+        store.start()
+        store.wait()
+
+    def add_small(l, row, value):
+        small_ref[l, row : row + 1, :] += jnp.sum(value, axis=0, keepdims=True)
+
+    start_up = load(0, up_ref, da)
+    start_up.start()
+    start_hot = load(1, hot_ref, hot_buf)
+    start_hot.start()
+    start_up.wait()
+    start_hot.wait()
+    small_ref[...] = jnp.zeros_like(small_ref)
+
+    def widen(at):
+        acc[at, :] = da[at, :].astype(F32)
+
+    row_tiles(rows, widen)
+    done = 0
+    for l in reversed(range(layers)):
+        qkv_ref, sib_ref, ctx_ref, ctx_sib_ref, lse_ref, r1_ref, r2_ref, hl_ref, hl_sib_ref, g_ref, g_sib_ref, slope_ref, xb_ref, xb_sib_ref = saved[l]
+        first = l * GROUPS
+        base = (layers - 1 - l) * GROUPS
+        clock = 11 * (layers - 1 - l)
+
+        r_load = load(0, r2_ref, r_buf)
+        r_load.start()
+        r_load.wait()
+
+        def second(at):
+            dy = acc[at, :]
+            dr, part = norm_back(dy, r_buf[at, :], vec_ref[l, 4:5, :])
+            acc[at, :] = dr
+            dm[at, :] = dr.astype(BF16)
+            add_small(l, 0, part)
+            add_small(l, 1, dy)
+            add_small(l, 2, dr)
+
+        row_tiles(rows, second)
+        dm_copy = exchange(0, dm, dm_sib)
+        dm_copy.start()
+        r_load = load(0, r1_ref, r_buf)
+        r_load.start()
+        right_load = load(1, hl_ref, right_buf)
+        right_load.start()
+        right_sib_load = load(2, hl_sib_ref, right_sib_buf)
+        right_sib_load.start()
+        dm_copy.wait()
+
+        def down_feeds(i, slot):
+            return (
+                feed(0, slot, columns(g_ref, i, 512), left_buf.at[slot]),
+                feed(1, slot, columns(g_sib_ref, i, 512), left_sib_buf.at[slot]),
+            )
+
+        def down_body(i, slot):
+            unit(left_buf[slot], left_sib_buf[slot], dm[...], dm_sib[...], base + i)
+            pl.when(lax.rem(i, 3) == 0)(lambda: reduction.tick(clock + lax.div(i, 3)))
+
+        stream(FF_GROUPS, down_feeds, down_body)
+
+        def place_of(i):
+            a = 1 - lax.div(i, FF_GROUPS)
+            return a, lax.rem(i, FF_GROUPS)
+
+        def ff_feeds(i, slot):
+            a, n = place_of(i)
+            j = a * FF_GROUPS + n
+            return (
+                feed(0, slot, weight(a, first + down_group(n)), wa_buf.at[slot]),
+                feed(1, slot, weight(a, first + in_group(n)), wb_buf.at[slot]),
+                feed(2, slot, columns(slope_ref, j, 512), slope_buf.at[slot]),
+            )
+
+        def ff_body(i, slot):
+            a, n = place_of(i)
+            j = a * FF_GROUPS + n
+            dg = nt(dm[...], block_of(wa_buf.at[slot]))
+            d = (dg * slope_buf[slot].astype(F32)).astype(BF16)
+            du[j] = d
+            pl.when(a == 1)(lambda: give_du(j, n).start())
+            dbi_ref[l, a, n] = jnp.sum(d.astype(F32), axis=0, keepdims=True)
+            acc[...] += nn(d, block_of(wb_buf.at[slot]))
+            pl.when(lax.rem(i, 3) == 2)(lambda: reduction.tick(clock + 2 + lax.div(i, 3)))
+
+        stream(2 * FF_GROUPS, ff_feeds, ff_body)
+
+        r_load.wait()
+
+        def first_norm(at):
+            dy = acc[at, :]
+            dr, part = norm_back(dy, r_buf[at, :], vec_ref[l, 1:2, :])
+            dr1[at, :] = dr
+            da[at, :] = dr.astype(BF16)
+            add_small(l, 3, part)
+            add_small(l, 4, dy)
+            add_small(l, 5, dr)
+
+        row_tiles(rows, first_norm)
+        da_copy = exchange(1, da, da_sib)
+        da_copy.start()
+
+        def out_feeds(i, slot):
+            return (feed(0, slot, weight(i, first + OUT_GROUP), wa_buf.at[slot]),)
+
+        def out_body(i, slot):
+            dctx[:, pl.ds(pl.multiple_of(i * 512, 512), 512)] = nt(da[...], block_of(wa_buf.at[slot])).astype(BF16)
+
+        stream(2, out_feeds, out_body)
+
+        right_load.wait()
+        right_sib_load.wait()
+
+        def in_body(n, _):
+            give_du(FF_GROUPS + n, n).wait()
+            unit(du[n], du_sib[n], right_buf[...], right_sib_buf[...], base + FF_GROUPS + n)
+            pl.when(lax.rem(n, 3) == 0)(lambda: reduction.tick(clock + 4 + lax.div(n, 3)))
+            return 0
+
+        lax.fori_loop(0, FF_GROUPS, in_body, 0)
+
+        right_load = load(1, xb_ref, right_buf)
+        right_load.start()
+        right_sib_load = load(2, xb_sib_ref, right_sib_buf)
+        right_sib_load.start()
+        left_load = load(3, columns(ctx_ref, 0, 512), left_buf.at[0])
+        left_load.start()
+        left_sib_load = load(4, ctx_sib_ref, left_sib_buf.at[0])
+        left_sib_load.start()
+        da_copy.wait()
+        left_load.wait()
+        left_sib_load.wait()
+        unit(left_buf[0], left_sib_buf[0], da[...], da_sib[...], base + 2 * FF_GROUPS)
+
+        pairs = width // 128
+
+        def pair_feeds(p, slot):
+            far = lax.rem(p + pairs // 2, pairs)
+            return (
+                feed(0, slot, columns(qkv_ref.at[0], p, 128), pair_buf.at[slot, 0, pl.ds(0, rows)]),
+                feed(1, slot, columns(qkv_ref.at[1], p, 128), pair_buf.at[slot, 1, pl.ds(0, rows)]),
+                feed(2, slot, columns(sib_ref.at[0], far, 128), pair_buf.at[slot, 1, pl.ds(rows, rows)]),
+                feed(3, slot, columns(qkv_ref.at[2], p, 128), pair_buf.at[slot, 2, pl.ds(0, rows)]),
+                feed(4, slot, columns(sib_ref.at[1], far, 128), pair_buf.at[slot, 2, pl.ds(rows, rows)]),
+                feed(5, slot, columns(ctx_ref, p, 128), pair_buf.at[slot, 3, pl.ds(0, rows)]),
+                feed(6, slot, lse_ref.at[p], lse_buf.at[slot]),
+                feed(7, slot, mask_ref.at[pl.ds(2 * p, 2)], mask_buf.at[slot]),
+            )
+
+        def pair_body(p, slot):
+            far = lax.rem(p + pairs // 2, pairs)
+            here = pl.ds(pl.multiple_of(p * 128, 128), 128)
+            dq, dk, dv = attend_back_pair(
+                pair_buf[slot, 0, 0:rows], pair_buf[slot, 1], pair_buf[slot, 2], hot_buf[...], mask_buf[slot],
+                pair_buf[slot, 3, 0:rows], lse_buf[slot], dctx[:, here],
+            )
+            dqkv[0, :, here] = dq.astype(BF16)
+            dqkv[1, :, here] = dk[:rows].astype(BF16)
+            dqkv[2, :, here] = dv[:rows].astype(BF16)
+            there = pl.ds(pl.multiple_of(far * 128, 128), 128)
+            kv_out[0, :, there] = dk[rows:].astype(BF16)
+            kv_out[1, :, there] = dv[rows:].astype(BF16)
+            pl.when(lax.rem(p, 3) == 1)(lambda: reduction.tick(clock + 6 + lax.div(p, 3)))
+
+        stream(pairs, pair_feeds, pair_body)
+        kv_copy = exchange(2, kv_out, kv_far)
+        kv_copy.start()
+        kv_copy.wait()
+        for n in range(2):
+            add_rows(dqkv.at[1 + n], kv_far.at[n], rows)
+        d_copy = exchange(3, dqkv.at[:, :, pl.ds(512, 512)], d_sib)
+        d_copy.start()
+        right_load.wait()
+        right_sib_load.wait()
+        d_copy.wait()
+
+        def qkv_body(n, _):
+            unit(dqkv[n, :, 0:512], d_sib[n], right_buf[...], right_sib_buf[...], base + 2 * FF_GROUPS + 1 + n)
+            return 0
+
+        lax.fori_loop(0, 3, qkv_body, 0)
+        reduction.tick(clock + 9)
+
+        def start_dx(at):
+            acc[at, :] = dr1[at, :]
+
+        row_tiles(rows, start_dx)
+
+        def dx_feeds(i, slot):
+            return (feed(0, slot, weight(lax.rem(i, 2), first + lax.div(i, 2)), wa_buf.at[slot]),)
+
+        def dx_body(i, slot):
+            a, n = lax.rem(i, 2), lax.div(i, 2)
+            d = dqkv[n, :, pl.ds(pl.multiple_of(a * 512, 512), 512)]
+            qkv_sums_ref[l, n, a] = jnp.sum(d.astype(F32), axis=0, keepdims=True)
+            acc[...] += nn(d, block_of(wa_buf.at[slot]))
+            pl.when(i == 3)(lambda: reduction.tick(clock + 10))
+
+        stream(6, dx_feeds, dx_body)
+        done = clock + 11
+
+    def narrow(at):
+        da[at, :] = acc[at, :].astype(BF16)
+
+    row_tiles(rows, narrow)
+    dx_store = load(0, da, dx_out)
+    dx_store.start()
+    dx_store.wait()
+
+    def rest(t, _):
+        reduction.tick(t)
+        return 0
+
+    lax.fori_loop(done, total + LAST_TICK, rest, 0)
+
+
+def backward(upstream, weights, hot, mask, vectors, saved):
+    rows, width = upstream.shape
+    layers = len(saved)
+    total = layers * GROUPS
+    anywhere = pl.BlockSpec(memory_space=pl.ANY)
+    in_vmem = pl.BlockSpec(memory_space=pltpu.VMEM)
+    low = lambda *shape: pltpu.VMEM(shape, BF16)
+    dma = lambda *shape: pltpu.SemaphoreType.DMA(shape)
     return pl.pallas_call(
-        attend_back_kernel,
+        functools.partial(backward_kernel, layers),
         out_shape=(
+            jax.ShapeDtypeStruct((total, 512, width), BF16),
+            jax.ShapeDtypeStruct((total, 512, width), BF16),
             jax.ShapeDtypeStruct((rows, width), BF16),
-            jax.ShapeDtypeStruct((rows, width), F32),
-            jax.ShapeDtypeStruct((rows, width), F32),
-            jax.ShapeDtypeStruct((rows, width), BF16),
-            jax.ShapeDtypeStruct((rows, width), BF16),
+            jax.ShapeDtypeStruct((layers, 2, FF_GROUPS, 1, 512), F32),
+            jax.ShapeDtypeStruct((layers, 3, 2, 1, 512), F32),
+            jax.ShapeDtypeStruct((layers, 8, width), F32),
         ),
-        grid=(pairs,),
-        in_specs=[
-            own,
-            own,
-            own,
-            sib,
-            sib,
-            pl.BlockSpec((rows, 128), lambda p: (0, 0)),
-            pl.BlockSpec((2, 2 * rows, 128), lambda p: (p, 0, 0)),
-            own,
-            pl.BlockSpec((1, 2, rows), lambda p: (p, 0, 0)),
-            own,
+        in_specs=[anywhere] * 4 + [in_vmem] + [anywhere] * (PER_LAYER * layers),
+        out_specs=(anywhere, anywhere, anywhere, in_vmem, in_vmem, in_vmem),
+        scratch_shapes=[
+            pltpu.VMEM((rows, width), F32),
+            pltpu.VMEM((rows, width), F32),
+            low(rows, width),
+            low(rows, width),
+            low(rows, width),
+            low(rows, width),
+            low(2 * FF_GROUPS, rows, 512),
+            low(FF_GROUPS, rows, 512),
+            low(rows, width),
+            low(3, rows, width),
+            low(3, rows, 512),
+            low(2, rows, width),
+            low(2, rows, width),
+            low(2, 2, 256, width),
+            low(2, 2, 256, width),
+            pltpu.VMEM((rows, width), F32),
+            low(2, rows, 512),
+            low(2, rows, 512),
+            low(2, rows, 512),
+            low(rows, width),
+            low(rows, width),
+            low(2, 4, 2 * rows, 128),
+            pltpu.VMEM((2, 2, rows), F32),
+            low(2, 2, 2 * rows, 128),
+            low(rows, 128),
+            low(512, width),
+            low(SLOTS, 256, width),
+            low(SLOTS, 128, width),
+            low(SLOTS, 64, width),
+            low(SLOTS, 32, width),
+            low(SLOTS, 256, width),
+            low(2, 256, width),
+            dma(8, 2),
+            dma(5),
+            dma(1),
+            dma(4),
+            dma(4),
+            dma(FF_GROUPS),
+            dma(FF_GROUPS),
+            dma(8, SLOTS),
+            dma(8, SLOTS),
+            dma(2),
+            dma(SLOTS),
+            pltpu.SemaphoreType.REGULAR((4,)),
+            pltpu.SemaphoreType.REGULAR((3,)),
         ],
-        out_specs=(own, own, own, sib, sib),
-        compiler_params=pltpu.CompilerParams(vmem_limit_bytes=VMEM_LIMIT),
-        cost_estimate=pl.CostEstimate(
-            flops=20 * rows * rows * 128 * pairs * 2, bytes_accessed=24 << 20, transcendentals=4 * rows * rows * pairs
+        compiler_params=pltpu.CompilerParams(
+            collective_id=1, has_side_effects=True, vmem_limit_bytes=60 << 20
         ),
-        name="attend_back",
-    )(q, k, v, k_sib, v_sib, hot, mask, ctx, lse, dctx)
+        cost_estimate=pl.CostEstimate(flops=60 << 30, bytes_accessed=300 << 20, transcendentals=1 << 24),
+        name="backward",
+    )(upstream, weights, hot, mask, vectors, *[ref for one in saved for ref in one])
 
 
 def flip_order(values, axis, bits):
@@ -867,64 +1083,43 @@
         xb_sib, hidden_sib = flip((xb, hidden), FLIP_C)
         ctx_sib = flip(ctx[:, half:], FLIP_C)
         g_sib = flip(g[:, 4 * half :], FLIP_C)
-        saved.append((xb, xb_sib, q, k, v, k_sib, v_sib, ctx, ctx_sib, lse, r1, hidden, hidden_sib, g, g_sib, slope, r2))
+        kv_sib = jnp.stack([k_sib, v_sib])
+        saved.append((qkv, kv_sib, ctx, ctx_sib, lse, r1, r2, hidden, hidden_sib, g, g_sib, slope, xb, xb_sib))
     block_output = swap_core_and_y(stream_now).astype(F32)[:, None]
 
-    upstream = upstream_low.astype(F32)
-    grads = None
-    small = [None] * layers
-    for layer in reversed(range(layers)):
-        first = layer * GROUPS
-        xb, xb_sib, q, k, v, k_sib, v_sib, ctx, ctx_sib, lse, r1, hidden, hidden_sib, g, g_sib, slope, r2 = saved[layer]
-        dm, du, dr1, da, dctx, d_b_in, rows_small = backward_head(
-            upstream, r2, r1, slope, weights, vectors[layer], first
-        )
-        dm_sib, da_sib = flip((dm, da), FLIP_C)
-        du_sib = flip(du[:, 4 * half :], FLIP_C)
-        unit = functools.partial(unit_gradient, total=total)
-        grads = unit(g, g_sib, dm, dm_sib, grads, count=FF_GROUPS, group=lambda i, f=first: f + down_group(i))
-        grads = unit(du, du_sib, hidden, hidden_sib, grads, count=FF_GROUPS, group=lambda i, f=first: f + in_group(i))
-        grads = unit(ctx, ctx_sib, da, da_sib, grads, count=1, group=lambda i, f=first: f + OUT_GROUP)
-        dq, dk, dv, dk_sib, dv_sib = attend_back(q, k, v, k_sib, v_sib, hot, mask, ctx, lse, dctx)
-        dk_far, dv_far = flip((dk_sib, dv_sib), FLIP_C)
-        d_qkv = jnp.stack(
-            [dq, (dk + dk_far.astype(F32)).astype(BF16), (dv + dv_far.astype(F32)).astype(BF16)]
-        )
-        d_qkv_sib = flip(d_qkv[:, :, half:], FLIP_C)
-        grads = unit(d_qkv, d_qkv_sib, xb, xb_sib, grads, count=3, group=lambda i, f=first: f + i)
-        upstream, qkv_sums = input_gradient(d_qkv, dr1, weights, first)
-        small[layer] = (
-            jnp.stack([qkv_sums[0], qkv_sums[2]]),
-            rows_small[5],
-            d_b_in,
-            rows_small[2],
-            jnp.stack([rows_small[3], rows_small[0]]),
-            jnp.stack([rows_small[4], rows_small[1]]),
-        )
-    input_grad = swap_core_and_y(upstream.astype(BF16)).astype(F32)[:, None]
-    grads = reduce_gradients(grads, tuple(range(total)))
+    _, grads, dx_low, d_b_in, qkv_sums, rows_small = backward(
+        upstream_low, weights, hot, mask, jnp.stack(vectors), saved
+    )
+    input_grad = swap_core_and_y(dx_low).astype(F32)[:, None]
 
     placed = [None] * 4
     for layer in range(layers):
-        first = layer * GROUPS
+        first = (layers - 1 - layer) * GROUPS
         put = functools.partial(place, grads, code=code_arg)
         placed[0] = put(
-            w_qkv.shape, (1, 1, width, 512), lambda i, l=layer: (l, i, 0, 0), True, 3, lambda i, f=first: f + i, placed[0]
+            w_qkv.shape, (1, 1, width, 512), lambda i, l=layer: (l, i, 0, 0), True, 3,
+            lambda i, f=first: f + 2 * FF_GROUPS + 1 + i, placed[0],
         )
         placed[1] = put(
             w_out.shape, (1, 512, width), lambda i, l=layer: (l, 0, 0), False, 1,
-            lambda i, f=first: f + OUT_GROUP, placed[1],
+            lambda i, f=first: f + 2 * FF_GROUPS, placed[1],
         )
         placed[2] = put(
             w_in.shape, (1, width, 512), lambda i, l=layer: (l, 0, i), True, FF_GROUPS,
-            lambda i, f=first: f + in_group(i), placed[2],
+            lambda i, f=first: f + FF_GROUPS + i, placed[2],
         )
         placed[3] = put(
             w_down.shape, (1, 512, width), lambda i, l=layer: (l, i, 0), False, FF_GROUPS,
-            lambda i, f=first: f + down_group(i), placed[3],
-        )
-    stacks = [jnp.stack([small[layer][member] for layer in range(layers)]) for member in range(6)]
-    stacks[2] = stacks[2].swapaxes(1, 2)
+            lambda i, f=first: f + i, placed[3],
+        )
+    stacks = [
+        jnp.stack([qkv_sums[:, 0], qkv_sums[:, 2]], axis=1),
+        rows_small[:, 5],
+        d_b_in.swapaxes(1, 2),
+        rows_small[:, 2],
+        jnp.stack([rows_small[:, 3], rows_small[:, 0]], axis=1),
+        jnp.stack([rows_small[:, 4], rows_small[:, 1]], axis=1),
+    ]
 
     def global_order(values, lead):
         values = values.reshape(lead, 2, 2, 2, 2, 2, 32).swapaxes(1, 2)

time: 977 us -> 822 us (0.84)
  Pallas kernels: 816 us -> 688 us
  waiting for transfers between devices: 4.98 us -> 23.1 us
  starting transfers between devices: 48.6 us -> 31.3 us
  other arithmetic: 30.7 us -> 15.8 us
  local copies, waits for them, and re-layouts: 58.7 us -> 48.4 us
    pallas_call x15 -> x1, Pallas kernels: 489 us -> 362 us  [backward(): pl.pallas_call(functools.partial(backward_kernel, layers), out_shape=(jax...]
    ppermute x32 -> x20, waiting for transfers between devices: 4.97 us -> 23.1 us  [flip(): lax.ppermute(v, ('dp', 'tensor'), pairs)]
    unnamed x143 -> x115, local copies, waits for them, and re-layouts: 19.8 us -> 15.1 us
  transfers between devices with their start and end apart: 36 -> 24, of which waited for: 5 -> 6; matrix products, arithmetic and copies ran while one was open for 8% -> 6% of each run, Pallas kernels for 38% -> 77%
where the time goes in v2:
time: 822 us; the launch traced here: 809 us
  Pallas kernels  688 us (84%)
  local copies, waits for them, and re-layouts  48.4 us (6%)
  starting transfers between devices  31.3 us (4%)
  waiting for transfers between devices  23.1 us (3%)
  other arithmetic  15.8 us (2%)
    pallas_call x1, Pallas kernels, backward(): pl.pallas_call(functools.partial(backward_kernel, layers), out_shape=(jax...  362 us
    pallas_call x1, Pallas kernels, spread_weights(): pl.pallas_call(functools.partial(spread_kernel, chunks), out_shape=jax.Sh...  133 us
    pallas_call x2, Pallas kernels, forward_tail(): pl.pallas_call(forward_kernel, out_shape=(sums, low, wide, wide, sums, su...  51.9 us
    pallas_call x8, Pallas kernels, convert(): pl.pallas_call(functools.partial(convert_kernel, transposed), out_shape=j...  44.7 us
    pallas_call x8, Pallas kernels, place(): pl.pallas_call(functools.partial(place_kernel, transposed), out_shape=jax...  40.8 us
    pallas_call x2, Pallas kernels, attend(): pl.pallas_call(attend_kernel, out_shape=(jax.ShapeDtypeStruct((rows, widt...  38.1 us
    ppermute x20, waiting for transfers between devices, flip(): lax.ppermute(v, ('dp', 'tensor'), pairs)  23.1 us
    ppermute x4, starting transfers between devices, swap_core_and_y(): lax.ppermute(v, ('dp', 'tensor'), pairs)  21.8 us
  transfers between devices with their start and end apart: 24, of which 6 were waited for; matrix products, arithmetic and copies ran while one was open for 6% of the time, Pallas kernels for 77%

profile of v2, /device:TPU:0, one launch (start us, length us, event | category | flops | bytes accessed | tf_op | source)
XLA Modules:
  0.0 809.0 jit_solution(17515600268587747694)
XLA Ops:
  0.8 0.8 reshape.306
  2.1 0.8 reshape.304
  3.7 3.0 collective-permute-start.1
  6.7 2.9 copy.78
  9.6 9.5 %collective-permute-start = (bf16[512,1024]{1,0:T(8,128)(2,1)}, bf16[512,1024]{1,0:T(8,128)(2,1)}, u32[]{:S(2)}, u32[]{:S(2)}) collective-permute-start(bf16[512,1024]{1,0:T(8,128)(2,1)} %bitcast.92), channel_id=1, source_target_pairs={{0,0},{1,2},{2,1},{3,3},{4,4},{5,6},{6,5},{7,7},{8,8},{9,10},{10,9... | collective-permute-start | bytes 3145736 | tf_op jit(solution)/shard_map/ppermute | solution.py:40
  21.9 4.0 collective-permute-done.4
  27.5 0.7 reshape_reshape.21
  28.2 0.7 reshape_reshape.24
  28.9 6.3 convert.20.refs_0_
  35.2 2.8 convert.21.refs_0_
  38.1 7.1 convert.22.refs_0_
  45.2 6.1 convert.23.refs_0_
  51.2 6.3 convert.24.refs_0_
  57.6 2.8 convert.25.refs_0_
  60.4 7.2 convert.26.refs_0_
  67.5 6.1 convert.27.w_in_ref
  73.7 133.4 %spread_weights.1.w_ref.wo_ref.wi_ref.wd_ref.refs_1_ = bf16[2,24,2,256,1024]{4,3,2,1,0:T(8,128)(2,1)} custom-call(bf16[2,24,2,256,1024]{4,3,2,1,0:T(8,128)(2,1)} %convert.27.w_in_ref), custom_call_target="tpu_custom_call", output_to_operand_aliasing={{}: (0, {})} | custom-call | bytes 52428800 | tf_op jit(solution)/shard_map/spread_weights/pallas_call | solution.py:227
  210.5 8.5 %project_qkv.2.refs_5_ = bf16[3,512,1024]{2,1,0:T(8,128)(2,1)} custom-call(bf16[512,1024]{1,0:T(8,128)(2,1)} %collective-permute-done.x_ref.refs_17_, bf16[2,24,2,256,1024]{4,3,2,1,0:T(8,128)(2,1)} %spread_weights.1.w_ref.wo_ref.wi_ref.wd_ref.refs_1_, f32[3,2,1,512]{3,2,1,0:T(1,128)} %get-tuple-element.114.bias_ref), custom_call_target="tpu_custom_call" | custom-call | flops 3221225472 | bytes 10485760 | tf_op jit(solution)/shard_map/project_qkv/pallas_call | solution.py:399
  218.9 3.5 slice_bitcast_fusion.3
  222.4 0.9 collective-permute-start.2
  223.5 0.8 pad_maximum_fusion.3.hot_ref.refs_2_
  225.0 0.8 broadcast_in_dim.59
  225.8 3.7 pad_maximum_fusion.mask_ref.refs_3_
  229.5 0.7 slice.280
  231.0 2.8 convert_element_type.40.x_ref
  233.8 1.0 copy-done.4
  235.1 19.0 %attend.2 = (bf16[512,1024]{1,0:T(8,128)(2,1)}, f32[8,2,512]{2,1,0:T(2,128)}) custom-call(bf16[512,1024]{1,0:T(8,128)(2,1)} %get-tuple-element.97.q_ref, bf16[512,1024]{1,0:T(8,128)(2,1)} %get-tuple-element.96.ko_ref, bf16[512,1024]{1,0:T(8,128)(2,1)} %copy-done.12, bf16[512,1024]{1,0:T(8,128)(2,1)} %copy-done.4, bf16[512,1024]{1,0:T(8,128)(2,1)} %copy-done.6, ...), custom_call_target="tpu_custom_call" | custom-call | flops 4294967296 | bytes 16777216 | tf_op jit(solution)/shard_map/attend/pallas_call | solution.py:553
  254.1 26.1 %forward_tail.2 = (f32[512,1024]{1,0:T(8,128)}, bf16[512,1024]{1,0:T(8,128)(2,1)}, bf16[512,4096]{1,0:T(8,128)(2,1)}, bf16[512,4096]{1,0:T(8,128)(2,1)}, f32[512...) custom-call(bf16[512,1024]{1,0:T(8,128)(2,1)} %get-tuple-element.34.ctx_ref.refs_7_, ...), custom_call_target="tpu_custom_call" | custom-call | flops 9663676416 | bytes 41943040 | tf_op jit(solution)/shard_map/forward_tail/pallas_call | solution.py:501
  280.3 8.5 %project_qkv.3.refs_19_ = bf16[3,512,1024]{2,1,0:T(8,128)(2,1)} custom-call(bf16[512,1024]{1,0:T(8,128)(2,1)} %get-tuple-element.35.x_ref.refs_31_, bf16[2,24,2,256,1024]{4,3,2,1,0:T(8,128)(2,1)} %spread_weights.1.w_ref.wo_ref.wi_ref.wd_ref.refs_1_, f32[3,2,1,512]{3,2,1,0:T(1,128)} %get-tuple-element.113.bias_ref), custom_call_target="tpu_custom_call" | custom-call | flops 3221225472 | bytes 10485760 | tf_op jit(solution)/shard_map/project_qkv/pallas_call | solution.py:399
  288.8 3.6 slice_bitcast_fusion
  292.9 1.3 copy.79
  294.3 9.4 %collective-permute-start.9 = (bf16[512,1024]{1,0:T(8,128)(2,1)}, bf16[512,1024]{1,0:T(8,128)(2,1)}, u32[]{:S(2)}, u32[]{:S(2)}) collective-permute-start(bf16[512,1024]{1,0:T(8,128)(2,1)} %bitcast.93), channel_id=1, source_target_pairs={{0,0},{1,2},{2,1},{3,3},{4,4},{5,6},{6,5},{7,7},{8,8},{9,10},{10,9... | collective-permute-start | bytes 3145736 | tf_op jit(solution)/shard_map/ppermute | solution.py:40
  304.4 3.1 slice.248
  308.1 1.0 copy-done.8
  309.4 19.1 %attend.3 = (bf16[512,1024]{1,0:T(8,128)(2,1)}, f32[8,2,512]{2,1,0:T(2,128)}) custom-call(bf16[512,1024]{1,0:T(8,128)(2,1)} %get-tuple-element.94.q_ref, bf16[512,1024]{1,0:T(8,128)(2,1)} %get-tuple-element.93.ko_ref, bf16[512,1024]{1,0:T(8,128)(2,1)} %copy-done.13, bf16[512,1024]{1,0:T(8,128)(2,1)} %copy-done.8, bf16[512,1024]{1,0:T(8,128)(2,1)} %copy-done.10, ...), custom_call_target="tpu_custom_call" | custom-call | flops 4294967296 | bytes 16777216 | tf_op jit(solution)/shard_map/attend/pallas_call | solution.py:553
  328.4 25.7 %forward_tail.3 = (f32[512,1024]{1,0:T(8,128)}, bf16[512,1024]{1,0:T(8,128)(2,1)}, bf16[512,4096]{1,0:T(8,128)(2,1)}, bf16[512,4096]{1,0:T(8,128)(2,1)}, f32[512...) custom-call(bf16[512,1024]{1,0:T(8,128)(2,1)} %get-tuple-element.36.ctx_ref.refs_21_, ...), custom_call_target="tpu_custom_call" | custom-call | flops 9663676416 | bytes 41943040 | tf_op jit(solution)/shard_map/forward_tail/pallas_call | solution.py:501
  354.2 3.4 slice.250
  358.8 6.3 collective-permute-done.10.refs_8_
  365.5 0.8 slice.249
  366.4 0.9 copy-done.49
  368.1 1.5 pad_maximum_fusion.1.refs_6_
  369.6 1.5 pad_maximum_fusion.2.refs_20_
  371.1 1.9 collective-permute-start.8
  373.0 362.2 %backward.1 = (bf16[24,512,1024]{2,1,0:T(8,128)(2,1)}, bf16[24,512,1024]{2,1,0:T(8,128)(2,1)}, bf16[512,1024]{1,0:T(8,128)(2,1)}, f32[2,2,4,1,512]{4,3,2,1,0:T(1...) custom-call(bf16[512,1024]{1,0:T(8,128)(2,1)} %collective-permute-done.9.refs_0_, ...), custom_call_target="tpu_custom_call" | custom-call | flops 64424509440 | bytes 314572800 | tf_op jit(solution)/shard_map/backward/pallas_call | solution.py:883
  735.2 1.1 fusion.12
  736.4 0.8 copy.63
  738.1 0.7 fusion.13
  740.0 0.9 collective-permute-done.19
  741.3 1.0 collective-permute-start.18
  742.3 3.8 collective-permute-done.20
  746.4 4.4 collective-permute-done.21
  750.8 1.0 collective-permute-start.22
  751.8 3.7 collective-permute-done.22
  755.5 1.0 collective-permute-start.23
  756.7 3.5 copy.65
  760.2 5.9 place.14.refs_0_
  766.1 6.4 place.12.refs_0_
  772.6 2.7 place.10.refs_0_
  775.2 5.3 place.8.refs_0_
  780.6 5.9 place.15
  786.5 6.4 place.13
  793.0 2.7 place.11
  795.6 5.3 place.9
  805.1 3.5 copy.66
  (246 shorter events, 22.1 us)
Async XLA Ops:
  0.6 18.4 %copy-start.38 = (s32[1,8,16,3]{2,1,3,0:T(8,128)S(1)}, s32[1,8,16,3]{2,1,3,0:T(8,128)}, u32[]{:S(2)}) copy-start(s32[1,8,16,3]{2,1,3,0:T(8,128)} %param.16) | copy-start | bytes 4612
  0.7 18.5 %copy-start.35 = (f32[2,2,1024]{2,1,0:T(2,128)S(1)}, f32[2,2,1024]{2,1,0:T(2,128)}, u32[]{:S(2)}) copy-start(f32[2,2,1024]{2,1,0:T(2,128)} %param.25) | copy-start | bytes 49156
  0.7 18.5 %copy-start.34 = (f32[2,2,1024]{2,1,0:T(2,128)S(1)}, f32[2,2,1024]{2,1,0:T(2,128)}, u32[]{:S(2)}) copy-start(f32[2,2,1024]{2,1,0:T(2,128)} %param.26) | copy-start | bytes 49156
  0.7 19.1 %copy-start.41 = (f32[2,1024]{1,0:T(2,128)S(1)}, f32[2,1024]{1,0:T(2,128)}, u32[]{:S(2)}) copy-start(f32[2,1024]{1,0:T(2,128)} %param.20) | copy-start | bytes 24580
  0.7 19.1 %copy-start.40 = (f32[2,1024]{1,0:T(2,128)S(1)}, f32[2,1024]{1,0:T(2,128)}, u32[]{:S(2)}) copy-start(f32[2,1024]{1,0:T(2,128)} %param.24) | copy-start | bytes 24580
  0.7 25.5 %copy-start.32 = (s32[1,1024]{1,0:T(1,128)S(1)}, s32[1,1024]{1,0:T(1,128)}, u32[]{:S(2)}) copy-start(s32[1,1024]{1,0:T(1,128)} %param.15) | copy-start | bytes 12292
  3.7 205.3 %collective-permute-start.1 = (f32[6144]{0:T(1024)}, f32[6144]{0:T(1024)}, u32[]{:S(2)}, u32[]{:S(2)}) collective-permute-start(f32[6144]{0:T(1024)} %pad_maximum_fusion.6), channel_id=1, source_target_pairs={{0,1},{1,0},{2,3},{3,2},{4,5},{5,4},{6,7},{7,6},{8,9},{9,8},{10,11... | collective-permute-start | bytes 73736 | tf_op jit(solution)/shard_map/ppermute | solution.py:35
  9.6 200.9 %collective-permute-start = (bf16[512,1024]{1,0:T(8,128)(2,1)}, bf16[512,1024]{1,0:T(8,128)(2,1)}, u32[]{:S(2)}, u32[]{:S(2)}) collective-permute-start(bf16[512,1024]{1,0:T(8,128)(2,1)} %bitcast.92), channel_id=1, source_target_pairs={{0,0},{1,2},{2,1},{3,3},{4,4},{5,6},{6,5},{7,7},{8,8},{9,10},{10,9... | collective-permute-start | bytes 3145736 | tf_op jit(solution)/shard_map/ppermute | solution.py:40
  19.0 6.8 collective-permute-start.4
  19.1 16.2 %copy-start.43 = (s32[16]{0:T(128)}, s32[16]{0:T(128)S(1)}, u32[]{:S(2)}) copy-start(s32[16]{0:T(128)S(1)} %iota_xor_fusion) | copy-start | bytes 196
  21.9 13.3 %copy-start.20 = (s32[384]{0:T(512)}, s32[384]{0:T(512)S(1)}, u32[]{:S(2)}) copy-start(s32[384]{0:T(512)S(1)} %reshape_squeeze.9) | copy-start | bytes 4612
  26.2 9.0 %copy-start.22 = (s32[384]{0:T(512)}, s32[384]{0:T(512)S(1)}, u32[]{:S(2)}) copy-start(s32[384]{0:T(512)S(1)} %reshape.309) | copy-start | bytes 4612
  26.9 181.1 %collective-permute-start.5 = (s32[1792]{0:T(1024)}, s32[1792]{0:T(1024)}, u32[]{:S(2)}, u32[]{:S(2)}) collective-permute-start(s32[1792]{0:T(1024)} %pad_add_fusion), channel_id=1, source_target_pairs={{0,2},{1,3},{2,0},{3,1},{4,6},{5,7},{6,4},{7,5},{8,10},{9,11},{10,... | collective-permute-start | bytes 21512 | tf_op jit(solution)/shard_map/ppermute | solution.py:35
  73.6 133.6 %copy-start.18 = (f32[1,1024]{1,0:T(1,128)S(1)}, f32[1,1024]{1,0:T(1,128)}, u32[]{:S(2)}) copy-start(f32[1,1024]{1,0:T(1,128)} %get-tuple-element.137) | copy-start | bytes 12292
  73.6 133.6 %copy-start.28 = (f32[1,1024]{1,0:T(1,128)S(1)}, f32[1,1024]{1,0:T(1,128)}, u32[]{:S(2)}) copy-start(f32[1,1024]{1,0:T(1,128)} %get-tuple-element.116) | copy-start | bytes 12292
  73.6 133.6 %copy-start.29 = (f32[1,1024]{1,0:T(1,128)S(1)}, f32[1,1024]{1,0:T(1,128)}, u32[]{:S(2)}) copy-start(f32[1,1024]{1,0:T(1,128)} %get-tuple-element.117) | copy-start | bytes 12292
  73.6 133.6 %copy-start.30 = (f32[1,1024]{1,0:T(1,128)S(1)}, f32[1,1024]{1,0:T(1,128)}, u32[]{:S(2)}) copy-start(f32[1,1024]{1,0:T(1,128)} %get-tuple-element.134) | copy-start | bytes 12292
  73.6 133.6 %copy-start.31 = (f32[1,1024]{1,0:T(1,128)S(1)}, f32[1,1024]{1,0:T(1,128)}, u32[]{:S(2)}) copy-start(f32[1,1024]{1,0:T(1,128)} %get-tuple-element.135) | copy-start | bytes 12292
  73.6 133.6 %copy-start.37 = (f32[1,1024]{1,0:T(1,128)S(1)}, f32[1,1024]{1,0:T(1,128)}, u32[]{:S(2)}) copy-start(f32[1,1024]{1,0:T(1,128)} %get-tuple-element.126) | copy-start | bytes 12292
  73.7 134.3 %copy-start.21 = (s32[384]{0:T(512)S(1)}, s32[384]{0:T(512)}, u32[]{:S(2)}) copy-start(s32[384]{0:T(512)} %copy-done.20) | copy-start | bytes 4612
  73.7 134.3 %copy-start.23 = (s32[384]{0:T(512)S(1)}, s32[384]{0:T(512)}, u32[]{:S(2)}) copy-start(s32[384]{0:T(512)} %copy-done.22) | copy-start | bytes 4612
  73.7 134.3 %copy-start.33 = (s32[1,1024]{1,0:T(1,128)S(1)}, s32[1,1024]{1,0:T(1,128)}, u32[]{:S(2)}) copy-start(s32[1,1024]{1,0:T(1,128)} %param.15) | copy-start | bytes 12292
  73.7 134.8 %copy-start.44 = (s32[16]{0:T(128)S(1)}, s32[16]{0:T(128)}, u32[]{:S(2)}) copy-start(s32[16]{0:T(128)} %copy-done.43) | copy-start | bytes 196
  73.7 135.0 %copy-start.42 = (pred[16,8]{0,1:T(8,128)(4,1)S(1)}, pred[16,8]{0,1:T(8,128)(4,1)}, u32[]{:S(2)}) copy-start(pred[16,8]{0,1:T(8,128)(4,1)} %fusion.8) | copy-start | bytes 388
  73.7 136.0 %copy-start.19 = (f32[4,2,1,256]{3,2,1,0:T(1,128)S(1)}, f32[4,2,1,256]{3,2,1,0:T(1,128)}, u32[]{:S(2)}) copy-start(f32[4,2,1,256]{3,2,1,0:T(1,128)} %reshape_reshape.21) | copy-start | bytes 24580
  218.9 4.5 copy-start.39
  218.9 5.3 copy-start.45
  222.4 11.3 %collective-permute-start.2 = (bf16[512,1024]{1,0:T(8,128)(2,1)}, bf16[512,1024]{1,0:T(8,128)(2,1)S(1)}, u32[]{:S(2)}, u32[]{:S(2)}) collective-permute-start(bf16[512,1024]{1,0:T(8,128)(2,1)} %get-tuple-element.96.ko_ref), channel_id=1, source_target_pairs={{0,2},{1,3},{2,0},{3,1},{4,6},{5,7},{6,4},{7,5},{8,10},{9,11},{10,... | collective-permute-start | bytes 3145736 | tf_op jit(solution)/shard_map/ppermute | solution.py:35
  223.3 10.5 %collective-permute-start.3 = (bf16[512,1024]{1,0:T(8,128)(2,1)S(1)}, bf16[512,1024]{1,0:T(8,128)(2,1)S(1)}, u32[]{:S(2)}, u32[]{:S(2)}) collective-permute-start(bf16[512,1024]{1,0:T(8,128)(2,1)S(1)} %get-tuple-element.95.vo_ref), channel_id=1, source_target_pairs={{0,2},{1,3},{2,0},{3,1},{4,6},{5,7},{6,4},{7,5},{8,10},{9,11},{10,... | collective-permute-start | bytes 3145736 | tf_op jit(solution)/shard_map/ppermute | solution.py:35
  225.8 4.4 copy-start.16
  288.7 4.2 copy-start.2
  288.7 15.0 %copy-start.17 = (f32[1,1024]{1,0:T(1,128)S(1)}, f32[1,1024]{1,0:T(1,128)}, u32[]{:S(2)}) copy-start(f32[1,1024]{1,0:T(1,128)} %get-tuple-element.138) | copy-start | bytes 12292
  288.7 15.0 %copy-start.24 = (f32[1,1024]{1,0:T(1,128)S(1)}, f32[1,1024]{1,0:T(1,128)}, u32[]{:S(2)}) copy-start(f32[1,1024]{1,0:T(1,128)} %get-tuple-element.115) | copy-start | bytes 12292
  288.8 15.0 %copy-start.25 = (f32[1,1024]{1,0:T(1,128)S(1)}, f32[1,1024]{1,0:T(1,128)}, u32[]{:S(2)}) copy-start(f32[1,1024]{1,0:T(1,128)} %get-tuple-element.118) | copy-start | bytes 12292
  288.8 15.0 %copy-start.26 = (f32[1,1024]{1,0:T(1,128)S(1)}, f32[1,1024]{1,0:T(1,128)}, u32[]{:S(2)}) copy-start(f32[1,1024]{1,0:T(1,128)} %get-tuple-element.133) | copy-start | bytes 12292
  288.8 15.0 %copy-start.27 = (f32[1,1024]{1,0:T(1,128)S(1)}, f32[1,1024]{1,0:T(1,128)}, u32[]{:S(2)}) copy-start(f32[1,1024]{1,0:T(1,128)} %get-tuple-element.136) | copy-start | bytes 12292
  288.8 15.0 %copy-start.36 = (f32[1,1024]{1,0:T(1,128)S(1)}, f32[1,1024]{1,0:T(1,128)}, u32[]{:S(2)}) copy-start(f32[1,1024]{1,0:T(1,128)} %get-tuple-element.125) | copy-start | bytes 12292
  292.4 15.7 %copy-start.13 = (bf16[512,1024]{1,0:T(8,128)(2,1)}, bf16[512,1024]{1,0:T(8,128)(2,1)S(1)}, u32[]{:S(2)}) copy-start(bf16[512,1024]{1,0:T(8,128)(2,1)S(1)} %get-tuple-element.92.vo_ref) | copy-start | bytes 3145732
  292.4 15.7 %collective-permute-start.6 = (bf16[512,1024]{1,0:T(8,128)(2,1)}, bf16[512,1024]{1,0:T(8,128)(2,1)S(1)}, u32[]{:S(2)}, u32[]{:S(2)}) collective-permute-start(bf16[512,1024]{1,0:T(8,128)(2,1)} %get-tuple-element.93.ko_ref), channel_id=1, source_target_pairs={{0,2},{1,3},{2,0},{3,1},{4,6},{5,7},{6,4},{7,5},{8,10},{9,11},{10,... | collective-permute-start | bytes 3145736 | tf_op jit(solution)/shard_map/ppermute | solution.py:35
  292.9 15.1 %collective-permute-start.7 = (bf16[512,1024]{1,0:T(8,128)(2,1)S(1)}, bf16[512,1024]{1,0:T(8,128)(2,1)S(1)}, u32[]{:S(2)}, u32[]{:S(2)}) collective-permute-start(bf16[512,1024]{1,0:T(8,128)(2,1)S(1)} %get-tuple-element.92.vo_ref), channel_id=1, source_target_pairs={{0,2},{1,3},{2,0},{3,1},{4,6},{5,7},{6,4},{7,5},{8,10},{9,11},{10,... | collective-permute-start | bytes 3145736 | tf_op jit(solution)/shard_map/ppermute | solution.py:35
  294.3 64.0 %collective-permute-start.9 = (bf16[512,1024]{1,0:T(8,128)(2,1)}, bf16[512,1024]{1,0:T(8,128)(2,1)}, u32[]{:S(2)}, u32[]{:S(2)}) collective-permute-start(bf16[512,1024]{1,0:T(8,128)(2,1)} %bitcast.93), channel_id=1, source_target_pairs={{0,0},{1,2},{2,1},{3,3},{4,4},{5,6},{6,5},{7,7},{8,8},{9,10},{10,9... | collective-permute-start | bytes 3145736 | tf_op jit(solution)/shard_map/ppermute | solution.py:40
  304.4 53.9 %collective-permute-start.13 = (bf16[512,1024]{1,0:T(8,128)(2,1)}, bf16[512,1024]{1,0:T(8,128)(2,1)S(1)}, u32[]{:S(2)}, u32[]{:S(2)}) collective-permute-start(bf16[512,1024]{1,0:T(8,128)(2,1)} %collective-permute-done.x_ref.refs_17_), channel_id=1, source_target_pairs={{0,2},{1,3},{2,0},{3,1},{4,6},{5,7},{6,4},{7,5},{8,10},{9,11},{10,... | collective-permute-start | bytes 3145736 | tf_op jit(solution)/shard_map/ppermute | solution.py:35
  307.6 65.4 %collective-permute-start.12 = (bf16[512,2048]{1,0:T(8,128)(2,1)}, bf16[512,2048]{1,0:T(8,128)(2,1)}, u32[]{:S(2)}, u32[]{:S(2)}) collective-permute-start(bf16[512,2048]{1,0:T(8,128)(2,1)} %slice.248), channel_id=1, source_target_pairs={{0,2},{1,3},{2,0},{3,1},{4,6},{5,7},{6,4},{7,5},{8,10},{9,11},{10,... | collective-permute-start | bytes 6291464 | tf_op jit(solution)/shard_map/ppermute | solution.py:35
  328.4 29.2 %copy-start.47 = (bf16[512,1024]{1,0:T(8,128)(2,1)S(1)}, bf16[512,1024]{1,0:T(8,128)(2,1)}, u32[]{:S(2)}) copy-start(bf16[512,1024]{1,0:T(8,128)(2,1)} %get-tuple-element.42.refs_12_) | copy-start | bytes 3145732
  354.2 11.3 %copy-start.1 = (bf16[512,1024]{1,0:T(8,128)(2,1)S(1)}, bf16[512,1024]{1,0:T(8,128)(2,1)}, u32[]{:S(2)}) copy-start(bf16[512,1024]{1,0:T(8,128)(2,1)} %get-tuple-element.36.ctx_ref.refs_21_) | copy-start | bytes 3145732
  354.2 13.3 %copy-start.14 = (f32[8,1024]{1,0:T(8,128)S(1)}, f32[8,1024]{1,0:T(8,128)}, u32[]{:S(2)}) copy-start(f32[8,1024]{1,0:T(8,128)} %stack.46.vec_ref) | copy-start | bytes 98308
  354.2 13.3 %copy-start.15 = (f32[8,1024]{1,0:T(8,128)S(1)}, f32[8,1024]{1,0:T(8,128)}, u32[]{:S(2)}) copy-start(f32[8,1024]{1,0:T(8,128)} %stack.47.vec_ref) | copy-start | bytes 98308
  354.2 13.9 %copy-start.5 = (bf16[512,1024]{1,0:T(8,128)(2,1)S(1)}, bf16[512,1024]{1,0:T(8,128)(2,1)}, u32[]{:S(2)}) copy-start(bf16[512,1024]{1,0:T(8,128)(2,1)} %copy-done.4) | copy-start | bytes 3145732
  354.2 13.9 %copy-start.7 = (bf16[512,1024]{1,0:T(8,128)(2,1)S(1)}, bf16[512,1024]{1,0:T(8,128)(2,1)}, u32[]{:S(2)}) copy-start(bf16[512,1024]{1,0:T(8,128)(2,1)} %copy-done.6) | copy-start | bytes 3145732
  357.6 15.4 %collective-permute-start.16 = (bf16[512,2048]{1,0:T(8,128)(2,1)}, bf16[512,2048]{1,0:T(8,128)(2,1)}, u32[]{:S(2)}, u32[]{:S(2)}) collective-permute-start(bf16[512,2048]{1,0:T(8,128)(2,1)} %slice.250), channel_id=1, source_target_pairs={{0,2},{1,3},{2,0},{3,1},{4,6},{5,7},{6,4},{7,5},{8,10},{9,11},{10,... | collective-permute-start | bytes 6291464 | tf_op jit(solution)/shard_map/ppermute | solution.py:35
  357.7 8.7 %collective-permute-start.11 = (bf16[512,1024]{1,0:T(8,128)(2,1)S(1)}, bf16[512,1024]{1,0:T(8,128)(2,1)S(1)}, u32[]{:S(2)}, u32[]{:S(2)}) collective-permute-start(bf16[512,1024]{1,0:T(8,128)(2,1)S(1)} %copy-done.47), channel_id=1, source_target_pairs={{0,2},{1,3},{2,0},{3,1},{4,6},{5,7},{6,4},{7,5},{8,10},{9,11},{10,... | collective-permute-start | bytes 3145736 | tf_op jit(solution)/shard_map/ppermute | solution.py:35
  358.2 6.9 collective-permute-start.10
  358.3 8.0 copy-start.48
  358.3 12.8 %collective-permute-start.17 = (bf16[512,1024]{1,0:T(8,128)(2,1)S(1)}, bf16[512,1024]{1,0:T(8,128)(2,1)}, u32[]{:S(2)}, u32[]{:S(2)}) collective-permute-start(bf16[512,1024]{1,0:T(8,128)(2,1)S(1)} %copy-done.3), channel_id=1, source_target_pairs={{0,2},{1,3},{2,0},{3,1},{4,6},{5,7},{6,4},{7,5},{8,10},{9,11},{10,... | collective-permute-start | bytes 3145736 | tf_op jit(solution)/shard_map/ppermute | solution.py:35
  365.1 7.8 collective-permute-start.15
  367.3 5.6 collective-permute-start.14
  371.1 385.4 %collective-permute-start.8 = (bf16[512,1024]{1,0:T(8,128)(2,1)}, bf16[512,1024]{1,0:T(8,128)(2,1)S(1)}, u32[]{:S(2)}, u32[]{:S(2)}) collective-permute-start(bf16[512,1024]{1,0:T(8,128)(2,1)} %get-tuple-element.38), channel_id=1, source_target_pairs={{0,0},{1,2},{2,1},{3,3},{4,4},{5,6},{6,5},{7,7},{8,8},{9,10},{10,9... | collective-permute-start | bytes 3145736 | tf_op jit(solution)/shard_map/ppermute | solution.py:40
  735.2 6.1 copy-start.46
  739.6 1.4 collective-permute-start.19
  741.0 5.1 collective-permute-start.20
  741.3 63.5 %collective-permute-start.18 = (bf16[512,1024]{1,0:T(8,128)(2,1)S(1)}, bf16[512,1024]{1,0:T(8,128)(2,1)S(1)}, u32[]{:S(2)}, u32[]{:S(2)}) collective-permute-start(bf16[512,1024]{1,0:T(8,128)(2,1)S(1)} %copy-done.46), channel_id=1, source_target_pairs={{0,0},{1,2},{2,1},{3,3},{4,4},{5,6},{6,5},{7,7},{8,8},{9,10},{10,9... | collective-permute-start | bytes 3145736 | tf_op jit(solution)/shard_map/ppermute | solution.py:40
  746.1 4.7 collective-permute-start.21
  750.8 4.7 collective-permute-start.22
  755.5 45.5 %collective-permute-start.23 = (f32[24576]{0:T(1024)S(1)}, f32[24576]{0:T(1024)S(1)}, u32[]{:S(2)}, u32[]{:S(2)}) collective-permute-start(f32[24576]{0:T(1024)S(1)} %add.74), channel_id=1, source_target_pairs={{0,16},{1,17},{2,18},{3,19},{4,20},{5,21},{6,22},{7,23},{8,24},{9,... | collective-permute-start | bytes 294920 | tf_op jit(solution)/shard_map/ppermute | solution.py:35
  (11 other events, 22.0 us)

commit v3 on v2

--- a/solution.py
+++ b/solution.py
@@ -15,6 +15,7 @@
 VMEM_LIMIT = 56 << 20
 
 FLIP_Y, FLIP_C, FLIP_X, FLIP_Z0, FLIP_Z1 = 1, 2, 4, 8, 16
+SWAP = FLIP_Y + FLIP_C
 DEVICES = 32
 
 GROUPS = 12
@@ -35,11 +36,6 @@
     return jax.tree.map(lambda v: lax.ppermute(v, ("dp", "tensor"), pairs), values)
 
 
-def swap_core_and_y(values):
-    pairs = [(i, i ^ 3 if (i & 1) != ((i >> 1) & 1) else i) for i in range(DEVICES)]
-    return jax.tree.map(lambda v: lax.ppermute(v, ("dp", "tensor"), pairs), values)
-
-
 def nt(a, b):
     return lax.dot_general(a, b, (((1,), (1,)), ((), ())), preferred_element_type=F32)
 
@@ -55,37 +51,6 @@
 def block_of(ref):
     width = ref.shape[-1]
     return ref[...].reshape(-1, width)
-
-
-def convert_kernel(transposed, code_ref, w_ref, *refs):
-    o_ref, t_ref = refs[-2:]
-    code = code_ref[0]
-    half = w_ref[...].reshape(w_ref.shape[-2:])
-    t_ref[...] = half.T if transposed else half
-    for j in range(16):
-        start = pl.multiple_of((j ^ code) * 32, 32)
-        o_ref[j // 8, 0, 0, (j % 8) * 32 : (j % 8 + 1) * 32, :] = t_ref[pl.ds(start, 32), :].astype(BF16)
-
-
-def convert(w, block, index, transposed, count, group, into, total, code):
-    width = 1024
-    more = [] if into is None else [into]
-    return pl.pallas_call(
-        functools.partial(convert_kernel, transposed),
-        out_shape=jax.ShapeDtypeStruct((2, total, 2, 256, width), BF16),
-        grid_spec=pltpu.PrefetchScalarGridSpec(
-            num_scalar_prefetch=1,
-            grid=(count,),
-            in_specs=[pl.BlockSpec(block, lambda i, code: index(i))]
-            + [pl.BlockSpec(memory_space=pl.ANY) for _ in more],
-            out_specs=pl.BlockSpec((2, 1, 1, 256, width), lambda i, code: (0, group(i), 0, 0, 0)),
-            scratch_shapes=[pltpu.VMEM((512, width), F32)],
-        ),
-        input_output_aliases={2: 0} if more else {},
-        compiler_params=pltpu.CompilerParams(vmem_limit_bytes=VMEM_LIMIT),
-        cost_estimate=pl.CostEstimate(flops=0, bytes_accessed=count * 512 * width * 6, transcendentals=0),
-        name="convert",
-    )(code, w, *more)
 
 
 def place_kernel(transposed, code_ref, g_ref, *refs):
@@ -119,13 +84,13 @@
     )(code, grads, *more)
 
 
-def partner(bit):
+def partner(bits):
     dp, y = lax.axis_index("dp"), lax.axis_index("tensor")
-    if bit == FLIP_Y:
-        return (dp, 1 - y)
-    step = bit // 2
-    up = (dp // step) % 2
-    return (dp + step * (1 - 2 * up), y)
+    other = dp
+    for step in (1, 2, 4, 8):
+        if bits & (2 * step):
+            other = other + step * (1 - 2 * ((dp // step) % 2))
+    return (other, 1 - y if bits & FLIP_Y else y)
 
 
 def greet(bits):
@@ -135,108 +100,6 @@
     pl.semaphore_wait(barrier, len(bits))
 
 
-class Link:
-    def __init__(self, send_sem, recv_sem):
-        self.send_sem, self.recv_sem, self.used, self.open = send_sem, recv_sem, 0, []
-
-    def start(self, source, target, bit):
-        copy = pltpu.make_async_remote_copy(
-            src_ref=source,
-            dst_ref=target,
-            send_sem=self.send_sem.at[self.used],
-            recv_sem=self.recv_sem.at[self.used],
-            device_id=partner(bit),
-            device_id_type=MESH,
-        )
-        copy.start()
-        self.used += 1
-        self.open.append(copy)
-        return copy
-
-    def finish(self):
-        for copy in self.open:
-            copy.wait_send()
-
-
-def timetable(chains, window):
-    events, clock = [], 0.0
-    queue = {}
-    ready = [(i, 0) for i in range(len(chains))]
-    flying = []
-    free = {}
-    while ready or flying:
-        moved = True
-        while moved:
-            moved = False
-            for item in sorted(ready, key=lambda it: (it[0], it[1])):
-                link, time = chains[item[0]][item[1]]
-                if sum(1 for f in flying if f[2] == link) < window:
-                    begin = max(clock, free.get(link, 0.0))
-                    free[link] = begin + time
-                    flying.append((begin + time + 2.0, item, link))
-                    events.append(("start",) + item)
-                    ready.remove(item)
-                    moved = True
-                    break
-        flying.sort()
-        clock, item, _ = flying.pop(0)
-        events.append(("land",) + item)
-        if item[1] + 1 < len(chains[item[0]]):
-            ready.append((item[0], item[1] + 1))
-    return events
-
-
-def spread_kernel(chunks, w_in_ref, w_ref, send_sem, recv_sem):
-    del w_in_ref
-    greet((FLIP_Y, FLIP_X, FLIP_Z0, FLIP_C))
-    chains, copies = [], []
-    for k in chunks:
-        if k % GROUPS < 4:
-            steps = [
-                (FLIP_Y, 5.7, w_ref.at[0, k, 0, pl.ds(0, 128)], w_ref.at[0, k, 1, pl.ds(0, 128)]),
-                (FLIP_X, 5.7, w_ref.at[0, k, 1, pl.ds(0, 128)], w_ref.at[0, k, 1, pl.ds(128, 128)]),
-            ]
-        else:
-            steps = [
-                (FLIP_Y, 2.9, w_ref.at[0, k, 0, pl.ds(0, 64)], w_ref.at[0, k, 1, pl.ds(0, 64)]),
-                (FLIP_Z0, 2.9, w_ref.at[0, k, 1, pl.ds(0, 64)], w_ref.at[0, k, 1, pl.ds(64, 64)]),
-                (FLIP_X, 5.7, w_ref.at[0, k, 1, pl.ds(0, 128)], w_ref.at[0, k, 1, pl.ds(128, 128)]),
-            ]
-            if (k // 2) % 2 == 0:
-                steps = [
-                    (FLIP_Y, 2.9, w_ref.at[0, k, 0, pl.ds(0, 64)], w_ref.at[0, k, 1, pl.ds(0, 64)]),
-                    (FLIP_X, 2.9, w_ref.at[0, k, 1, pl.ds(0, 64)], w_ref.at[0, k, 1, pl.ds(128, 64)]),
-                    (FLIP_Z0, 2.9, w_ref.at[0, k, 1, pl.ds(0, 64)], w_ref.at[0, k, 1, pl.ds(64, 64)]),
-                    (FLIP_Z0, 2.9, w_ref.at[0, k, 1, pl.ds(128, 64)], w_ref.at[0, k, 1, pl.ds(192, 64)]),
-                ]
-        steps.append((FLIP_C, 0.9, w_ref.at[0, k, 1], w_ref.at[1, k, 1]))
-        chains.append(steps)
-        copies.append([None] * len(steps))
-    link = Link(send_sem, recv_sem)
-    for event, i, step in timetable([[(s[0], s[1]) for s in chain] for chain in chains], 2):
-        bit, _, source, target = chains[i][step]
-        if event == "start":
-            copies[i][step] = link.start(source, target, bit)
-        else:
-            copies[i][step].wait_recv()
-    link.finish()
-
-
-def spread_weights(weights, chunks):
-    count = sum(3 if k % GROUPS < 4 else (5 if (k // 2) % 2 == 0 else 4) for k in chunks)
-    return pl.pallas_call(
-        functools.partial(spread_kernel, chunks),
-        out_shape=jax.ShapeDtypeStruct(weights.shape, weights.dtype),
-        in_specs=[pl.BlockSpec(memory_space=pl.ANY)],
-        out_specs=pl.BlockSpec(memory_space=pl.ANY),
-        scratch_shapes=[pltpu.SemaphoreType.DMA((count,)), pltpu.SemaphoreType.DMA((count,))],
-        input_output_aliases={0: 0},
-        compiler_params=pltpu.CompilerParams(collective_id=0, has_side_effects=True),
-        cost_estimate=pl.CostEstimate(flops=0, bytes_accessed=50 << 20, transcendentals=0),
-        name="spread_weights",
-    )(weights)
-
-
 def add_rows(into, other, rows):
     def step(i, _):
         at = pl.ds(pl.multiple_of(i * 32, 32), 32)
@@ -254,7 +117,8 @@
     def __init__(self, grads, sums, count, bufs, sems):
         self.grads, self.sums, self.count = grads, sums, count
         self.y_buf, self.x_buf, self.z0_buf, self.z1_buf, self.all_buf, self.keep_buf = bufs
-        self.send_sem, self.recv_sem, self.keep_sem, self.out_sem, self.in_free, self.out_free = sems
+        self.send_sem, self.recv_sem, self.core_send, self.core_recv = sems[:4]
+        self.keep_sem, self.out_sem, self.in_free, self.out_free = sems[4:]
 
     def copy(self, step, i):
         slot = lax.rem(i, SLOTS)
@@ -272,8 +136,8 @@
         return pltpu.make_async_remote_copy(
             src_ref=source,
             dst_ref=target,
-            send_sem=self.send_sem.at[step, slot],
-            recv_sem=self.recv_sem.at[step, slot],
+            send_sem=self.send_sem.at[step, slot] if step < 7 else self.core_send.at[i],
+            recv_sem=self.recv_sem.at[step, slot] if step < 7 else self.core_recv.at[i],
             device_id=partner(bit),
             device_id_type=MESH,
         )
@@ -388,28 +252,6 @@
         return 0
 
     lax.fori_loop(0, count, step, 0)
-
-
-def qkv_kernel(x_ref, w_ref, bias_ref, o_ref):
-    o_ref[0] = (nt(x_ref[...], block_of(w_ref)) + bias_ref[0, 0]).astype(BF16)
-
-
-def project_qkv(x_low, weights, bias, first):
-    rows, width = x_low.shape
-    return pl.pallas_call(
-        qkv_kernel,
-        out_shape=jax.ShapeDtypeStruct((3, rows, width), BF16),
-        grid=(2, 3),
-        in_specs=[
-            pl.BlockSpec((rows, width), lambda a, t: (0, 0)),
-            pl.BlockSpec((1, 1, 2, 256, width), lambda a, t: (a, first + t, 0, 0, 0)),
-            pl.BlockSpec((1, 1, 1, 512), lambda a, t: (t, a, 0, 0)),
-        ],
-        out_specs=pl.BlockSpec((1, rows, 512), lambda a, t: (t, 0, a)),
-        compiler_params=pltpu.CompilerParams(vmem_limit_bytes=VMEM_LIMIT),
-        cost_estimate=pl.CostEstimate(flops=6 * rows * width * width, bytes_accessed=10 << 20, transcendentals=0),
-        name="project_qkv",
-    )(x_low, weights, bias)
 
 
 def norm(r, gain, shift):
@@ -448,131 +290,33 @@
     lax.fori_loop(0, rows // TILE, step, 0)
 
 
-def forward_kernel(
-    ctx_ref, x_ref, wo_ref, wi_ref, wd_ref, bi_ref, vec_ref,
-    r1_ref, hl_ref, g_ref, slope_ref, r2_ref, x2_ref, xl_ref, acc_ref,
-):
-    step = pl.program_id(0) * pl.num_programs(1) + pl.program_id(1)
-    rows = x_ref.shape[0]
-
-    @pl.when(step == 0)
-    def _():
-        acc_ref[...] = nn(ctx_ref[:, :512], block_of(wo_ref.at[0])) + nn(ctx_ref[:, 512:], block_of(wo_ref.at[1]))
-
-        def body(at):
-            r1 = x_ref[at, :] + acc_ref[at, :] + vec_ref[0:1, :]
-            r1_ref[at, :] = r1
-            h = norm(r1, vec_ref[1:2, :], vec_ref[2:3, :])
-            hl_ref[at, :] = h.astype(BF16)
-            acc_ref[at, :] = h + vec_ref[3:4, :]
-
-        row_tiles(rows, body)
-
-    u = nt(hl_ref[...], block_of(wi_ref)) + bi_ref[0, 0]
-    g, slope = gelu_and_slope(u)
-    g = g.astype(BF16)
-    g_ref[...] = g
-    slope_ref[...] = slope.astype(BF16)
-    acc_ref[...] += nn(g, block_of(wd_ref))
-
-    @pl.when(step == 2 * FF_GROUPS - 1)
-    def _():
-        def body(at):
-            r2 = acc_ref[at, :]
-            r2_ref[at, :] = r2
-            x2 = norm(r2, vec_ref[4:5, :], vec_ref[5:6, :])
-            x2_ref[at, :] = x2
-            xl_ref[at, :] = x2.astype(BF16)
-
-        row_tiles(rows, body)
-
-
-def weight_spec(group, width):
-    return pl.BlockSpec((1, 1, 2, 256, width), lambda a, s: (a, group(s), 0, 0, 0))
-
-
-def forward_tail(ctx, x, weights, bias_in, vectors, first):
-    rows, width = x.shape
-    whole = pl.BlockSpec((rows, width), lambda a, s: (0, 0))
-    hidden = pl.BlockSpec((rows, 512), lambda a, s: (0, a * FF_GROUPS + s))
-    sums = jax.ShapeDtypeStruct((rows, width), F32)
-    low = jax.ShapeDtypeStruct((rows, width), BF16)
-    wide = jax.ShapeDtypeStruct((rows, 4 * width), BF16)
-    return pl.pallas_call(
-        forward_kernel,
-        out_shape=(sums, low, wide, wide, sums, sums, low),
-        grid=(2, FF_GROUPS),
-        in_specs=[
-            whole,
-            whole,
-            pl.BlockSpec((2, 1, 2, 256, width), lambda a, s: (0, first + OUT_GROUP, 0, 0, 0)),
-            weight_spec(lambda s: first + in_group(s), width),
-            weight_spec(lambda s: first + down_group(s), width),
-            pl.BlockSpec((1, 1, 1, 512), lambda a, s: (a, s, 0, 0)),
-            pl.BlockSpec((8, width), lambda a, s: (0, 0)),
-        ],
-        out_specs=(whole, whole, hidden, hidden, whole, whole, whole),
-        scratch_shapes=[pltpu.VMEM((rows, width), F32)],
-        compiler_params=pltpu.CompilerParams(vmem_limit_bytes=VMEM_LIMIT),
-        cost_estimate=pl.CostEstimate(
-            flops=18 * rows * width * width, bytes_accessed=40 << 20, transcendentals=8 * rows * width
-        ),
-        name="forward_tail",
-    )(ctx, x, weights, weights, weights, bias_in, vectors)
-
-
 def pair_lanes(values, e):
     lane = lax.broadcasted_iota(jnp.int32, values.shape, 1)
     return jnp.where(lane // HEAD_DIM == e, values, jnp.zeros_like(values))
 
 
-def attend_kernel(q_ref, ko_ref, vo_ref, ks_ref, vs_ref, hot_ref, mask_ref, ctx_ref, lse_ref):
+def attend_pair(query, keys, values, hot, mask):
     scale = HEAD_DIM**-0.5
-    keys = jnp.concatenate([ko_ref[...], ks_ref[...]], axis=0)
-    values_t = jnp.concatenate([vo_ref[...], vs_ref[...]], axis=0).T
-    query = q_ref[...] * jnp.asarray(scale, BF16)
-    heads = []
-    for e in range(2):
-        right = jnp.concatenate([pair_lanes(query, e), hot_ref[...]], axis=1)
-        left = jnp.concatenate([keys, mask_ref[e]], axis=1)
-        s = nt(left, right)
-        top = jnp.max(s, axis=0, keepdims=True)
-        p = jnp.exp(s - top)
-        total = jnp.sum(p, axis=0, keepdims=True)
-        c = nn(values_t[e * HEAD_DIM : (e + 1) * HEAD_DIM, :], p.astype(BF16))
-        heads.append(c * (1.0 / total))
-        lse_ref[0, e : e + 1, :] = top + jnp.log(total)
-    ctx_ref[...] = jnp.concatenate(heads, axis=0).T.astype(BF16)
-
-
-def attend(q, k, v, k_sib, v_sib, hot, mask):
-    rows, width = q.shape
-    pairs = width // 128
-    own = pl.BlockSpec((rows, 128), lambda p: (0, p))
-    sib = pl.BlockSpec((rows, 128), lambda p: (0, p ^ (pairs // 2)))
-    return pl.pallas_call(
-        attend_kernel,
-        out_shape=(
-            jax.ShapeDtypeStruct((rows, width), BF16),
-            jax.ShapeDtypeStruct((pairs, 2, rows), F32),
-        ),
-        grid=(pairs,),
-        in_specs=[
-            own,
-            own,
-            own,
-            sib,
-            sib,
-            pl.BlockSpec((rows, 128), lambda p: (0, 0)),
-            pl.BlockSpec((2, 2 * rows, 128), lambda p: (p, 0, 0)),
-        ],
-        out_specs=(own, pl.BlockSpec((1, 2, rows), lambda p: (p, 0, 0))),
-        compiler_params=pltpu.CompilerParams(vmem_limit_bytes=VMEM_LIMIT),
-        cost_estimate=pl.CostEstimate(
-            flops=8 * rows * rows * 128 * pairs * 2, bytes_accessed=16 << 20, transcendentals=4 * rows * rows * pairs
-        ),
-        name="attend",
-    )(q, k, v, k_sib, v_sib, hot, mask)
+    rows = query.shape[0]
+    query = query * jnp.asarray(scale, BF16)
+    values_t = values.T
+    tile = rows // 2
+    contexts, lses = [], ([], [])
+    for part in range(2):
+        at = slice(part * tile, (part + 1) * tile)
+        heads = []
+        for e in range(2):
+            right = jnp.concatenate([pair_lanes(query[at], e), hot[at]], axis=1)
+            left = jnp.concatenate([keys, mask[e]], axis=1)
+            s = nt(left, right)
+            top = jnp.max(s, axis=0, keepdims=True)
+            p = jnp.exp(s - top)
+            total = jnp.sum(p, axis=0, keepdims=True)
+            c = nn(values_t[e * HEAD_DIM : (e + 1) * HEAD_DIM, :], p.astype(BF16))
+            heads.append(c * (1.0 / total))
+            lses[e].append(top + jnp.log(total))
+        contexts.append(jnp.concatenate(heads, axis=0).T)
+    return jnp.concatenate(contexts, axis=0), [jnp.concatenate(parts, axis=1) for parts in lses]
 
 
 def attend_back_pair(query, keys, values, hot, mask, ctx, lse, dctx):
@@ -603,7 +347,452 @@
     return jnp.concatenate(dq, axis=0), dk, dv
 
 
+class Spread:
+    def __init__(self, weights, pairs, send_sem, recv_sem):
+        self.weights, self.pairs, self.send_sem, self.recv_sem = weights, pairs, send_sem, recv_sem
+
+    def copy(self, step, t):
+        w = self.weights
+        even, odd = 2 * t, 2 * t + 1
+        bit, source, target = (
+            (FLIP_Y, w.at[0, even, 0, pl.ds(0, 64)], w.at[0, even, 1, pl.ds(0, 64)]),
+            (FLIP_Y, w.at[0, odd, 0, pl.ds(0, 64)], w.at[0, odd, 1, pl.ds(0, 64)]),
+            (FLIP_X, w.at[0, even, 1, pl.ds(0, 64)], w.at[0, even, 1, pl.ds(128, 64)]),
+            (FLIP_Z0, w.at[0, odd, 1, pl.ds(0, 64)], w.at[0, odd, 1, pl.ds(64, 64)]),
+            (FLIP_Z0, w.at[0, even, 1, pl.ds(0, 64)], w.at[0, even, 1, pl.ds(64, 64)]),
+            (FLIP_Z0, w.at[0, even, 1, pl.ds(128, 64)], w.at[0, even, 1, pl.ds(192, 64)]),
+            (FLIP_X, w.at[0, odd, 1, pl.ds(0, 128)], w.at[0, odd, 1, pl.ds(128, 128)]),
+            (FLIP_C, w.at[0, even, 1], w.at[1, even, 1]),
+            (FLIP_C, w.at[0, odd, 1], w.at[1, odd, 1]),
+        )[step]
+        return pltpu.make_async_remote_copy(
+            src_ref=source,
+            dst_ref=target,
+            send_sem=self.send_sem.at[step, t],
+            recv_sem=self.recv_sem.at[step, t],
+            device_id=partner(bit),
+            device_id_type=MESH,
+        )
+
+    def tick(self, t):
+        def at(offset, waits, starts):
+            i = t - offset
+
+            @pl.when((i >= 0) & (i < self.pairs))
+            def _():
+                for step in waits:
+                    self.copy(step, i).wait()
+                for step in starts:
+                    self.copy(step, i).start()
+
+        at(0, (), (0, 1))
+        at(4, (7, 8), ())
+        at(3, (4, 5, 6), (7, 8))
+        at(2, (2, 3), (4, 5, 6))
+        at(1, (0, 1), (2, 3))
+
+
+SPREAD_TICKS = 4
 PER_LAYER = 14
+
+
+def forward_kernel(layers, *refs):
+    refs = list(refs)
+    x_ref, up_ref, wq_ref, wo_ref, wi_ref, wd_ref, hot_ref, mask_ref, bq_ref, bi_ref, vec_ref = refs[:11]
+    w_ref, up_out, x_out = refs[11:14]
+    saved = [refs[14 + PER_LAYER * l : 14 + PER_LAYER * (l + 1)] for l in range(layers)]
+    (
+        x, acc, r_buf, low, xb, qkv, kv_sib, ctx, lse, hl, g_all, slope_all,
+        col_buf, row_buf, turn_buf, made_buf, wa_buf, wb_buf, mask_buf, hot_buf,
+        feed_sem, load_sem, col_sem, row_sem, made_sem, store_sem, block_sem,
+        core_send, core_recv, kv_send, kv_recv, g_send, g_recv, spread_send, spread_recv,
+    ) = refs[14 + PER_LAYER * layers :]
+    rows, width = acc.shape
+    dp, y = lax.axis_index("dp"), lax.axis_index("tensor")
+    core = dp % 2
+    stays = core == y
+    spread = Spread(w_ref, layers * GROUPS // 2, spread_send, spread_recv)
+    greet((FLIP_Y, FLIP_X, FLIP_Z0, FLIP_C, SWAP))
+
+    def feed(n, slot, source, target):
+        return pltpu.make_async_copy(source, target, feed_sem.at[n, slot])
+
+    def load(n, source, target):
+        return pltpu.make_async_copy(source, target, load_sem.at[n])
+
+    def store(n, source, target):
+        return pltpu.make_async_copy(source, target, store_sem.at[n])
+
+    def exchange(n, source, target, bits=FLIP_C):
+        return pltpu.make_async_remote_copy(
+            src_ref=source, dst_ref=target, send_sem=core_send.at[n], recv_sem=core_recv.at[n],
+            device_id=partner(bits), device_id_type=MESH,
+        )
+
+    def columns(ref, i, size):
+        return ref.at[:, pl.ds(pl.multiple_of(i * size, size), size)]
+
+    def swap(n, source, target, begin):
+        here = store(n, source, target)
+        there = exchange(n, source, target, SWAP)
+
+        @pl.when(stays)
+        def _():
+            here.start() if begin else here.wait()
+
+        @pl.when(jnp.logical_not(stays))
+        def _():
+            there.start() if begin else there.wait()
+
+    items = []
+    for l in range(layers):
+        items += [(True, wq_ref.at[l, t], l * GROUPS + t) for t in range(3)]
+        items += [(False, wo_ref.at[l], l * GROUPS + OUT_GROUP)]
+        for n in range(FF_GROUPS):
+            items += [(True, wi_ref.at[l, :, pl.ds(n * 512, 512)], l * GROUPS + in_group(n))]
+            items += [(False, wd_ref.at[l, pl.ds(n * 512, 512)], l * GROUPS + down_group(n))]
+    fetches, counts, ahead = [], [0, 0], [[], []]
+    for m, (turned, source, group) in enumerate(items):
+        slot = counts[turned] % 2
+        buf, sem = (col_buf, col_sem) if turned else (row_buf, row_sem)
+        fetches.append((pltpu.make_async_copy(source, buf.at[slot], sem.at[slot]), slot))
+        ahead[turned].append(m)
+        counts[turned] += 1
+    bits = [(dp // step) % 2 for step in (1, 2, 4, 8)]
+    made = {}
+
+    def convert(m):
+        turned, _, group = items[m]
+        copy, slot = fetches[m]
+        copy.wait()
+        if turned:
+
+            def turn(i, _):
+                turn_buf[pl.ds(pl.multiple_of(i * 128, 128), 128), :] = col_buf[
+                    slot, :, pl.ds(pl.multiple_of(i * 128, 128), 128)
+                ].T
+                return 0
+
+            lax.fori_loop(0, 4, turn, 0)
+        if m >= 2:
+            made[m - 2].wait()
+
+        def block(j, _):
+            where = 0
+            for bit, weight in zip(bits, (8, 4, 2, 1)):
+                own = (j // weight) % 2
+                where = where + weight * (own + bit - 2 * own * bit)
+            at = pl.ds(pl.multiple_of(where * 32, 32), 32)
+            rows_32 = turn_buf[at, :] if turned else row_buf[slot, at, :]
+            made_buf[m % 2, pl.ds(pl.multiple_of(j * 32, 32), 32), :] = rows_32.astype(BF16)
+            return 0
+
+        lax.fori_loop(0, 16, block, 0)
+        later = [n for n in ahead[turned] if n > m]
+        if len(later) > 1:
+            fetches[later[1]][0].start()
+        parts = [
+            pltpu.make_async_copy(
+                made_buf.at[m % 2, pl.ds(a * 256, 256)], w_ref.at[a, group, 0], made_sem.at[m % 2, a]
+            )
+            for a in range(2)
+        ]
+
+        class Both:
+            def wait(self):
+                for part in parts:
+                    part.wait()
+
+        for part in parts:
+            part.start()
+        made[m] = Both()
+
+    load_x = load(0, x_ref.at[:, 0], x)
+    load_x.start()
+    load_up = load(1, up_ref.at[:, 0], acc)
+    load_up.start()
+    load_hot = load(2, hot_ref, hot_buf)
+    load_hot.start()
+    for kind in range(2):
+        for m in ahead[kind][:2]:
+            fetches[m][0].start()
+    load_x.wait()
+
+    def narrow_x(at):
+        low[at, :] = x[at, :].astype(BF16)
+
+    row_tiles(rows, narrow_x)
+    swap(0, low, xb, True)
+    load_up.wait()
+
+    def narrow_up(at):
+        hl[at, :] = acc[at, :].astype(BF16)
+
+    row_tiles(rows, narrow_up)
+    swap(1, hl, up_out, True)
+
+    for m in range(len(items)):
+        convert(m)
+        if m % 4 == 3:
+            spread.tick(m // 4)
+    for m in range(len(items) - 2, len(items)):
+        made[m].wait()
+    swap(0, low, xb, False)
+    swap(1, hl, up_out, False)
+    load_hot.wait()
+
+    def widen(at):
+        x[at, :] = xb[at, :].astype(F32)
+
+    row_tiles(rows, widen)
+
+    pairs = width // 128
+    for l in range(layers):
+        (
+            qkv_out, sib_out, ctx_out, ctx_sib_out, lse_out, r1_out, r2_out, hl_out, hl_sib_out,
+            g_out, g_sib_out, slope_out, xb_out, xb_sib_out,
+        ) = saved[l]
+        first = l * GROUPS
+        clock = 6 + 7 * l
+        xb_store = store(0, xb, xb_out)
+        xb_store.start()
+        xb_copy = exchange(2 + 3 * l, xb, xb_sib_out)
+        xb_copy.start()
+
+        def give_kv(n, a):
+            at = pl.ds(pl.multiple_of(a * 512, 512), 512)
+            return pltpu.make_async_remote_copy(
+                src_ref=qkv.at[1 + n, :, at], dst_ref=kv_sib.at[n, :, at],
+                send_sem=kv_send.at[n, a], recv_sem=kv_recv.at[n, a],
+                device_id=partner(FLIP_C), device_id_type=MESH,
+            )
+
+        def which(i):
+            return (i // 2 + 1) % 3, i % 2
+
+        def qkv_feeds(i, slot):
+            t, a = which(i)
+            return (feed(0, slot, w_ref.at[a, first + t], wa_buf.at[slot]),)
+
+        def qkv_body(i, slot):
+            t, a = which(i)
+            at = pl.ds(pl.multiple_of(a * 512, 512), 512)
+            qkv[t, :, at] = (nt(xb[...], block_of(wa_buf.at[slot])) + bq_ref[l, t, a]).astype(BF16)
+            pl.when(i < 4)(lambda: give_kv(t - 1, a).start())
+            pl.when(i == 3)(lambda: spread.tick(clock))
+
+        stream(6, qkv_feeds, qkv_body)
+        qkv_store = store(1, qkv, qkv_out)
+        qkv_store.start()
+        for n in range(2):
+            for a in range(2):
+                give_kv(n, a).wait()
+        sib_store = store(2, kv_sib, sib_out)
+        sib_store.start()
+
+        def pair_feeds(p, slot):
+            return (feed(1, slot, mask_ref.at[pl.ds(2 * p, 2)], mask_buf.at[slot]),)
+
+        def pair_body(p, slot):
+            far = lax.rem(p + pairs // 2, pairs)
+            here = pl.ds(pl.multiple_of(p * 128, 128), 128)
+            there = pl.ds(pl.multiple_of(far * 128, 128), 128)
+            keys = jnp.concatenate([qkv[1, :, here], kv_sib[0, :, there]], axis=0)
+            values = jnp.concatenate([qkv[2, :, here], kv_sib[1, :, there]], axis=0)
+            context, parts = attend_pair(qkv[0, :, here], keys, values, hot_buf[...], mask_buf[slot])
+            ctx[:, here] = context.astype(BF16)
+            for e in range(2):
+                lse[p, e : e + 1, :] = parts[e]
+            pl.when(lax.rem(p, 3) == 1)(lambda: spread.tick(clock + 1 + lax.div(p, 3)))
+
+        stream(pairs, pair_feeds, pair_body)
+        ctx_store = store(3, ctx, ctx_out)
+        ctx_store.start()
+        lse_store = store(4, lse, lse_out)
+        lse_store.start()
+        ctx_copy = exchange(3 + 3 * l, ctx.at[:, pl.ds(512, 512)], ctx_sib_out)
+        ctx_copy.start()
+
+        def out_feeds(i, slot):
+            return (feed(0, slot, w_ref.at[i, first + OUT_GROUP], wa_buf.at[slot]),)
+
+        def out_body(i, slot):
+            part = nn(ctx[:, pl.ds(pl.multiple_of(i * 512, 512), 512)], block_of(wa_buf.at[slot]))
+
+            @pl.when(i == 0)
+            def _():
+                acc[...] = part
+
+            @pl.when(i == 1)
+            def _():
+                acc[...] += part
+
+        stream(2, out_feeds, out_body)
+        sib_store.wait()
+
+        def first_norm(at):
+            r1 = x[at, :] + acc[at, :] + vec_ref[l, 0:1, :]
+            r_buf[at, :] = r1
+            h = norm(r1, vec_ref[l, 1:2, :], vec_ref[l, 2:3, :])
+            hl[at, :] = h.astype(BF16)
+            acc[at, :] = h + vec_ref[l, 3:4, :]
+
+        row_tiles(rows, first_norm)
+        r1_store = store(5, r_buf, r1_out)
+        r1_store.start()
+        hl_store = store(6, hl, hl_out)
+        hl_store.start()
+        hl_copy = exchange(4 + 3 * l, hl, hl_sib_out)
+        hl_copy.start()
+
+        def place_of(i):
+            a = 1 - lax.div(i, FF_GROUPS)
+            return a, lax.rem(i, FF_GROUPS)
+
+        def ff_feeds(i, slot):
+            a, n = place_of(i)
+            return (
+                feed(0, slot, w_ref.at[a, first + in_group(n)], wa_buf.at[slot]),
+                feed(2, slot, w_ref.at[a, first + down_group(n)], wb_buf.at[slot]),
+            )
+
+        def g_store(j):
+            return pltpu.make_async_copy(g_all.at[j], columns(g_out, j, 512), block_sem.at[0, j])
+
+        def slope_store(j):
+            return pltpu.make_async_copy(slope_all.at[j], columns(slope_out, j, 512), block_sem.at[1, j])
+
+        def g_copy(n):
+            return pltpu.make_async_remote_copy(
+                src_ref=g_all.at[FF_GROUPS + n], dst_ref=columns(g_sib_out, n, 512),
+                send_sem=g_send.at[l, n], recv_sem=g_recv.at[l, n],
+                device_id=partner(FLIP_C), device_id_type=MESH,
+            )
+
+        def ff_body(i, slot):
+            a, n = place_of(i)
+            j = a * FF_GROUPS + n
+            u = nt(hl[...], block_of(wa_buf.at[slot])) + bi_ref[l, a, n]
+            g, slope = gelu_and_slope(u)
+            g = g.astype(BF16)
+            g_all[j] = g
+            slope_all[j] = slope.astype(BF16)
+            g_store(j).start()
+            slope_store(j).start()
+            pl.when(a == 1)(lambda: g_copy(n).start())
+            acc[...] += nn(g, block_of(wb_buf.at[slot]))
+            pl.when(lax.rem(i, 3) == 1)(lambda: spread.tick(clock + 4 + lax.div(i, 3)))
+
+        stream(2 * FF_GROUPS, ff_feeds, ff_body)
+        r1_store.wait()
+        xb_store.wait()
+        xb_copy.wait()
+
+        def second_norm(at):
+            r2 = acc[at, :]
+            r_buf[at, :] = r2
+            x2 = norm(r2, vec_ref[l, 4:5, :], vec_ref[l, 5:6, :])
+            x[at, :] = x2
+            xb[at, :] = x2.astype(BF16)
+
+        row_tiles(rows, second_norm)
+        r2_store = store(5, r_buf, r2_out)
+        r2_store.start()
+        if l == layers - 1:
+            swap(10, xb, x_out, True)
+
+        def settle(j, _):
+            g_store(j).wait()
+            slope_store(j).wait()
+            return 0
+
+        lax.fori_loop(0, 2 * FF_GROUPS, settle, 0)
+
+        def settle_sent(n, _):
+            g_copy(n).wait()
+            return 0
+
+        lax.fori_loop(0, FF_GROUPS, settle_sent, 0)
+        for copy in (qkv_store, ctx_store, lse_store, ctx_copy, hl_store, hl_copy, r2_store):
+            copy.wait()
+    swap(10, xb, x_out, False)
+
+
+def forward(block_input, cotangent, w_qkv, w_out, w_in, w_down, hot, mask, bias_qkv, bias_in, vectors):
+    rows, _, width = block_input.shape
+    layers = w_qkv.shape[0]
+    total = layers * GROUPS
+    anywhere = pl.BlockSpec(memory_space=pl.ANY)
+    in_vmem = pl.BlockSpec(memory_space=pltpu.VMEM)
+    low = lambda *shape: pltpu.VMEM(shape, BF16)
+    full = lambda *shape: pltpu.VMEM(shape, F32)
+    dma = lambda *shape: pltpu.SemaphoreType.DMA(shape)
+    low_out = lambda *shape: jax.ShapeDtypeStruct(shape, BF16)
+    full_out = lambda *shape: jax.ShapeDtypeStruct(shape, F32)
+    layer_out = (
+        low_out(3, rows, width),
+        low_out(2, rows, width),
+        low_out(rows, width),
+        low_out(rows, width // 2),
+        full_out(width // 128, 2, rows),
+        full_out(rows, width),
+        full_out(rows, width),
+        low_out(rows, width),
+        low_out(rows, width),
+        low_out(rows, 4 * width),
+        low_out(rows, 2 * width),
+        low_out(rows, 4 * width),
+        low_out(rows, width),
+        low_out(rows, width),
+    )
+    outs = pl.pallas_call(
+        functools.partial(forward_kernel, layers),
+        out_shape=(low_out(2, total, 2, 256, width), low_out(rows, width), low_out(rows, width)) + layer_out * layers,
+        in_specs=[anywhere] * 8 + [in_vmem] * 3,
+        out_specs=(anywhere,) * (3 + PER_LAYER * layers),
+        scratch_shapes=[
+            full(rows, width),
+            full(rows, width),
+            full(rows, width),
+            low(rows, width),
+            low(rows, width),
+            low(3, rows, width),
+            low(2, rows, width),
+            low(rows, width),
+            full(width // 128, 2, rows),
+            low(rows, width),
+            low(2 * FF_GROUPS, rows, 512),
+            low(2 * FF_GROUPS, rows, 512),
+            full(2, width, 512),
+            full(2, 512, width),
+            full(512, width),
+            low(2, 512, width),
+            low(2, 2, 256, width),
+            low(2, 2, 256, width),
+            low(2, 2, 2 * rows, 128),
+            low(rows, 128),
+            dma(3, 2),
+            dma(3),
+            dma(2),
+            dma(2),
+            dma(2, 2),
+            dma(11),
+            dma(2, 2 * FF_GROUPS),
+            dma(11),
+            dma(11),
+            dma(2, 2),
+            dma(2, 2),
+            dma(layers, FF_GROUPS),
+            dma(layers, FF_GROUPS),
+            dma(9, total // 2),
+            dma(9, total // 2),
+        ],
+        compiler_params=pltpu.CompilerParams(collective_id=0, has_side_effects=True, vmem_limit_bytes=60 << 20),
+        cost_estimate=pl.CostEstimate(flops=30 << 30, bytes_accessed=300 << 20, transcendentals=1 << 24),
+        name="forward",
+    )(block_input, cotangent, w_qkv, w_out, w_in, w_down, hot, mask, bias_qkv, bias_in, vectors)
+    saved = [outs[3 + PER_LAYER * l : 3 + PER_LAYER * (l + 1)] for l in range(layers)]
+    return outs[0], outs[1], outs[2], saved
 
 
 def backward_kernel(layers, *refs):
@@ -618,16 +807,16 @@
         pair_buf, lse_buf, mask_buf, hot_buf, unit_buf,
         y_buf, x_buf, z0_buf, z1_buf, all_buf, keep_buf,
         feed_sem, load_sem, store_sem, core_send, core_recv, du_send, du_recv,
-        send_sem, recv_sem, keep_sem, out_sem, in_free, out_free,
+        send_sem, recv_sem, sum_send, sum_recv, keep_sem, out_sem, in_free, out_free,
     ) = refs[at_ref + 6 :]
     rows, width = acc.shape
     total = layers * GROUPS
     reduction = Reduction(
         grads, sums, total,
         (y_buf, x_buf, z0_buf, z1_buf, all_buf, keep_buf),
-        (send_sem, recv_sem, keep_sem, out_sem, in_free, out_free),
+        (send_sem, recv_sem, sum_send, sum_recv, keep_sem, out_sem, in_free, out_free),
     )
-    greet((FLIP_Y, FLIP_X, FLIP_Z0, FLIP_Z1, FLIP_C))
+    greet((FLIP_Y, FLIP_X, FLIP_Z0, FLIP_Z1, FLIP_C, SWAP))
 
     def feed(n, slot, source, target):
         return pltpu.make_async_copy(source, target, feed_sem.at[n, slot])
@@ -861,15 +1050,22 @@
         da[at, :] = acc[at, :].astype(BF16)
 
     row_tiles(rows, narrow)
+    stays = lax.axis_index("dp") % 2 == lax.axis_index("tensor")
     dx_store = load(0, da, dx_out)
-    dx_store.start()
-    dx_store.wait()
+    dx_copy = pltpu.make_async_remote_copy(
+        src_ref=da, dst_ref=dx_out, send_sem=core_send.at[4], recv_sem=core_recv.at[4],
+        device_id=partner(SWAP), device_id_type=MESH,
+    )
+    pl.when(stays)(lambda: dx_store.start())
+    pl.when(jnp.logical_not(stays))(lambda: dx_copy.start())
 
     def rest(t, _):
         reduction.tick(t)
         return 0
 
     lax.fori_loop(done, total + LAST_TICK, rest, 0)
+    pl.when(stays)(lambda: dx_store.wait())
+    pl.when(jnp.logical_not(stays))(lambda: dx_copy.wait())
 
 
 def backward(upstream, weights, hot, mask, vectors, saved):
@@ -928,12 +1124,14 @@
             dma(8, 2),
             dma(5),
             dma(1),
-            dma(4),
-            dma(4),
+            dma(5),
+            dma(5),
             dma(FF_GROUPS),
             dma(FF_GROUPS),
-            dma(8, SLOTS),
-            dma(8, SLOTS),
+            dma(7, SLOTS),
+            dma(7, SLOTS),
+            dma(total),
+            dma(total),
             dma(2),
             dma(SLOTS),
             pltpu.SemaphoreType.REGULAR((4,)),
@@ -976,14 +1174,13 @@
     own_blocks = blocks // 2
     heads = random_blocks.shape[1] * 2
 
-    stream_low = swap_core_and_y(block_input[:, 0].astype(BF16))
-    upstream_low = swap_core_and_y(cotangent[:, 0].astype(BF16))
-
     chosen = random_blocks[0]
-    packed = jnp.concatenate(
-        [chosen.reshape(-1), flip(chosen, FLIP_Y).reshape(-1), segment_ids[0]]
-    )
-    packed = jnp.where(core == y, packed, flip(packed, FLIP_C))
+    near = jnp.concatenate([chosen.reshape(-1), segment_ids[0]])
+    sibling = flip(near, FLIP_C)
+    across, diagonal = flip(chosen.reshape(-1), FLIP_Y), flip(chosen.reshape(-1), SWAP)
+    mine = jnp.concatenate([near[: chosen.size], across, near[chosen.size :]])
+    other = jnp.concatenate([sibling[: chosen.size], diagonal, sibling[chosen.size :]])
+    packed = jnp.where(core == y, mine, other)
     chosen = packed[: 2 * chosen.size].reshape(2, heads // 2, blocks, -1)
     segments = packed[2 * random_blocks.size :]
     chosen = flip_order(chosen.reshape(2, 2, 2, 2, blocks, -1), 1, device_bits[:3])
@@ -1037,27 +1234,6 @@
     bias_in = local_bias(bias_pack[n_qv:], bias_far[n_qv:], layers * FF_GROUPS)
     bias_in = bias_in.reshape(layers, FF_GROUPS, 2, 1, 512).swapaxes(1, 2)
 
-    total = layers * GROUPS
-    weights = None
-    for layer in range(layers):
-        first = layer * GROUPS
-        put = functools.partial(convert, total=total, code=code_arg)
-        weights = put(
-            w_qkv, (1, 1, width, 512), lambda i, l=layer: (l, i, 0, 0), True, 3, lambda i, f=first: f + i, weights
-        )
-        weights = put(
-            w_out, (1, 512, width), lambda i, l=layer: (l, 0, 0), False, 1, lambda i, f=first: f + OUT_GROUP, weights
-        )
-        weights = put(
-            w_in, (1, width, 512), lambda i, l=layer: (l, 0, i), True, FF_GROUPS,
-            lambda i, f=first: f + in_group(i), weights,
-        )
-        weights = put(
-            w_down, (1, 512, width), lambda i, l=layer: (l, i, 0), False, FF_GROUPS,
-            lambda i, f=first: f + down_group(i), weights,
-        )
-    weights = spread_weights(weights, tuple(range(total)))
-
     vectors = [
         jnp.stack(
             [
@@ -1067,30 +1243,13 @@
         )
         for l in range(layers)
     ]
-    stream, stream_now = stream_low.astype(F32), stream_low
-    saved = []
-    half = width // 2
-    for layer in range(layers):
-        first = layer * GROUPS
-        xb = stream_now
-        qkv = project_qkv(xb, weights, bias_qkv[layer], first)
-        q, k, v = qkv[0], qkv[1], qkv[2]
-        k_sib, v_sib = flip((k, v), FLIP_C)
-        ctx, lse = attend(q, k, v, k_sib, v_sib, hot, mask)
-        r1, hidden, g, slope, r2, stream, stream_now = forward_tail(
-            ctx, stream, weights, bias_in[layer], vectors[layer], first
-        )
-        xb_sib, hidden_sib = flip((xb, hidden), FLIP_C)
-        ctx_sib = flip(ctx[:, half:], FLIP_C)
-        g_sib = flip(g[:, 4 * half :], FLIP_C)
-        kv_sib = jnp.stack([k_sib, v_sib])
-        saved.append((qkv, kv_sib, ctx, ctx_sib, lse, r1, r2, hidden, hidden_sib, g, g_sib, slope, xb, xb_sib))
-    block_output = swap_core_and_y(stream_now).astype(F32)[:, None]
-
-    _, grads, dx_low, d_b_in, qkv_sums, rows_small = backward(
-        upstream_low, weights, hot, mask, jnp.stack(vectors), saved
+    vectors = jnp.stack(vectors)
+    weights, upstream_low, stream_low, saved = forward(
+        block_input, cotangent, w_qkv, w_out, w_in, w_down, hot, mask, bias_qkv, bias_in, vectors
     )
-    input_grad = swap_core_and_y(dx_low).astype(F32)[:, None]
+    block_output = stream_low.astype(F32)[:, None]
+    _, grads, dx_low, d_b_in, qkv_sums, rows_small = backward(upstream_low, weights, hot, mask, vectors, saved)
+    input_grad = dx_low.astype(F32)[:, None]
 
     placed = [None] * 4
     for layer in range(layers):

time: 822 us -> 690 us (0.84)
  Pallas kernels: 688 us -> 629 us
  local copies, waits for them, and re-layouts: 48.4 us -> 22.4 us
  starting transfers between devices: 31.3 us -> 7.87 us
  waiting for transfers between devices: 23.1 us -> 13.6 us
    pallas_call x15 -> x1, Pallas kernels: 285 us -> 204 us  [forward(): pl.pallas_call(functools.partial(forward_kernel, layers), out_shape=(low_...]
    pallas_call x1, Pallas kernels: 362 us -> 384 us  [backward(): pl.pallas_call(functools.partial(backward_kernel, layers), out_shape=(jax...]
    ppermute x4 -> x0, starting transfers between devices: 21.8 us -> none  [swap_core_and_y(): lax.ppermute(v, ('dp', 'tensor'), pairs)]
    ppermute x20 -> x9, waiting for transfers between devices: 23.1 us -> 13.6 us  [flip(): lax.ppermute(v, ('dp', 'tensor'), pairs)]
    squeeze x4 -> x0, local copies, waits for them, and re-layouts: 8.32 us -> none  [the longest x2 7.09 us: sequence_shards(): q, k, v = (qkv[0], qkv[1], qkv[2])]
  transfers between devices with their start and end apart: 24 -> 9, of which waited for: 6 -> 4; matrix products, arithmetic and copies ran while one was open for 6% -> 3% of each run, Pallas kernels for 77% -> 6%
where the time goes in v3:
time: 690 us; the launch traced here: 684 us
  Pallas kernels  629 us (91%)
  local copies, waits for them, and re-layouts  22.4 us (3%)
  waiting for transfers between devices  13.6 us (2%)
  other arithmetic  9.04 us (1%)
  starting transfers between devices  7.87 us (1%)
    pallas_call x1, Pallas kernels, backward(): pl.pallas_call(functools.partial(backward_kernel, layers), out_shape=(jax...  384 us
    pallas_call x1, Pallas kernels, forward(): pl.pallas_call(functools.partial(forward_kernel, layers), out_shape=(low_...  204 us
    pallas_call x8, Pallas kernels, place(): pl.pallas_call(functools.partial(place_kernel, transposed), out_shape=jax...  41.3 us
  transfers between devices with their start and end apart: 9, of which 4 were waited for; matrix products, arithmetic and copies ran while one was open for 3% of the time, Pallas kernels for 6%

profile of v3, /device:TPU:0, one launch (start us, length us, event | category | flops | bytes accessed | tf_op | source)
XLA Modules:
  0.0 683.5 jit_solution(11691446330769826320)
XLA Ops:
  0.6 0.8 copy.41
  1.5 0.2 reshape_squeeze.11
  1.7 3.0 collective-permute-start
  4.7 0.8 reshape.304
  5.7 0.2 rev.98
  5.9 0.1 reshape.305
  6.0 0.8 reshape.302
  7.1 1.2 collective-permute-start.3
  8.3 0.7 pad_add_fusion
  9.0 0.7 collective-permute-start.1
  9.7 0.8 slice_bitcast_fusion.4
  10.6 0.8 fusion.13
  11.5 0.6 pad_maximum_fusion.2.refs_10_.refs_4_
  12.2 0.1 reshape_reshape.24
  12.6 0.7 add_select_fusion
  13.3 0.2 reshape_reshape.21
  13.5 0.2 copy.42
  13.8 0.1 compare_reduce_fusion
  14.1 0.1 rev.87
  14.3 0.1 fusion.1
  14.4 0.2 select_convert_fusion
  14.6 0.5 broadcast_in_dim.56
  15.2 0.8 broadcast_in_dim.59
  16.0 3.7 pad_maximum_fusion.refs_7_.refs_3_
  19.7 0.8 pad_maximum_fusion.1.refs_6_.refs_2_
  20.5 0.6 copy.57
  21.2 0.7 pad_maximum_fusion.5.refs_8_
  21.9 203.8 %forward.1 = (bf16[2,24,2,256,1024]{4,3,2,1,0:T(8,128)(2,1)}, bf16[512,1024]{1,0:T(8,128)(2,1)}, bf16[512,1024]{1,0:T(8,128)(2,1)}, bf16[3,512,1024]{2,1,0:T(8,1...) custom-call(f32[512,1,1024]{2,1,0:T(1,128)} %refs_0_.1, ...), custom_call_target="tpu_custom_call" | custom-call | flops 32212254720 | bytes 314572800 | tf_op jit(solution)/shard_map/forward/pallas_call | solution.py:748
  225.7 384.1 %backward.1 = (bf16[24,512,1024]{2,1,0:T(8,128)(2,1)}, bf16[24,512,1024]{2,1,0:T(8,128)(2,1)}, bf16[512,1024]{1,0:T(8,128)(2,1)}, f32[2,2,4,1,512]{4,3,2,1,0:T(1...) custom-call(bf16[512,1024]{1,0:T(8,128)(2,1)} %get-tuple-element.49.refs_0_, ...), custom_call_target="tpu_custom_call" | custom-call | flops 64424509440 | bytes 314572800 | tf_op jit(solution)/shard_map/backward/pallas_call | solution.py:1079
  609.8 1.2 fusion.10
  611.1 0.8 copy.47
  611.9 0.2 reshape.308
  612.3 0.3 rev.108
  612.7 0.2 reshape_reshape.27
  612.8 0.7 fusion.11
  613.6 0.1 reshape.307
  613.9 0.2 rev.103
  614.3 0.4 collective-permute-start.4
  614.7 0.9 collective-permute-done.4
  615.7 0.5 collective-permute-start.5
  616.1 4.7 collective-permute-done.5
  620.8 0.6 collective-permute-start.6
  621.4 4.1 collective-permute-done.6
  625.5 0.6 collective-permute-start.7
  626.1 0.2 bitcast_convert_fusion
  626.3 3.8 collective-permute-done.7
  630.2 0.8 collective-permute-start.8
  631.0 0.2 bitcast_convert_fusion.1
  631.3 6.0 place.14.refs_0_
  637.2 6.4 place.12.refs_0_
  643.7 2.7 place.10.refs_0_
  646.4 5.3 place.8.refs_0_
  651.7 5.9 place.15
  657.6 6.4 place.13
  664.1 2.7 place.11
  666.8 5.8 place.9
  672.5 3.5 copy.50
  676.0 3.5 copy.49
  679.6 0.6 reshape.313
  680.3 0.6 reshape.311
  680.9 0.6 slice.219
  681.5 0.6 slice.221
  682.2 0.6 slice.214
  682.8 0.6 slice.217
  (91 shorter events, 2.1 us)
Async XLA Ops:
  1.7 10.9 %collective-permute-start = (s32[384]{0:T(512)S(1)}, s32[384]{0:T(512)S(1)}, u32[]{:S(2)}, u32[]{:S(2)}) collective-permute-start(s32[384]{0:T(512)S(1)} %reshape_squeeze.11), channel_id=1, source_target_pairs={{0,1},{1,0},{2,3},{3,2},{4,5},{5,4},{6,7},{7,6},{8,9},{9,8},{10,11... | collective-permute-start | bytes 4616 | tf_op jit(solution)/shard_map/ppermute | solution.py:36
  4.7 7.8 %collective-permute-start.2 = (s32[384]{0:T(512)S(1)}, s32[384]{0:T(512)S(1)}, u32[]{:S(2)}, u32[]{:S(2)}) collective-permute-start(s32[384]{0:T(512)S(1)} %reshape_squeeze.11), channel_id=1, source_target_pairs={{0,3},{1,2},{2,1},{3,0},{4,7},{5,6},{6,5},{7,4},{8,11},{9,10},{10,... | collective-permute-start | bytes 4616 | tf_op jit(solution)/shard_map/ppermute | solution.py:36
  7.1 13.4 %collective-permute-start.3 = (f32[6144]{0:T(1024)S(1)}, f32[6144]{0:T(1024)S(1)}, u32[]{:S(2)}, u32[]{:S(2)}) collective-permute-start(f32[6144]{0:T(1024)S(1)} %pad_maximum_fusion.4), channel_id=1, source_target_pairs={{0,1},{1,0},{2,3},{3,2},{4,5},{5,4},{6,7},{7,6},{8,9},{9,8},{10,11... | collective-permute-start | bytes 73736 | tf_op jit(solution)/shard_map/ppermute | solution.py:36
  9.0 3.5 collective-permute-start.1
  609.8 16.3 %copy-start.1 = (bf16[512,1024]{1,0:T(8,128)(2,1)S(1)}, bf16[512,1024]{1,0:T(8,128)(2,1)}, u32[]{:S(2)}) copy-start(bf16[512,1024]{1,0:T(8,128)(2,1)} %get-tuple-element.79) | copy-start | bytes 3145732
  609.8 21.2 %copy-start = (bf16[512,1024]{1,0:T(8,128)(2,1)S(1)}, bf16[512,1024]{1,0:T(8,128)(2,1)}, u32[]{:S(2)}) copy-start(bf16[512,1024]{1,0:T(8,128)(2,1)} %get-tuple-element.48) | copy-start | bytes 3145732
  614.3 1.4 collective-permute-start.4
  615.7 5.1 collective-permute-start.5
  620.8 4.7 collective-permute-start.6
  625.5 4.7 collective-permute-start.7
  630.2 49.3 %collective-permute-start.8 = (f32[24576]{0:T(1024)S(1)}, f32[24576]{0:T(1024)S(1)}, u32[]{:S(2)}, u32[]{:S(2)}) collective-permute-start(f32[24576]{0:T(1024)S(1)} %add.74), channel_id=1, source_target_pairs={{0,16},{1,17},{2,18},{3,19},{4,20},{5,21},{6,22},{7,23},{8,24},{9,... | collective-permute-start | bytes 294920 | tf_op jit(solution)/shard_map/ppermute | solution.py:36

commit v4 on v3

--- a/solution.py
+++ b/solution.py
@@ -53,35 +53,37 @@
     return ref[...].reshape(-1, width)
 
 
-def place_kernel(transposed, code_ref, g_ref, *refs):
-    o_ref, t_ref = refs[-2:]
+def place_kernel(turned, code_ref, g_ref, o_ref, *scratch):
     code = code_ref[0]
     for j in range(16):
         start = pl.multiple_of((j ^ code) * 32, 32)
-        t_ref[j * 32 : (j + 1) * 32, :] = g_ref[0, pl.ds(start, 32), :].astype(F32)
-    placed = t_ref[...].T if transposed else t_ref[...]
-    o_ref[...] = placed.reshape(o_ref.shape)
-
-
-def place(grads, shape, block, index, transposed, count, group, into, code):
-    width = grads.shape[-1]
-    more = [] if into is None else [into]
+        block = g_ref[0, pl.ds(start, 32), :].astype(F32)
+        if turned:
+            scratch[0][j * 32 : (j + 1) * 32, :] = block
+        else:
+            o_ref[0, j * 32 : (j + 1) * 32, :] = block
+    if turned:
+        o_ref[...] = scratch[0][...].T.reshape(o_ref.shape)
+
+
+def place(sums, shape, block, index, turned, count, group, code):
+    width = sums.shape[-1]
     return pl.pallas_call(
-        functools.partial(place_kernel, transposed),
+        functools.partial(place_kernel, turned),
         out_shape=jax.ShapeDtypeStruct(shape, F32),
         grid_spec=pltpu.PrefetchScalarGridSpec(
             num_scalar_prefetch=1,
-            grid=(count,),
-            in_specs=[pl.BlockSpec((1, 512, width), lambda i, code: (group(i), 0, 0))]
-            + [pl.BlockSpec(memory_space=pl.ANY) for _ in more],
-            out_specs=pl.BlockSpec(block, lambda i, code: index(i)),
-            scratch_shapes=[pltpu.VMEM((512, width), F32)],
+            grid=(shape[0], count),
+            in_specs=[pl.BlockSpec((1, 512, width), lambda l, i, code: (group(l, i), 0, 0))],
+            out_specs=pl.BlockSpec(block, lambda l, i, code: index(l, i)),
+            scratch_shapes=[pltpu.VMEM((512, width), F32)] if turned else [],
         ),
-        input_output_aliases={2: 0} if more else {},
         compiler_params=pltpu.CompilerParams(vmem_limit_bytes=VMEM_LIMIT),
-        cost_estimate=pl.CostEstimate(flops=0, bytes_accessed=count * 512 * width * 6, transcendentals=0),
+        cost_estimate=pl.CostEstimate(
+            flops=0, bytes_accessed=shape[0] * count * 512 * width * 6, transcendentals=0
+        ),
         name="place",
-    )(code, grads, *more)
+    )(code, sums)
 
 
 def partner(bits):
@@ -230,8 +232,8 @@
         at(6, back_z0)
         at(5, back_z1)
         at(4, on_z1)
+        at(1, on_x)
         at(3, on_z0)
-        at(1, on_x)
 
 
 def stream(count, feeds, body):
@@ -293,6 +295,13 @@
 def pair_lanes(values, e):
     lane = lax.broadcasted_iota(jnp.int32, values.shape, 1)
     return jnp.where(lane // HEAD_DIM == e, values, jnp.zeros_like(values))
+
+
+def spread_mask(block_part, document_part):
+    blocks, lanes = block_part.shape
+    each = document_part.shape[0] // blocks
+    part = jnp.broadcast_to(block_part[:, None, :], (blocks, each, lanes)).reshape(blocks * each, lanes)
+    return (part + document_part).astype(BF16)
 
 
 def attend_pair(query, keys, values, hot, mask):
@@ -386,27 +395,28 @@
                     self.copy(step, i).start()
 
         at(0, (), (0, 1))
-        at(4, (7, 8), ())
-        at(3, (4, 5, 6), (7, 8))
+        at(5, (7, 8), ())
+        at(1, (0, 1), (2, 3))
         at(2, (2, 3), (4, 5, 6))
-        at(1, (0, 1), (2, 3))
-
-
-SPREAD_TICKS = 4
+        at(4, (4, 5, 6), (7, 8))
+
+
 PER_LAYER = 14
+DEPTH = 3
 
 
 def forward_kernel(layers, *refs):
     refs = list(refs)
-    x_ref, up_ref, wq_ref, wo_ref, wi_ref, wd_ref, hot_ref, mask_ref, bq_ref, bi_ref, vec_ref = refs[:11]
-    w_ref, up_out, x_out = refs[11:14]
-    saved = [refs[14 + PER_LAYER * l : 14 + PER_LAYER * (l + 1)] for l in range(layers)]
+    x_ref, up_ref, wq_ref, wo_ref, wi_ref, wd_ref = refs[:6]
+    hot_buf, mask_ref, key_ref, bq_ref, bi_ref, vec_ref = refs[6:12]
+    w_ref, up_out, x_out = refs[12:15]
+    saved = [refs[15 + PER_LAYER * l : 15 + PER_LAYER * (l + 1)] for l in range(layers)]
     (
         x, acc, r_buf, low, xb, qkv, kv_sib, ctx, lse, hl, g_all, slope_all,
-        col_buf, row_buf, turn_buf, made_buf, wa_buf, wb_buf, mask_buf, hot_buf,
+        col_buf, row_buf, turn_buf, made_buf, wa_buf, wb_buf,
         feed_sem, load_sem, col_sem, row_sem, made_sem, store_sem, block_sem,
         core_send, core_recv, kv_send, kv_recv, g_send, g_recv, spread_send, spread_recv,
-    ) = refs[14 + PER_LAYER * layers :]
+    ) = refs[15 + PER_LAYER * layers :]
     rows, width = acc.shape
     dp, y = lax.axis_index("dp"), lax.axis_index("tensor")
     core = dp % 2
@@ -453,7 +463,7 @@
             items += [(False, wd_ref.at[l, pl.ds(n * 512, 512)], l * GROUPS + down_group(n))]
     fetches, counts, ahead = [], [0, 0], [[], []]
     for m, (turned, source, group) in enumerate(items):
-        slot = counts[turned] % 2
+        slot = counts[turned] % DEPTH
         buf, sem = (col_buf, col_sem) if turned else (row_buf, row_sem)
         fetches.append((pltpu.make_async_copy(source, buf.at[slot], sem.at[slot]), slot))
         ahead[turned].append(m)
@@ -489,8 +499,8 @@
 
         lax.fori_loop(0, 16, block, 0)
         later = [n for n in ahead[turned] if n > m]
-        if len(later) > 1:
-            fetches[later[1]][0].start()
+        if len(later) >= DEPTH:
+            fetches[later[DEPTH - 1]][0].start()
         parts = [
             pltpu.make_async_copy(
                 made_buf.at[m % 2, pl.ds(a * 256, 256)], w_ref.at[a, group, 0], made_sem.at[m % 2, a]
@@ -511,10 +521,8 @@
     load_x.start()
     load_up = load(1, up_ref.at[:, 0], acc)
     load_up.start()
-    load_hot = load(2, hot_ref, hot_buf)
-    load_hot.start()
     for kind in range(2):
-        for m in ahead[kind][:2]:
+        for m in ahead[kind][:DEPTH]:
             fetches[m][0].start()
     load_x.wait()
 
@@ -539,7 +547,6 @@
         made[m].wait()
     swap(0, low, xb, False)
     swap(1, hl, up_out, False)
-    load_hot.wait()
 
     def widen(at):
         x[at, :] = xb[at, :].astype(F32)
@@ -553,7 +560,7 @@
             g_out, g_sib_out, slope_out, xb_out, xb_sib_out,
         ) = saved[l]
         first = l * GROUPS
-        clock = 6 + 7 * l
+        clock = 6 + 6 * l
         xb_store = store(0, xb, xb_out)
         xb_store.start()
         xb_copy = exchange(2 + 3 * l, xb, xb_sib_out)
@@ -568,7 +575,8 @@
             )
 
         def which(i):
-            return (i // 2 + 1) % 3, i % 2
+            n = lax.div(i, 2)
+            return 1 - n + 3 * lax.div(n, 2), lax.rem(i, 2)
 
         def qkv_feeds(i, slot):
             t, a = which(i)
@@ -578,8 +586,8 @@
             t, a = which(i)
             at = pl.ds(pl.multiple_of(a * 512, 512), 512)
             qkv[t, :, at] = (nt(xb[...], block_of(wa_buf.at[slot])) + bq_ref[l, t, a]).astype(BF16)
-            pl.when(i < 4)(lambda: give_kv(t - 1, a).start())
-            pl.when(i == 3)(lambda: spread.tick(clock))
+            pl.when(t > 0)(lambda: give_kv(t - 1, a).start())
+            pl.when(i == 2)(lambda: spread.tick(clock))
 
         stream(6, qkv_feeds, qkv_body)
         qkv_store = store(1, qkv, qkv_out)
@@ -590,22 +598,21 @@
         sib_store = store(2, kv_sib, sib_out)
         sib_store.start()
 
-        def pair_feeds(p, slot):
-            return (feed(1, slot, mask_ref.at[pl.ds(2 * p, 2)], mask_buf.at[slot]),)
-
-        def pair_body(p, slot):
+        def pair_body(p, _):
             far = lax.rem(p + pairs // 2, pairs)
             here = pl.ds(pl.multiple_of(p * 128, 128), 128)
             there = pl.ds(pl.multiple_of(far * 128, 128), 128)
+            mask = [spread_mask(mask_ref[2 * p + e], key_ref[...]) for e in range(2)]
             keys = jnp.concatenate([qkv[1, :, here], kv_sib[0, :, there]], axis=0)
             values = jnp.concatenate([qkv[2, :, here], kv_sib[1, :, there]], axis=0)
-            context, parts = attend_pair(qkv[0, :, here], keys, values, hot_buf[...], mask_buf[slot])
+            context, parts = attend_pair(qkv[0, :, here], keys, values, hot_buf[...], mask)
             ctx[:, here] = context.astype(BF16)
             for e in range(2):
                 lse[p, e : e + 1, :] = parts[e]
-            pl.when(lax.rem(p, 3) == 1)(lambda: spread.tick(clock + 1 + lax.div(p, 3)))
-
-        stream(pairs, pair_feeds, pair_body)
+            pl.when(lax.rem(p, 5) == 2)(lambda: spread.tick(clock + 1 + lax.div(p, 5)))
+            return 0
+
+        lax.fori_loop(0, pairs, pair_body, 0)
         ctx_store = store(3, ctx, ctx_out)
         ctx_store.start()
         lse_store = store(4, lse, lse_out)
@@ -646,8 +653,7 @@
         hl_copy.start()
 
         def place_of(i):
-            a = 1 - lax.div(i, FF_GROUPS)
-            return a, lax.rem(i, FF_GROUPS)
+            return 1 - lax.rem(i, 2), lax.div(i, 2)
 
         def ff_feeds(i, slot):
             a, n = place_of(i)
@@ -681,7 +687,7 @@
             slope_store(j).start()
             pl.when(a == 1)(lambda: g_copy(n).start())
             acc[...] += nn(g, block_of(wb_buf.at[slot]))
-            pl.when(lax.rem(i, 3) == 1)(lambda: spread.tick(clock + 4 + lax.div(i, 3)))
+            pl.when(lax.rem(i, 3) == 1)(lambda: spread.tick(clock + 3 + lax.div(i, 3)))
 
         stream(2 * FF_GROUPS, ff_feeds, ff_body)
         r1_store.wait()
@@ -699,7 +705,8 @@
         r2_store = store(5, r_buf, r2_out)
         r2_store.start()
         if l == layers - 1:
-            swap(10, xb, x_out, True)
+            x_store = store(10, xb, x_out)
+            x_store.start()
 
         def settle(j, _):
             g_store(j).wait()
@@ -715,10 +722,10 @@
         lax.fori_loop(0, FF_GROUPS, settle_sent, 0)
         for copy in (qkv_store, ctx_store, lse_store, ctx_copy, hl_store, hl_copy, r2_store):
             copy.wait()
-    swap(10, xb, x_out, False)
-
-
-def forward(block_input, cotangent, w_qkv, w_out, w_in, w_down, hot, mask, bias_qkv, bias_in, vectors):
+    x_store.wait()
+
+
+def forward(block_input, cotangent, w_qkv, w_out, w_in, w_down, hot, mask, mask_rows, bias_qkv, bias_in, vectors):
     rows, _, width = block_input.shape
     layers = w_qkv.shape[0]
     total = layers * GROUPS
@@ -748,7 +755,7 @@
     outs = pl.pallas_call(
         functools.partial(forward_kernel, layers),
         out_shape=(low_out(2, total, 2, 256, width), low_out(rows, width), low_out(rows, width)) + layer_out * layers,
-        in_specs=[anywhere] * 8 + [in_vmem] * 3,
+        in_specs=[anywhere] * 6 + [in_vmem] * 6,
         out_specs=(anywhere,) * (3 + PER_LAYER * layers),
         scratch_shapes=[
             full(rows, width),
@@ -763,18 +770,16 @@
             low(rows, width),
             low(2 * FF_GROUPS, rows, 512),
             low(2 * FF_GROUPS, rows, 512),
-            full(2, width, 512),
-            full(2, 512, width),
+            full(DEPTH, width, 512),
+            full(DEPTH, 512, width),
             full(512, width),
             low(2, 512, width),
             low(2, 2, 256, width),
             low(2, 2, 256, width),
-            low(2, 2, 2 * rows, 128),
-            low(rows, 128),
             dma(3, 2),
             dma(3),
-            dma(2),
-            dma(2),
+            dma(DEPTH),
+            dma(DEPTH),
             dma(2, 2),
             dma(11),
             dma(2, 2 * FF_GROUPS),
@@ -790,25 +795,25 @@
         compiler_params=pltpu.CompilerParams(collective_id=0, has_side_effects=True, vmem_limit_bytes=60 << 20),
         cost_estimate=pl.CostEstimate(flops=30 << 30, bytes_accessed=300 << 20, transcendentals=1 << 24),
         name="forward",
-    )(block_input, cotangent, w_qkv, w_out, w_in, w_down, hot, mask, bias_qkv, bias_in, vectors)
+    )(block_input, cotangent, w_qkv, w_out, w_in, w_down, hot, mask, mask_rows, bias_qkv, bias_in, vectors)
     saved = [outs[3 + PER_LAYER * l : 3 + PER_LAYER * (l + 1)] for l in range(layers)]
     return outs[0], outs[1], outs[2], saved
 
 
 def backward_kernel(layers, *refs):
     refs = list(refs)
-    up_ref, w_ref, hot_ref, mask_ref, vec_ref = refs[:5]
-    saved = [refs[5 + PER_LAYER * l : 5 + PER_LAYER * (l + 1)] for l in range(layers)]
-    at_ref = 5 + PER_LAYER * layers
-    grads, sums, dx_out, dbi_ref, qkv_sums_ref, small_ref = refs[at_ref : at_ref + 6]
+    up_ref, x_ref, w_ref, hot_buf, mask_ref, key_ref, vec_ref = refs[:7]
+    saved = [refs[7 + PER_LAYER * l : 7 + PER_LAYER * (l + 1)] for l in range(layers)]
+    at_ref = 7 + PER_LAYER * layers
+    grads, sums, dx_out, x_out, dbi_ref, qkv_sums_ref, small_ref = refs[at_ref : at_ref + 7]
     (
         acc, dr1, dm, dm_sib, da, da_sib, du, du_sib, dctx, dqkv, d_sib, kv_out, kv_far,
         wa_buf, wb_buf, r_buf, slope_buf, left_buf, left_sib_buf, right_buf, right_sib_buf,
-        pair_buf, lse_buf, mask_buf, hot_buf, unit_buf,
+        pair_buf, lse_buf, unit_buf,
         y_buf, x_buf, z0_buf, z1_buf, all_buf, keep_buf,
-        feed_sem, load_sem, store_sem, core_send, core_recv, du_send, du_recv,
+        feed_sem, load_sem, store_sem, swap_sem, core_send, core_recv, du_send, du_recv,
         send_sem, recv_sem, sum_send, sum_recv, keep_sem, out_sem, in_free, out_free,
-    ) = refs[at_ref + 6 :]
+    ) = refs[at_ref + 7 :]
     rows, width = acc.shape
     total = layers * GROUPS
     reduction = Reduction(
@@ -851,12 +856,27 @@
     def add_small(l, row, value):
         small_ref[l, row : row + 1, :] += jnp.sum(value, axis=0, keepdims=True)
 
+    stays = lax.axis_index("dp") % 2 == lax.axis_index("tensor")
+
+    def swap(n, source, target, begin):
+        here = pltpu.make_async_copy(source, target, swap_sem.at[n])
+        there = pltpu.make_async_remote_copy(
+            src_ref=source, dst_ref=target, send_sem=core_send.at[4 + n], recv_sem=core_recv.at[4 + n],
+            device_id=partner(SWAP), device_id_type=MESH,
+        )
+
+        @pl.when(stays)
+        def _():
+            here.start() if begin else here.wait()
+
+        @pl.when(jnp.logical_not(stays))
+        def _():
+            there.start() if begin else there.wait()
+
+    swap(1, x_ref, x_out, True)
     start_up = load(0, up_ref, da)
     start_up.start()
-    start_hot = load(1, hot_ref, hot_buf)
-    start_hot.start()
     start_up.wait()
-    start_hot.wait()
     small_ref[...] = jnp.zeros_like(small_ref)
 
     def widen(at):
@@ -991,14 +1011,14 @@
                 feed(4, slot, columns(sib_ref.at[1], far, 128), pair_buf.at[slot, 2, pl.ds(rows, rows)]),
                 feed(5, slot, columns(ctx_ref, p, 128), pair_buf.at[slot, 3, pl.ds(0, rows)]),
                 feed(6, slot, lse_ref.at[p], lse_buf.at[slot]),
-                feed(7, slot, mask_ref.at[pl.ds(2 * p, 2)], mask_buf.at[slot]),
             )
 
         def pair_body(p, slot):
             far = lax.rem(p + pairs // 2, pairs)
             here = pl.ds(pl.multiple_of(p * 128, 128), 128)
+            mask = [spread_mask(mask_ref[2 * p + e], key_ref[...]) for e in range(2)]
             dq, dk, dv = attend_back_pair(
-                pair_buf[slot, 0, 0:rows], pair_buf[slot, 1], pair_buf[slot, 2], hot_buf[...], mask_buf[slot],
+                pair_buf[slot, 0, 0:rows], pair_buf[slot, 1], pair_buf[slot, 2], hot_buf[...], mask,
                 pair_buf[slot, 3, 0:rows], lse_buf[slot], dctx[:, here],
             )
             dqkv[0, :, here] = dq.astype(BF16)
@@ -1050,25 +1070,18 @@
         da[at, :] = acc[at, :].astype(BF16)
 
     row_tiles(rows, narrow)
-    stays = lax.axis_index("dp") % 2 == lax.axis_index("tensor")
-    dx_store = load(0, da, dx_out)
-    dx_copy = pltpu.make_async_remote_copy(
-        src_ref=da, dst_ref=dx_out, send_sem=core_send.at[4], recv_sem=core_recv.at[4],
-        device_id=partner(SWAP), device_id_type=MESH,
-    )
-    pl.when(stays)(lambda: dx_store.start())
-    pl.when(jnp.logical_not(stays))(lambda: dx_copy.start())
+    swap(0, da, dx_out, True)
 
     def rest(t, _):
         reduction.tick(t)
         return 0
 
     lax.fori_loop(done, total + LAST_TICK, rest, 0)
-    pl.when(stays)(lambda: dx_store.wait())
-    pl.when(jnp.logical_not(stays))(lambda: dx_copy.wait())
-
-
-def backward(upstream, weights, hot, mask, vectors, saved):
+    swap(0, da, dx_out, False)
+    swap(1, x_ref, x_out, False)
+
+
+def backward(upstream, stream_low, weights, hot, mask, mask_rows, vectors, saved):
     rows, width = upstream.shape
     layers = len(saved)
     total = layers * GROUPS
@@ -1082,12 +1095,13 @@
             jax.ShapeDtypeStruct((total, 512, width), BF16),
             jax.ShapeDtypeStruct((total, 512, width), BF16),
             jax.ShapeDtypeStruct((rows, width), BF16),
+            jax.ShapeDtypeStruct((rows, width), BF16),
             jax.ShapeDtypeStruct((layers, 2, FF_GROUPS, 1, 512), F32),
             jax.ShapeDtypeStruct((layers, 3, 2, 1, 512), F32),
             jax.ShapeDtypeStruct((layers, 8, width), F32),
         ),
-        in_specs=[anywhere] * 4 + [in_vmem] + [anywhere] * (PER_LAYER * layers),
-        out_specs=(anywhere, anywhere, anywhere, in_vmem, in_vmem, in_vmem),
+        in_specs=[anywhere] * 3 + [in_vmem] * 4 + [anywhere] * (PER_LAYER * layers),
+        out_specs=(anywhere, anywhere, anywhere, anywhere, in_vmem, in_vmem, in_vmem),
         scratch_shapes=[
             pltpu.VMEM((rows, width), F32),
             pltpu.VMEM((rows, width), F32),
@@ -1112,8 +1126,6 @@
             low(rows, width),
             low(2, 4, 2 * rows, 128),
             pltpu.VMEM((2, 2, rows), F32),
-            low(2, 2, 2 * rows, 128),
-            low(rows, 128),
             low(512, width),
             low(SLOTS, 256, width),
             low(SLOTS, 128, width),
@@ -1124,8 +1136,9 @@
             dma(8, 2),
             dma(5),
             dma(1),
-            dma(5),
-            dma(5),
+            dma(2),
+            dma(6),
+            dma(6),
             dma(FF_GROUPS),
             dma(FF_GROUPS),
             dma(7, SLOTS),
@@ -1142,18 +1155,12 @@
         ),
         cost_estimate=pl.CostEstimate(flops=60 << 30, bytes_accessed=300 << 20, transcendentals=1 << 24),
         name="backward",
-    )(upstream, weights, hot, mask, vectors, *[ref for one in saved for ref in one])
+    )(upstream, stream_low, weights, hot, mask, mask_rows, vectors, *[ref for one in saved for ref in one])
 
 
 def flip_order(values, axis, bits):
     for i, bit in enumerate(bits):
         values = jnp.where(bit == 0, values, jnp.flip(values, axis + i))
-    return values
-
-
-def sum_everywhere(values):
-    for bit in (FLIP_C, FLIP_Y, FLIP_X, FLIP_Z0, FLIP_Z1):
-        values = values + flip(values, bit)
     return values
 
 
@@ -1199,15 +1206,15 @@
     chosen = lax.dynamic_slice_in_dim(chosen, core * own_blocks, own_blocks, axis=1)
     allowed = allowed[None] | jnp.any(chosen[:, :, None, :] == key_block[None, None, :, None], axis=3)
     block_rows = rows // own_blocks
-    block_part = jnp.where(allowed, 0.0, BIG).astype(BF16).transpose(0, 2, 1)
-    block_part = jnp.repeat(block_part, block_rows, axis=1)
     documents = jnp.arange(128 - own_blocks)
+    mask = jnp.pad(
+        jnp.where(allowed, 0.0, BIG).astype(F32).transpose(0, 2, 1), ((0, 0), (0, 0), (0, 128 - own_blocks))
+    )
     document_part = jnp.where(
         (segments[:, None] == documents[None, :]) | (documents[None, :] > 7), 0.0, BIG
-    ).astype(BF16)
-    mask = jnp.concatenate(
-        [block_part, jnp.broadcast_to(document_part[None], (heads,) + document_part.shape)], axis=2
-    )
+    ).astype(F32)
+    mask_rows = jnp.pad(document_part, ((0, 0), (own_blocks, 0)))
+    block_rows = rows // own_blocks
     hot = jnp.concatenate(
         [
             jnp.repeat(jnp.eye(own_blocks, dtype=BF16), block_rows, axis=0),
@@ -1245,32 +1252,14 @@
     ]
     vectors = jnp.stack(vectors)
     weights, upstream_low, stream_low, saved = forward(
-        block_input, cotangent, w_qkv, w_out, w_in, w_down, hot, mask, bias_qkv, bias_in, vectors
+        block_input, cotangent, w_qkv, w_out, w_in, w_down, hot, mask, mask_rows, bias_qkv, bias_in, vectors
     )
-    block_output = stream_low.astype(F32)[:, None]
-    _, grads, dx_low, d_b_in, qkv_sums, rows_small = backward(upstream_low, weights, hot, mask, vectors, saved)
+    _, grads, dx_low, x_low, d_b_in, qkv_sums, rows_small = backward(
+        upstream_low, stream_low, weights, hot, mask, mask_rows, vectors, saved
+    )
+    block_output = x_low.astype(F32)[:, None]
     input_grad = dx_low.astype(F32)[:, None]
 
-    placed = [None] * 4
-    for layer in range(layers):
-        first = (layers - 1 - layer) * GROUPS
-        put = functools.partial(place, grads, code=code_arg)
-        placed[0] = put(
-            w_qkv.shape, (1, 1, width, 512), lambda i, l=layer: (l, i, 0, 0), True, 3,
-            lambda i, f=first: f + 2 * FF_GROUPS + 1 + i, placed[0],
-        )
-        placed[1] = put(
-            w_out.shape, (1, 512, width), lambda i, l=layer: (l, 0, 0), False, 1,
-            lambda i, f=first: f + 2 * FF_GROUPS, placed[1],
-        )
-        placed[2] = put(
-            w_in.shape, (1, width, 512), lambda i, l=layer: (l, 0, i), True, FF_GROUPS,
-            lambda i, f=first: f + FF_GROUPS + i, placed[2],
-        )
-        placed[3] = put(
-            w_down.shape, (1, 512, width), lambda i, l=layer: (l, i, 0), False, FF_GROUPS,
-            lambda i, f=first: f + i, placed[3],
-        )
     stacks = [
         jnp.stack([qkv_sums[:, 0], qkv_sums[:, 2]], axis=1),
         rows_small[:, 5],
@@ -1287,7 +1276,25 @@
 
     stacks[0] = global_order(stacks[0], layers * 2)
     stacks[2] = global_order(stacks[2], layers * FF_GROUPS)
-    summed = sum_everywhere(jnp.concatenate([s.reshape(-1) for s in stacks]))
+    def placing(shape, block, index, turned, count, start):
+        return lambda values: place(
+            values, shape, block, index, turned, count, lambda l, i: (layers - 1 - l) * GROUPS + start + i, code_arg
+        )
+
+    summed = jnp.concatenate([s.reshape(-1) for s in stacks])
+    summed = summed + flip(summed, FLIP_C)
+    placed = []
+    for bit, put in (
+        (FLIP_Y, placing(w_down.shape, (1, 512, width), lambda l, i: (l, i, 0), False, FF_GROUPS, 0)),
+        (FLIP_X, placing(w_in.shape, (1, width, 512), lambda l, i: (l, 0, i), True, FF_GROUPS, FF_GROUPS)),
+        (FLIP_Z0, placing(w_qkv.shape, (1, 1, width, 512), lambda l, i: (l, i, 0, 0), True, 3, 2 * FF_GROUPS + 1)),
+        (FLIP_Z1, placing(w_out.shape, (1, 512, width), lambda l, i: (l, 0, 0), False, 1, 2 * FF_GROUPS)),
+    ):
+        summed, grads = lax.optimization_barrier((summed, grads))
+        far = flip(summed, bit)
+        done, summed, far = lax.optimization_barrier((put(grads), summed, far))
+        placed.append(done)
+        summed = summed + far
     parts, at = [], 0
     for s in stacks:
         parts.append(summed[at : at + s.size].reshape(s.shape))
@@ -1297,13 +1304,13 @@
     return (
         block_output,
         input_grad,
+        placed[2],
+        g_b_qv,
+        placed[3],
+        parts[1],
+        placed[1],
+        g_b_in,
         placed[0],
-        g_b_qv,
-        placed[1],
-        parts[1],
-        placed[2],
-        g_b_in,
-        placed[3],
         parts[3],
         parts[4],
         parts[5],

time: 690 us -> 642 us (0.930)
  Pallas kernels: 629 us -> 596 us
  waiting for transfers between devices: 13.6 us -> 0.97 us
    pallas_call x1, Pallas kernels: 204 us -> 186 us  [forward(): pl.pallas_call(functools.partial(forward_kernel, layers), out_shape=(low_...]
    ppermute x9, waiting for transfers between devices: 13.6 us -> 0.97 us  [flip(): lax.ppermute(v, ('dp', 'tensor'), pairs)]
    pallas_call x1, Pallas kernels: 384 us -> 376 us  [backward(): pl.pallas_call(functools.partial(backward_kernel, layers), out_shape=(jax...]
    pallas_call x8 -> x4, Pallas kernels: 41.3 us -> 34.3 us  [place(): pl.pallas_call(functools.partial(place_kernel, turned), out_shape=jax.Sha...]
  transfers between devices with their start and end apart: 9 -> 9, of which waited for: 4 -> 1; matrix products, arithmetic and copies ran while one was open for 3% -> 3% of each run, Pallas kernels for 6% -> 5%
where the time goes in v4:
time: 642 us; the launch traced here: 636 us
  Pallas kernels  596 us (93%)
  local copies, waits for them, and re-layouts  22.8 us (4%)
  starting transfers between devices  9.49 us (1%)
    pallas_call x1, Pallas kernels, backward(): pl.pallas_call(functools.partial(backward_kernel, layers), out_shape=(jax...  376 us
    pallas_call x1, Pallas kernels, forward(): pl.pallas_call(functools.partial(forward_kernel, layers), out_shape=(low_...  186 us
    pallas_call x4, Pallas kernels, place(): pl.pallas_call(functools.partial(place_kernel, turned), out_shape=jax.Sha...  34.3 us
  transfers between devices with their start and end apart: 9, of which 1 were waited for; matrix products, arithmetic and copies ran while one was open for 3% of the time, Pallas kernels for 5%

profile of v4, /device:TPU:0, one launch (start us, length us, event | category | flops | bytes accessed | tf_op | source)
XLA Modules:
  0.0 636.4 jit_solution(7726865995012021921)
XLA Ops:
  0.6 0.8 copy.47
  1.5 0.2 reshape_squeeze.11
  1.7 2.5 collective-permute-start.2
  4.1 0.6 collective-permute-start
  4.8 0.7 pad_add_fusion
  5.5 0.8 reshape.261
  6.4 0.1 rev.94
  6.5 0.1 reshape.262
  6.6 0.8 reshape.263
  7.5 0.2 rev.98
  7.7 0.1 reshape.264
  7.8 1.8 collective-permute-start.3
  9.7 0.8 fusion.15
  10.5 0.8 slice_bitcast_fusion.4
  11.5 0.6 pad_maximum_fusion.1.refs_11_.refs_6_
  12.1 0.1 fusion.8
  12.2 0.1 reshape_reshape.22
  12.3 0.1 reshape_reshape.24
  12.4 0.1 copy.48
  12.6 0.7 add_select_fusion
  13.4 0.1 rev.87
  13.5 0.2 reshape_reshape.21
  13.8 0.2 copy.49
  14.0 0.1 constant_dynamic-slice_fusion
  14.1 0.1 compare_reduce_fusion
  14.2 0.1 copy.51
  14.3 0.1 fusion.2
  14.5 0.2 fusion.1
  14.7 0.8 pad_maximum_fusion.refs_6_.refs_3_
  15.5 0.7 pad.8.refs_7_.refs_4_
  16.2 1.0 pad.9.refs_8_.refs_5_
  17.3 0.6 copy.64
  18.0 0.7 pad_maximum_fusion.4.refs_9_
  18.7 186.3 %forward.1 = (bf16[2,24,2,256,1024]{4,3,2,1,0:T(8,128)(2,1)}, bf16[512,1024]{1,0:T(8,128)(2,1)}, bf16[512,1024]{1,0:T(8,128)(2,1)}, bf16[3,512,1024]{2,1,0:T(8,1...) custom-call(f32[512,1,1024]{2,1,0:T(1,128)} %refs_0_.1, ...), custom_call_target="tpu_custom_call" | custom-call | flops 32212254720 | bytes 314572800 | tf_op jit(solution)/shard_map/forward/pallas_call | solution.py:755
  205.0 375.6 %backward.1 = (bf16[24,512,1024]{2,1,0:T(8,128)(2,1)}, bf16[24,512,1024]{2,1,0:T(8,128)(2,1)}, bf16[512,1024]{1,0:T(8,128)(2,1)}, bf16[512,1024]{1,0:T(8,128)(2,...) custom-call(bf16[512,1024]{1,0:T(8,128)(2,1)} %get-tuple-element.69.refs_0_, ...), custom_call_target="tpu_custom_call" | custom-call | flops 64424509440 | bytes 314572800 | tf_op jit(solution)/shard_map/backward/pallas_call | solution.py:1092
  580.7 0.7 fusion.13
  581.4 0.8 copy.54
  582.2 0.1 reshape.266
  582.5 1.1 fusion.12
  583.7 0.2 rev.103
  583.9 0.1 reshape_reshape.26
  584.0 0.2 reshape.267
  584.4 0.3 rev.108
  584.7 0.1 select_bitcast_fusion
  584.8 0.2 reshape_reshape.27
  585.0 0.4 collective-permute-start.4
  585.4 0.9 collective-permute-done.4
  586.4 1.5 collective-permute-start.5
  587.9 10.3 %place.4 = f32[2,2048,1024]{2,1,0:T(8,128)} custom-call(s32[1]{0:T(128)} %bitcast.21.code_ref, bf16[24,512,1024]{2,1,0:T(8,128)(2,1)} %get-tuple-element.119.g_ref), custom_call_target="tpu_custom_call" | custom-call | bytes 25165824 | tf_op jit(solution)/shard_map/place/pallas_call | solution.py:71
  598.2 0.7 collective-permute-start.6
  598.9 11.4 %place.5 = f32[2,1024,2048]{2,1,0:T(8,128)} custom-call(s32[1]{0:T(128)} %bitcast.21.code_ref, bf16[24,512,1024]{2,1,0:T(8,128)(2,1)} %get-tuple-element.119.g_ref), custom_call_target="tpu_custom_call" | custom-call | bytes 25165824 | tf_op jit(solution)/shard_map/place/pallas_call | solution.py:71
  610.5 0.2 bitcast_convert_fusion.1
  610.7 9.2 %place.6 = f32[2,3,1024,512]{3,2,1,0:T(8,128)} custom-call(s32[1]{0:T(128)} %bitcast.21.code_ref, bf16[24,512,1024]{2,1,0:T(8,128)(2,1)} %get-tuple-element.119.g_ref), custom_call_target="tpu_custom_call" | custom-call | bytes 18874368 | tf_op jit(solution)/shard_map/place/pallas_call | solution.py:71
  619.9 1.8 collective-permute-start.8
  621.8 0.2 bitcast_convert_fusion
  622.0 3.5 copy.56
  625.5 3.5 copy.57
  629.0 3.4 place.7
  632.4 0.6 slice.217
  633.0 0.6 slice.214
  633.6 0.6 slice.221
  634.3 0.6 reshape.272
  634.9 0.6 slice.219
  635.6 0.6 reshape.270
  (87 shorter events, 1.5 us)
Async XLA Ops:
  1.7 10.9 %collective-permute-start.2 = (s32[384]{0:T(512)S(1)}, s32[384]{0:T(512)S(1)}, u32[]{:S(2)}, u32[]{:S(2)}) collective-permute-start(s32[384]{0:T(512)S(1)} %reshape_squeeze.11), channel_id=1, source_target_pairs={{0,3},{1,2},{2,1},{3,0},{4,7},{5,6},{6,5},{7,4},{8,11},{9,10},{10,... | collective-permute-start | bytes 4616 | tf_op jit(solution)/shard_map/ppermute | solution.py:36
  4.1 8.5 %collective-permute-start = (s32[384]{0:T(512)S(1)}, s32[384]{0:T(512)S(1)}, u32[]{:S(2)}, u32[]{:S(2)}) collective-permute-start(s32[384]{0:T(512)S(1)} %reshape_squeeze.11), channel_id=1, source_target_pairs={{0,1},{1,0},{2,3},{3,2},{4,5},{5,4},{6,7},{7,6},{8,9},{9,8},{10,11... | collective-permute-start | bytes 4616 | tf_op jit(solution)/shard_map/ppermute | solution.py:36
  5.5 7.1 %collective-permute-start.1 = (s32[1408]{0:T(1024)S(1)}, s32[1408]{0:T(1024)S(1)}, u32[]{:S(2)}, u32[]{:S(2)}) collective-permute-start(s32[1408]{0:T(1024)S(1)} %pad_add_fusion), channel_id=1, source_target_pairs={{0,2},{1,3},{2,0},{3,1},{4,6},{5,7},{6,4},{7,5},{8,10},{9,11},{10,... | collective-permute-start | bytes 16904 | tf_op jit(solution)/shard_map/ppermute | solution.py:36
  7.8 9.3 %collective-permute-start.3 = (f32[6144]{0:T(1024)S(1)}, f32[6144]{0:T(1024)S(1)}, u32[]{:S(2)}, u32[]{:S(2)}) collective-permute-start(f32[6144]{0:T(1024)S(1)} %pad_maximum_fusion.3), channel_id=1, source_target_pairs={{0,1},{1,0},{2,3},{3,2},{4,5},{5,4},{6,7},{7,6},{8,9},{9,8},{10,11... | collective-permute-start | bytes 73736 | tf_op jit(solution)/shard_map/ppermute | solution.py:36
  585.0 1.4 collective-permute-start.4
  586.4 11.8 %collective-permute-start.5 = (f32[24576]{0:T(1024)S(1)}, f32[24576]{0:T(1024)S(1)}, u32[]{:S(2)}, u32[]{:S(2)}) collective-permute-start(f32[24576]{0:T(1024)S(1)} %add.75), channel_id=1, source_target_pairs={{0,1},{1,0},{2,3},{3,2},{4,5},{5,4},{6,7},{7,6},{8,9},{9,8},{10,11... | collective-permute-start | bytes 294920 | tf_op jit(solution)/shard_map/ppermute | solution.py:36
  598.2 12.1 %collective-permute-start.6 = (f32[24576]{0:T(1024)S(1)}, f32[24576]{0:T(1024)S(1)}, u32[]{:S(2)}, u32[]{:S(2)}) collective-permute-start(f32[24576]{0:T(1024)S(1)} %add.76), channel_id=1, source_target_pairs={{0,4},{1,5},{2,6},{3,7},{4,0},{5,1},{6,2},{7,3},{8,12},{9,13},{10,... | collective-permute-start | bytes 294920 | tf_op jit(solution)/shard_map/ppermute | solution.py:36
  598.9 11.5 %copy-start.1 = (bf16[512,1024]{1,0:T(8,128)(2,1)S(1)}, bf16[512,1024]{1,0:T(8,128)(2,1)}, u32[]{:S(2)}) copy-start(bf16[512,1024]{1,0:T(8,128)(2,1)} %get-tuple-element.100) | copy-start | bytes 3145732
  610.4 9.5 %collective-permute-start.7 = (f32[24576]{0:T(1024)S(1)}, f32[24576]{0:T(1024)S(1)}, u32[]{:S(2)}, u32[]{:S(2)}) collective-permute-start(f32[24576]{0:T(1024)S(1)} %add.77), channel_id=1, source_target_pairs={{0,8},{1,9},{2,10},{3,11},{4,12},{5,13},{6,14},{7,15},{8,0},{9,1},... | collective-permute-start | bytes 294920 | tf_op jit(solution)/shard_map/ppermute | solution.py:36
  610.7 11.1 %copy-start = (bf16[512,1024]{1,0:T(8,128)(2,1)S(1)}, bf16[512,1024]{1,0:T(8,128)(2,1)}, u32[]{:S(2)}) copy-start(bf16[512,1024]{1,0:T(8,128)(2,1)} %get-tuple-element.101) | copy-start | bytes 3145732
  619.9 12.4 %collective-permute-start.8 = (f32[24576]{0:T(1024)S(1)}, f32[24576]{0:T(1024)S(1)}, u32[]{:S(2)}, u32[]{:S(2)}) collective-permute-start(f32[24576]{0:T(1024)S(1)} %add.78), channel_id=1, source_target_pairs={{0,16},{1,17},{2,18},{3,19},{4,20},{5,21},{6,22},{7,23},{8,24},{9,... | collective-permute-start | bytes 294920 | tf_op jit(solution)/shard_map/ppermute | solution.py:36

commit v5 on v4

--- a/solution.py
+++ b/solution.py
@@ -86,6 +86,29 @@
     )(code, sums)
 
 
+def widen_kernel(a_ref, b_ref, a_out, b_out, a_buf, b_buf, sem):
+    copies = []
+    for n, (source, target, buf) in enumerate(((a_ref, a_out, a_buf), (b_ref, b_out, b_buf))):
+        buf[...] = source[...].astype(F32)
+        copies.append(pltpu.make_async_copy(buf, target.at[:, 0], sem.at[n]))
+        copies[-1].start()
+    for copy in copies:
+        copy.wait()
+
+
+def widen_rows(a, b):
+    rows, width = a.shape
+    out = jax.ShapeDtypeStruct((rows, 1, width), F32)
+    return pl.pallas_call(
+        widen_kernel,
+        out_shape=(out, out),
+        in_specs=[pl.BlockSpec(memory_space=pltpu.VMEM)] * 2,
+        out_specs=(pl.BlockSpec(memory_space=pl.ANY),) * 2,
+        scratch_shapes=[pltpu.VMEM((rows, width), F32), pltpu.VMEM((rows, width), F32), pltpu.SemaphoreType.DMA((2,))],
+        name="widen_rows",
+    )(a, b)
+
+
 def partner(bits):
     dp, y = lax.axis_index("dp"), lax.axis_index("tensor")
     other = dp
@@ -102,6 +125,14 @@
     pl.semaphore_wait(barrier, len(bits))
 
 
+def add_into(into, other, count):
+    def step(i, _):
+        into[i] = (into[i].astype(F32) + other[i].astype(F32)).astype(BF16)
+        return 0
+
+    lax.fori_loop(0, count, step, 0)
+
+
 def add_rows(into, other, rows):
     def step(i, _):
         at = pl.ds(pl.multiple_of(i * 32, 32), 32)
@@ -111,7 +142,7 @@
     lax.fori_loop(0, rows // 32, step, 0)
 
 
-SLOTS = 8
+SLOTS = 12
 LAST_TICK = 10
 
 
@@ -122,18 +153,22 @@
         self.send_sem, self.recv_sem, self.core_send, self.core_recv = sems[:4]
         self.keep_sem, self.out_sem, self.in_free, self.out_free = sems[4:]
 
+    def blocks(self, ref, i, first):
+        part = pl.ds(pl.multiple_of(lax.rem(i, 2) * 16, 16), 16)
+        return ref.at[lax.div(i, 2), pl.ds(first, 8), part]
+
     def copy(self, step, i):
         slot = lax.rem(i, SLOTS)
         ys, al = self.y_buf.at[slot], self.all_buf.at[slot]
         bit, source, target = (
-            (FLIP_Y, self.grads.at[i, pl.ds(256, 256)], ys),
-            (FLIP_X, ys.at[pl.ds(128, 128)], self.x_buf.at[slot]),
-            (FLIP_Z0, ys.at[pl.ds(64, 64)], self.z0_buf.at[slot]),
-            (FLIP_Z1, ys.at[pl.ds(32, 32)], self.z1_buf.at[slot]),
-            (FLIP_Z1, al.at[pl.ds(0, 32)], al.at[pl.ds(32, 32)]),
-            (FLIP_Z0, al.at[pl.ds(0, 64)], al.at[pl.ds(64, 64)]),
-            (FLIP_X, al.at[pl.ds(0, 128)], al.at[pl.ds(128, 128)]),
-            (FLIP_C, al, self.sums.at[i, pl.ds(256, 256)]),
+            (FLIP_Y, self.blocks(self.grads, i, 8), ys),
+            (FLIP_X, ys.at[pl.ds(4, 4)], self.x_buf.at[slot]),
+            (FLIP_Z0, ys.at[pl.ds(2, 2)], self.z0_buf.at[slot]),
+            (FLIP_Z1, ys.at[pl.ds(1, 1)], self.z1_buf.at[slot]),
+            (FLIP_Z1, al.at[pl.ds(0, 1)], al.at[pl.ds(1, 1)]),
+            (FLIP_Z0, al.at[pl.ds(0, 2)], al.at[pl.ds(2, 2)]),
+            (FLIP_X, al.at[pl.ds(0, 4)], al.at[pl.ds(4, 4)]),
+            (FLIP_C, al, self.blocks(self.sums, i, 8)),
         )[step]
         return pltpu.make_async_remote_copy(
             src_ref=source,
@@ -147,13 +182,13 @@
     def keep(self, i):
         slot = lax.rem(i, 2)
         return pltpu.make_async_copy(
-            self.grads.at[i, pl.ds(0, 256)], self.keep_buf.at[slot], self.keep_sem.at[slot]
+            self.blocks(self.grads, i, 0), self.keep_buf.at[slot], self.keep_sem.at[slot]
         )
 
     def out(self, i):
         slot = lax.rem(i, SLOTS)
         return pltpu.make_async_copy(
-            self.all_buf.at[slot], self.sums.at[i, pl.ds(0, 256)], self.out_sem.at[slot]
+            self.all_buf.at[slot], self.blocks(self.sums, i, 0), self.out_sem.at[slot]
         )
 
     def take(self, sem, i):
@@ -199,8 +234,8 @@
 
         def back_z1(i, slot):
             self.copy(3, i).wait()
-            add_rows(self.y_buf.at[slot], self.z1_buf.at[slot], 32)
-            self.all_buf[slot, 0:32, :] = self.y_buf[slot, 0:32, :]
+            add_into(self.y_buf.at[slot], self.z1_buf.at[slot], 1)
+            self.all_buf[slot, 0] = self.y_buf[slot, 0]
             for n, bit in enumerate((FLIP_Y, FLIP_X, FLIP_Z0, FLIP_Z1)):
                 self.give(self.in_free.at[n], bit, i)
             self.take(self.out_free.at[2], i)
@@ -208,20 +243,20 @@
 
         def on_z1(i, slot):
             self.copy(2, i).wait()
-            add_rows(self.y_buf.at[slot], self.z0_buf.at[slot], 64)
+            add_into(self.y_buf.at[slot], self.z0_buf.at[slot], 2)
             self.take(self.in_free.at[3], i)
             self.copy(3, i).start()
 
         def on_z0(i, slot):
             self.copy(1, i).wait()
-            add_rows(self.y_buf.at[slot], self.x_buf.at[slot], 128)
+            add_into(self.y_buf.at[slot], self.x_buf.at[slot], 4)
             self.take(self.in_free.at[2], i)
             self.copy(2, i).start()
 
         def on_x(i, slot):
             self.copy(0, i).wait()
             self.keep(i).wait()
-            add_rows(self.y_buf.at[slot], self.keep_buf.at[lax.rem(i, 2)], 256)
+            add_into(self.y_buf.at[slot], self.keep_buf.at[lax.rem(i, 2)], 8)
             self.take(self.in_free.at[1], i)
             self.copy(1, i).start()
 
@@ -817,7 +852,7 @@
     rows, width = acc.shape
     total = layers * GROUPS
     reduction = Reduction(
-        grads, sums, total,
+        grads, sums, 2 * total,
         (y_buf, x_buf, z0_buf, z1_buf, all_buf, keep_buf),
         (send_sem, recv_sem, sum_send, sum_recv, keep_sem, out_sem, in_free, out_free),
     )
@@ -848,7 +883,8 @@
         return ref.at[:, pl.ds(pl.multiple_of(i * size, size), size)]
 
     def unit(left, left_sib, right, right_sib, index):
-        unit_buf[...] = (tn(left, right) + tn(left_sib, right_sib)).astype(BF16)
+        made = (tn(left, right) + tn(left_sib, right_sib)).astype(BF16)
+        unit_buf[...] = made.reshape(unit_buf.shape)
         store = pltpu.make_async_copy(unit_buf, grads.at[index], store_sem.at[0])
         store.start()
         store.wait()
@@ -888,7 +924,7 @@
         qkv_ref, sib_ref, ctx_ref, ctx_sib_ref, lse_ref, r1_ref, r2_ref, hl_ref, hl_sib_ref, g_ref, g_sib_ref, slope_ref, xb_ref, xb_sib_ref = saved[l]
         first = l * GROUPS
         base = (layers - 1 - l) * GROUPS
-        clock = 11 * (layers - 1 - l)
+        clock = 22 * (layers - 1 - l)
 
         r_load = load(0, r2_ref, r_buf)
         r_load.start()
@@ -922,7 +958,7 @@
 
         def down_body(i, slot):
             unit(left_buf[slot], left_sib_buf[slot], dm[...], dm_sib[...], base + i)
-            pl.when(lax.rem(i, 3) == 0)(lambda: reduction.tick(clock + lax.div(i, 3)))
+            reduction.tick(clock + i)
 
         stream(FF_GROUPS, down_feeds, down_body)
 
@@ -948,7 +984,7 @@
             pl.when(a == 1)(lambda: give_du(j, n).start())
             dbi_ref[l, a, n] = jnp.sum(d.astype(F32), axis=0, keepdims=True)
             acc[...] += nn(d, block_of(wb_buf.at[slot]))
-            pl.when(lax.rem(i, 3) == 2)(lambda: reduction.tick(clock + 2 + lax.div(i, 3)))
+            pl.when(lax.rem(i, 2) == 1)(lambda: reduction.tick(clock + 4 + lax.div(i, 2)))
 
         stream(2 * FF_GROUPS, ff_feeds, ff_body)
 
@@ -981,7 +1017,7 @@
         def in_body(n, _):
             give_du(FF_GROUPS + n, n).wait()
             unit(du[n], du_sib[n], right_buf[...], right_sib_buf[...], base + FF_GROUPS + n)
-            pl.when(lax.rem(n, 3) == 0)(lambda: reduction.tick(clock + 4 + lax.div(n, 3)))
+            reduction.tick(clock + 8 + n)
             return 0
 
         lax.fori_loop(0, FF_GROUPS, in_body, 0)
@@ -1027,7 +1063,7 @@
             there = pl.ds(pl.multiple_of(far * 128, 128), 128)
             kv_out[0, :, there] = dk[rows:].astype(BF16)
             kv_out[1, :, there] = dv[rows:].astype(BF16)
-            pl.when(lax.rem(p, 3) == 1)(lambda: reduction.tick(clock + 6 + lax.div(p, 3)))
+            pl.when(lax.rem(p, 4) < 3)(lambda: reduction.tick(clock + 12 + 3 * lax.div(p, 4) + lax.rem(p, 4)))
 
         stream(pairs, pair_feeds, pair_body)
         kv_copy = exchange(2, kv_out, kv_far)
@@ -1043,10 +1079,10 @@
 
         def qkv_body(n, _):
             unit(dqkv[n, :, 0:512], d_sib[n], right_buf[...], right_sib_buf[...], base + 2 * FF_GROUPS + 1 + n)
+            pl.when(n > 0)(lambda: reduction.tick(clock + 17 + n))
             return 0
 
         lax.fori_loop(0, 3, qkv_body, 0)
-        reduction.tick(clock + 9)
 
         def start_dx(at):
             acc[at, :] = dr1[at, :]
@@ -1061,10 +1097,10 @@
             d = dqkv[n, :, pl.ds(pl.multiple_of(a * 512, 512), 512)]
             qkv_sums_ref[l, n, a] = jnp.sum(d.astype(F32), axis=0, keepdims=True)
             acc[...] += nn(d, block_of(wa_buf.at[slot]))
-            pl.when(i == 3)(lambda: reduction.tick(clock + 10))
+            pl.when(lax.rem(i, 3) == 2)(lambda: reduction.tick(clock + 20 + lax.div(i, 3)))
 
         stream(6, dx_feeds, dx_body)
-        done = clock + 11
+        done = clock + 22
 
     def narrow(at):
         da[at, :] = acc[at, :].astype(BF16)
@@ -1076,7 +1112,7 @@
         reduction.tick(t)
         return 0
 
-    lax.fori_loop(done, total + LAST_TICK, rest, 0)
+    lax.fori_loop(done, 2 * total + LAST_TICK, rest, 0)
     swap(0, da, dx_out, False)
     swap(1, x_ref, x_out, False)
 
@@ -1092,8 +1128,8 @@
     return pl.pallas_call(
         functools.partial(backward_kernel, layers),
         out_shape=(
-            jax.ShapeDtypeStruct((total, 512, width), BF16),
-            jax.ShapeDtypeStruct((total, 512, width), BF16),
+            jax.ShapeDtypeStruct((total, 16, 32, width), BF16),
+            jax.ShapeDtypeStruct((total, 16, 32, width), BF16),
             jax.ShapeDtypeStruct((rows, width), BF16),
             jax.ShapeDtypeStruct((rows, width), BF16),
             jax.ShapeDtypeStruct((layers, 2, FF_GROUPS, 1, 512), F32),
@@ -1126,13 +1162,13 @@
             low(rows, width),
             low(2, 4, 2 * rows, 128),
             pltpu.VMEM((2, 2, rows), F32),
-            low(512, width),
-            low(SLOTS, 256, width),
-            low(SLOTS, 128, width),
-            low(SLOTS, 64, width),
-            low(SLOTS, 32, width),
-            low(SLOTS, 256, width),
-            low(2, 256, width),
+            low(16, 32, width),
+            low(SLOTS, 8, 16, width),
+            low(SLOTS, 4, 16, width),
+            low(SLOTS, 2, 16, width),
+            low(SLOTS, 1, 16, width),
+            low(SLOTS, 8, 16, width),
+            low(2, 8, 16, width),
             dma(8, 2),
             dma(5),
             dma(1),
@@ -1143,8 +1179,8 @@
             dma(FF_GROUPS),
             dma(7, SLOTS),
             dma(7, SLOTS),
-            dma(total),
-            dma(total),
+            dma(2 * total),
+            dma(2 * total),
             dma(2),
             dma(SLOTS),
             pltpu.SemaphoreType.REGULAR((4,)),
@@ -1257,8 +1293,8 @@
     _, grads, dx_low, x_low, d_b_in, qkv_sums, rows_small = backward(
         upstream_low, stream_low, weights, hot, mask, mask_rows, vectors, saved
     )
-    block_output = x_low.astype(F32)[:, None]
-    input_grad = dx_low.astype(F32)[:, None]
+    grads = grads.reshape(layers * GROUPS, 512, width)
+    block_output, input_grad = widen_rows(x_low, dx_low)
 
     stacks = [
         jnp.stack([qkv_sums[:, 0], qkv_sums[:, 2]], axis=1),

time: 642 us -> 650 us (1.012)
  Pallas kernels: 596 us -> 612 us
  local copies, waits for them, and re-layouts: 22.8 us -> 15.9 us
    pallas_call x1, Pallas kernels: 376 us -> 388 us  [backward(): pl.pallas_call(functools.partial(backward_kernel, layers), out_shape=(jax...]
    unnamed x15 -> x9, local copies, waits for them, and re-layouts: 7.81 us -> 0.85 us
  transfers between devices with their start and end apart: 9 -> 9, of which waited for: 1 -> 1; matrix products, arithmetic and copies ran while one was open for 3% -> 2% of each run, Pallas kernels for 5% -> 6%
where the time goes in v5:
time: 650 us; the launch traced here: 645 us
  Pallas kernels  612 us (94%)
  local copies, waits for them, and re-layouts  15.9 us (2%)
  starting transfers between devices  8.87 us (1%)
    pallas_call x1, Pallas kernels, backward(): pl.pallas_call(functools.partial(backward_kernel, layers), out_shape=(jax...  388 us
    pallas_call x1, Pallas kernels, forward(): pl.pallas_call(functools.partial(forward_kernel, layers), out_shape=(low_...  187 us
    pallas_call x4, Pallas kernels, place(): pl.pallas_call(functools.partial(place_kernel, turned), out_shape=jax.Sha...  33.9 us
  transfers between devices with their start and end apart: 9, of which 1 were waited for; matrix products, arithmetic and copies ran while one was open for 2% of the time, Pallas kernels for 6%

profile of v5, /device:TPU:0, one launch (start us, length us, event | category | flops | bytes accessed | tf_op | source)
XLA Modules:
  0.0 644.6 jit_solution(14611337094282967994)
XLA Ops:
  0.6 0.8 copy.41
  1.5 0.2 reshape_squeeze.11
  1.7 2.5 collective-permute-start.2
  4.1 0.6 collective-permute-start
  4.8 0.7 pad_add_fusion
  5.5 0.8 reshape.264
  6.4 0.1 rev.94
  6.5 0.1 reshape.265
  6.6 0.8 reshape.266
  7.5 0.2 rev.98
  7.7 0.1 reshape.267
  7.8 1.8 collective-permute-start.3
  9.7 0.8 fusion.15
  10.5 0.8 slice_bitcast_fusion.4
  11.3 0.1 stack.28
  11.5 0.6 pad_maximum_fusion.1.refs_11_.refs_6_
  12.1 0.1 fusion.8
  12.2 0.1 reshape_reshape.22
  12.3 0.1 reshape_reshape.24
  12.4 0.1 copy.42
  12.5 0.1 pad.21.clone
  12.6 0.7 add_select_fusion
  13.4 0.1 rev.87
  13.5 0.2 reshape_reshape.21
  13.8 0.2 copy.43
  14.0 0.1 constant_dynamic-slice_fusion
  14.1 0.1 compare_reduce_fusion
  14.2 0.1 copy.45
  14.3 0.1 fusion.2
  14.5 0.2 fusion.1
  14.7 0.8 pad_maximum_fusion.refs_6_.refs_3_
  15.5 0.7 pad.8.refs_7_.refs_4_
  16.2 1.0 pad.9.refs_8_.refs_5_
  17.3 0.6 copy.56
  18.0 0.7 pad_maximum_fusion.4.refs_9_
  18.7 186.6 %forward.1 = (bf16[2,24,2,256,1024]{4,3,2,1,0:T(8,128)(2,1)}, bf16[512,1024]{1,0:T(8,128)(2,1)}, bf16[512,1024]{1,0:T(8,128)(2,1)}, bf16[3,512,1024]{2,1,0:T(8,1...) custom-call(f32[512,1,1024]{2,1,0:T(1,128)} %refs_0_.1, ...), custom_call_target="tpu_custom_call" | custom-call | flops 32212254720 | bytes 314572800 | tf_op jit(solution)/shard_map/forward/pallas_call | solution.py:790
  205.3 388.3 %backward.1 = (bf16[24,16,32,1024]{3,2,1,0:T(8,128)(2,1)}, bf16[24,16,32,1024]{3,2,1,0:T(8,128)(2,1)}, bf16[512,1024]{1,0:T(8,128)(2,1)}, bf16[512,1024]{1,0:T(8...) custom-call(bf16[512,1024]{1,0:T(8,128)(2,1)} %get-tuple-element.71.refs_0_, ...), custom_call_target="tpu_custom_call" | custom-call | flops 64424509440 | bytes 314572800 | tf_op jit(solution)/shard_map/backward/pallas_call | solution.py:1128
  593.5 0.7 fusion.13
  594.2 0.8 copy.48
  595.1 0.1 reshape.269
  595.3 1.1 fusion.12
  596.6 0.2 rev.103
  596.8 0.1 reshape_reshape.26
  596.9 0.2 reshape.270
  597.3 0.3 rev.108
  597.6 0.1 select_bitcast_fusion
  597.7 0.2 reshape_reshape.27
  597.9 0.4 collective-permute-start.4
  598.3 0.9 collective-permute-done.4
  599.3 1.3 collective-permute-start.5
  600.5 10.3 %place.4 = f32[2,2048,1024]{2,1,0:T(8,128)} custom-call(s32[1]{0:T(128)} %bitcast.19.code_ref, bf16[24,512,1024]{2,1,0:T(8,128)(2,1)} %bitcast.59), custom_call_target="tpu_custom_call" | custom-call | bytes 25165824 | tf_op jit(solution)/shard_map/place/pallas_call | solution.py:71
  610.9 0.4 collective-permute-start.6
  611.3 11.3 %place.5 = f32[2,1024,2048]{2,1,0:T(8,128)} custom-call(s32[1]{0:T(128)} %bitcast.19.code_ref, bf16[24,512,1024]{2,1,0:T(8,128)(2,1)} %bitcast.60), custom_call_target="tpu_custom_call" | custom-call | bytes 25165824 | tf_op jit(solution)/shard_map/place/pallas_call | solution.py:71
  622.6 1.0 collective-permute-start.7
  623.6 8.9 %place.6 = f32[2,3,1024,512]{3,2,1,0:T(8,128)} custom-call(s32[1]{0:T(128)} %bitcast.19.code_ref, bf16[24,512,1024]{2,1,0:T(8,128)(2,1)} %bitcast.61), custom_call_target="tpu_custom_call" | custom-call | bytes 18874368 | tf_op jit(solution)/shard_map/place/pallas_call | solution.py:71
  632.6 0.8 collective-permute-start.8
  633.3 3.7 widen_rows.1
  637.1 3.4 place.7
  640.5 0.6 slice.217
  641.1 0.6 slice.214
  641.7 0.6 slice.221
  642.4 0.6 reshape.276
  643.0 0.6 slice.219
  643.7 0.6 reshape.274
  (80 shorter events, 1.3 us)
Async XLA Ops:
  1.7 10.9 %collective-permute-start.2 = (s32[384]{0:T(512)S(1)}, s32[384]{0:T(512)S(1)}, u32[]{:S(2)}, u32[]{:S(2)}) collective-permute-start(s32[384]{0:T(512)S(1)} %reshape_squeeze.11), channel_id=1, source_target_pairs={{0,3},{1,2},{2,1},{3,0},{4,7},{5,6},{6,5},{7,4},{8,11},{9,10},{10,... | collective-permute-start | bytes 4616 | tf_op jit(solution)/shard_map/ppermute | solution.py:36
  4.1 8.5 %collective-permute-start = (s32[384]{0:T(512)S(1)}, s32[384]{0:T(512)S(1)}, u32[]{:S(2)}, u32[]{:S(2)}) collective-permute-start(s32[384]{0:T(512)S(1)} %reshape_squeeze.11), channel_id=1, source_target_pairs={{0,1},{1,0},{2,3},{3,2},{4,5},{5,4},{6,7},{7,6},{8,9},{9,8},{10,11... | collective-permute-start | bytes 4616 | tf_op jit(solution)/shard_map/ppermute | solution.py:36
  5.5 7.1 %collective-permute-start.1 = (s32[1408]{0:T(1024)S(1)}, s32[1408]{0:T(1024)S(1)}, u32[]{:S(2)}, u32[]{:S(2)}) collective-permute-start(s32[1408]{0:T(1024)S(1)} %pad_add_fusion), channel_id=1, source_target_pairs={{0,2},{1,3},{2,0},{3,1},{4,6},{5,7},{6,4},{7,5},{8,10},{9,11},{10,... | collective-permute-start | bytes 16904 | tf_op jit(solution)/shard_map/ppermute | solution.py:36
  7.8 9.3 %collective-permute-start.3 = (f32[6144]{0:T(1024)S(1)}, f32[6144]{0:T(1024)S(1)}, u32[]{:S(2)}, u32[]{:S(2)}) collective-permute-start(f32[6144]{0:T(1024)S(1)} %pad_maximum_fusion.3), channel_id=1, source_target_pairs={{0,1},{1,0},{2,3},{3,2},{4,5},{5,4},{6,7},{7,6},{8,9},{9,8},{10,11... | collective-permute-start | bytes 73736 | tf_op jit(solution)/shard_map/ppermute | solution.py:36
  597.9 1.4 collective-permute-start.4
  599.3 11.6 %collective-permute-start.5 = (f32[24576]{0:T(1024)S(1)}, f32[24576]{0:T(1024)S(1)}, u32[]{:S(2)}, u32[]{:S(2)}) collective-permute-start(f32[24576]{0:T(1024)S(1)} %add.75), channel_id=1, source_target_pairs={{0,1},{1,0},{2,3},{3,2},{4,5},{5,4},{6,7},{7,6},{8,9},{9,8},{10,11... | collective-permute-start | bytes 294920 | tf_op jit(solution)/shard_map/ppermute | solution.py:36
  610.9 11.8 %collective-permute-start.6 = (f32[24576]{0:T(1024)S(1)}, f32[24576]{0:T(1024)S(1)}, u32[]{:S(2)}, u32[]{:S(2)}) collective-permute-start(f32[24576]{0:T(1024)S(1)} %add.76), channel_id=1, source_target_pairs={{0,4},{1,5},{2,6},{3,7},{4,0},{5,1},{6,2},{7,3},{8,12},{9,13},{10,... | collective-permute-start | bytes 294920 | tf_op jit(solution)/shard_map/ppermute | solution.py:36
  622.6 9.9 %collective-permute-start.7 = (f32[24576]{0:T(1024)S(1)}, f32[24576]{0:T(1024)S(1)}, u32[]{:S(2)}, u32[]{:S(2)}) collective-permute-start(f32[24576]{0:T(1024)S(1)} %add.77), channel_id=1, source_target_pairs={{0,8},{1,9},{2,10},{3,11},{4,12},{5,13},{6,14},{7,15},{8,0},{9,1},... | collective-permute-start | bytes 294920 | tf_op jit(solution)/shard_map/ppermute | solution.py:36
  632.6 7.9 %collective-permute-start.8 = (f32[24576]{0:T(1024)S(1)}, f32[24576]{0:T(1024)S(1)}, u32[]{:S(2)}, u32[]{:S(2)}) collective-permute-start(f32[24576]{0:T(1024)S(1)} %add.78), channel_id=1, source_target_pairs={{0,16},{1,17},{2,18},{3,19},{4,20},{5,21},{6,22},{7,23},{8,24},{9,... | collective-permute-start | bytes 294920 | tf_op jit(solution)/shard_map/ppermute | solution.py:36

commit v6 on v5

--- a/solution.py
+++ b/solution.py
@@ -143,7 +143,7 @@
 
 
 SLOTS = 12
-LAST_TICK = 10
+LAST_TICK = 8
 
 
 class Reduction:
@@ -261,20 +261,22 @@
             self.copy(1, i).start()
 
         at(0, set_out)
-        at(10, finish)
-        at(9, to_core)
-        at(7, back_x)
-        at(6, back_z0)
-        at(5, back_z1)
-        at(4, on_z1)
+        at(8, finish)
+        at(7, to_core)
+        at(6, back_x)
+        at(5, back_z0)
+        at(4, back_z1)
+        at(3, on_z1)
+        at(2, on_z0)
         at(1, on_x)
-        at(3, on_z0)
-
-
-def stream(count, feeds, body):
+
+
+def begin(feeds):
     for copy in feeds(0, 0):
         copy.start()
 
+
+def stream(count, feeds, body):
     def step(i, _):
         slot = lax.rem(i, 2)
 
@@ -491,7 +493,7 @@
 
     items = []
     for l in range(layers):
-        items += [(True, wq_ref.at[l, t], l * GROUPS + t) for t in range(3)]
+        items += [(True, wq_ref.at[l, (t + 1) % 3], l * GROUPS + t) for t in range(3)]
         items += [(False, wo_ref.at[l], l * GROUPS + OUT_GROUP)]
         for n in range(FF_GROUPS):
             items += [(True, wi_ref.at[l, :, pl.ds(n * 512, 512)], l * GROUPS + in_group(n))]
@@ -611,19 +613,21 @@
 
         def which(i):
             n = lax.div(i, 2)
-            return 1 - n + 3 * lax.div(n, 2), lax.rem(i, 2)
+            return lax.rem(n + 1, 3), n, lax.rem(i, 2)
 
         def qkv_feeds(i, slot):
-            t, a = which(i)
-            return (feed(0, slot, w_ref.at[a, first + t], wa_buf.at[slot]),)
+            _, n, a = which(i)
+            return (feed(0, slot, w_ref.at[a, first + n], wa_buf.at[slot]),)
 
         def qkv_body(i, slot):
-            t, a = which(i)
+            t, _, a = which(i)
             at = pl.ds(pl.multiple_of(a * 512, 512), 512)
             qkv[t, :, at] = (nt(xb[...], block_of(wa_buf.at[slot])) + bq_ref[l, t, a]).astype(BF16)
             pl.when(t > 0)(lambda: give_kv(t - 1, a).start())
             pl.when(i == 2)(lambda: spread.tick(clock))
 
+        if l == 0:
+            begin(qkv_feeds)
         stream(6, qkv_feeds, qkv_body)
         qkv_store = store(1, qkv, qkv_out)
         qkv_store.start()
@@ -632,6 +636,8 @@
                 give_kv(n, a).wait()
         sib_store = store(2, kv_sib, sib_out)
         sib_store.start()
+
+        feed(2, 0, w_ref.at[0, first + OUT_GROUP], wb_buf.at[0]).start()
 
         def pair_body(p, _):
             far = lax.rem(p + pairs // 2, pairs)
@@ -655,11 +661,23 @@
         ctx_copy = exchange(3 + 3 * l, ctx.at[:, pl.ds(512, 512)], ctx_sib_out)
         ctx_copy.start()
 
+        def place_of(i):
+            return 1 - lax.rem(i, 2), lax.div(i, 2)
+
+        def ff_feeds(i, slot):
+            a, n = place_of(i)
+            return (
+                feed(0, slot, w_ref.at[a, first + in_group(n)], wa_buf.at[slot]),
+                feed(2, slot, w_ref.at[a, first + down_group(n)], wb_buf.at[slot]),
+            )
+
+        ff_feeds(0, 0)[0].start()
+
         def out_feeds(i, slot):
-            return (feed(0, slot, w_ref.at[i, first + OUT_GROUP], wa_buf.at[slot]),)
+            return (feed(2, slot, w_ref.at[i, first + OUT_GROUP], wb_buf.at[slot]),)
 
         def out_body(i, slot):
-            part = nn(ctx[:, pl.ds(pl.multiple_of(i * 512, 512), 512)], block_of(wa_buf.at[slot]))
+            part = nn(ctx[:, pl.ds(pl.multiple_of(i * 512, 512), 512)], block_of(wb_buf.at[slot]))
 
             @pl.when(i == 0)
             def _():
@@ -670,6 +688,7 @@
                 acc[...] += part
 
         stream(2, out_feeds, out_body)
+        ff_feeds(0, 0)[1].start()
         sib_store.wait()
 
         def first_norm(at):
@@ -686,16 +705,6 @@
         hl_store.start()
         hl_copy = exchange(4 + 3 * l, hl, hl_sib_out)
         hl_copy.start()
-
-        def place_of(i):
-            return 1 - lax.rem(i, 2), lax.div(i, 2)
-
-        def ff_feeds(i, slot):
-            a, n = place_of(i)
-            return (
-                feed(0, slot, w_ref.at[a, first + in_group(n)], wa_buf.at[slot]),
-                feed(2, slot, w_ref.at[a, first + down_group(n)], wb_buf.at[slot]),
-            )
 
         def g_store(j):
             return pltpu.make_async_copy(g_all.at[j], columns(g_out, j, 512), block_sem.at[0, j])
@@ -728,6 +737,8 @@
         r1_store.wait()
         xb_store.wait()
         xb_copy.wait()
+        if l + 1 < layers:
+            feed(0, 0, w_ref.at[0, first + GROUPS], wa_buf.at[0]).start()
 
         def second_norm(at):
             r2 = acc[at, :]
@@ -846,7 +857,7 @@
         wa_buf, wb_buf, r_buf, slope_buf, left_buf, left_sib_buf, right_buf, right_sib_buf,
         pair_buf, lse_buf, unit_buf,
         y_buf, x_buf, z0_buf, z1_buf, all_buf, keep_buf,
-        feed_sem, load_sem, store_sem, swap_sem, core_send, core_recv, du_send, du_recv,
+        feed_sem, load_sem, store_sem, swap_sem, core_send, core_recv, du_send, du_recv, pair_send, pair_recv,
         send_sem, recv_sem, sum_send, sum_recv, keep_sem, out_sem, in_free, out_free,
     ) = refs[at_ref + 7 :]
     rows, width = acc.shape
@@ -882,12 +893,17 @@
     def columns(ref, i, size):
         return ref.at[:, pl.ds(pl.multiple_of(i * size, size), size)]
 
-    def unit(left, left_sib, right, right_sib, index):
+    def unit_store(slot, index):
+        return pltpu.make_async_copy(unit_buf.at[slot], grads.at[index], store_sem.at[0])
+
+    def unit(left, left_sib, right, right_sib, slot, index, fresh=False):
         made = (tn(left, right) + tn(left_sib, right_sib)).astype(BF16)
-        unit_buf[...] = made.reshape(unit_buf.shape)
-        store = pltpu.make_async_copy(unit_buf, grads.at[index], store_sem.at[0])
-        store.start()
-        store.wait()
+        unit_buf[slot] = made.reshape(unit_buf.shape[1:])
+        if fresh is not False:
+            pl.when(jnp.logical_not(fresh))(lambda: unit_store(slot, index).wait())
+        else:
+            unit_store(slot, index).wait()
+        unit_store(slot, index).start()
 
     def add_small(l, row, value):
         small_ref[l, row : row + 1, :] += jnp.sum(value, axis=0, keepdims=True)
@@ -910,7 +926,8 @@
             there.start() if begin else there.wait()
 
     swap(1, x_ref, x_out, True)
-    start_up = load(0, up_ref, da)
+    load(0, saved[-1][6], r_buf).start()
+    start_up = load(1, up_ref, da)
     start_up.start()
     start_up.wait()
     small_ref[...] = jnp.zeros_like(small_ref)
@@ -926,9 +943,14 @@
         base = (layers - 1 - l) * GROUPS
         clock = 22 * (layers - 1 - l)
 
-        r_load = load(0, r2_ref, r_buf)
-        r_load.start()
-        r_load.wait()
+        def down_feeds(i, slot):
+            return (
+                feed(0, slot, columns(g_ref, i, 512), left_buf.at[slot]),
+                feed(1, slot, columns(g_sib_ref, i, 512), left_sib_buf.at[slot]),
+            )
+
+        begin(down_feeds)
+        load(0, r2_ref, r_buf).wait()
 
         def second(at):
             dy = acc[at, :]
@@ -950,17 +972,10 @@
         right_sib_load.start()
         dm_copy.wait()
 
-        def down_feeds(i, slot):
-            return (
-                feed(0, slot, columns(g_ref, i, 512), left_buf.at[slot]),
-                feed(1, slot, columns(g_sib_ref, i, 512), left_sib_buf.at[slot]),
-            )
-
         def down_body(i, slot):
-            unit(left_buf[slot], left_sib_buf[slot], dm[...], dm_sib[...], base + i)
-            reduction.tick(clock + i)
-
-        stream(FF_GROUPS, down_feeds, down_body)
+            fresh = (i == 0) if l == layers - 1 else False
+            unit(left_buf[slot], left_sib_buf[slot], dm[...], dm_sib[...], lax.rem(i, 2), base + i, fresh)
+            pl.when(i > 0)(lambda: reduction.tick(clock + i - 1))
 
         def place_of(i):
             a = 1 - lax.div(i, FF_GROUPS)
@@ -970,10 +985,14 @@
             a, n = place_of(i)
             j = a * FF_GROUPS + n
             return (
-                feed(0, slot, weight(a, first + down_group(n)), wa_buf.at[slot]),
-                feed(1, slot, weight(a, first + in_group(n)), wb_buf.at[slot]),
-                feed(2, slot, columns(slope_ref, j, 512), slope_buf.at[slot]),
+                feed(2, slot, weight(a, first + down_group(n)), wa_buf.at[slot]),
+                feed(3, slot, weight(a, first + in_group(n)), wb_buf.at[slot]),
+                feed(4, slot, columns(slope_ref, j, 512), slope_buf.at[slot]),
             )
+
+        begin(ff_feeds)
+        stream(FF_GROUPS, down_feeds, down_body)
+        unit_store(1, base + FF_GROUPS - 1).wait()
 
         def ff_body(i, slot):
             a, n = place_of(i)
@@ -984,10 +1003,14 @@
             pl.when(a == 1)(lambda: give_du(j, n).start())
             dbi_ref[l, a, n] = jnp.sum(d.astype(F32), axis=0, keepdims=True)
             acc[...] += nn(d, block_of(wb_buf.at[slot]))
-            pl.when(lax.rem(i, 2) == 1)(lambda: reduction.tick(clock + 4 + lax.div(i, 2)))
+            pl.when(lax.rem(i, 2) == 1)(lambda: reduction.tick(clock + 3 + lax.div(i, 2)))
 
         stream(2 * FF_GROUPS, ff_feeds, ff_body)
 
+        def out_feeds(i, slot):
+            return (feed(2, slot, weight(i, first + OUT_GROUP), wa_buf.at[slot]),)
+
+        begin(out_feeds)
         r_load.wait()
 
         def first_norm(at):
@@ -1000,24 +1023,38 @@
             add_small(l, 5, dr)
 
         row_tiles(rows, first_norm)
+        if l > 0:
+            load(0, saved[l - 1][6], r_buf).start()
         da_copy = exchange(1, da, da_sib)
         da_copy.start()
 
-        def out_feeds(i, slot):
-            return (feed(0, slot, weight(i, first + OUT_GROUP), wa_buf.at[slot]),)
-
         def out_body(i, slot):
             dctx[:, pl.ds(pl.multiple_of(i * 512, 512), 512)] = nt(da[...], block_of(wa_buf.at[slot])).astype(BF16)
 
         stream(2, out_feeds, out_body)
 
+        pairs = width // 128
+
+        def pair_feeds(p, slot):
+            far = lax.rem(p + pairs // 2, pairs)
+            return (
+                feed(5, slot, columns(qkv_ref.at[0], p, 128), pair_buf.at[slot, 0, pl.ds(0, rows)]),
+                feed(6, slot, columns(qkv_ref.at[1], p, 128), pair_buf.at[slot, 1, pl.ds(0, rows)]),
+                feed(7, slot, columns(sib_ref.at[0], far, 128), pair_buf.at[slot, 1, pl.ds(rows, rows)]),
+                feed(8, slot, columns(qkv_ref.at[2], p, 128), pair_buf.at[slot, 2, pl.ds(0, rows)]),
+                feed(9, slot, columns(sib_ref.at[1], far, 128), pair_buf.at[slot, 2, pl.ds(rows, rows)]),
+                feed(10, slot, columns(ctx_ref, p, 128), pair_buf.at[slot, 3, pl.ds(0, rows)]),
+                feed(11, slot, lse_ref.at[p], lse_buf.at[slot]),
+            )
+
+        begin(pair_feeds)
         right_load.wait()
         right_sib_load.wait()
 
         def in_body(n, _):
             give_du(FF_GROUPS + n, n).wait()
-            unit(du[n], du_sib[n], right_buf[...], right_sib_buf[...], base + FF_GROUPS + n)
-            reduction.tick(clock + 8 + n)
+            unit(du[n], du_sib[n], right_buf[...], right_sib_buf[...], lax.rem(n, 2), base + FF_GROUPS + n, n == 0)
+            reduction.tick(clock + 7 + n)
             return 0
 
         lax.fori_loop(0, FF_GROUPS, in_body, 0)
@@ -1033,20 +1070,21 @@
         da_copy.wait()
         left_load.wait()
         left_sib_load.wait()
-        unit(left_buf[0], left_sib_buf[0], da[...], da_sib[...], base + 2 * FF_GROUPS)
-
-        pairs = width // 128
-
-        def pair_feeds(p, slot):
+        unit(left_buf[0], left_sib_buf[0], da[...], da_sib[...], 0, base + 2 * FF_GROUPS)
+        reduction.tick(clock + 11)
+        unit_store(0, base + 2 * FF_GROUPS).wait()
+
+        def dx_feeds(i, slot):
+            return (feed(3, slot, weight(lax.rem(i, 2), first + lax.rem(lax.div(i, 2) + 2, 3)), wa_buf.at[slot]),)
+
+        begin(dx_feeds)
+
+        def give_pair(p):
             far = lax.rem(p + pairs // 2, pairs)
-            return (
-                feed(0, slot, columns(qkv_ref.at[0], p, 128), pair_buf.at[slot, 0, pl.ds(0, rows)]),
-                feed(1, slot, columns(qkv_ref.at[1], p, 128), pair_buf.at[slot, 1, pl.ds(0, rows)]),
-                feed(2, slot, columns(sib_ref.at[0], far, 128), pair_buf.at[slot, 1, pl.ds(rows, rows)]),
-                feed(3, slot, columns(qkv_ref.at[2], p, 128), pair_buf.at[slot, 2, pl.ds(0, rows)]),
-                feed(4, slot, columns(sib_ref.at[1], far, 128), pair_buf.at[slot, 2, pl.ds(rows, rows)]),
-                feed(5, slot, columns(ctx_ref, p, 128), pair_buf.at[slot, 3, pl.ds(0, rows)]),
-                feed(6, slot, lse_ref.at[p], lse_buf.at[slot]),
+            at = pl.ds(pl.multiple_of(far * 128, 128), 128)
+            return pltpu.make_async_remote_copy(
+                src_ref=kv_out.at[:, :, at], dst_ref=kv_far.at[:, :, at], send_sem=pair_send.at[p], recv_sem=pair_recv.at[far],
+                device_id=partner(FLIP_C), device_id_type=MESH,
             )
 
         def pair_body(p, slot):
@@ -1063,12 +1101,16 @@
             there = pl.ds(pl.multiple_of(far * 128, 128), 128)
             kv_out[0, :, there] = dk[rows:].astype(BF16)
             kv_out[1, :, there] = dv[rows:].astype(BF16)
+            give_pair(p).start()
             pl.when(lax.rem(p, 4) < 3)(lambda: reduction.tick(clock + 12 + 3 * lax.div(p, 4) + lax.rem(p, 4)))
 
         stream(pairs, pair_feeds, pair_body)
-        kv_copy = exchange(2, kv_out, kv_far)
-        kv_copy.start()
-        kv_copy.wait()
+
+        def settle_pair(p, _):
+            give_pair(p).wait()
+            return 0
+
+        lax.fori_loop(0, pairs, settle_pair, 0)
         for n in range(2):
             add_rows(dqkv.at[1 + n], kv_far.at[n], rows)
         d_copy = exchange(3, dqkv.at[:, :, pl.ds(512, 512)], d_sib)
@@ -1078,7 +1120,10 @@
         d_copy.wait()
 
         def qkv_body(n, _):
-            unit(dqkv[n, :, 0:512], d_sib[n], right_buf[...], right_sib_buf[...], base + 2 * FF_GROUPS + 1 + n)
+            unit(
+                dqkv[n, :, 0:512], d_sib[n], right_buf[...], right_sib_buf[...],
+                lax.rem(n + 1, 2), base + 2 * FF_GROUPS + 1 + n, n == 0,
+            )
             pl.when(n > 0)(lambda: reduction.tick(clock + 17 + n))
             return 0
 
@@ -1088,9 +1133,6 @@
             acc[at, :] = dr1[at, :]
 
         row_tiles(rows, start_dx)
-
-        def dx_feeds(i, slot):
-            return (feed(0, slot, weight(lax.rem(i, 2), first + lax.div(i, 2)), wa_buf.at[slot]),)
 
         def dx_body(i, slot):
             a, n = lax.rem(i, 2), lax.div(i, 2)
@@ -1106,6 +1148,7 @@
         da[at, :] = acc[at, :].astype(BF16)
 
     row_tiles(rows, narrow)
+    unit_store(1, total - 1).wait()
     swap(0, da, dx_out, True)
 
     def rest(t, _):
@@ -1162,14 +1205,14 @@
             low(rows, width),
             low(2, 4, 2 * rows, 128),
             pltpu.VMEM((2, 2, rows), F32),
-            low(16, 32, width),
+            low(2, 16, 32, width),
             low(SLOTS, 8, 16, width),
             low(SLOTS, 4, 16, width),
             low(SLOTS, 2, 16, width),
             low(SLOTS, 1, 16, width),
             low(SLOTS, 8, 16, width),
             low(2, 8, 16, width),
-            dma(8, 2),
+            dma(12, 2),
             dma(5),
             dma(1),
             dma(2),
@@ -1177,6 +1220,8 @@
             dma(6),
             dma(FF_GROUPS),
             dma(FF_GROUPS),
+            dma(width // 128),
+            dma(width // 128),
             dma(7, SLOTS),
             dma(7, SLOTS),
             dma(2 * total),

time: 650 us -> 620 us (0.954)
  Pallas kernels: 612 us -> 582 us
    pallas_call x1, Pallas kernels: 388 us -> 364 us  [backward(): pl.pallas_call(functools.partial(backward_kernel, layers), out_shape=(jax...]
    pallas_call x1, Pallas kernels: 187 us -> 180 us  [forward(): pl.pallas_call(functools.partial(forward_kernel, layers), out_shape=(low_...]
where the time goes in v6:
time: 620 us; the launch traced here: 615 us
  Pallas kernels  582 us (94%)
  local copies, waits for them, and re-layouts  15.9 us (3%)
  starting transfers between devices  10.2 us (2%)
    pallas_call x1, Pallas kernels, backward(): pl.pallas_call(functools.partial(backward_kernel, layers), out_shape=(jax...  364 us
    pallas_call x1, Pallas kernels, forward(): pl.pallas_call(functools.partial(forward_kernel, layers), out_shape=(low_...  180 us
    pallas_call x4, Pallas kernels, place(): pl.pallas_call(functools.partial(place_kernel, turned), out_shape=jax.Sha...  33.9 us
  transfers between devices with their start and end apart: 9, of which 1 were waited for; matrix products, arithmetic and copies ran while one was open for 2% of the time, Pallas kernels for 6%

profile of v6, /device:TPU:0, one launch (start us, length us, event | category | flops | bytes accessed | tf_op | source)
XLA Modules:
  0.0 615.1 jit_solution(1175893542800168244)
XLA Ops:
  0.6 0.8 copy.41
  1.5 0.2 reshape_squeeze.11
  1.7 2.5 collective-permute-start.2
  4.1 0.6 collective-permute-start
  4.8 0.7 pad_add_fusion
  5.5 0.8 reshape.264
  6.4 0.1 rev.94
  6.5 0.1 reshape.265
  6.6 0.8 reshape.266
  7.5 0.2 rev.98
  7.7 0.1 reshape.267
  7.8 1.8 collective-permute-start.3
  9.7 0.8 fusion.15
  10.5 0.8 slice_bitcast_fusion.4
  11.3 0.1 stack.28
  11.5 0.6 pad_maximum_fusion.1.refs_11_.refs_6_
  12.1 0.1 fusion.8
  12.2 0.1 reshape_reshape.22
  12.3 0.1 reshape_reshape.24
  12.4 0.1 copy.42
  12.5 0.1 pad.21.clone
  12.6 0.7 add_select_fusion
  13.4 0.1 rev.87
  13.5 0.2 reshape_reshape.21
  13.8 0.2 copy.43
  14.0 0.1 constant_dynamic-slice_fusion
  14.1 0.1 compare_reduce_fusion
  14.2 0.1 copy.45
  14.3 0.1 fusion.2
  14.5 0.2 fusion.1
  14.7 0.8 pad_maximum_fusion.refs_6_.refs_3_
  15.5 0.7 pad.8.refs_7_.refs_4_
  16.2 1.0 pad.9.refs_8_.refs_5_
  17.3 0.6 copy.56
  18.0 0.7 pad_maximum_fusion.4.refs_9_
  18.7 179.9 %forward.1 = (bf16[2,24,2,256,1024]{4,3,2,1,0:T(8,128)(2,1)}, bf16[512,1024]{1,0:T(8,128)(2,1)}, bf16[512,1024]{1,0:T(8,128)(2,1)}, bf16[3,512,1024]{2,1,0:T(8,1...) custom-call(f32[512,1,1024]{2,1,0:T(1,128)} %refs_0_.1, ...), custom_call_target="tpu_custom_call" | custom-call | flops 32212254720 | bytes 314572800 | tf_op jit(solution)/shard_map/forward/pallas_call | solution.py:801
  198.6 364.1 %backward.1 = (bf16[24,16,32,1024]{3,2,1,0:T(8,128)(2,1)}, bf16[24,16,32,1024]{3,2,1,0:T(8,128)(2,1)}, bf16[512,1024]{1,0:T(8,128)(2,1)}, bf16[512,1024]{1,0:T(8...) custom-call(bf16[512,1024]{1,0:T(8,128)(2,1)} %get-tuple-element.71.refs_0_, ...), custom_call_target="tpu_custom_call" | custom-call | flops 64424509440 | bytes 314572800 | tf_op jit(solution)/shard_map/backward/pallas_call | solution.py:1171
  562.7 0.7 fusion.13
  563.4 0.8 copy.48
  564.2 0.1 reshape.269
  564.5 1.1 fusion.12
  565.7 0.2 rev.103
  565.9 0.1 reshape_reshape.26
  566.0 0.2 reshape.270
  566.4 0.3 rev.108
  566.7 0.1 select_bitcast_fusion
  566.8 0.2 reshape_reshape.27
  567.0 0.4 collective-permute-start.4
  567.4 0.9 collective-permute-done.4
  568.4 1.0 collective-permute-start.5
  569.4 10.3 %place.4 = f32[2,2048,1024]{2,1,0:T(8,128)} custom-call(s32[1]{0:T(128)} %bitcast.19.code_ref, bf16[24,512,1024]{2,1,0:T(8,128)(2,1)} %bitcast.59), custom_call_target="tpu_custom_call" | custom-call | bytes 25165824 | tf_op jit(solution)/shard_map/place/pallas_call | solution.py:71
  579.7 1.0 collective-permute-start.6
  580.8 11.3 %place.5 = f32[2,1024,2048]{2,1,0:T(8,128)} custom-call(s32[1]{0:T(128)} %bitcast.19.code_ref, bf16[24,512,1024]{2,1,0:T(8,128)(2,1)} %bitcast.60), custom_call_target="tpu_custom_call" | custom-call | bytes 25165824 | tf_op jit(solution)/shard_map/place/pallas_call | solution.py:71
  592.1 0.8 collective-permute-start.7
  592.9 8.9 %place.6 = f32[2,3,1024,512]{3,2,1,0:T(8,128)} custom-call(s32[1]{0:T(128)} %bitcast.19.code_ref, bf16[24,512,1024]{2,1,0:T(8,128)(2,1)} %bitcast.61), custom_call_target="tpu_custom_call" | custom-call | bytes 18874368 | tf_op jit(solution)/shard_map/place/pallas_call | solution.py:71
  601.8 2.0 collective-permute-start.8
  603.9 3.7 widen_rows.1
  607.6 3.4 place.7
  611.0 0.6 slice.217
  611.6 0.6 slice.214
  612.2 0.6 slice.221
  612.9 0.6 reshape.276
  613.5 0.6 slice.219
  614.2 0.6 reshape.274
  (80 shorter events, 1.3 us)
Async XLA Ops:
  1.7 10.9 %collective-permute-start.2 = (s32[384]{0:T(512)S(1)}, s32[384]{0:T(512)S(1)}, u32[]{:S(2)}, u32[]{:S(2)}) collective-permute-start(s32[384]{0:T(512)S(1)} %reshape_squeeze.11), channel_id=1, source_target_pairs={{0,3},{1,2},{2,1},{3,0},{4,7},{5,6},{6,5},{7,4},{8,11},{9,10},{10,... | collective-permute-start | bytes 4616 | tf_op jit(solution)/shard_map/ppermute | solution.py:36
  4.1 8.5 %collective-permute-start = (s32[384]{0:T(512)S(1)}, s32[384]{0:T(512)S(1)}, u32[]{:S(2)}, u32[]{:S(2)}) collective-permute-start(s32[384]{0:T(512)S(1)} %reshape_squeeze.11), channel_id=1, source_target_pairs={{0,1},{1,0},{2,3},{3,2},{4,5},{5,4},{6,7},{7,6},{8,9},{9,8},{10,11... | collective-permute-start | bytes 4616 | tf_op jit(solution)/shard_map/ppermute | solution.py:36
  5.5 7.1 %collective-permute-start.1 = (s32[1408]{0:T(1024)S(1)}, s32[1408]{0:T(1024)S(1)}, u32[]{:S(2)}, u32[]{:S(2)}) collective-permute-start(s32[1408]{0:T(1024)S(1)} %pad_add_fusion), channel_id=1, source_target_pairs={{0,2},{1,3},{2,0},{3,1},{4,6},{5,7},{6,4},{7,5},{8,10},{9,11},{10,... | collective-permute-start | bytes 16904 | tf_op jit(solution)/shard_map/ppermute | solution.py:36
  7.8 9.3 %collective-permute-start.3 = (f32[6144]{0:T(1024)S(1)}, f32[6144]{0:T(1024)S(1)}, u32[]{:S(2)}, u32[]{:S(2)}) collective-permute-start(f32[6144]{0:T(1024)S(1)} %pad_maximum_fusion.3), channel_id=1, source_target_pairs={{0,1},{1,0},{2,3},{3,2},{4,5},{5,4},{6,7},{7,6},{8,9},{9,8},{10,11... | collective-permute-start | bytes 73736 | tf_op jit(solution)/shard_map/ppermute | solution.py:36
  567.0 1.4 collective-permute-start.4
  568.4 11.3 %collective-permute-start.5 = (f32[24576]{0:T(1024)S(1)}, f32[24576]{0:T(1024)S(1)}, u32[]{:S(2)}, u32[]{:S(2)}) collective-permute-start(f32[24576]{0:T(1024)S(1)} %add.75), channel_id=1, source_target_pairs={{0,1},{1,0},{2,3},{3,2},{4,5},{5,4},{6,7},{7,6},{8,9},{9,8},{10,11... | collective-permute-start | bytes 294920 | tf_op jit(solution)/shard_map/ppermute | solution.py:36
  579.7 12.4 %collective-permute-start.6 = (f32[24576]{0:T(1024)S(1)}, f32[24576]{0:T(1024)S(1)}, u32[]{:S(2)}, u32[]{:S(2)}) collective-permute-start(f32[24576]{0:T(1024)S(1)} %add.76), channel_id=1, source_target_pairs={{0,4},{1,5},{2,6},{3,7},{4,0},{5,1},{6,2},{7,3},{8,12},{9,13},{10,... | collective-permute-start | bytes 294920 | tf_op jit(solution)/shard_map/ppermute | solution.py:36
  592.1 9.7 %collective-permute-start.7 = (f32[24576]{0:T(1024)S(1)}, f32[24576]{0:T(1024)S(1)}, u32[]{:S(2)}, u32[]{:S(2)}) collective-permute-start(f32[24576]{0:T(1024)S(1)} %add.77), channel_id=1, source_target_pairs={{0,8},{1,9},{2,10},{3,11},{4,12},{5,13},{6,14},{7,15},{8,0},{9,1},... | collective-permute-start | bytes 294920 | tf_op jit(solution)/shard_map/ppermute | solution.py:36
  601.8 9.1 %collective-permute-start.8 = (f32[24576]{0:T(1024)S(1)}, f32[24576]{0:T(1024)S(1)}, u32[]{:S(2)}, u32[]{:S(2)}) collective-permute-start(f32[24576]{0:T(1024)S(1)} %add.78), channel_id=1, source_target_pairs={{0,16},{1,17},{2,18},{3,19},{4,20},{5,21},{6,22},{7,23},{8,24},{9,... | collective-permute-start | bytes 294920 | tf_op jit(solution)/shard_map/ppermute | solution.py:36

commit v7 on v6

--- a/solution.py
+++ b/solution.py
@@ -142,7 +142,7 @@
     lax.fori_loop(0, rows // 32, step, 0)
 
 
-SLOTS = 12
+SLOTS = 6
 LAST_TICK = 8
 
 
@@ -153,22 +153,18 @@
         self.send_sem, self.recv_sem, self.core_send, self.core_recv = sems[:4]
         self.keep_sem, self.out_sem, self.in_free, self.out_free = sems[4:]
 
-    def blocks(self, ref, i, first):
-        part = pl.ds(pl.multiple_of(lax.rem(i, 2) * 16, 16), 16)
-        return ref.at[lax.div(i, 2), pl.ds(first, 8), part]
-
     def copy(self, step, i):
         slot = lax.rem(i, SLOTS)
         ys, al = self.y_buf.at[slot], self.all_buf.at[slot]
         bit, source, target = (
-            (FLIP_Y, self.blocks(self.grads, i, 8), ys),
-            (FLIP_X, ys.at[pl.ds(4, 4)], self.x_buf.at[slot]),
-            (FLIP_Z0, ys.at[pl.ds(2, 2)], self.z0_buf.at[slot]),
-            (FLIP_Z1, ys.at[pl.ds(1, 1)], self.z1_buf.at[slot]),
-            (FLIP_Z1, al.at[pl.ds(0, 1)], al.at[pl.ds(1, 1)]),
-            (FLIP_Z0, al.at[pl.ds(0, 2)], al.at[pl.ds(2, 2)]),
-            (FLIP_X, al.at[pl.ds(0, 4)], al.at[pl.ds(4, 4)]),
-            (FLIP_C, al, self.blocks(self.sums, i, 8)),
+            (FLIP_Y, self.grads.at[i, pl.ds(256, 256)], ys),
+            (FLIP_X, ys.at[pl.ds(128, 128)], self.x_buf.at[slot]),
+            (FLIP_Z0, ys.at[pl.ds(64, 64)], self.z0_buf.at[slot]),
+            (FLIP_Z1, ys.at[pl.ds(32, 32)], self.z1_buf.at[slot]),
+            (FLIP_Z1, al.at[pl.ds(0, 32)], al.at[pl.ds(32, 32)]),
+            (FLIP_Z0, al.at[pl.ds(0, 64)], al.at[pl.ds(64, 64)]),
+            (FLIP_X, al.at[pl.ds(0, 128)], al.at[pl.ds(128, 128)]),
+            (FLIP_C, al, self.sums.at[i, pl.ds(256, 256)]),
         )[step]
         return pltpu.make_async_remote_copy(
             src_ref=source,
@@ -182,13 +178,13 @@
     def keep(self, i):
         slot = lax.rem(i, 2)
         return pltpu.make_async_copy(
-            self.blocks(self.grads, i, 0), self.keep_buf.at[slot], self.keep_sem.at[slot]
+            self.grads.at[i, pl.ds(0, 256)], self.keep_buf.at[slot], self.keep_sem.at[slot]
         )
 
     def out(self, i):
         slot = lax.rem(i, SLOTS)
         return pltpu.make_async_copy(
-            self.all_buf.at[slot], self.blocks(self.sums, i, 0), self.out_sem.at[slot]
+            self.all_buf.at[slot], self.sums.at[i, pl.ds(0, 256)], self.out_sem.at[slot]
         )
 
     def take(self, sem, i):
@@ -234,8 +230,8 @@
 
         def back_z1(i, slot):
             self.copy(3, i).wait()
-            add_into(self.y_buf.at[slot], self.z1_buf.at[slot], 1)
-            self.all_buf[slot, 0] = self.y_buf[slot, 0]
+            add_rows(self.y_buf.at[slot], self.z1_buf.at[slot], 32)
+            self.all_buf[slot, 0:32, :] = self.y_buf[slot, 0:32, :]
             for n, bit in enumerate((FLIP_Y, FLIP_X, FLIP_Z0, FLIP_Z1)):
                 self.give(self.in_free.at[n], bit, i)
             self.take(self.out_free.at[2], i)
@@ -243,20 +239,20 @@
 
         def on_z1(i, slot):
             self.copy(2, i).wait()
-            add_into(self.y_buf.at[slot], self.z0_buf.at[slot], 2)
+            add_rows(self.y_buf.at[slot], self.z0_buf.at[slot], 64)
             self.take(self.in_free.at[3], i)
             self.copy(3, i).start()
 
         def on_z0(i, slot):
             self.copy(1, i).wait()
-            add_into(self.y_buf.at[slot], self.x_buf.at[slot], 4)
+            add_rows(self.y_buf.at[slot], self.x_buf.at[slot], 128)
             self.take(self.in_free.at[2], i)
             self.copy(2, i).start()
 
         def on_x(i, slot):
             self.copy(0, i).wait()
             self.keep(i).wait()
-            add_into(self.y_buf.at[slot], self.keep_buf.at[lax.rem(i, 2)], 8)
+            add_rows(self.y_buf.at[slot], self.keep_buf.at[lax.rem(i, 2)], 256)
             self.take(self.in_free.at[1], i)
             self.copy(1, i).start()
 
@@ -341,28 +337,23 @@
     return (part + document_part).astype(BF16)
 
 
+def both_heads(values):
+    return jnp.concatenate([pair_lanes(values, 0), pair_lanes(values, 1)], axis=0)
+
+
 def attend_pair(query, keys, values, hot, mask):
     scale = HEAD_DIM**-0.5
     rows = query.shape[0]
     query = query * jnp.asarray(scale, BF16)
-    values_t = values.T
-    tile = rows // 2
-    contexts, lses = [], ([], [])
-    for part in range(2):
-        at = slice(part * tile, (part + 1) * tile)
-        heads = []
-        for e in range(2):
-            right = jnp.concatenate([pair_lanes(query[at], e), hot[at]], axis=1)
-            left = jnp.concatenate([keys, mask[e]], axis=1)
-            s = nt(left, right)
-            top = jnp.max(s, axis=0, keepdims=True)
-            p = jnp.exp(s - top)
-            total = jnp.sum(p, axis=0, keepdims=True)
-            c = nn(values_t[e * HEAD_DIM : (e + 1) * HEAD_DIM, :], p.astype(BF16))
-            heads.append(c * (1.0 / total))
-            lses[e].append(top + jnp.log(total))
-        contexts.append(jnp.concatenate(heads, axis=0).T)
-    return jnp.concatenate(contexts, axis=0), [jnp.concatenate(parts, axis=1) for parts in lses]
+    right = jnp.concatenate([both_heads(query), both_heads(hot)], axis=1)
+    s = nt(jnp.concatenate([keys, mask], axis=1), right)
+    top = jnp.max(s, axis=0, keepdims=True)
+    p = jnp.exp(s - top)
+    total = jnp.sum(p, axis=0, keepdims=True)
+    c = nn(values.T, p.astype(BF16)) * (1.0 / total)
+    context = jnp.concatenate([c[:HEAD_DIM, :rows], c[HEAD_DIM:, rows:]], axis=0).T
+    lse = top + jnp.log(total)
+    return context, [lse[:, :rows], lse[:, rows:]]
 
 
 def attend_back_pair(query, keys, values, hot, mask, ctx, lse, dctx):
@@ -371,6 +362,7 @@
     query = query * jnp.asarray(scale, BF16)
     keys_t = keys.T
     delta_t = (dctx.astype(F32) * ctx.astype(F32)).T
+    left = jnp.concatenate([keys, mask], axis=1)
     tile = rows // 2
     dk, dv, dq = 0.0, 0.0, []
     for part in range(2):
@@ -380,8 +372,7 @@
             lanes = slice(e * HEAD_DIM, (e + 1) * HEAD_DIM)
             query_e = pair_lanes(query[at], e)
             dctx_e = pair_lanes(dctx[at], e)
-            right = jnp.concatenate([query_e, hot[at]], axis=1)
-            left = jnp.concatenate([keys, mask[e]], axis=1)
+            right = jnp.concatenate([query_e, pair_lanes(hot[at], e)], axis=1)
             p = jnp.exp(nt(left, right) - lse[e : e + 1, at])
             dp = nt(values, dctx_e)
             delta = jnp.sum(delta_t[lanes, at], axis=0, keepdims=True)
@@ -515,9 +506,8 @@
         if turned:
 
             def turn(i, _):
-                turn_buf[pl.ds(pl.multiple_of(i * 128, 128), 128), :] = col_buf[
-                    slot, :, pl.ds(pl.multiple_of(i * 128, 128), 128)
-                ].T
+                strip = col_buf[slot, :, pl.ds(pl.multiple_of(i * 128, 128), 128)]
+                turn_buf[pl.ds(pl.multiple_of(i * 128, 128), 128), :] = strip.astype(BF16).T
                 return 0
 
             lax.fori_loop(0, 4, turn, 0)
@@ -643,7 +633,7 @@
             far = lax.rem(p + pairs // 2, pairs)
             here = pl.ds(pl.multiple_of(p * 128, 128), 128)
             there = pl.ds(pl.multiple_of(far * 128, 128), 128)
-            mask = [spread_mask(mask_ref[2 * p + e], key_ref[...]) for e in range(2)]
+            mask = spread_mask(mask_ref[p], key_ref[...])
             keys = jnp.concatenate([qkv[1, :, here], kv_sib[0, :, there]], axis=0)
             values = jnp.concatenate([qkv[2, :, here], kv_sib[1, :, there]], axis=0)
             context, parts = attend_pair(qkv[0, :, here], keys, values, hot_buf[...], mask)
@@ -818,7 +808,7 @@
             low(2 * FF_GROUPS, rows, 512),
             full(DEPTH, width, 512),
             full(DEPTH, 512, width),
-            full(512, width),
+            low(512, width),
             low(2, 512, width),
             low(2, 2, 256, width),
             low(2, 2, 256, width),
@@ -863,7 +853,7 @@
     rows, width = acc.shape
     total = layers * GROUPS
     reduction = Reduction(
-        grads, sums, 2 * total,
+        grads, sums, total,
         (y_buf, x_buf, z0_buf, z1_buf, all_buf, keep_buf),
         (send_sem, recv_sem, sum_send, sum_recv, keep_sem, out_sem, in_free, out_free),
     )
@@ -898,7 +888,7 @@
 
     def unit(left, left_sib, right, right_sib, slot, index, fresh=False):
         made = (tn(left, right) + tn(left_sib, right_sib)).astype(BF16)
-        unit_buf[slot] = made.reshape(unit_buf.shape[1:])
+        unit_buf[slot] = made
         if fresh is not False:
             pl.when(jnp.logical_not(fresh))(lambda: unit_store(slot, index).wait())
         else:
@@ -941,7 +931,7 @@
         qkv_ref, sib_ref, ctx_ref, ctx_sib_ref, lse_ref, r1_ref, r2_ref, hl_ref, hl_sib_ref, g_ref, g_sib_ref, slope_ref, xb_ref, xb_sib_ref = saved[l]
         first = l * GROUPS
         base = (layers - 1 - l) * GROUPS
-        clock = 22 * (layers - 1 - l)
+        clock = 11 * (layers - 1 - l)
 
         def down_feeds(i, slot):
             return (
@@ -975,7 +965,7 @@
         def down_body(i, slot):
             fresh = (i == 0) if l == layers - 1 else False
             unit(left_buf[slot], left_sib_buf[slot], dm[...], dm_sib[...], lax.rem(i, 2), base + i, fresh)
-            pl.when(i > 0)(lambda: reduction.tick(clock + i - 1))
+            pl.when(lax.rem(i, 2) == 1)(lambda: reduction.tick(clock + lax.div(i, 2)))
 
         def place_of(i):
             a = 1 - lax.div(i, FF_GROUPS)
@@ -1003,7 +993,7 @@
             pl.when(a == 1)(lambda: give_du(j, n).start())
             dbi_ref[l, a, n] = jnp.sum(d.astype(F32), axis=0, keepdims=True)
             acc[...] += nn(d, block_of(wb_buf.at[slot]))
-            pl.when(lax.rem(i, 2) == 1)(lambda: reduction.tick(clock + 3 + lax.div(i, 2)))
+            pl.when(lax.rem(i, 4) == 3)(lambda: reduction.tick(clock + 2 + lax.div(i, 4)))
 
         stream(2 * FF_GROUPS, ff_feeds, ff_body)
 
@@ -1054,7 +1044,7 @@
         def in_body(n, _):
             give_du(FF_GROUPS + n, n).wait()
             unit(du[n], du_sib[n], right_buf[...], right_sib_buf[...], lax.rem(n, 2), base + FF_GROUPS + n, n == 0)
-            reduction.tick(clock + 7 + n)
+            pl.when(lax.rem(n, 2) == 1)(lambda: reduction.tick(clock + 4 + lax.div(n, 2)))
             return 0
 
         lax.fori_loop(0, FF_GROUPS, in_body, 0)
@@ -1071,7 +1061,6 @@
         left_load.wait()
         left_sib_load.wait()
         unit(left_buf[0], left_sib_buf[0], da[...], da_sib[...], 0, base + 2 * FF_GROUPS)
-        reduction.tick(clock + 11)
         unit_store(0, base + 2 * FF_GROUPS).wait()
 
         def dx_feeds(i, slot):
@@ -1090,7 +1079,7 @@
         def pair_body(p, slot):
             far = lax.rem(p + pairs // 2, pairs)
             here = pl.ds(pl.multiple_of(p * 128, 128), 128)
-            mask = [spread_mask(mask_ref[2 * p + e], key_ref[...]) for e in range(2)]
+            mask = spread_mask(mask_ref[p], key_ref[...])
             dq, dk, dv = attend_back_pair(
                 pair_buf[slot, 0, 0:rows], pair_buf[slot, 1], pair_buf[slot, 2], hot_buf[...], mask,
                 pair_buf[slot, 3, 0:rows], lse_buf[slot], dctx[:, here],
@@ -1102,7 +1091,7 @@
             kv_out[0, :, there] = dk[rows:].astype(BF16)
             kv_out[1, :, there] = dv[rows:].astype(BF16)
             give_pair(p).start()
-            pl.when(lax.rem(p, 4) < 3)(lambda: reduction.tick(clock + 12 + 3 * lax.div(p, 4) + lax.rem(p, 4)))
+            pl.when(lax.rem(p, 3) == 1)(lambda: reduction.tick(clock + 6 + lax.div(p, 3)))
 
         stream(pairs, pair_feeds, pair_body)
 
@@ -1124,7 +1113,7 @@
                 dqkv[n, :, 0:512], d_sib[n], right_buf[...], right_sib_buf[...],
                 lax.rem(n + 1, 2), base + 2 * FF_GROUPS + 1 + n, n == 0,
             )
-            pl.when(n > 0)(lambda: reduction.tick(clock + 17 + n))
+            pl.when(n == 1)(lambda: reduction.tick(clock + 9))
             return 0
 
         lax.fori_loop(0, 3, qkv_body, 0)
@@ -1139,10 +1128,10 @@
             d = dqkv[n, :, pl.ds(pl.multiple_of(a * 512, 512), 512)]
             qkv_sums_ref[l, n, a] = jnp.sum(d.astype(F32), axis=0, keepdims=True)
             acc[...] += nn(d, block_of(wa_buf.at[slot]))
-            pl.when(lax.rem(i, 3) == 2)(lambda: reduction.tick(clock + 20 + lax.div(i, 3)))
+            pl.when(i == 3)(lambda: reduction.tick(clock + 10))
 
         stream(6, dx_feeds, dx_body)
-        done = clock + 22
+        done = clock + 11
 
     def narrow(at):
         da[at, :] = acc[at, :].astype(BF16)
@@ -1155,7 +1144,7 @@
         reduction.tick(t)
         return 0
 
-    lax.fori_loop(done, 2 * total + LAST_TICK, rest, 0)
+    lax.fori_loop(done, total + LAST_TICK, rest, 0)
     swap(0, da, dx_out, False)
     swap(1, x_ref, x_out, False)
 
@@ -1171,8 +1160,8 @@
     return pl.pallas_call(
         functools.partial(backward_kernel, layers),
         out_shape=(
-            jax.ShapeDtypeStruct((total, 16, 32, width), BF16),
-            jax.ShapeDtypeStruct((total, 16, 32, width), BF16),
+            jax.ShapeDtypeStruct((total, 512, width), BF16),
+            jax.ShapeDtypeStruct((total, 512, width), BF16),
             jax.ShapeDtypeStruct((rows, width), BF16),
             jax.ShapeDtypeStruct((rows, width), BF16),
             jax.ShapeDtypeStruct((layers, 2, FF_GROUPS, 1, 512), F32),
@@ -1205,13 +1194,13 @@
             low(rows, width),
             low(2, 4, 2 * rows, 128),
             pltpu.VMEM((2, 2, rows), F32),
-            low(2, 16, 32, width),
-            low(SLOTS, 8, 16, width),
-            low(SLOTS, 4, 16, width),
-            low(SLOTS, 2, 16, width),
-            low(SLOTS, 1, 16, width),
-            low(SLOTS, 8, 16, width),
-            low(2, 8, 16, width),
+            low(2, 512, width),
+            low(SLOTS, 256, width),
+            low(SLOTS, 128, width),
+            low(SLOTS, 64, width),
+            low(SLOTS, 32, width),
+            low(SLOTS, 256, width),
+            low(2, 256, width),
             dma(12, 2),
             dma(5),
             dma(1),
@@ -1224,8 +1213,8 @@
             dma(width // 128),
             dma(7, SLOTS),
             dma(7, SLOTS),
-            dma(2 * total),
-            dma(2 * total),
+            dma(total),
+            dma(total),
             dma(2),
             dma(SLOTS),
             pltpu.SemaphoreType.REGULAR((4,)),
@@ -1287,14 +1276,16 @@
     chosen = lax.dynamic_slice_in_dim(chosen, core * own_blocks, own_blocks, axis=1)
     allowed = allowed[None] | jnp.any(chosen[:, :, None, :] == key_block[None, None, :, None], axis=3)
     block_rows = rows // own_blocks
-    documents = jnp.arange(128 - own_blocks)
+    documents = jnp.arange(HEAD_DIM - own_blocks)
     mask = jnp.pad(
-        jnp.where(allowed, 0.0, BIG).astype(F32).transpose(0, 2, 1), ((0, 0), (0, 0), (0, 128 - own_blocks))
+        jnp.where(allowed, 0.0, BIG).astype(F32).transpose(0, 2, 1), ((0, 0), (0, 0), (0, HEAD_DIM - own_blocks))
     )
+    mask = mask.reshape(heads // 2, 2, blocks, HEAD_DIM).transpose(0, 2, 1, 3).reshape(heads // 2, blocks, 2 * HEAD_DIM)
     document_part = jnp.where(
         (segments[:, None] == documents[None, :]) | (documents[None, :] > 7), 0.0, BIG
     ).astype(F32)
     mask_rows = jnp.pad(document_part, ((0, 0), (own_blocks, 0)))
+    mask_rows = jnp.concatenate([mask_rows, mask_rows], axis=1)
     block_rows = rows // own_blocks
     hot = jnp.concatenate(
         [
@@ -1303,6 +1294,7 @@
         ],
         axis=1,
     )
+    hot = jnp.concatenate([hot, hot], axis=1)
 
     bias_pack = jnp.concatenate(
         [
@@ -1338,7 +1330,6 @@
     _, grads, dx_low, x_low, d_b_in, qkv_sums, rows_small = backward(
         upstream_low, stream_low, weights, hot, mask, mask_rows, vectors, saved
     )
-    grads = grads.reshape(layers * GROUPS, 512, width)
     block_output, input_grad = widen_rows(x_low, dx_low)
 
     stacks = [

time: 620 us -> 594 us (0.958)
  Pallas kernels: 582 us -> 554 us
    pallas_call x1, Pallas kernels: 364 us -> 350 us  [backward(): pl.pallas_call(functools.partial(backward_kernel, layers), out_shape=(jax...]
    pallas_call x1, Pallas kernels: 180 us -> 166 us  [forward(): pl.pallas_call(functools.partial(forward_kernel, layers), out_shape=(low_...]
where the time goes in v7:
time: 594 us; the launch traced here: 589 us
  Pallas kernels  554 us (93%)
  local copies, waits for them, and re-layouts  15 us (3%)
  starting transfers between devices  11.7 us (2%)
  other arithmetic  5.98 us (1%)
    pallas_call x1, Pallas kernels, backward(): pl.pallas_call(functools.partial(backward_kernel, layers), out_shape=(jax...  350 us
    pallas_call x1, Pallas kernels, forward(): pl.pallas_call(functools.partial(forward_kernel, layers), out_shape=(low_...  166 us
    pallas_call x4, Pallas kernels, place(): pl.pallas_call(functools.partial(place_kernel, turned), out_shape=jax.Sha...  33.9 us
  transfers between devices with their start and end apart: 9, of which 1 were waited for; matrix products, arithmetic and copies ran while one was open for 2% of the time, Pallas kernels for 6%

profile of v7, /device:TPU:0, one launch (start us, length us, event | category | flops | bytes accessed | tf_op | source)
XLA Modules:
  0.0 588.6 jit_solution(11886716705636789094)
XLA Ops:
  0.6 0.8 copy.34
  1.5 0.2 reshape_squeeze.11
  1.7 2.5 collective-permute-start.2
  4.1 0.6 collective-permute-start
  4.8 0.7 pad_add_fusion
  5.5 0.8 reshape.271
  6.4 0.1 rev.94
  6.5 0.1 reshape.272
  6.6 0.8 reshape.273
  7.5 0.2 rev.98
  7.7 0.1 reshape.274
  7.8 1.8 collective-permute-start.3
  9.7 0.8 fusion.15
  10.5 0.8 slice_bitcast_fusion.4
  11.3 0.1 stack.28
  11.4 0.1 stack.30
  11.5 0.6 pad_maximum_fusion.2.refs_11_.refs_6_
  12.1 0.1 fusion.8
  12.2 0.1 reshape_reshape.22
  12.3 0.1 reshape_reshape.24
  12.4 0.1 pad.21.clone
  12.6 0.7 add_select_fusion
  13.3 0.1 rev.87
  13.5 0.2 reshape_reshape.21
  13.7 0.2 copy.35
  13.9 0.1 constant_dynamic-slice_fusion
  14.0 0.1 compare_reduce_fusion
  14.1 0.1 fusion.2
  14.3 0.2 fusion.1
  14.5 0.2 pad.9
  14.7 1.0 pad_maximum_fusion.refs_8_.refs_5_
  15.7 0.8 pad_maximum_fusion.1.refs_6_.refs_3_
  16.6 0.8 copy.44.refs_7_.refs_4_
  17.5 0.6 copy.51
  18.2 0.7 pad_maximum_fusion.5.refs_9_
  18.9 166.0 %forward.1 = (bf16[2,24,2,256,1024]{4,3,2,1,0:T(8,128)(2,1)}, bf16[512,1024]{1,0:T(8,128)(2,1)}, bf16[512,1024]{1,0:T(8,128)(2,1)}, bf16[3,512,1024]{2,1,0:T(8,1...) custom-call(f32[512,1,1024]{2,1,0:T(1,128)} %refs_0_.1, ...), custom_call_target="tpu_custom_call" | custom-call | flops 32212254720 | bytes 314572800 | tf_op jit(solution)/shard_map/forward/pallas_call | solution.py:791
  185.0 349.9 %backward.1 = (bf16[24,512,1024]{2,1,0:T(8,128)(2,1)}, bf16[24,512,1024]{2,1,0:T(8,128)(2,1)}, bf16[512,1024]{1,0:T(8,128)(2,1)}, bf16[512,1024]{1,0:T(8,128)(2,...) custom-call(bf16[512,1024]{1,0:T(8,128)(2,1)} %get-tuple-element.71.refs_0_, ...), custom_call_target="tpu_custom_call" | custom-call | flops 64424509440 | bytes 314572800 | tf_op jit(solution)/shard_map/backward/pallas_call | solution.py:1160
  534.8 0.7 fusion.13
  535.6 0.8 copy.41
  536.4 0.1 reshape.276
  536.6 1.1 fusion.12
  537.9 0.2 rev.103
  538.1 0.1 reshape_reshape.26
  538.2 0.2 reshape.277
  538.6 0.3 rev.108
  538.9 0.1 select_bitcast_fusion
  539.0 0.2 reshape_reshape.27
  539.2 0.4 collective-permute-start.4
  539.6 0.9 collective-permute-done.4
  540.6 4.1 collective-permute-start.5
  544.6 10.3 %place.4 = f32[2,2048,1024]{2,1,0:T(8,128)} custom-call(s32[1]{0:T(128)} %bitcast.23.code_ref, bf16[24,512,1024]{2,1,0:T(8,128)(2,1)} %get-tuple-element.123.g_ref), custom_call_target="tpu_custom_call" | custom-call | bytes 25165824 | tf_op jit(solution)/shard_map/place/pallas_call | solution.py:71
  555.0 0.6 collective-permute-start.6
  555.6 11.3 %place.5 = f32[2,1024,2048]{2,1,0:T(8,128)} custom-call(s32[1]{0:T(128)} %bitcast.23.code_ref, bf16[24,512,1024]{2,1,0:T(8,128)(2,1)} %get-tuple-element.123.g_ref), custom_call_target="tpu_custom_call" | custom-call | bytes 25165824 | tf_op jit(solution)/shard_map/place/pallas_call | solution.py:71
  567.0 0.9 collective-permute-start.7
  567.8 8.9 %place.6 = f32[2,3,1024,512]{3,2,1,0:T(8,128)} custom-call(s32[1]{0:T(128)} %bitcast.23.code_ref, bf16[24,512,1024]{2,1,0:T(8,128)(2,1)} %get-tuple-element.123.g_ref), custom_call_target="tpu_custom_call" | custom-call | bytes 18874368 | tf_op jit(solution)/shard_map/place/pallas_call | solution.py:71
  576.7 0.7 collective-permute-start.8
  577.5 3.7 widen_rows.1
  581.2 3.4 place.7
  584.6 0.6 slice.217
  585.2 0.6 slice.214
  585.8 0.6 slice.221
  586.5 0.6 reshape.282
  587.1 0.6 slice.219
  587.8 0.6 reshape.280
  (80 shorter events, 1.2 us)
Async XLA Ops:
  1.7 10.9 %collective-permute-start.2 = (s32[384]{0:T(512)S(1)}, s32[384]{0:T(512)S(1)}, u32[]{:S(2)}, u32[]{:S(2)}) collective-permute-start(s32[384]{0:T(512)S(1)} %reshape_squeeze.11), channel_id=1, source_target_pairs={{0,3},{1,2},{2,1},{3,0},{4,7},{5,6},{6,5},{7,4},{8,11},{9,10},{10,... | collective-permute-start | bytes 4616 | tf_op jit(solution)/shard_map/ppermute | solution.py:36
  4.1 8.4 %collective-permute-start = (s32[384]{0:T(512)S(1)}, s32[384]{0:T(512)S(1)}, u32[]{:S(2)}, u32[]{:S(2)}) collective-permute-start(s32[384]{0:T(512)S(1)} %reshape_squeeze.11), channel_id=1, source_target_pairs={{0,1},{1,0},{2,3},{3,2},{4,5},{5,4},{6,7},{7,6},{8,9},{9,8},{10,11... | collective-permute-start | bytes 4616 | tf_op jit(solution)/shard_map/ppermute | solution.py:36
  5.5 7.0 %collective-permute-start.1 = (s32[1408]{0:T(1024)S(1)}, s32[1408]{0:T(1024)S(1)}, u32[]{:S(2)}, u32[]{:S(2)}) collective-permute-start(s32[1408]{0:T(1024)S(1)} %pad_add_fusion), channel_id=1, source_target_pairs={{0,2},{1,3},{2,0},{3,1},{4,6},{5,7},{6,4},{7,5},{8,10},{9,11},{10,... | collective-permute-start | bytes 16904 | tf_op jit(solution)/shard_map/ppermute | solution.py:36
  7.8 9.6 %collective-permute-start.3 = (f32[6144]{0:T(1024)S(1)}, f32[6144]{0:T(1024)S(1)}, u32[]{:S(2)}, u32[]{:S(2)}) collective-permute-start(f32[6144]{0:T(1024)S(1)} %pad_maximum_fusion.4), channel_id=1, source_target_pairs={{0,1},{1,0},{2,3},{3,2},{4,5},{5,4},{6,7},{7,6},{8,9},{9,8},{10,11... | collective-permute-start | bytes 73736 | tf_op jit(solution)/shard_map/ppermute | solution.py:36
  539.2 1.4 collective-permute-start.4
  540.6 14.4 %collective-permute-start.5 = (f32[24576]{0:T(1024)S(1)}, f32[24576]{0:T(1024)S(1)}, u32[]{:S(2)}, u32[]{:S(2)}) collective-permute-start(f32[24576]{0:T(1024)S(1)} %add.75), channel_id=1, source_target_pairs={{0,1},{1,0},{2,3},{3,2},{4,5},{5,4},{6,7},{7,6},{8,9},{9,8},{10,11... | collective-permute-start | bytes 294920 | tf_op jit(solution)/shard_map/ppermute | solution.py:36
  555.0 12.0 %collective-permute-start.6 = (f32[24576]{0:T(1024)S(1)}, f32[24576]{0:T(1024)S(1)}, u32[]{:S(2)}, u32[]{:S(2)}) collective-permute-start(f32[24576]{0:T(1024)S(1)} %add.76), channel_id=1, source_target_pairs={{0,4},{1,5},{2,6},{3,7},{4,0},{5,1},{6,2},{7,3},{8,12},{9,13},{10,... | collective-permute-start | bytes 294920 | tf_op jit(solution)/shard_map/ppermute | solution.py:36
  567.0 9.8 %collective-permute-start.7 = (f32[24576]{0:T(1024)S(1)}, f32[24576]{0:T(1024)S(1)}, u32[]{:S(2)}, u32[]{:S(2)}) collective-permute-start(f32[24576]{0:T(1024)S(1)} %add.77), channel_id=1, source_target_pairs={{0,8},{1,9},{2,10},{3,11},{4,12},{5,13},{6,14},{7,15},{8,0},{9,1},... | collective-permute-start | bytes 294920 | tf_op jit(solution)/shard_map/ppermute | solution.py:36
  576.7 7.8 %collective-permute-start.8 = (f32[24576]{0:T(1024)S(1)}, f32[24576]{0:T(1024)S(1)}, u32[]{:S(2)}, u32[]{:S(2)}) collective-permute-start(f32[24576]{0:T(1024)S(1)} %add.78), channel_id=1, source_target_pairs={{0,16},{1,17},{2,18},{3,19},{4,20},{5,21},{6,22},{7,23},{8,24},{9,... | collective-permute-start | bytes 294920 | tf_op jit(solution)/shard_map/ppermute | solution.py:36

commit v8 on v7

--- a/solution.py
+++ b/solution.py
@@ -109,6 +109,48 @@
     )(a, b)
 
 
+def hand_out_kernel(layers, y_ref, packed, out, down, gain, shift, qv, hidden):
+    y = y_ref[0]
+    width = packed.shape[1]
+    out[...] = packed[0:layers, :]
+    down[...] = packed[layers : 2 * layers, :]
+    for l in range(layers):
+        for n in range(2):
+            row = 2 * layers + 2 * l + n
+            gain[l, n : n + 1, :] = packed[row : row + 1, :]
+            row += 2 * layers
+            shift[l, n : n + 1, :] = packed[row : row + 1, :]
+            at = 8 * layers + 2 * l + n
+            hidden[l : l + 1, n * width : (n + 1) * width] = jnp.where(
+                y == 0, packed[at : at + 1, :], packed[at + 2 * layers : at + 2 * layers + 1, :]
+            )
+            half = slice(n * width // 2, (n + 1) * width // 2)
+            at = 6 * layers + l
+            qv[l, n : n + 1, :] = jnp.where(
+                y == 0, packed[at : at + 1, half], packed[at + layers : at + layers + 1, half]
+            )
+
+
+def hand_out(packed, y, layers):
+    width = packed.shape[1]
+    full = lambda *shape: jax.ShapeDtypeStruct(shape, F32)
+    in_vmem = pl.BlockSpec(memory_space=pltpu.VMEM)
+    return pl.pallas_call(
+        functools.partial(hand_out_kernel, layers),
+        out_shape=(
+            full(layers, width),
+            full(layers, width),
+            full(layers, 2, width),
+            full(layers, 2, width),
+            full(layers, 2, width // 2),
+            full(layers, 2 * width),
+        ),
+        in_specs=[pl.BlockSpec(memory_space=pltpu.SMEM), in_vmem],
+        out_specs=(in_vmem,) * 6,
+        name="hand_out",
+    )(y, packed)
+
+
 def partner(bits):
     dp, y = lax.axis_index("dp"), lax.axis_index("tensor")
     other = dp
@@ -118,11 +160,15 @@
     return (other, 1 - y if bits & FLIP_Y else y)
 
 
-def greet(bits):
+def all_partners(bits):
+    return {bit: partner(bit) for bit in bits}
+
+
+def greet(partners):
     barrier = pltpu.get_barrier_semaphore()
-    for bit in bits:
-        pl.semaphore_signal(barrier, inc=1, device_id=partner(bit), device_id_type=MESH)
-    pl.semaphore_wait(barrier, len(bits))
+    for other in partners.values():
+        pl.semaphore_signal(barrier, inc=1, device_id=other, device_id_type=MESH)
+    pl.semaphore_wait(barrier, len(partners))
 
 
 def add_into(into, other, count):
@@ -147,8 +193,8 @@
 
 
 class Reduction:
-    def __init__(self, grads, sums, count, bufs, sems):
-        self.grads, self.sums, self.count = grads, sums, count
+    def __init__(self, grads, sums, count, partners, bufs, sems):
+        self.grads, self.sums, self.count, self.partners = grads, sums, count, partners
         self.y_buf, self.x_buf, self.z0_buf, self.z1_buf, self.all_buf, self.keep_buf = bufs
         self.send_sem, self.recv_sem, self.core_send, self.core_recv = sems[:4]
         self.keep_sem, self.out_sem, self.in_free, self.out_free = sems[4:]
@@ -171,7 +217,7 @@
             dst_ref=target,
             send_sem=self.send_sem.at[step, slot] if step < 7 else self.core_send.at[i],
             recv_sem=self.recv_sem.at[step, slot] if step < 7 else self.core_recv.at[i],
-            device_id=partner(bit),
+            device_id=self.partners[bit],
             device_id_type=MESH,
         )
 
@@ -195,7 +241,7 @@
     def give(self, sem, bit, i):
         @pl.when(i + SLOTS < self.count)
         def _():
-            pl.semaphore_signal(sem, inc=1, device_id=partner(bit), device_id_type=MESH)
+            pl.semaphore_signal(sem, inc=1, device_id=self.partners[bit], device_id_type=MESH)
 
     def tick(self, t):
         def at(offset, body):
@@ -265,6 +311,16 @@
         at(3, on_z1)
         at(2, on_z0)
         at(1, on_x)
+
+
+def unit_order(y, core_free_bits):
+    taken = lax.broadcasted_iota(jnp.int32, (512, 512), 0)
+    column = lax.broadcasted_iota(jnp.int32, (512, 512), 1)
+    where = lax.rem(column, 32)
+    for own, weight in zip((y,) + core_free_bits, (256, 128, 64, 32)):
+        bit = lax.rem(lax.div(column, weight), 2)
+        where = where + weight * (bit + own - 2 * own * bit)
+    return (taken == where).astype(F32)
 
 
 def begin(feeds):
@@ -385,8 +441,9 @@
 
 
 class Spread:
-    def __init__(self, weights, pairs, send_sem, recv_sem):
-        self.weights, self.pairs, self.send_sem, self.recv_sem = weights, pairs, send_sem, recv_sem
+    def __init__(self, weights, pairs, partners, send_sem, recv_sem):
+        self.weights, self.pairs, self.partners = weights, pairs, partners
+        self.send_sem, self.recv_sem = send_sem, recv_sem
 
     def copy(self, step, t):
         w = self.weights
@@ -407,7 +464,7 @@
             dst_ref=target,
             send_sem=self.send_sem.at[step, t],
             recv_sem=self.recv_sem.at[step, t],
-            device_id=partner(bit),
+            device_id=self.partners[bit],
             device_id_type=MESH,
         )
 
@@ -449,8 +506,9 @@
     dp, y = lax.axis_index("dp"), lax.axis_index("tensor")
     core = dp % 2
     stays = core == y
-    spread = Spread(w_ref, layers * GROUPS // 2, spread_send, spread_recv)
-    greet((FLIP_Y, FLIP_X, FLIP_Z0, FLIP_C, SWAP))
+    partners = all_partners((FLIP_Y, FLIP_X, FLIP_Z0, FLIP_C, SWAP))
+    spread = Spread(w_ref, layers * GROUPS // 2, partners, spread_send, spread_recv)
+    greet(partners)
 
     def feed(n, slot, source, target):
         return pltpu.make_async_copy(source, target, feed_sem.at[n, slot])
@@ -464,7 +522,7 @@
     def exchange(n, source, target, bits=FLIP_C):
         return pltpu.make_async_remote_copy(
             src_ref=source, dst_ref=target, send_sem=core_send.at[n], recv_sem=core_recv.at[n],
-            device_id=partner(bits), device_id_type=MESH,
+            device_id=partners[bits], device_id_type=MESH,
         )
 
     def columns(ref, i, size):
@@ -598,7 +656,7 @@
             return pltpu.make_async_remote_copy(
                 src_ref=qkv.at[1 + n, :, at], dst_ref=kv_sib.at[n, :, at],
                 send_sem=kv_send.at[n, a], recv_sem=kv_recv.at[n, a],
-                device_id=partner(FLIP_C), device_id_type=MESH,
+                device_id=partners[FLIP_C], device_id_type=MESH,
             )
 
         def which(i):
@@ -706,7 +764,7 @@
             return pltpu.make_async_remote_copy(
                 src_ref=g_all.at[FF_GROUPS + n], dst_ref=columns(g_sib_out, n, 512),
                 send_sem=g_send.at[l, n], recv_sem=g_recv.at[l, n],
-                device_id=partner(FLIP_C), device_id_type=MESH,
+                device_id=partners[FLIP_C], device_id_type=MESH,
             )
 
         def ff_body(i, slot):
@@ -841,7 +899,7 @@
     up_ref, x_ref, w_ref, hot_buf, mask_ref, key_ref, vec_ref = refs[:7]
     saved = [refs[7 + PER_LAYER * l : 7 + PER_LAYER * (l + 1)] for l in range(layers)]
     at_ref = 7 + PER_LAYER * layers
-    grads, sums, dx_out, x_out, dbi_ref, qkv_sums_ref, small_ref = refs[at_ref : at_ref + 7]
+    grads, sums, dx_out, x_out, packed = refs[at_ref : at_ref + 5]
     (
         acc, dr1, dm, dm_sib, da, da_sib, du, du_sib, dctx, dqkv, d_sib, kv_out, kv_far,
         wa_buf, wb_buf, r_buf, slope_buf, left_buf, left_sib_buf, right_buf, right_sib_buf,
@@ -849,15 +907,17 @@
         y_buf, x_buf, z0_buf, z1_buf, all_buf, keep_buf,
         feed_sem, load_sem, store_sem, swap_sem, core_send, core_recv, du_send, du_recv, pair_send, pair_recv,
         send_sem, recv_sem, sum_send, sum_recv, keep_sem, out_sem, in_free, out_free,
-    ) = refs[at_ref + 7 :]
+        dbi_ref, qkv_sums_ref, small_ref, far_buf, far_send, far_recv,
+    ) = refs[at_ref + 5 :]
     rows, width = acc.shape
     total = layers * GROUPS
+    partners = all_partners((FLIP_Y, FLIP_X, FLIP_Z0, FLIP_Z1, FLIP_C, SWAP))
     reduction = Reduction(
-        grads, sums, total,
+        grads, sums, total, partners,
         (y_buf, x_buf, z0_buf, z1_buf, all_buf, keep_buf),
         (send_sem, recv_sem, sum_send, sum_recv, keep_sem, out_sem, in_free, out_free),
     )
-    greet((FLIP_Y, FLIP_X, FLIP_Z0, FLIP_Z1, FLIP_C, SWAP))
+    greet(partners)
 
     def feed(n, slot, source, target):
         return pltpu.make_async_copy(source, target, feed_sem.at[n, slot])
@@ -868,13 +928,13 @@
     def exchange(n, source, target):
         return pltpu.make_async_remote_copy(
             src_ref=source, dst_ref=target, send_sem=core_send.at[n], recv_sem=core_recv.at[n],
-            device_id=partner(FLIP_C), device_id_type=MESH,
+            device_id=partners[FLIP_C], device_id_type=MESH,
         )
 
     def give_du(j, n):
         return pltpu.make_async_remote_copy(
             src_ref=du.at[j], dst_ref=du_sib.at[n], send_sem=du_send.at[n], recv_sem=du_recv.at[n],
-            device_id=partner(FLIP_C), device_id_type=MESH,
+            device_id=partners[FLIP_C], device_id_type=MESH,
         )
 
     def weight(a, group):
@@ -904,7 +964,7 @@
         here = pltpu.make_async_copy(source, target, swap_sem.at[n])
         there = pltpu.make_async_remote_copy(
             src_ref=source, dst_ref=target, send_sem=core_send.at[4 + n], recv_sem=core_recv.at[4 + n],
-            device_id=partner(SWAP), device_id_type=MESH,
+            device_id=partners[SWAP], device_id_type=MESH,
         )
 
         @pl.when(stays)
@@ -1073,7 +1133,7 @@
             at = pl.ds(pl.multiple_of(far * 128, 128), 128)
             return pltpu.make_async_remote_copy(
                 src_ref=kv_out.at[:, :, at], dst_ref=kv_far.at[:, :, at], send_sem=pair_send.at[p], recv_sem=pair_recv.at[far],
-                device_id=partner(FLIP_C), device_id_type=MESH,
+                device_id=partners[FLIP_C], device_id_type=MESH,
             )
 
         def pair_body(p, slot):
@@ -1140,11 +1200,51 @@
     unit_store(1, total - 1).wait()
     swap(0, da, dx_out, True)
 
+    dp, y = lax.axis_index("dp"), lax.axis_index("tensor")
+    core = dp % 2
+    turned = unit_order(y, ((dp // 2) % 2, (dp // 4) % 2, (dp // 8) % 2))
+
+    def in_order(pair):
+        rows_ab = lax.dot_general(
+            jnp.concatenate(pair, axis=0), turned, (((1,), (0,)), ((), ())),
+            precision=lax.Precision.HIGHEST, preferred_element_type=F32,
+        )
+        near = jnp.where(core == 0, rows_ab[0:1], rows_ab[1:2])
+        far = jnp.where(core == 0, rows_ab[1:2], rows_ab[0:1])
+        return [
+            jnp.concatenate([near[:, h * 256 : (h + 1) * 256], far[:, h * 256 : (h + 1) * 256]], axis=1)
+            for h in range(2)
+        ]
+
+    for l in range(layers):
+        for n, source in enumerate((5, 2, 3, 0, 4, 1)):
+            row = n * layers + l if n < 2 else 2 * layers + (n // 2 - 1) * 2 * layers + 2 * l + n % 2
+            packed[row : row + 1, :] = small_ref[l, source : source + 1, :]
+        for n, t in enumerate((0, 2)):
+            for h, part in enumerate(in_order([qkv_sums_ref[l, t, a] for a in range(2)])):
+                packed[6 * layers + h * layers + l : 6 * layers + h * layers + l + 1, n * 512 : (n + 1) * 512] = part
+        for n in range(FF_GROUPS):
+            for h, part in enumerate(in_order([dbi_ref[l, a, n] for a in range(2)])):
+                row = 8 * layers + h * 2 * layers + 2 * l + n // 2
+                packed[row : row + 1, (n % 2) * 512 : (n % 2 + 1) * 512] = part
+
+    tick_at = done
+    for n, bit in enumerate((FLIP_C, FLIP_Y, FLIP_X, FLIP_Z0, FLIP_Z1)):
+        cross = pltpu.make_async_remote_copy(
+            src_ref=packed, dst_ref=far_buf.at[n], send_sem=far_send.at[n], recv_sem=far_recv.at[n],
+            device_id=partners[bit], device_id_type=MESH,
+        )
+        cross.start()
+        reduction.tick(tick_at)
+        cross.wait()
+        packed[...] += far_buf[n]
+        tick_at += 1
+
     def rest(t, _):
         reduction.tick(t)
         return 0
 
-    lax.fori_loop(done, total + LAST_TICK, rest, 0)
+    lax.fori_loop(tick_at, total + LAST_TICK, rest, 0)
     swap(0, da, dx_out, False)
     swap(1, x_ref, x_out, False)
 
@@ -1164,12 +1264,10 @@
             jax.ShapeDtypeStruct((total, 512, width), BF16),
             jax.ShapeDtypeStruct((rows, width), BF16),
             jax.ShapeDtypeStruct((rows, width), BF16),
-            jax.ShapeDtypeStruct((layers, 2, FF_GROUPS, 1, 512), F32),
-            jax.ShapeDtypeStruct((layers, 3, 2, 1, 512), F32),
-            jax.ShapeDtypeStruct((layers, 8, width), F32),
+            jax.ShapeDtypeStruct((12 * layers, width), F32),
         ),
         in_specs=[anywhere] * 3 + [in_vmem] * 4 + [anywhere] * (PER_LAYER * layers),
-        out_specs=(anywhere, anywhere, anywhere, anywhere, in_vmem, in_vmem, in_vmem),
+        out_specs=(anywhere, anywhere, anywhere, anywhere, in_vmem),
         scratch_shapes=[
             pltpu.VMEM((rows, width), F32),
             pltpu.VMEM((rows, width), F32),
@@ -1219,6 +1317,12 @@
             dma(SLOTS),
             pltpu.SemaphoreType.REGULAR((4,)),
             pltpu.SemaphoreType.REGULAR((3,)),
+            pltpu.VMEM((layers, 2, FF_GROUPS, 1, 512), F32),
+            pltpu.VMEM((layers, 3, 2, 1, 512), F32),
+            pltpu.VMEM((layers, 8, width), F32),
+            pltpu.VMEM((5, 12 * layers, width), F32),
+            dma(5),
+            dma(5),
         ],
         compiler_params=pltpu.CompilerParams(
             collective_id=1, has_side_effects=True, vmem_limit_bytes=60 << 20
@@ -1327,65 +1431,34 @@
     weights, upstream_low, stream_low, saved = forward(
         block_input, cotangent, w_qkv, w_out, w_in, w_down, hot, mask, mask_rows, bias_qkv, bias_in, vectors
     )
-    _, grads, dx_low, x_low, d_b_in, qkv_sums, rows_small = backward(
+    _, grads, dx_low, x_low, packed = backward(
         upstream_low, stream_low, weights, hot, mask, mask_rows, vectors, saved
     )
     block_output, input_grad = widen_rows(x_low, dx_low)
 
-    stacks = [
-        jnp.stack([qkv_sums[:, 0], qkv_sums[:, 2]], axis=1),
-        rows_small[:, 5],
-        d_b_in.swapaxes(1, 2),
-        rows_small[:, 2],
-        jnp.stack([rows_small[:, 3], rows_small[:, 0]], axis=1),
-        jnp.stack([rows_small[:, 4], rows_small[:, 1]], axis=1),
-    ]
-
-    def global_order(values, lead):
-        values = values.reshape(lead, 2, 2, 2, 2, 2, 32).swapaxes(1, 2)
-        values = flip_order(values, 1, (y,) + device_bits)
-        return values.swapaxes(0, 1).reshape(2, -1)
-
-    stacks[0] = global_order(stacks[0], layers * 2)
-    stacks[2] = global_order(stacks[2], layers * FF_GROUPS)
     def placing(shape, block, index, turned, count, start):
-        return lambda values: place(
-            values, shape, block, index, turned, count, lambda l, i: (layers - 1 - l) * GROUPS + start + i, code_arg
-        )
-
-    summed = jnp.concatenate([s.reshape(-1) for s in stacks])
-    summed = summed + flip(summed, FLIP_C)
-    placed = []
-    for bit, put in (
-        (FLIP_Y, placing(w_down.shape, (1, 512, width), lambda l, i: (l, i, 0), False, FF_GROUPS, 0)),
-        (FLIP_X, placing(w_in.shape, (1, width, 512), lambda l, i: (l, 0, i), True, FF_GROUPS, FF_GROUPS)),
-        (FLIP_Z0, placing(w_qkv.shape, (1, 1, width, 512), lambda l, i: (l, i, 0, 0), True, 3, 2 * FF_GROUPS + 1)),
-        (FLIP_Z1, placing(w_out.shape, (1, 512, width), lambda l, i: (l, 0, 0), False, 1, 2 * FF_GROUPS)),
-    ):
-        summed, grads = lax.optimization_barrier((summed, grads))
-        far = flip(summed, bit)
-        done, summed, far = lax.optimization_barrier((put(grads), summed, far))
-        placed.append(done)
-        summed = summed + far
-    parts, at = [], 0
-    for s in stacks:
-        parts.append(summed[at : at + s.size].reshape(s.shape))
-        at += s.size
-    g_b_qv = lax.dynamic_index_in_dim(parts[0], y, axis=0, keepdims=False).reshape(b_qv.shape)
-    g_b_in = lax.dynamic_index_in_dim(parts[2], y, axis=0, keepdims=False).reshape(b_in.shape)
+        return place(
+            grads, shape, block, index, turned, count, lambda l, i: (layers - 1 - l) * GROUPS + start + i, code_arg
+        )
+
+    g_b_out, g_b_down, g_gain, g_shift, g_b_qv, g_b_in = hand_out(packed, y.reshape(1).astype(jnp.int32), layers)
+    g_down = placing(w_down.shape, (1, 512, width), lambda l, i: (l, i, 0), False, FF_GROUPS, 0)
+    g_in = placing(w_in.shape, (1, width, 512), lambda l, i: (l, 0, i), True, FF_GROUPS, FF_GROUPS)
+    g_qkv = placing(w_qkv.shape, (1, 1, width, 512), lambda l, i: (l, i, 0, 0), True, 3, 2 * FF_GROUPS + 1)
+    g_out = placing(w_out.shape, (1, 512, width), lambda l, i: (l, 0, 0), False, 1, 2 * FF_GROUPS)
     return (
         block_output,
         input_grad,
-        placed[2],
+        g_qkv,
         g_b_qv,
-        placed[3],
-        parts[1],
-        placed[1],
+        g_out,
+        g_b_out,
+        g_in,
         g_b_in,
-        placed[0],
-        parts[3],
-        parts[4],
-        parts[5],
+        g_down,
+        g_b_down,
+        g_gain,
+        g_shift,
     )
 
 

time: 594 us -> 585 us (0.985)
  local copies, waits for them, and re-layouts: 15 us -> 7.58 us
  starting transfers between devices: 11.7 us -> 4.95 us
    ppermute x9 -> x4, starting transfers between devices: 11.7 us -> 4.95 us  [flip(): lax.ppermute(v, ('dp', 'tensor'), pairs)]
  transfers between devices with their start and end apart: 9 -> 4, of which waited for: 1 -> 0; matrix products, arithmetic and copies ran while one was open for 2% -> 2% of each run, Pallas kernels for 6% -> 0%
where the time goes in v8:
time: 585 us; the launch traced here: 577 us
  Pallas kernels  558 us (95%)
  local copies, waits for them, and re-layouts  7.58 us (1%)
    pallas_call x1, Pallas kernels, backward(): pl.pallas_call(functools.partial(backward_kernel, layers), out_shape=(jax...  353 us
    pallas_call x1, Pallas kernels, forward(): pl.pallas_call(functools.partial(forward_kernel, layers), out_shape=(low_...  166 us
    pallas_call x4, Pallas kernels, place(): pl.pallas_call(functools.partial(place_kernel, turned), out_shape=jax.Sha...  33.9 us
  transfers between devices with their start and end apart: 4, of which 0 were waited for; matrix products, arithmetic and copies ran while one was open for 2% of the time, Pallas kernels for 0%

profile of v8, /device:TPU:0, one launch (start us, length us, event | category | flops | bytes accessed | tf_op | source)
XLA Modules:
  0.0 577.5 jit_solution(16727723396250540113)
XLA Ops:
  0.6 0.8 copy.31
  1.5 0.2 reshape_squeeze.2
  1.7 2.5 collective-permute-start.2
  4.1 0.6 collective-permute-start
  4.8 0.7 pad_add_fusion
  5.5 0.0 collective-permute-start.1
  5.5 0.8 reshape.206
  6.4 0.1 rev.54
  6.5 0.1 reshape.207
  6.6 0.8 reshape.208
  7.5 0.2 rev.58
  7.7 0.1 reshape.209
  7.8 1.8 collective-permute-start.3
  9.7 0.8 fusion.11
  10.5 0.8 slice_bitcast_fusion.4
  11.3 0.1 stack.19
  11.4 0.1 stack.21
  11.5 0.6 pad_maximum_fusion.2.refs_11_.refs_6_
  12.1 0.1 fusion.8
  12.2 0.1 reshape_reshape.16
  12.3 0.1 reshape_reshape.18
  12.4 0.1 pad.15.clone
  12.5 0.0 collective-permute-done.1
  12.5 0.0 collective-permute-done.2
  12.5 0.0 collective-permute-done
  12.6 0.7 add_select_fusion
  13.3 0.1 rev.47
  13.5 0.2 reshape_reshape.15
  13.7 0.2 copy.32
  13.9 0.1 constant_dynamic-slice_fusion
  14.0 0.1 compare_reduce_fusion
  14.1 0.1 fusion.2
  14.3 0.2 fusion.1
  14.5 0.2 pad.9
  14.7 1.0 pad_maximum_fusion.refs_8_.refs_5_
  15.7 0.8 pad_maximum_fusion.1.refs_6_.refs_3_
  16.6 0.8 copy.38.refs_7_.refs_4_
  17.4 0.0 collective-permute-done.3
  17.5 0.6 copy.41
  18.2 0.7 pad_maximum_fusion.5.refs_9_
  18.9 166.1 %forward.1 = (bf16[2,24,2,256,1024]{4,3,2,1,0:T(8,128)(2,1)}, bf16[512,1024]{1,0:T(8,128)(2,1)}, bf16[512,1024]{1,0:T(8,128)(2,1)}, bf16[3,512,1024]{2,1,0:T(8,1...) custom-call(f32[512,1,1024]{2,1,0:T(1,128)} %refs_0_.1, ...), custom_call_target="tpu_custom_call" | custom-call | flops 32212254720 | bytes 314572800 | tf_op jit(solution)/shard_map/forward/pallas_call | solution.py:849
  185.0 353.1 %backward.1 = (bf16[24,512,1024]{2,1,0:T(8,128)(2,1)}, bf16[24,512,1024]{2,1,0:T(8,128)(2,1)}, bf16[512,1024]{1,0:T(8,128)(2,1)}, bf16[512,1024]{1,0:T(8,128)(2,1)}, f32[24,1024]{1,0:T(8,128)}) custom-call(bf16[512,1024]{1,0:T(8,128)(2,1)} %get-tuple-element.55.refs_0_, bf16[512,1024]{1,0:T(8,128)(2,1)} %get-tuple-element.56.refs_1_, ...), custom_call_target="tpu_custom_call" | custom-call | flops 64424509440 | bytes 314572800 | tf_op jit(solution)/shard_map/backward/pallas_call | solution.py:1260
  538.1 3.4 place.5
  541.5 8.9 %place.4 = f32[2,3,1024,512]{3,2,1,0:T(8,128)} custom-call(s32[1]{0:T(128)} %bitcast.23.code_ref, bf16[24,512,1024]{2,1,0:T(8,128)(2,1)} %get-tuple-element.90.g_ref), custom_call_target="tpu_custom_call" | custom-call | bytes 18874368 | tf_op jit(solution)/shard_map/place/pallas_call | solution.py:71
  550.4 10.3 %place.7 = f32[2,2048,1024]{2,1,0:T(8,128)} custom-call(s32[1]{0:T(128)} %bitcast.23.code_ref, bf16[24,512,1024]{2,1,0:T(8,128)(2,1)} %get-tuple-element.90.g_ref), custom_call_target="tpu_custom_call" | custom-call | bytes 25165824 | tf_op jit(solution)/shard_map/place/pallas_call | solution.py:71
  560.7 11.3 %place.6 = f32[2,1024,2048]{2,1,0:T(8,128)} custom-call(s32[1]{0:T(128)} %bitcast.23.code_ref, bf16[24,512,1024]{2,1,0:T(8,128)(2,1)} %get-tuple-element.90.g_ref), custom_call_target="tpu_custom_call" | custom-call | bytes 25165824 | tf_op jit(solution)/shard_map/place/pallas_call | solution.py:71
  572.0 1.5 hand_out.1
  573.6 3.7 widen_rows.1
  (37 shorter events, 0.5 us)
Async XLA Ops:
  1.7 10.9 %collective-permute-start.2 = (s32[384]{0:T(512)S(1)}, s32[384]{0:T(512)S(1)}, u32[]{:S(2)}, u32[]{:S(2)}) collective-permute-start(s32[384]{0:T(512)S(1)} %reshape_squeeze.2), channel_id=1, source_target_pairs={{0,3},{1,2},{2,1},{3,0},{4,7},{5,6},{6,5},{7,4},{8,11},{9,10},{10,... | collective-permute-start | bytes 4616 | tf_op jit(solution)/shard_map/ppermute | solution.py:36
  4.1 8.4 %collective-permute-start = (s32[384]{0:T(512)S(1)}, s32[384]{0:T(512)S(1)}, u32[]{:S(2)}, u32[]{:S(2)}) collective-permute-start(s32[384]{0:T(512)S(1)} %reshape_squeeze.2), channel_id=1, source_target_pairs={{0,1},{1,0},{2,3},{3,2},{4,5},{5,4},{6,7},{7,6},{8,9},{9,8},{10,11... | collective-permute-start | bytes 4616 | tf_op jit(solution)/shard_map/ppermute | solution.py:36
  5.5 7.0 %collective-permute-start.1 = (s32[1408]{0:T(1024)S(1)}, s32[1408]{0:T(1024)S(1)}, u32[]{:S(2)}, u32[]{:S(2)}) collective-permute-start(s32[1408]{0:T(1024)S(1)} %pad_add_fusion), channel_id=1, source_target_pairs={{0,2},{1,3},{2,0},{3,1},{4,6},{5,7},{6,4},{7,5},{8,10},{9,11},{10,... | collective-permute-start | bytes 16904 | tf_op jit(solution)/shard_map/ppermute | solution.py:36
  7.8 9.6 %collective-permute-start.3 = (f32[6144]{0:T(1024)S(1)}, f32[6144]{0:T(1024)S(1)}, u32[]{:S(2)}, u32[]{:S(2)}) collective-permute-start(f32[6144]{0:T(1024)S(1)} %pad_maximum_fusion.4), channel_id=1, source_target_pairs={{0,1},{1,0},{2,3},{3,2},{4,5},{5,4},{6,7},{7,6},{8,9},{9,8},{10,11... | collective-permute-start | bytes 73736 | tf_op jit(solution)/shard_map/ppermute | solution.py:36

commit v9 on v8

--- a/solution.py
+++ b/solution.py
@@ -188,29 +188,48 @@
     lax.fori_loop(0, rows // 32, step, 0)
 
 
+def add_into(into, other, count):
+    def step(i, _):
+        into[i] = (into[i].astype(F32) + other[i].astype(F32)).astype(BF16)
+        return 0
+
+    lax.fori_loop(0, count, step, 0)
+
+
 SLOTS = 6
+PARTED = 2
+PARTS = 2
 LAST_TICK = 8
 
 
 class Reduction:
-    def __init__(self, grads, sums, count, partners, bufs, sems):
-        self.grads, self.sums, self.count, self.partners = grads, sums, count, partners
+    def __init__(self, grads, sums, first, groups, parts, partners, bufs, sems):
+        self.grads, self.sums, self.first, self.parts, self.partners = grads, sums, first, parts, partners
+        self.count = groups * parts
         self.y_buf, self.x_buf, self.z0_buf, self.z1_buf, self.all_buf, self.keep_buf = bufs
-        self.send_sem, self.recv_sem, self.core_send, self.core_recv = sems[:4]
-        self.keep_sem, self.out_sem, self.in_free, self.out_free = sems[4:]
+        self.slots = self.y_buf.shape[0]
+        self.send_sem, self.recv_sem, self.core_send, self.core_recv, self.keep_sem, self.out_sem = sems[:6]
+        self.in_free, self.out_free = sems[6:] if len(sems) > 6 else (None, None)
+
+    def blocks(self, ref, i, at):
+        if self.parts == 1:
+            return ref.at[self.first + i, pl.ds(at, 8)]
+        size = 32 // self.parts
+        part = pl.ds(pl.multiple_of(lax.rem(i, self.parts) * size, size), size)
+        return ref.at[self.first + lax.div(i, self.parts), pl.ds(at, 8), part]
 
     def copy(self, step, i):
-        slot = lax.rem(i, SLOTS)
+        slot = lax.rem(i, self.slots)
         ys, al = self.y_buf.at[slot], self.all_buf.at[slot]
         bit, source, target = (
-            (FLIP_Y, self.grads.at[i, pl.ds(256, 256)], ys),
-            (FLIP_X, ys.at[pl.ds(128, 128)], self.x_buf.at[slot]),
-            (FLIP_Z0, ys.at[pl.ds(64, 64)], self.z0_buf.at[slot]),
-            (FLIP_Z1, ys.at[pl.ds(32, 32)], self.z1_buf.at[slot]),
-            (FLIP_Z1, al.at[pl.ds(0, 32)], al.at[pl.ds(32, 32)]),
-            (FLIP_Z0, al.at[pl.ds(0, 64)], al.at[pl.ds(64, 64)]),
-            (FLIP_X, al.at[pl.ds(0, 128)], al.at[pl.ds(128, 128)]),
-            (FLIP_C, al, self.sums.at[i, pl.ds(256, 256)]),
+            (FLIP_Y, self.blocks(self.grads, i, 8), ys),
+            (FLIP_X, ys.at[pl.ds(4, 4)], self.x_buf.at[slot]),
+            (FLIP_Z0, ys.at[pl.ds(2, 2)], self.z0_buf.at[slot]),
+            (FLIP_Z1, ys.at[pl.ds(1, 1)], self.z1_buf.at[slot]),
+            (FLIP_Z1, al.at[pl.ds(0, 1)], al.at[pl.ds(1, 1)]),
+            (FLIP_Z0, al.at[pl.ds(0, 2)], al.at[pl.ds(2, 2)]),
+            (FLIP_X, al.at[pl.ds(0, 4)], al.at[pl.ds(4, 4)]),
+            (FLIP_C, al, self.blocks(self.sums, i, 8)),
         )[step]
         return pltpu.make_async_remote_copy(
             src_ref=source,
@@ -224,32 +243,34 @@
     def keep(self, i):
         slot = lax.rem(i, 2)
         return pltpu.make_async_copy(
-            self.grads.at[i, pl.ds(0, 256)], self.keep_buf.at[slot], self.keep_sem.at[slot]
+            self.blocks(self.grads, i, 0), self.keep_buf.at[slot], self.keep_sem.at[slot]
         )
 
     def out(self, i):
-        slot = lax.rem(i, SLOTS)
+        slot = lax.rem(i, self.slots)
         return pltpu.make_async_copy(
-            self.all_buf.at[slot], self.sums.at[i, pl.ds(0, 256)], self.out_sem.at[slot]
-        )
-
-    def take(self, sem, i):
-        @pl.when(i >= SLOTS)
-        def _():
-            pl.semaphore_wait(sem, 1)
-
-    def give(self, sem, bit, i):
-        @pl.when(i + SLOTS < self.count)
-        def _():
-            pl.semaphore_signal(sem, inc=1, device_id=self.partners[bit], device_id_type=MESH)
+            self.all_buf.at[slot], self.blocks(self.sums, i, 0), self.out_sem.at[slot]
+        )
+
+    def take(self, sems, n, i):
+        if sems is not None:
+            pl.when(i >= self.slots)(lambda: pl.semaphore_wait(sems.at[n], 1))
+
+    def give(self, sems, n, bit, i):
+        if sems is not None:
+            pl.when(i + self.slots < self.count)(
+                lambda: pl.semaphore_signal(
+                    sems.at[n], inc=1, device_id=self.partners[bit], device_id_type=MESH
+                )
+            )
 
     def tick(self, t):
         def at(offset, body):
             i = t - offset
-            pl.when((i >= 0) & (i < self.count))(lambda: body(i, lax.rem(i, SLOTS)))
+            pl.when((i >= 0) & (i < self.count))(lambda: body(i, lax.rem(i, self.slots)))
 
         def set_out(i, slot):
-            self.take(self.in_free.at[0], i)
+            self.take(self.in_free, 0, i)
             self.copy(0, i).start()
             self.keep(i).start()
 
@@ -257,7 +278,7 @@
             self.copy(7, i).wait()
             self.out(i).wait()
             for n, bit in enumerate((FLIP_X, FLIP_Z0, FLIP_Z1)):
-                self.give(self.out_free.at[n], bit, i)
+                self.give(self.out_free, n, bit, i)
 
         def to_core(i, slot):
             self.copy(6, i).wait()
@@ -266,40 +287,40 @@
 
         def back_x(i, slot):
             self.copy(5, i).wait()
-            self.take(self.out_free.at[0], i)
+            self.take(self.out_free, 0, i)
             self.copy(6, i).start()
 
         def back_z0(i, slot):
             self.copy(4, i).wait()
-            self.take(self.out_free.at[1], i)
+            self.take(self.out_free, 1, i)
             self.copy(5, i).start()
 
         def back_z1(i, slot):
             self.copy(3, i).wait()
-            add_rows(self.y_buf.at[slot], self.z1_buf.at[slot], 32)
-            self.all_buf[slot, 0:32, :] = self.y_buf[slot, 0:32, :]
+            add_into(self.y_buf.at[slot], self.z1_buf.at[slot], 1)
+            self.all_buf[slot, 0] = self.y_buf[slot, 0]
             for n, bit in enumerate((FLIP_Y, FLIP_X, FLIP_Z0, FLIP_Z1)):
-                self.give(self.in_free.at[n], bit, i)
-            self.take(self.out_free.at[2], i)
+                self.give(self.in_free, n, bit, i)
+            self.take(self.out_free, 2, i)
             self.copy(4, i).start()
 
         def on_z1(i, slot):
             self.copy(2, i).wait()
-            add_rows(self.y_buf.at[slot], self.z0_buf.at[slot], 64)
-            self.take(self.in_free.at[3], i)
+            add_into(self.y_buf.at[slot], self.z0_buf.at[slot], 2)
+            self.take(self.in_free, 3, i)
             self.copy(3, i).start()
 
         def on_z0(i, slot):
             self.copy(1, i).wait()
-            add_rows(self.y_buf.at[slot], self.x_buf.at[slot], 128)
-            self.take(self.in_free.at[2], i)
+            add_into(self.y_buf.at[slot], self.x_buf.at[slot], 4)
+            self.take(self.in_free, 2, i)
             self.copy(2, i).start()
 
         def on_x(i, slot):
             self.copy(0, i).wait()
             self.keep(i).wait()
-            add_rows(self.y_buf.at[slot], self.keep_buf.at[lax.rem(i, 2)], 256)
-            self.take(self.in_free.at[1], i)
+            add_into(self.y_buf.at[slot], self.keep_buf.at[lax.rem(i, 2)], 8)
+            self.take(self.in_free, 1, i)
             self.copy(1, i).start()
 
         at(0, set_out)
@@ -604,8 +625,6 @@
 
     load_x = load(0, x_ref.at[:, 0], x)
     load_x.start()
-    load_up = load(1, up_ref.at[:, 0], acc)
-    load_up.start()
     for kind in range(2):
         for m in ahead[kind][:DEPTH]:
             fetches[m][0].start()
@@ -616,14 +635,6 @@
 
     row_tiles(rows, narrow_x)
     swap(0, low, xb, True)
-    load_up.wait()
-
-    def narrow_up(at):
-        hl[at, :] = acc[at, :].astype(BF16)
-
-    row_tiles(rows, narrow_up)
-    swap(1, hl, up_out, True)
-
     for m in range(len(items)):
         convert(m)
         if m % 4 == 3:
@@ -631,7 +642,8 @@
     for m in range(len(items) - 2, len(items)):
         made[m].wait()
     swap(0, low, xb, False)
-    swap(1, hl, up_out, False)
+    load_up = load(1, up_ref.at[:, 0], row_buf.at[0])
+    load_up.start()
 
     def widen(at):
         x[at, :] = xb[at, :].astype(F32)
@@ -787,6 +799,14 @@
         xb_copy.wait()
         if l + 1 < layers:
             feed(0, 0, w_ref.at[0, first + GROUPS], wa_buf.at[0]).start()
+        if l == 0:
+            load_up.wait()
+
+            def narrow_up(at):
+                low[at, :] = row_buf[0, at, :].astype(BF16)
+
+            row_tiles(rows, narrow_up)
+            swap(9, low, up_out, True)
 
         def second_norm(at):
             r2 = acc[at, :]
@@ -817,6 +837,7 @@
         for copy in (qkv_store, ctx_store, lse_store, ctx_copy, hl_store, hl_copy, r2_store):
             copy.wait()
     x_store.wait()
+    swap(9, low, up_out, False)
 
 
 def forward(block_input, cotangent, w_qkv, w_out, w_in, w_down, hot, mask, mask_rows, bias_qkv, bias_in, vectors):
@@ -908,15 +929,18 @@
         feed_sem, load_sem, store_sem, swap_sem, core_send, core_recv, du_send, du_recv, pair_send, pair_recv,
         send_sem, recv_sem, sum_send, sum_recv, keep_sem, out_sem, in_free, out_free,
         dbi_ref, qkv_sums_ref, small_ref, far_buf, far_send, far_recv,
-    ) = refs[at_ref + 5 :]
+    ) = refs[at_ref + 5 : -12]
+    part_bufs, part_sems = refs[-12:-6], refs[-6:]
     rows, width = acc.shape
     total = layers * GROUPS
     partners = all_partners((FLIP_Y, FLIP_X, FLIP_Z0, FLIP_Z1, FLIP_C, SWAP))
+    whole = total - PARTED
     reduction = Reduction(
-        grads, sums, total, partners,
+        grads, sums, 0, whole, 1, partners,
         (y_buf, x_buf, z0_buf, z1_buf, all_buf, keep_buf),
         (send_sem, recv_sem, sum_send, sum_recv, keep_sem, out_sem, in_free, out_free),
     )
+    ending = Reduction(grads, sums, whole, PARTED, PARTS, partners, part_bufs, part_sems)
     greet(partners)
 
     def feed(n, slot, source, target):
@@ -948,7 +972,7 @@
 
     def unit(left, left_sib, right, right_sib, slot, index, fresh=False):
         made = (tn(left, right) + tn(left_sib, right_sib)).astype(BF16)
-        unit_buf[slot] = made
+        unit_buf[slot] = made.reshape(unit_buf.shape[1:])
         if fresh is not False:
             pl.when(jnp.logical_not(fresh))(lambda: unit_store(slot, index).wait())
         else:
@@ -975,7 +999,6 @@
         def _():
             there.start() if begin else there.wait()
 
-    swap(1, x_ref, x_out, True)
     load(0, saved[-1][6], r_buf).start()
     start_up = load(1, up_ref, da)
     start_up.start()
@@ -1198,8 +1221,7 @@
 
     row_tiles(rows, narrow)
     unit_store(1, total - 1).wait()
-    swap(0, da, dx_out, True)
-
+    ending.tick(0)
     dp, y = lax.axis_index("dp"), lax.axis_index("tensor")
     core = dp % 2
     turned = unit_order(y, ((dp // 2) % 2, (dp // 4) % 2, (dp // 8) % 2))
@@ -1228,23 +1250,26 @@
                 row = 8 * layers + h * 2 * layers + 2 * l + n // 2
                 packed[row : row + 1, (n % 2) * 512 : (n % 2 + 1) * 512] = part
 
-    tick_at = done
     for n, bit in enumerate((FLIP_C, FLIP_Y, FLIP_X, FLIP_Z0, FLIP_Z1)):
         cross = pltpu.make_async_remote_copy(
             src_ref=packed, dst_ref=far_buf.at[n], send_sem=far_send.at[n], recv_sem=far_recv.at[n],
             device_id=partners[bit], device_id_type=MESH,
         )
         cross.start()
-        reduction.tick(tick_at)
+        reduction.tick(done + n)
+        ending.tick(1 + n)
         cross.wait()
         packed[...] += far_buf[n]
-        tick_at += 1
-
-    def rest(t, _):
-        reduction.tick(t)
+
+    swap(0, da, dx_out, True)
+    swap(1, x_ref, x_out, True)
+
+    def rest(n, _):
+        reduction.tick(done + n)
+        ending.tick(1 + n)
         return 0
 
-    lax.fori_loop(tick_at, total + LAST_TICK, rest, 0)
+    lax.fori_loop(5, PARTED * PARTS + LAST_TICK - 1, rest, 0)
     swap(0, da, dx_out, False)
     swap(1, x_ref, x_out, False)
 
@@ -1257,11 +1282,12 @@
     in_vmem = pl.BlockSpec(memory_space=pltpu.VMEM)
     low = lambda *shape: pltpu.VMEM(shape, BF16)
     dma = lambda *shape: pltpu.SemaphoreType.DMA(shape)
+    ends = PARTED * PARTS
     return pl.pallas_call(
         functools.partial(backward_kernel, layers),
         out_shape=(
-            jax.ShapeDtypeStruct((total, 512, width), BF16),
-            jax.ShapeDtypeStruct((total, 512, width), BF16),
+            jax.ShapeDtypeStruct((total, 16, 32, width), BF16),
+            jax.ShapeDtypeStruct((total, 16, 32, width), BF16),
             jax.ShapeDtypeStruct((rows, width), BF16),
             jax.ShapeDtypeStruct((rows, width), BF16),
             jax.ShapeDtypeStruct((12 * layers, width), F32),
@@ -1292,13 +1318,13 @@
             low(rows, width),
             low(2, 4, 2 * rows, 128),
             pltpu.VMEM((2, 2, rows), F32),
-            low(2, 512, width),
-            low(SLOTS, 256, width),
-            low(SLOTS, 128, width),
-            low(SLOTS, 64, width),
-            low(SLOTS, 32, width),
-            low(SLOTS, 256, width),
-            low(2, 256, width),
+            low(2, 16, 32, width),
+            low(SLOTS, 8, 32, width),
+            low(SLOTS, 4, 32, width),
+            low(SLOTS, 2, 32, width),
+            low(SLOTS, 1, 32, width),
+            low(SLOTS, 8, 32, width),
+            low(2, 8, 32, width),
             dma(12, 2),
             dma(5),
             dma(1),
@@ -1323,6 +1349,18 @@
             pltpu.VMEM((5, 12 * layers, width), F32),
             dma(5),
             dma(5),
+            low(ends, 8, 32 // PARTS, width),
+            low(ends, 4, 32 // PARTS, width),
+            low(ends, 2, 32 // PARTS, width),
+            low(ends, 1, 32 // PARTS, width),
+            low(ends, 8, 32 // PARTS, width),
+            low(2, 8, 32 // PARTS, width),
+            dma(7, ends),
+            dma(7, ends),
+            dma(ends),
+            dma(ends),
+            dma(2),
+            dma(ends),
         ],
         compiler_params=pltpu.CompilerParams(
             collective_id=1, has_side_effects=True, vmem_limit_bytes=60 << 20
@@ -1434,6 +1472,7 @@
     _, grads, dx_low, x_low, packed = backward(
         upstream_low, stream_low, weights, hot, mask, mask_rows, vectors, saved
     )
+    grads = grads.reshape(layers * GROUPS, 512, width)
     block_output, input_grad = widen_rows(x_low, dx_low)
 
     def placing(shape, block, index, turned, count, start):

time: 585 us -> 566 us (0.968)
  Pallas kernels: 558 us -> 541 us
    pallas_call x1, Pallas kernels: 166 us -> 155 us  [forward(): pl.pallas_call(functools.partial(forward_kernel, layers), out_shape=(low_...]
    pallas_call x1, Pallas kernels: 353 us -> 347 us  [backward(): pl.pallas_call(functools.partial(backward_kernel, layers), out_shape=(jax...]
where the time goes in v9:
time: 566 us; the launch traced here: 560 us
  Pallas kernels  541 us (96%)
  local copies, waits for them, and re-layouts  7.58 us (1%)
    pallas_call x1, Pallas kernels, backward(): pl.pallas_call(functools.partial(backward_kernel, layers), out_shape=(jax...  347 us
    pallas_call x1, Pallas kernels, forward(): pl.pallas_call(functools.partial(forward_kernel, layers), out_shape=(low_...  155 us
    pallas_call x4, Pallas kernels, place(): pl.pallas_call(functools.partial(place_kernel, turned), out_shape=jax.Sha...  33.9 us
  transfers between devices with their start and end apart: 4, of which 0 were waited for; matrix products, arithmetic and copies ran while one was open for 2% of the time, Pallas kernels for 0%

profile of v9, /device:TPU:0, one launch (start us, length us, event | category | flops | bytes accessed | tf_op | source)
XLA Modules:
  0.0 560.3 jit_solution(2512615283816815987)
XLA Ops:
  0.6 0.8 copy.31
  1.5 0.2 reshape_squeeze.2
  1.7 2.5 collective-permute-start.2
  4.1 0.6 collective-permute-start
  4.8 0.7 pad_add_fusion
  5.5 0.0 collective-permute-start.1
  5.5 0.8 reshape.209
  6.4 0.1 rev.54
  6.5 0.1 reshape.210
  6.6 0.8 reshape.211
  7.5 0.2 rev.58
  7.7 0.1 reshape.212
  7.8 1.8 collective-permute-start.3
  9.7 0.8 fusion.11
  10.5 0.8 slice_bitcast_fusion.4
  11.3 0.1 stack.19
  11.4 0.1 stack.21
  11.5 0.6 pad_maximum_fusion.2.refs_11_.refs_6_
  12.1 0.1 fusion.8
  12.2 0.1 reshape_reshape.16
  12.3 0.1 reshape_reshape.18
  12.4 0.1 pad.15.clone
  12.5 0.0 collective-permute-done.1
  12.5 0.0 collective-permute-done.2
  12.5 0.0 collective-permute-done
  12.6 0.7 add_select_fusion
  13.3 0.1 rev.47
  13.5 0.2 reshape_reshape.15
  13.7 0.2 copy.32
  13.9 0.1 constant_dynamic-slice_fusion
  14.0 0.1 compare_reduce_fusion
  14.1 0.1 fusion.2
  14.3 0.2 fusion.1
  14.5 0.2 pad.9
  14.7 1.0 pad_maximum_fusion.refs_8_.refs_5_
  15.7 0.8 pad_maximum_fusion.1.refs_6_.refs_3_
  16.6 0.8 copy.38.refs_7_.refs_4_
  17.4 0.0 collective-permute-done.3
  17.5 0.6 copy.41
  18.2 0.7 pad_maximum_fusion.5.refs_9_
  18.9 154.8 %forward.1 = (bf16[2,24,2,256,1024]{4,3,2,1,0:T(8,128)(2,1)}, bf16[512,1024]{1,0:T(8,128)(2,1)}, bf16[512,1024]{1,0:T(8,128)(2,1)}, bf16[3,512,1024]{2,1,0:T(8,1...) custom-call(f32[512,1,1024]{2,1,0:T(1,128)} %refs_0_.1, ...), custom_call_target="tpu_custom_call" | custom-call | flops 32212254720 | bytes 314572800 | tf_op jit(solution)/shard_map/forward/pallas_call | solution.py:870
  173.8 347.2 %backward.1 = (bf16[24,16,32,1024]{3,2,1,0:T(8,128)(2,1)}, bf16[24,16,32,1024]{3,2,1,0:T(8,128)(2,1)}, bf16[512,1024]{1,0:T(8,128)(2,1)}, bf16[512,1024]{1,0:T(8,128)(2,1)}, f32[24,1024]{1,0:T(8,128)}) custom-call(bf16[512,1024]{1,0:T(8,128)(2,1)} %get-tuple-element.55.refs_0_, bf16[512,1024]{1,0:T(8,128)(2,1)} %get-tuple-element.56.refs_1_, ...), custom_call_target="tpu_custom_call" | custom-call | flops 64424509440 | bytes 314572800 | tf_op jit(solution)/shard_map/backward/pallas_call | solution.py:1286
  521.0 3.4 place.5
  524.4 8.9 %place.4 = f32[2,3,1024,512]{3,2,1,0:T(8,128)} custom-call(s32[1]{0:T(128)} %bitcast.23.code_ref, bf16[24,512,1024]{2,1,0:T(8,128)(2,1)} %bitcast.47), custom_call_target="tpu_custom_call" | custom-call | bytes 18874368 | tf_op jit(solution)/shard_map/place/pallas_call | solution.py:71
  533.3 10.3 %place.7 = f32[2,2048,1024]{2,1,0:T(8,128)} custom-call(s32[1]{0:T(128)} %bitcast.23.code_ref, bf16[24,512,1024]{2,1,0:T(8,128)(2,1)} %bitcast.48), custom_call_target="tpu_custom_call" | custom-call | bytes 25165824 | tf_op jit(solution)/shard_map/place/pallas_call | solution.py:71
  543.6 11.3 %place.6 = f32[2,1024,2048]{2,1,0:T(8,128)} custom-call(s32[1]{0:T(128)} %bitcast.23.code_ref, bf16[24,512,1024]{2,1,0:T(8,128)(2,1)} %bitcast.49), custom_call_target="tpu_custom_call" | custom-call | bytes 25165824 | tf_op jit(solution)/shard_map/place/pallas_call | solution.py:71
  554.9 1.5 hand_out.1
  556.4 3.7 widen_rows.1
  (37 shorter events, 0.5 us)
Async XLA Ops:
  1.7 10.9 %collective-permute-start.2 = (s32[384]{0:T(512)S(1)}, s32[384]{0:T(512)S(1)}, u32[]{:S(2)}, u32[]{:S(2)}) collective-permute-start(s32[384]{0:T(512)S(1)} %reshape_squeeze.2), channel_id=1, source_target_pairs={{0,3},{1,2},{2,1},{3,0},{4,7},{5,6},{6,5},{7,4},{8,11},{9,10},{10,... | collective-permute-start | bytes 4616 | tf_op jit(solution)/shard_map/ppermute | solution.py:36
  4.1 8.4 %collective-permute-start = (s32[384]{0:T(512)S(1)}, s32[384]{0:T(512)S(1)}, u32[]{:S(2)}, u32[]{:S(2)}) collective-permute-start(s32[384]{0:T(512)S(1)} %reshape_squeeze.2), channel_id=1, source_target_pairs={{0,1},{1,0},{2,3},{3,2},{4,5},{5,4},{6,7},{7,6},{8,9},{9,8},{10,11... | collective-permute-start | bytes 4616 | tf_op jit(solution)/shard_map/ppermute | solution.py:36
  5.5 7.0 %collective-permute-start.1 = (s32[1408]{0:T(1024)S(1)}, s32[1408]{0:T(1024)S(1)}, u32[]{:S(2)}, u32[]{:S(2)}) collective-permute-start(s32[1408]{0:T(1024)S(1)} %pad_add_fusion), channel_id=1, source_target_pairs={{0,2},{1,3},{2,0},{3,1},{4,6},{5,7},{6,4},{7,5},{8,10},{9,11},{10,... | collective-permute-start | bytes 16904 | tf_op jit(solution)/shard_map/ppermute | solution.py:36
  7.8 9.6 %collective-permute-start.3 = (f32[6144]{0:T(1024)S(1)}, f32[6144]{0:T(1024)S(1)}, u32[]{:S(2)}, u32[]{:S(2)}) collective-permute-start(f32[6144]{0:T(1024)S(1)} %pad_maximum_fusion.4), channel_id=1, source_target_pairs={{0,1},{1,0},{2,3},{3,2},{4,5},{5,4},{6,7},{7,6},{8,9},{9,8},{10,11... | collective-permute-start | bytes 73736 | tf_op jit(solution)/shard_map/ppermute | solution.py:36

commit v10 on v9

--- a/solution.py
+++ b/solution.py
@@ -53,60 +53,69 @@
     return ref[...].reshape(-1, width)
 
 
-def place_kernel(turned, code_ref, g_ref, o_ref, *scratch):
+def place_kernel(turned, rows_too, code_ref, g_ref, *refs):
+    refs = list(refs)
+    sources = [refs.pop(0) for _ in range(rows_too)]
+    o_ref = refs.pop(0)
+    targets = [refs.pop(0) for _ in range(rows_too)]
     code = code_ref[0]
+    step = pl.program_id(0) * pl.num_programs(1) + pl.program_id(1)
+    if rows_too:
+        wide, sem = refs[-2:]
+        copies = [
+            pltpu.make_async_copy(wide.at[n], target.at[:, 0], sem.at[n]) for n, target in enumerate(targets)
+        ]
+
+        @pl.when(step == 0)
+        def _():
+            for n, source in enumerate(sources):
+                wide[n] = source[...].astype(F32)
+                copies[n].start()
+
     for j in range(16):
         start = pl.multiple_of((j ^ code) * 32, 32)
         block = g_ref[0, pl.ds(start, 32), :].astype(F32)
         if turned:
-            scratch[0][j * 32 : (j + 1) * 32, :] = block
+            refs[0][j * 32 : (j + 1) * 32, :] = block
         else:
             o_ref[0, j * 32 : (j + 1) * 32, :] = block
     if turned:
-        o_ref[...] = scratch[0][...].T.reshape(o_ref.shape)
-
-
-def place(sums, shape, block, index, turned, count, group, code):
+        o_ref[...] = refs[0][...].T.reshape(o_ref.shape)
+    if rows_too:
+
+        @pl.when(step == pl.num_programs(0) * pl.num_programs(1) - 1)
+        def _():
+            for copy in copies:
+                copy.wait()
+
+
+def place(sums, shape, block, index, turned, count, group, code, rows_too=()):
     width = sums.shape[-1]
+    anywhere = pl.BlockSpec(memory_space=pl.ANY)
+    scratch = [pltpu.VMEM((512, width), F32)] if turned else []
+    if rows_too:
+        scratch += [
+            pltpu.VMEM((len(rows_too),) + rows_too[0].shape, F32),
+            pltpu.SemaphoreType.DMA((len(rows_too),)),
+        ]
     return pl.pallas_call(
-        functools.partial(place_kernel, turned),
-        out_shape=jax.ShapeDtypeStruct(shape, F32),
+        functools.partial(place_kernel, turned, len(rows_too)),
+        out_shape=[jax.ShapeDtypeStruct(shape, F32)]
+        + [jax.ShapeDtypeStruct((r.shape[0], 1, r.shape[1]), F32) for r in rows_too],
         grid_spec=pltpu.PrefetchScalarGridSpec(
             num_scalar_prefetch=1,
             grid=(shape[0], count),
-            in_specs=[pl.BlockSpec((1, 512, width), lambda l, i, code: (group(l, i), 0, 0))],
-            out_specs=pl.BlockSpec(block, lambda l, i, code: index(l, i)),
-            scratch_shapes=[pltpu.VMEM((512, width), F32)] if turned else [],
+            in_specs=[pl.BlockSpec((1, 512, width), lambda l, i, code: (group(l, i), 0, 0))]
+            + [pl.BlockSpec(r.shape, lambda l, i, code: (0, 0)) for r in rows_too],
+            out_specs=[pl.BlockSpec(block, lambda l, i, code: index(l, i))] + [anywhere for _ in rows_too],
+            scratch_shapes=scratch,
         ),
         compiler_params=pltpu.CompilerParams(vmem_limit_bytes=VMEM_LIMIT),
         cost_estimate=pl.CostEstimate(
             flops=0, bytes_accessed=shape[0] * count * 512 * width * 6, transcendentals=0
         ),
         name="place",
-    )(code, sums)
-
-
-def widen_kernel(a_ref, b_ref, a_out, b_out, a_buf, b_buf, sem):
-    copies = []
-    for n, (source, target, buf) in enumerate(((a_ref, a_out, a_buf), (b_ref, b_out, b_buf))):
-        buf[...] = source[...].astype(F32)
-        copies.append(pltpu.make_async_copy(buf, target.at[:, 0], sem.at[n]))
-        copies[-1].start()
-    for copy in copies:
-        copy.wait()
-
-
-def widen_rows(a, b):
-    rows, width = a.shape
-    out = jax.ShapeDtypeStruct((rows, 1, width), F32)
-    return pl.pallas_call(
-        widen_kernel,
-        out_shape=(out, out),
-        in_specs=[pl.BlockSpec(memory_space=pltpu.VMEM)] * 2,
-        out_specs=(pl.BlockSpec(memory_space=pl.ANY),) * 2,
-        scratch_shapes=[pltpu.VMEM((rows, width), F32), pltpu.VMEM((rows, width), F32), pltpu.SemaphoreType.DMA((2,))],
-        name="widen_rows",
-    )(a, b)
+    )(code, sums, *rows_too)
 
 
 def hand_out_kernel(layers, y_ref, packed, out, down, gain, shift, qv, hidden):
@@ -999,6 +1008,7 @@
         def _():
             there.start() if begin else there.wait()
 
+    swap(1, x_ref, x_out, True)
     load(0, saved[-1][6], r_buf).start()
     start_up = load(1, up_ref, da)
     start_up.start()
@@ -1262,7 +1272,6 @@
         packed[...] += far_buf[n]
 
     swap(0, da, dx_out, True)
-    swap(1, x_ref, x_out, True)
 
     def rest(n, _):
         reduction.tick(done + n)
@@ -1473,18 +1482,20 @@
         upstream_low, stream_low, weights, hot, mask, mask_rows, vectors, saved
     )
     grads = grads.reshape(layers * GROUPS, 512, width)
-    block_output, input_grad = widen_rows(x_low, dx_low)
-
-    def placing(shape, block, index, turned, count, start):
+
+    def placing(shape, block, index, turned, count, start, rows_too=()):
         return place(
-            grads, shape, block, index, turned, count, lambda l, i: (layers - 1 - l) * GROUPS + start + i, code_arg
+            grads, shape, block, index, turned, count, lambda l, i: (layers - 1 - l) * GROUPS + start + i, code_arg,
+            rows_too,
         )
 
     g_b_out, g_b_down, g_gain, g_shift, g_b_qv, g_b_in = hand_out(packed, y.reshape(1).astype(jnp.int32), layers)
-    g_down = placing(w_down.shape, (1, 512, width), lambda l, i: (l, i, 0), False, FF_GROUPS, 0)
-    g_in = placing(w_in.shape, (1, width, 512), lambda l, i: (l, 0, i), True, FF_GROUPS, FF_GROUPS)
-    g_qkv = placing(w_qkv.shape, (1, 1, width, 512), lambda l, i: (l, i, 0, 0), True, 3, 2 * FF_GROUPS + 1)
-    g_out = placing(w_out.shape, (1, 512, width), lambda l, i: (l, 0, 0), False, 1, 2 * FF_GROUPS)
+    g_down, block_output, input_grad = placing(
+        w_down.shape, (1, 512, width), lambda l, i: (l, i, 0), False, FF_GROUPS, 0, (x_low, dx_low)
+    )
+    (g_in,) = placing(w_in.shape, (1, width, 512), lambda l, i: (l, 0, i), True, FF_GROUPS, FF_GROUPS)
+    (g_qkv,) = placing(w_qkv.shape, (1, 1, width, 512), lambda l, i: (l, i, 0, 0), True, 3, 2 * FF_GROUPS + 1)
+    (g_out,) = placing(w_out.shape, (1, 512, width), lambda l, i: (l, 0, 0), False, 1, 2 * FF_GROUPS)
     return (
         block_output,
         input_grad,

time: 566 us -> 559 us (0.988)
  Pallas kernels: 541 us -> 535 us
    pallas_call x5 -> x4, Pallas kernels: 37.6 us -> 36.3 us  [place(): pl.pallas_call(functools.partial(place_kernel, turned, len(rows_too)), ou...]
where the time goes in v10:
time: 559 us; the launch traced here: 554 us
  Pallas kernels  535 us (96%)
  local copies, waits for them, and re-layouts  7.58 us (1%)
    pallas_call x1, Pallas kernels, backward(): pl.pallas_call(functools.partial(backward_kernel, layers), out_shape=(jax...  342 us
    pallas_call x1, Pallas kernels, forward(): pl.pallas_call(functools.partial(forward_kernel, layers), out_shape=(low_...  155 us
    pallas_call x4, Pallas kernels, place(): pl.pallas_call(functools.partial(place_kernel, turned, len(rows_too)), ou...  36.3 us
  transfers between devices with their start and end apart: 4, of which 0 were waited for; matrix products, arithmetic and copies ran while one was open for 2% of the time, Pallas kernels for 0%

profile of v10, /device:TPU:0, one launch (start us, length us, event | category | flops | bytes accessed | tf_op | source)
XLA Modules:
  0.0 554.1 jit_solution(11006817805008672444)
XLA Ops:
  0.6 0.8 copy.31
  1.5 0.2 reshape_squeeze.2
  1.7 2.5 collective-permute-start.2
  4.1 0.6 collective-permute-start
  4.8 0.7 pad_add_fusion
  5.5 0.0 collective-permute-start.1
  5.5 0.8 reshape.210
  6.4 0.1 rev.54
  6.5 0.1 reshape.211
  6.6 0.8 reshape.212
  7.5 0.2 rev.58
  7.7 0.1 reshape.213
  7.8 1.8 collective-permute-start.3
  9.7 0.8 fusion.11
  10.5 0.8 slice_bitcast_fusion.4
  11.3 0.1 stack.19
  11.4 0.1 stack.21
  11.5 0.6 pad_maximum_fusion.2.refs_11_.refs_6_
  12.1 0.1 fusion.8
  12.2 0.1 reshape_reshape.16
  12.3 0.1 reshape_reshape.18
  12.4 0.1 pad.15.clone
  12.5 0.0 collective-permute-done.1
  12.5 0.0 collective-permute-done.2
  12.5 0.0 collective-permute-done
  12.6 0.7 add_select_fusion
  13.3 0.1 rev.47
  13.5 0.2 reshape_reshape.15
  13.7 0.2 copy.32
  13.9 0.1 constant_dynamic-slice_fusion
  14.0 0.1 compare_reduce_fusion
  14.1 0.1 fusion.2
  14.3 0.2 fusion.1
  14.5 0.2 pad.9
  14.7 1.0 pad_maximum_fusion.refs_8_.refs_5_
  15.7 0.8 pad_maximum_fusion.1.refs_6_.refs_3_
  16.6 0.8 copy.38.refs_7_.refs_4_
  17.4 0.0 collective-permute-done.3
  17.5 0.6 copy.41
  18.2 0.7 pad_maximum_fusion.5.refs_9_
  18.9 154.8 %forward.1 = (bf16[2,24,2,256,1024]{4,3,2,1,0:T(8,128)(2,1)}, bf16[512,1024]{1,0:T(8,128)(2,1)}, bf16[512,1024]{1,0:T(8,128)(2,1)}, bf16[3,512,1024]{2,1,0:T(8,1...) custom-call(f32[512,1,1024]{2,1,0:T(1,128)} %refs_0_.1, ...), custom_call_target="tpu_custom_call" | custom-call | flops 32212254720 | bytes 314572800 | tf_op jit(solution)/shard_map/forward/pallas_call | solution.py:879
  173.8 342.3 %backward.1 = (bf16[24,16,32,1024]{3,2,1,0:T(8,128)(2,1)}, bf16[24,16,32,1024]{3,2,1,0:T(8,128)(2,1)}, bf16[512,1024]{1,0:T(8,128)(2,1)}, bf16[512,1024]{1,0:T(8,128)(2,1)}, f32[24,1024]{1,0:T(8,128)}) custom-call(bf16[512,1024]{1,0:T(8,128)(2,1)} %get-tuple-element.56.refs_0_, bf16[512,1024]{1,0:T(8,128)(2,1)} %get-tuple-element.57.refs_1_, ...), custom_call_target="tpu_custom_call" | custom-call | flops 64424509440 | bytes 314572800 | tf_op jit(solution)/shard_map/backward/pallas_call | solution.py:1295
  516.1 3.4 place.6
  519.5 8.9 %place.5 = f32[2,3,1024,512]{3,2,1,0:T(8,128)} custom-call(s32[1]{0:T(128)} %bitcast.code_ref, bf16[24,512,1024]{2,1,0:T(8,128)(2,1)} %bitcast.47), custom_call_target="tpu_custom_call" | custom-call | bytes 18874368 | tf_op jit(solution)/shard_map/place/pallas_call | solution.py:101
  528.4 11.3 %place.7 = f32[2,1024,2048]{2,1,0:T(8,128)} custom-call(s32[1]{0:T(128)} %bitcast.code_ref, bf16[24,512,1024]{2,1,0:T(8,128)(2,1)} %bitcast.48), custom_call_target="tpu_custom_call" | custom-call | bytes 25165824 | tf_op jit(solution)/shard_map/place/pallas_call | solution.py:101
  539.7 1.5 hand_out.1
  541.2 12.7 %place.4 = (f32[2,2048,1024]{2,1,0:T(8,128)}, f32[512,1,1024]{2,1,0:T(1,128)}, f32[512,1,1024]{2,1,0:T(1,128)}) custom-call(s32[1]{0:T(128)} %bitcast.code_ref, bf16[24,512,1024]{2,1,0:T(8,128)(2,1)} %bitcast.49, bf16[512,1024]{1,0:T(8,128)(2,1)} %get-tuple-element.88.refs_0_, bf16[512,1024]{1,0:T(8,128)(2,1)} %get-tuple-element.89.refs_1_), custom_call_target="tpu_custom_call" | custom-call | bytes 25165824 | tf_op jit(solution)/shard_map/place/pallas_call | solution.py:101
  (37 shorter events, 0.5 us)
Async XLA Ops:
  1.7 10.9 %collective-permute-start.2 = (s32[384]{0:T(512)S(1)}, s32[384]{0:T(512)S(1)}, u32[]{:S(2)}, u32[]{:S(2)}) collective-permute-start(s32[384]{0:T(512)S(1)} %reshape_squeeze.2), channel_id=1, source_target_pairs={{0,3},{1,2},{2,1},{3,0},{4,7},{5,6},{6,5},{7,4},{8,11},{9,10},{10,... | collective-permute-start | bytes 4616 | tf_op jit(solution)/shard_map/ppermute | solution.py:36
  4.1 8.4 %collective-permute-start = (s32[384]{0:T(512)S(1)}, s32[384]{0:T(512)S(1)}, u32[]{:S(2)}, u32[]{:S(2)}) collective-permute-start(s32[384]{0:T(512)S(1)} %reshape_squeeze.2), channel_id=1, source_target_pairs={{0,1},{1,0},{2,3},{3,2},{4,5},{5,4},{6,7},{7,6},{8,9},{9,8},{10,11... | collective-permute-start | bytes 4616 | tf_op jit(solution)/shard_map/ppermute | solution.py:36
  5.5 7.0 %collective-permute-start.1 = (s32[1408]{0:T(1024)S(1)}, s32[1408]{0:T(1024)S(1)}, u32[]{:S(2)}, u32[]{:S(2)}) collective-permute-start(s32[1408]{0:T(1024)S(1)} %pad_add_fusion), channel_id=1, source_target_pairs={{0,2},{1,3},{2,0},{3,1},{4,6},{5,7},{6,4},{7,5},{8,10},{9,11},{10,... | collective-permute-start | bytes 16904 | tf_op jit(solution)/shard_map/ppermute | solution.py:36
  7.8 9.6 %collective-permute-start.3 = (f32[6144]{0:T(1024)S(1)}, f32[6144]{0:T(1024)S(1)}, u32[]{:S(2)}, u32[]{:S(2)}) collective-permute-start(f32[6144]{0:T(1024)S(1)} %pad_maximum_fusion.4), channel_id=1, source_target_pairs={{0,1},{1,0},{2,3},{3,2},{4,5},{5,4},{6,7},{7,6},{8,9},{9,8},{10,11... | collective-permute-start | bytes 73736 | tf_op jit(solution)/shard_map/ppermute | solution.py:36

commit v11 on v10

--- a/solution.py
+++ b/solution.py
@@ -400,7 +400,7 @@
     return u * cdf, cdf + u * pdf
 
 
-TILE = 64
+TILE = 128
 
 
 def row_tiles(rows, body):

time: 559 us -> 557 us (level)
  no operation moved by 1% of the time
where the time goes in v11:
time: 557 us; the launch traced here: 552 us
  Pallas kernels  532 us (96%)
  local copies, waits for them, and re-layouts  7.58 us (1%)
    pallas_call x1, Pallas kernels, backward(): pl.pallas_call(functools.partial(backward_kernel, layers), out_shape=(jax...  341 us
    pallas_call x1, Pallas kernels, forward(): pl.pallas_call(functools.partial(forward_kernel, layers), out_shape=(low_...  154 us
    pallas_call x4, Pallas kernels, place(): pl.pallas_call(functools.partial(place_kernel, turned, len(rows_too)), ou...  36.3 us
  transfers between devices with their start and end apart: 4, of which 0 were waited for; matrix products, arithmetic and copies ran while one was open for 2% of the time, Pallas kernels for 0%

profile of v11, /device:TPU:0, one launch (start us, length us, event | category | flops | bytes accessed | tf_op | source)
XLA Modules:
  0.0 551.8 jit_solution(13706101760813679109)
XLA Ops:
  0.6 0.8 copy.31
  1.5 0.2 reshape_squeeze.2
  1.7 2.5 collective-permute-start.2
  4.1 0.6 collective-permute-start
  4.8 0.7 pad_add_fusion
  5.5 0.0 collective-permute-start.1
  5.5 0.8 reshape.210
  6.4 0.1 rev.54
  6.5 0.1 reshape.211
  6.6 0.8 reshape.212
  7.5 0.2 rev.58
  7.7 0.1 reshape.213
  7.8 1.8 collective-permute-start.3
  9.7 0.8 fusion.11
  10.5 0.8 slice_bitcast_fusion.4
  11.3 0.1 stack.19
  11.4 0.1 stack.21
  11.5 0.6 pad_maximum_fusion.2.refs_11_.refs_6_
  12.1 0.1 fusion.8
  12.2 0.1 reshape_reshape.16
  12.3 0.1 reshape_reshape.18
  12.4 0.1 pad.15.clone
  12.5 0.0 collective-permute-done.1
  12.5 0.0 collective-permute-done.2
  12.5 0.0 collective-permute-done
  12.6 0.7 add_select_fusion
  13.3 0.1 rev.47
  13.5 0.2 reshape_reshape.15
  13.7 0.2 copy.32
  13.9 0.1 constant_dynamic-slice_fusion
  14.0 0.1 compare_reduce_fusion
  14.1 0.1 fusion.2
  14.3 0.2 fusion.1
  14.5 0.2 pad.9
  14.7 1.0 pad_maximum_fusion.refs_8_.refs_5_
  15.7 0.8 pad_maximum_fusion.1.refs_6_.refs_3_
  16.6 0.8 copy.38.refs_7_.refs_4_
  17.4 0.0 collective-permute-done.3
  17.5 0.6 copy.41
  18.2 0.7 pad_maximum_fusion.5.refs_9_
  18.9 153.5 %forward.1 = (bf16[2,24,2,256,1024]{4,3,2,1,0:T(8,128)(2,1)}, bf16[512,1024]{1,0:T(8,128)(2,1)}, bf16[512,1024]{1,0:T(8,128)(2,1)}, bf16[3,512,1024]{2,1,0:T(8,1...) custom-call(f32[512,1,1024]{2,1,0:T(1,128)} %refs_0_.1, ...), custom_call_target="tpu_custom_call" | custom-call | flops 32212254720 | bytes 314572800 | tf_op jit(solution)/shard_map/forward/pallas_call | solution.py:879
  172.5 341.0 %backward.1 = (bf16[24,16,32,1024]{3,2,1,0:T(8,128)(2,1)}, bf16[24,16,32,1024]{3,2,1,0:T(8,128)(2,1)}, bf16[512,1024]{1,0:T(8,128)(2,1)}, bf16[512,1024]{1,0:T(8,128)(2,1)}, f32[24,1024]{1,0:T(8,128)}) custom-call(bf16[512,1024]{1,0:T(8,128)(2,1)} %get-tuple-element.56.refs_0_, bf16[512,1024]{1,0:T(8,128)(2,1)} %get-tuple-element.57.refs_1_, ...), custom_call_target="tpu_custom_call" | custom-call | flops 64424509440 | bytes 314572800 | tf_op jit(solution)/shard_map/backward/pallas_call | solution.py:1295
  513.5 3.4 place.6
  516.9 8.9 %place.5 = f32[2,3,1024,512]{3,2,1,0:T(8,128)} custom-call(s32[1]{0:T(128)} %bitcast.code_ref, bf16[24,512,1024]{2,1,0:T(8,128)(2,1)} %bitcast.47), custom_call_target="tpu_custom_call" | custom-call | bytes 18874368 | tf_op jit(solution)/shard_map/place/pallas_call | solution.py:101
  525.8 11.3 %place.7 = f32[2,1024,2048]{2,1,0:T(8,128)} custom-call(s32[1]{0:T(128)} %bitcast.code_ref, bf16[24,512,1024]{2,1,0:T(8,128)(2,1)} %bitcast.48), custom_call_target="tpu_custom_call" | custom-call | bytes 25165824 | tf_op jit(solution)/shard_map/place/pallas_call | solution.py:101
  537.2 1.5 hand_out.1
  538.7 12.7 %place.4 = (f32[2,2048,1024]{2,1,0:T(8,128)}, f32[512,1,1024]{2,1,0:T(1,128)}, f32[512,1,1024]{2,1,0:T(1,128)}) custom-call(s32[1]{0:T(128)} %bitcast.code_ref, bf16[24,512,1024]{2,1,0:T(8,128)(2,1)} %bitcast.49, bf16[512,1024]{1,0:T(8,128)(2,1)} %get-tuple-element.88.refs_0_, bf16[512,1024]{1,0:T(8,128)(2,1)} %get-tuple-element.89.refs_1_), custom_call_target="tpu_custom_call" | custom-call | bytes 25165824 | tf_op jit(solution)/shard_map/place/pallas_call | solution.py:101
  (37 shorter events, 0.5 us)
Async XLA Ops:
  1.7 10.9 %collective-permute-start.2 = (s32[384]{0:T(512)S(1)}, s32[384]{0:T(512)S(1)}, u32[]{:S(2)}, u32[]{:S(2)}) collective-permute-start(s32[384]{0:T(512)S(1)} %reshape_squeeze.2), channel_id=1, source_target_pairs={{0,3},{1,2},{2,1},{3,0},{4,7},{5,6},{6,5},{7,4},{8,11},{9,10},{10,... | collective-permute-start | bytes 4616 | tf_op jit(solution)/shard_map/ppermute | solution.py:36
  4.1 8.4 %collective-permute-start = (s32[384]{0:T(512)S(1)}, s32[384]{0:T(512)S(1)}, u32[]{:S(2)}, u32[]{:S(2)}) collective-permute-start(s32[384]{0:T(512)S(1)} %reshape_squeeze.2), channel_id=1, source_target_pairs={{0,1},{1,0},{2,3},{3,2},{4,5},{5,4},{6,7},{7,6},{8,9},{9,8},{10,11... | collective-permute-start | bytes 4616 | tf_op jit(solution)/shard_map/ppermute | solution.py:36
  5.5 7.0 %collective-permute-start.1 = (s32[1408]{0:T(1024)S(1)}, s32[1408]{0:T(1024)S(1)}, u32[]{:S(2)}, u32[]{:S(2)}) collective-permute-start(s32[1408]{0:T(1024)S(1)} %pad_add_fusion), channel_id=1, source_target_pairs={{0,2},{1,3},{2,0},{3,1},{4,6},{5,7},{6,4},{7,5},{8,10},{9,11},{10,... | collective-permute-start | bytes 16904 | tf_op jit(solution)/shard_map/ppermute | solution.py:36
  7.8 9.6 %collective-permute-start.3 = (f32[6144]{0:T(1024)S(1)}, f32[6144]{0:T(1024)S(1)}, u32[]{:S(2)}, u32[]{:S(2)}) collective-permute-start(f32[6144]{0:T(1024)S(1)} %pad_maximum_fusion.4), channel_id=1, source_target_pairs={{0,1},{1,0},{2,3},{3,2},{4,5},{5,4},{6,7},{7,6},{8,9},{9,8},{10,11... | collective-permute-start | bytes 73736 | tf_op jit(solution)/shard_map/ppermute | solution.py:36
